TPU v7x, 512 devices: a whole 4x8x8 slice. The times are simulated.
512 devices in a mesh: seq: 64 (over z, x, y_lo), tp: 8 (over y_hi, core).
Axes of the slice: x: 4, y: 8 (y_hi: 4, y_lo: 2; y = y_hi * 2 + y_lo), z: 8, core: 2. Of those that a mesh axis runs over, the one named last changes fastest.
Arguments:
- tokens: bfloat16 [16384, 3200], P('seq'), may hold values from -8 to 8
- norm_gain: float32 [3200], replicated, may hold values from 0.5 to 1.5
- qkv_weight: bfloat16 [3200, 3, 2048], P('seq', None, 'tp'), may hold values from -1 to 1
- q_gain: float32 [2048], P('tp'), may hold values from 0.5 to 5, as said below
- k_gain: float32 [2048], P('tp'), may hold values from 0.5 to 5, as said below
- out_weight: bfloat16 [2048, 3200], P('tp', 'seq'), may hold values from -0.125 to 0.125
- layer_scale: float32 [3200], P('tp'), may hold values from 0.5 to 2
- segment_ids: int32 [16384], replicated, may hold values from 0 to 63, never falling along the last dimension, each value on 1 to 512 neighbouring positions
Outputs:
- mixed: bfloat16 [16384, 3200], P('seq', 'tp')
Inputs may be any that keep to these rules, and one draw needn't show every extreme that they name: `segment_ids`: image numbers never fall along the row; each image has 1 to 512 patches, one exactly 512. `q_gain`: positive gains. `k_gain`: positive gains.
All inputs are finite; a program needn't handle non-finite values.
Results may differ from a plain program's by a relative error of at most 0.0078.
Values may be sent and summed in bfloat16 or wider, within the bound.
A program may use at most 64 MiB of HBM per device.

v0:
```python
import jax
import jax.numpy as jnp
from jax import lax
from jax.sharding import PartitionSpec as P

HEAD_DIM = 128


eps = 1e-06
floor_score = -1e30


def passed_along(x, axis, by):
    size = lax.axis_size(axis)
    pairs = [(i, i + by) for i in range(size) if 0 <= i + by < size]
    return lax.ppermute(x, axis, pairs)


def masked_scores(query, keys, query_seg, key_seg):
    scores = jnp.einsum(
        "qhd,khd->hqk", query, keys, preferred_element_type=jnp.float32
    ) * HEAD_DIM ** (-0.5)
    mask = (query_seg[:, None] == key_seg[None, :])[None]
    return (jnp.where(mask, scores, floor_score), mask)


def shards(tokens, norm_gain, qkv_weight, q_gain, k_gain, out_weight, layer_scale, segment_ids):
    count = tokens.shape[0]
    source = tokens.astype(jnp.float32)
    normed = (
        source * lax.rsqrt(jnp.mean(source * source, axis=-1, keepdims=True) + eps) * norm_gain
    ).astype(jnp.bfloat16)
    local_width = qkv_weight.shape[2]
    heads = local_width // HEAD_DIM
    joined = jnp.einsum(
        "td,dch->tch",
        normed,
        lax.all_gather(qkv_weight, "seq", axis=0, tiled=True),
        preferred_element_type=jnp.float32,
    )
    query = joined[:, 0]
    keys = joined[:, 1]
    values = joined[:, 2]
    query_sq, key_sq = lax.psum(
        (jnp.sum(query * query, axis=-1), jnp.sum(keys * keys, axis=-1)), "tp"
    )
    full_width = local_width * lax.axis_size("tp")
    query_normed = (query * lax.rsqrt(query_sq / full_width + eps)[:, None] * q_gain).astype(
        jnp.bfloat16
    )
    key_normed = (keys * lax.rsqrt(key_sq / full_width + eps)[:, None] * k_gain).astype(
        jnp.bfloat16
    )
    paired = jnp.stack([key_normed, values.astype(jnp.bfloat16)], axis=1)
    pieces = []
    for offset in (2, 1, 0, -1, -2):
        if offset == 0:
            pieces.append(paired)
        else:
            pieces.append(passed_along(paired, "seq", offset))
    widened = jnp.concatenate(pieces, axis=0)
    position = lax.axis_index("seq")
    outside = jnp.full((2 * count,), -1, jnp.int32)
    seg_pad = jnp.concatenate([outside, segment_ids, outside], axis=0)
    key_seg = lax.dynamic_slice_in_dim(seg_pad, position * count, 5 * count, 0)
    query_seg = lax.dynamic_slice_in_dim(segment_ids, position * count, count, 0)
    query_heads = query_normed.reshape(count, heads, HEAD_DIM)
    key_heads = widened[:, 0].reshape(5 * count, heads, HEAD_DIM)
    value_heads = widened[:, 1].reshape(5 * count, heads, HEAD_DIM)
    scores, mask = masked_scores(query_heads, key_heads, query_seg, key_seg)
    peak = jnp.max(scores, axis=-1, keepdims=True)
    weights = jnp.where(mask, jnp.exp(scores - peak), 0.0)
    total = jnp.sum(weights, axis=-1)
    probs = weights.astype(jnp.bfloat16)
    summed = jnp.einsum("hqk,khd->qhd", probs, value_heads, preferred_element_type=jnp.float32)
    context = (
        (summed / jnp.transpose(total)[:, :, None]).reshape(count, local_width).astype(jnp.bfloat16)
    )
    terms = jnp.dot(
        context,
        lax.all_gather(out_weight, "seq", axis=1, tiled=True),
        preferred_element_type=jnp.float32,
    )
    projected = lax.psum_scatter(terms, "tp", scatter_dimension=1, tiled=True)
    share = layer_scale.shape[0]
    residual = lax.dynamic_slice_in_dim(source, lax.axis_index("tp") * share, share, 1)
    return (residual + layer_scale * projected).astype(jnp.bfloat16)


def solution(mesh):
    return jax.shard_map(
        shards,
        mesh=mesh,
        in_specs=(
            P("seq", None),
            P(),
            P("seq", None, "tp"),
            P("tp"),
            P("tp"),
            P("tp", "seq"),
            P("tp"),
            P(),
        ),
        out_specs=P("seq", "tp"),
        check_vma=False,
    )
```

profile of v0, /device:TPU:31, one launch (start us, length us, event | category | flops | bytes accessed | tf_op | source)
XLA Modules:
  0.0 731.1 jit_solution(13992945000066790552)
XLA Ops:
  6.5 0.0 all-gather.4.cloned.1.call-start
  6.5 1.6 copy.18
  8.1 0.0 all-gather.4.cloned.1.call-update
  8.2 0.0 all-gather.6.cloned.1.call-start
  8.2 0.7 all-gather.6.cloned.1.call-update
  8.9 0.0 reduce-scatter.2.cloned.1.call-start
  9.0 3.0 copy.17
  12.0 0.0 copy-done.1
  12.0 0.1 dynamic_slice.10
  12.1 0.1 fusion.24
  12.2 0.5 multiply_reduce_fusion
  12.6 0.0 copy-start.3
  12.6 271.9 %all-gather.4.cloned.1.call-done = bf16[3200,3,256]{2,1,0:T(4,128)(2,1)} async-done(((bf16[50,3,256]{2,1,0:T(4,128)(2,1)}), bf16[3200,3,256]{2,1,0:T(4,128)(2,1)}) %all-gather.4.cloned.1.call-update) | async-done | bytes 4915216 | tf_op jit(solution)/shard_map/all_gather | solution.py:38
  284.5 0.0 copy-done.5
  284.5 5.3 fusion.1
  289.8 0.1 multiply_reduce_fusion.1
  289.9 54.9 %all-reduce = (f32[256]{0:T(256)S(1)}, f32[256]{0:T(256)S(1)}) all-reduce(f32[256]{0:T(256)S(1)} %get-tuple-element.6, f32[256]{0:T(256)S(1)} %get-tuple-element.5), channel_id=1, replica_groups=mesh['seq'=64,'tp'=8] {'tp'}, use_global_device_ids=true, to_apply=%region_2.0 | all-reduce | flops 512 | bytes 4096 | tf_op jit(solution)/shard_map/psum | solution.py:44
  344.9 0.0 copy-done.3
  344.9 0.7 fusion.35
  345.6 0.7 pad_maximum_fusion
  346.3 2.4 collective-permute-start
  348.7 1.0 broadcast_compare_fusion
  349.7 234.7 %all-gather.6.cloned.1.call-done = bf16[64,50,256]{2,1,0:T(8,128)(2,1)} async-done(((bf16[1,50,256]{2,1,0:T(8,128)(2,1)}), bf16[64,50,256]{2,1,0:T(8,128)(2,1)}) %all-gather.6.cloned.1.call-update) | async-done | bytes 1638416 | tf_op jit(solution)/shard_map/all_gather | solution.py:81
  584.4 2.5 reshape.70
  586.9 5.1 collective-permute-start.1
  592.0 2.6 collective-permute-start.2
  594.7 6.4 collective-permute-start.3
  601.1 1.8 copy.21
  602.9 0.0 copy-done.4
  602.9 1.7 multiply_convert_fusion.1
  604.6 0.0 collective-permute-done
  604.6 1.0 constant_dynamic-update-slice_fusion.4
  605.6 0.0 collective-permute-done.1
  605.6 1.0 constant_dynamic-update-slice_fusion.3
  606.6 0.0 copy-start
  606.6 0.0 collective-permute-done.2
  606.6 1.0 constant_dynamic-update-slice_fusion.1
  607.6 0.0 collective-permute-done.3
  607.6 1.0 constant_dynamic-update-slice_fusion
  608.6 1.2 fusion.34
  609.7 2.6 fusion.36
  612.4 2.8 fusion.20
  615.2 2.3 fusion.37
  617.5 0.0 reduce-scatter.2.cloned.1.call-update
  617.5 0.0 copy-start.2
  617.5 2.0 convert_element_type.28
  619.5 103.2 %reduce-scatter.2.cloned.1.call-done = f32[256,400]{0,1:T(8,128)} async-done(((f32[256,3200]{0,1:T(8,128)}), f32[256,400]{0,1:T(8,128)}) %reduce-scatter.2.cloned.1.call-update) | async-done | bytes 409616 | tf_op jit(solution)/shard_map/reduce_scatter | solution.py:84
  722.7 1.9 add_convert_fusion
  (10 shorter events, 0.1 us)
Async XLA Ops:
  6.5 5.4 copy-start.1
  6.5 277.9 %all-gather.4.cloned.1.call-start = ((), (), s32[]{:S(2)}) async-start(), calls=%async_computation.1 | async-start | bytes 6656000 | tf_op jit(solution)/shard_map/all_gather | solution.py:38
  8.1 276.3 %copy-start.5 = (f32[3200]{0:T(1024)S(1)}, f32[3200]{0:T(1024)}, u32[]{:S(2)}) copy-start(f32[3200]{0:T(1024)} %param.9) | copy-start | bytes 38404
  8.2 576.2 %all-gather.6.cloned.1.call-start = ((), (), s32[]{:S(2)}) async-start(), calls=%async_computation.3 | async-start | bytes 1863680 | tf_op jit(solution)/shard_map/all_gather | solution.py:81
  8.9 713.8 %reduce-scatter.2.cloned.1.call-start = ((), (), s32[]{:S(2)}) async-start(), calls=%async_computation.2 | async-start | bytes 3686400 | tf_op jit(solution)/shard_map/reduce_scatter | solution.py:84
  12.6 332.2 %copy-start.3 = (f32[256]{0:T(256)S(1)}, f32[256]{0:T(256)}, u32[]{:S(2)}) copy-start(f32[256]{0:T(256)} %param.12) | copy-start | bytes 3076
  345.6 257.3 %copy-start.4 = (f32[256]{0:T(256)S(1)}, f32[256]{0:T(256)}, u32[]{:S(2)}) copy-start(f32[256]{0:T(256)} %param.11) | copy-start | bytes 3076
  346.3 258.3 %collective-permute-start = (bf16[256,2,256]{0,2,1:T(8,128)(2,1)}, bf16[256,2,256]{0,2,1:T(8,128)(2,1)}, u32[]{:S(2)}, u32[]{:S(2)}) collective-permute-start(bf16[256,2,256]{0,2,1:T(8,128)(2,1)} %pad_maximum_fusion), channel_id=1, source_target_pairs={{0,16},{8,24},{16,32},{24,40},{32,48},{40,56},{48,64},{56,72},{64,... | collective-permute-start | bytes 786440 | tf_op jit(solution)/shard_map/ppermute | solution.py:16
  586.9 18.7 %collective-permute-start.1 = (bf16[256,2,256]{0,2,1:T(8,128)(2,1)}, bf16[256,2,256]{0,2,1:T(8,128)(2,1)}, u32[]{:S(2)}, u32[]{:S(2)}) collective-permute-start(bf16[256,2,256]{0,2,1:T(8,128)(2,1)} %pad_maximum_fusion), channel_id=1, source_target_pairs={{0,8},{8,16},{16,24},{24,32},{32,40},{40,48},{48,56},{56,64},{64,7... | collective-permute-start | bytes 786440 | tf_op jit(solution)/shard_map/ppermute | solution.py:16
  592.0 14.6 %collective-permute-start.2 = (bf16[256,2,256]{0,2,1:T(8,128)(2,1)}, bf16[256,2,256]{0,2,1:T(8,128)(2,1)}, u32[]{:S(2)}, u32[]{:S(2)}) collective-permute-start(bf16[256,2,256]{0,2,1:T(8,128)(2,1)} %pad_maximum_fusion), channel_id=1, source_target_pairs={{8,0},{16,8},{24,16},{32,24},{40,32},{48,40},{56,48},{64,56},{72,6... | collective-permute-start | bytes 786440 | tf_op jit(solution)/shard_map/ppermute | solution.py:16
  594.7 12.9 %collective-permute-start.3 = (bf16[256,2,256]{0,2,1:T(8,128)(2,1)}, bf16[256,2,256]{0,2,1:T(8,128)(2,1)}, u32[]{:S(2)}, u32[]{:S(2)}) collective-permute-start(bf16[256,2,256]{0,2,1:T(8,128)(2,1)} %pad_maximum_fusion), channel_id=1, source_target_pairs={{16,0},{24,8},{32,16},{40,24},{48,32},{56,40},{64,48},{72,56},{80,... | collective-permute-start | bytes 786440 | tf_op jit(solution)/shard_map/ppermute | solution.py:16
  606.6 3.2 copy-start
  617.5 105.2 %copy-start.2 = (f32[400]{0:T(512)S(1)}, f32[400]{0:T(512)}, u32[]{:S(2)}) copy-start(f32[400]{0:T(512)} %param.14) | copy-start | bytes 4804
Sparse Core Ops, SparseCore 0:
  9.4 275.0 all-gather.3
  286.6 297.7 all-gather.5
  617.6 105.0 reduce-scatter.1
where the time goes:
time: 732 us; the launch traced here: 731 us
  waiting for transfers between devices  611 us (83%)
  blocking collectives  54.9 us (8%)
  starting transfers between devices  16.6 us (2%)
  local copies, waits for them, and re-layouts  14.1 us (2%)
  between operations  13.3 us (2%)
  matrix products  13 us (2%)
  other arithmetic  8.7 us (1%)
    all_gather x1, waiting for transfers between devices, shards(): lax.all_gather(qkv_weight, 'seq', axis=0, tiled=True)  272 us
    all_gather x1, waiting for transfers between devices, shards(): lax.all_gather(out_weight, 'seq', axis=1, tiled=True)  235 us
    reduce_scatter x1, waiting for transfers between devices, shards(): projected = lax.psum_scatter(terms, 'tp', scatter_dimension=1, tiled=True)  103 us
    psum x1, blocking collectives, shards(): lax.psum((jnp.sum(query * query, axis=-1), jnp.sum(keys * keys, axis=-1))...  54.9 us
    ppermute x4, starting transfers between devices, passed_along(): return lax.ppermute(x, axis, pairs)  16.5 us
  transfers between devices with their start and end apart: 7, of which 3 were waited for; matrix products, arithmetic and copies ran while one was open for 3% of the time, Pallas kernels for 0%

commit v1 on v0

--- a/solution.py
+++ b/solution.py
@@ -32,10 +32,12 @@
     ).astype(jnp.bfloat16)
     local_width = qkv_weight.shape[2]
     heads = local_width // HEAD_DIM
+    stacked = jnp.concatenate([qkv_weight, jnp.transpose(out_weight)[:, None, :]], axis=1)
+    gathered = lax.all_gather(stacked, "seq", axis=0, tiled=True)
     joined = jnp.einsum(
         "td,dch->tch",
         normed,
-        lax.all_gather(qkv_weight, "seq", axis=0, tiled=True),
+        gathered[:, :3],
         preferred_element_type=jnp.float32,
     )
     query = joined[:, 0]
@@ -76,10 +78,8 @@
     context = (
         (summed / jnp.transpose(total)[:, :, None]).reshape(count, local_width).astype(jnp.bfloat16)
     )
-    terms = jnp.dot(
-        context,
-        lax.all_gather(out_weight, "seq", axis=1, tiled=True),
-        preferred_element_type=jnp.float32,
+    terms = jnp.einsum(
+        "th,dh->td", context, gathered[:, 3], preferred_element_type=jnp.float32
     )
     projected = lax.psum_scatter(terms, "tp", scatter_dimension=1, tiled=True)
     share = layer_scale.shape[0]

time: 732 us -> 452 us (0.62)
  the two profiles are of different devices: /device:TPU:31 before, /device:TPU:27 now
where the time goes in v1:
time: 452 us
  waiting for transfers between devices  335 us (74%)
  blocking collectives  55.5 us (12%)
  local copies, waits for them, and re-layouts  15 us (3%)
  starting transfers between devices  14.5 us (3%)
  between operations  13.6 us (3%)
  matrix products  12.3 us (3%)
  other arithmetic  6.43 us (1%)
    all_gather x1, waiting for transfers between devices, shards(): gathered = lax.all_gather(stacked, 'seq', axis=0, tiled=True)  279 us
    reduce_scatter x1, waiting for transfers between devices, shards(): projected = lax.psum_scatter(terms, 'tp', scatter_dimension=1, tiled=True)  55.5 us
    psum x1, blocking collectives, shards(): lax.psum((jnp.sum(query * query, axis=-1), jnp.sum(keys * keys, axis=-1))...  55.5 us
    ppermute x4, starting transfers between devices, passed_along(): return lax.ppermute(x, axis, pairs)  14.4 us
  transfers between devices with their start and end apart: 6, of which 3 were waited for; matrix products, arithmetic and copies ran while one was open for 4% of the time, Pallas kernels for 0%

profile of v1, /device:TPU:27, one launch (start us, length us, event | category | flops | bytes accessed | tf_op | source)
XLA Modules:
  0.0 451.8 jit_solution(6886616252011911383)
XLA Ops:
  6.5 0.0 copy-start.1
  6.5 0.0 all-gather.2.cloned.1.call-start
  6.5 1.0 copy.22
  7.5 0.8 copy.23
  8.3 0.8 pad_maximum_fusion.1
  9.1 0.0 copy-start.5
  9.1 0.0 all-gather.2.cloned.1.call-update
  9.1 0.0 reduce-scatter.2.cloned.1.call-start
  9.1 3.0 copy.21
  12.1 0.0 copy-done.1
  12.1 0.1 dynamic_slice.10
  12.2 0.1 fusion.25
  12.3 0.5 multiply_reduce_fusion
  12.8 278.5 %all-gather.2.cloned.1.call-done = bf16[3200,4,256]{2,1,0:T(4,128)(2,1)} async-done(((bf16[50,4,256]{2,1,0:T(4,128)(2,1)}), bf16[3200,4,256]{2,1,0:T(4,128)(2,1)}) %all-gather.2.cloned.1.call-update) | async-done | bytes 6553616 | tf_op jit(solution)/shard_map/all_gather | solution.py:36
  291.3 0.0 copy-done.5
  291.3 5.3 %fusion.1 = f32[256,3,256]{0,2,1:T(8,128)S(1)} fusion(bf16[3200,3,256]{2,1,0:T(4,128)(2,1)} %bitcast.28, f32[3200]{0:T(1024)S(1)} %copy-done.5, f32[256]{0:T(256)S(1)} %add_rsqrt_fusion.2, bf16[256,3200]{0,1:T(8,128)(2,1)S(1)} %copy.21), kind=kOutput, calls=%fused_computation.1 | convolution fusion | flops 1261568000 | bytes 7353856 | tf_op jit(solution)/shard_map/td,dch->tch/dot_general | solution.py:37
  296.7 0.1 multiply_reduce_fusion.1
  296.7 55.5 %all-reduce = (f32[256]{0:T(256)S(1)}, f32[256]{0:T(256)S(1)}) all-reduce(f32[256]{0:T(256)S(1)} %get-tuple-element.6, f32[256]{0:T(256)S(1)} %get-tuple-element.5), channel_id=1, replica_groups=mesh['seq'=64,'tp'=8] {'tp'}, use_global_device_ids=true, to_apply=%region_2.0 | all-reduce | flops 512 | bytes 4096 | tf_op jit(solution)/shard_map/psum | solution.py:46
  352.2 0.0 copy-done.3
  352.2 0.1 fusion.36
  352.4 1.9 collective-permute-start
  354.3 0.2 broadcast_compare_fusion
  354.6 3.5 collective-permute-start.1
  358.0 4.9 %collective-permute-start.2 = (bf16[256,2,256]{0,2,1:T(8,128)(2,1)S(1)}, bf16[256,2,256]{0,2,1:T(8,128)(2,1)S(1)}, u32[]{:S(2)}, u32[]{:S(2)}) collective-permute-start(bf16[256,2,256]{0,2,1:T(8,128)(2,1)S(1)} %pad_maximum_fusion), channel_id=1, source_target_pairs={{8,0},{16,8},{24,16},{32,24},{40,32},{48,40},{56,48},{64,56},{72,6... | collective-permute-start | bytes 786440 | tf_op jit(solution)/shard_map/ppermute | solution.py:16
  363.0 4.1 collective-permute-start.3
  367.1 0.1 copy.26
  367.2 0.0 copy-start.4
  367.2 7.6 %slice.29 = bf16[3200,1,256]{2,1,0:T(2,128)(2,1)} slice(bf16[3200,4,256]{2,1,0:T(4,128)(2,1)} %all-gather.2.cloned.1.call-done), slice={[0:3200], [3:4], [0:256]} | slice | bytes 3276800 | tf_op jit(solution)/shard_map/slice | solution.py:82
  374.8 0.0 copy-done.4
  374.8 0.8 multiply_convert_fusion.1
  375.6 0.0 collective-permute-done
  375.6 1.0 constant_dynamic-update-slice_fusion.4
  376.6 0.0 collective-permute-done.1
  376.6 1.0 constant_dynamic-update-slice_fusion.3
  377.6 0.0 collective-permute-done.2
  377.6 0.0 copy-start
  377.6 0.4 collective-permute-done.3
  378.0 0.1 fusion.35
  378.1 0.4 copy-done
  378.5 1.4 fusion.37
  379.9 1.4 fusion.21
  381.3 4.2 fusion.9
  385.5 0.0 reduce-scatter.2.cloned.1.call-update
  385.5 0.0 copy-start.2
  385.5 2.0 convert_element_type.28
  387.5 55.5 %reduce-scatter.2.cloned.1.call-done = f32[256,400]{0,1:T(8,128)} async-done(((f32[256,3200]{0,1:T(8,128)}), f32[256,400]{0,1:T(8,128)}) %reduce-scatter.2.cloned.1.call-update) | async-done | bytes 409616 | tf_op jit(solution)/shard_map/reduce_scatter | solution.py:84
  443.0 0.0 copy-done.2
  443.0 1.9 add_convert_fusion
  (9 shorter events, 0.1 us)
Async XLA Ops:
  6.5 5.6 %copy-start.1 = (s32[16384]{0:T(1024)S(1)}, s32[16384]{0:T(1024)}, u32[]{:S(2)}) copy-start(s32[16384]{0:T(1024)} %param.15) | copy-start | bytes 196612
  6.5 284.8 %all-gather.2.cloned.1.call-start = ((), (), s32[]{:S(2)}) async-start(), calls=%async_computation.1 | async-start | bytes 6656000 | tf_op jit(solution)/shard_map/all_gather | solution.py:36
  9.1 282.3 %copy-start.5 = (f32[3200]{0:T(1024)S(1)}, f32[3200]{0:T(1024)}, u32[]{:S(2)}) copy-start(f32[3200]{0:T(1024)} %param.9) | copy-start | bytes 38404
  9.1 433.9 %reduce-scatter.2.cloned.1.call-start = ((), (), s32[]{:S(2)}) async-start(), calls=%async_computation.2 | async-start | bytes 3686400 | tf_op jit(solution)/shard_map/reduce_scatter | solution.py:84
  291.3 60.9 %copy-start.3 = (f32[256]{0:T(256)S(1)}, f32[256]{0:T(256)}, u32[]{:S(2)}) copy-start(f32[256]{0:T(256)} %param.12) | copy-start | bytes 3076
  352.4 23.2 %collective-permute-start = (bf16[256,2,256]{0,2,1:T(8,128)(2,1)S(1)}, bf16[256,2,256]{0,2,1:T(8,128)(2,1)}, u32[]{:S(2)}, u32[]{:S(2)}) collective-permute-start(bf16[256,2,256]{0,2,1:T(8,128)(2,1)S(1)} %pad_maximum_fusion), channel_id=1, source_target_pairs={{0,16},{8,24},{16,32},{24,40},{32,48},{40,56},{48,64},{56,72},{64,... | collective-permute-start | bytes 786440 | tf_op jit(solution)/shard_map/ppermute | solution.py:16
  354.6 22.0 %collective-permute-start.1 = (bf16[256,2,256]{0,2,1:T(8,128)(2,1)S(1)}, bf16[256,2,256]{0,2,1:T(8,128)(2,1)}, u32[]{:S(2)}, u32[]{:S(2)}) collective-permute-start(bf16[256,2,256]{0,2,1:T(8,128)(2,1)S(1)} %pad_maximum_fusion), channel_id=1, source_target_pairs={{0,8},{8,16},{16,24},{24,32},{32,40},{40,48},{48,56},{56,64},{64,7... | collective-permute-start | bytes 786440 | tf_op jit(solution)/shard_map/ppermute | solution.py:16
  358.0 19.5 %collective-permute-start.2 = (bf16[256,2,256]{0,2,1:T(8,128)(2,1)S(1)}, bf16[256,2,256]{0,2,1:T(8,128)(2,1)S(1)}, u32[]{:S(2)}, u32[]{:S(2)}) collective-permute-start(bf16[256,2,256]{0,2,1:T(8,128)(2,1)S(1)} %pad_maximum_fusion), channel_id=1, source_target_pairs={{8,0},{16,8},{24,16},{32,24},{40,32},{48,40},{56,48},{64,56},{72,6... | collective-permute-start | bytes 786440 | tf_op jit(solution)/shard_map/ppermute | solution.py:16
  363.0 15.0 %collective-permute-start.3 = (bf16[256,2,256]{0,2,1:T(8,128)(2,1)S(1)}, bf16[256,2,256]{0,2,1:T(8,128)(2,1)S(1)}, u32[]{:S(2)}, u32[]{:S(2)}) collective-permute-start(bf16[256,2,256]{0,2,1:T(8,128)(2,1)S(1)} %pad_maximum_fusion), channel_id=1, source_target_pairs={{16,0},{24,8},{32,16},{40,24},{48,32},{56,40},{64,48},{72,56},{80,... | collective-permute-start | bytes 786440 | tf_op jit(solution)/shard_map/ppermute | solution.py:16
  367.2 7.6 %copy-start.4 = (f32[256]{0:T(256)S(1)}, f32[256]{0:T(256)}, u32[]{:S(2)}) copy-start(f32[256]{0:T(256)} %param.11) | copy-start | bytes 3076
  377.6 0.9 copy-start
  385.5 57.5 %copy-start.2 = (f32[400]{0:T(512)S(1)}, f32[400]{0:T(512)}, u32[]{:S(2)}) copy-start(f32[400]{0:T(512)} %param.14) | copy-start | bytes 4804
Sparse Core Ops, SparseCore 0:
  9.4 281.8 all-gather.1
  385.6 57.3 reduce-scatter.1

commit v2 on v1

--- a/solution.py
+++ b/solution.py
@@ -1,7 +1,11 @@
+import functools
+
 import jax
 import jax.numpy as jnp
 from jax import lax
 from jax.sharding import PartitionSpec as P
+from jax.experimental import pallas as pl
+from jax.experimental.pallas import tpu as pltpu
 
 HEAD_DIM = 128
 
@@ -14,6 +18,64 @@
     size = lax.axis_size(axis)
     pairs = [(i, i + by) for i in range(size) if 0 <= i + by < size]
     return lax.ppermute(x, axis, pairs)
+
+
+def gather_kernel(n, x_ref, out_ref, send_sem, recv_sem, local_sem):
+    me = lax.axis_index("seq")
+    tp = lax.axis_index("tp")
+    mesh_id = pl.DeviceIdType.MESH
+    barrier = pltpu.get_barrier_semaphore()
+
+    def greet(k, carry):
+        peer = lax.rem(me + k, n)
+        pl.semaphore_signal(barrier, inc=1, device_id=(peer, tp), device_id_type=mesh_id)
+        return carry
+
+    lax.fori_loop(1, n, greet, 0)
+    pl.semaphore_wait(barrier, n - 1)
+    local = pltpu.make_async_copy(x_ref, out_ref.at[me], local_sem)
+    local.start()
+
+    def remote(k):
+        peer = lax.rem(me + k, n)
+        return pltpu.make_async_remote_copy(
+            src_ref=x_ref,
+            dst_ref=out_ref.at[me],
+            send_sem=send_sem.at[k],
+            recv_sem=recv_sem.at[k],
+            device_id=(peer, tp),
+            device_id_type=mesh_id,
+        )
+
+    def send(k, carry):
+        remote(k).start()
+        return carry
+
+    def finish(k, carry):
+        copy = remote(k)
+        copy.wait_send()
+        copy.wait_recv()
+        return carry
+
+    lax.fori_loop(1, n, send, 0)
+    lax.fori_loop(1, n, finish, 0)
+    local.wait()
+
+
+def gather_seq(block):
+    n = lax.axis_size("seq")
+    return pl.pallas_call(
+        functools.partial(gather_kernel, n),
+        out_shape=jax.ShapeDtypeStruct((n,) + block.shape, block.dtype),
+        in_specs=[pl.BlockSpec(memory_space=pl.ANY)],
+        out_specs=pl.BlockSpec(memory_space=pl.ANY),
+        scratch_shapes=[
+            pltpu.SemaphoreType.DMA((n,)),
+            pltpu.SemaphoreType.DMA((n,)),
+            pltpu.SemaphoreType.DMA(()),
+        ],
+        compiler_params=pltpu.CompilerParams(collective_id=0, has_side_effects=True),
+    )(block)
 
 
 def masked_scores(query, keys, query_seg, key_seg):
@@ -33,7 +95,8 @@
     local_width = qkv_weight.shape[2]
     heads = local_width // HEAD_DIM
     stacked = jnp.concatenate([qkv_weight, jnp.transpose(out_weight)[:, None, :]], axis=1)
-    gathered = lax.all_gather(stacked, "seq", axis=0, tiled=True)
+    rows, kinds, width = stacked.shape
+    gathered = gather_seq(stacked.reshape(rows, kinds * width)).reshape(-1, kinds, width)
     joined = jnp.einsum(
         "td,dch->tch",
         normed,

time: 452 us -> 326 us (0.72)
  waiting for transfers between devices: 335 us -> 55 us
  Pallas kernels: 0 us -> 180 us
  blocking collectives: 55.5 us -> 18.8 us
  local copies, waits for them, and re-layouts: 15 us -> 25.6 us
    all_gather x1 -> x0, waiting for transfers between devices: 279 us -> none  [shards(): gathered = lax.all_gather(stacked, 'seq', axis=0, tiled=True)]
    pallas_call x0 -> x1, Pallas kernels: none -> 180 us  [gather_seq(): pl.pallas_call(functools.partial(gather_kernel, n), out_shape=jax.ShapeDt...]
    psum x1, blocking collectives: 55.5 us -> 18.8 us  [shards(): lax.psum((jnp.sum(query * query, axis=-1), jnp.sum(keys * keys, axis=-1))...]
    reshape x0 -> x1, local copies, waits for them, and re-layouts: none -> 13.4 us  [shards(): gather_seq(stacked.reshape(rows, kinds * width)).reshape(-1, kinds, width)]
  transfers between devices with their start and end apart: 6 -> 5, of which waited for: 3 -> 2; matrix products, arithmetic and copies ran while one was open for 4% -> 4% of each run, Pallas kernels for 0% -> 0%
where the time goes in v2:
time: 326 us; the launch traced here: 325 us
  Pallas kernels  180 us (55%)
  waiting for transfers between devices  55 us (17%)
  local copies, waits for them, and re-layouts  25.6 us (8%)
  blocking collectives  18.8 us (6%)
  between operations  13.6 us (4%)
  starting transfers between devices  13.2 us (4%)
  matrix products  12.4 us (4%)
  other arithmetic  6.57 us (2%)
    pallas_call x1, Pallas kernels, gather_seq(): pl.pallas_call(functools.partial(gather_kernel, n), out_shape=jax.ShapeDt...  180 us
    reduce_scatter x1, waiting for transfers between devices, shards(): projected = lax.psum_scatter(terms, 'tp', scatter_dimension=1, tiled=True)  52.8 us
    psum x1, blocking collectives, shards(): lax.psum((jnp.sum(query * query, axis=-1), jnp.sum(keys * keys, axis=-1))...  18.8 us
    reshape x1, local copies, waits for them, and re-layouts, shards(): gather_seq(stacked.reshape(rows, kinds * width)).reshape(-1, kinds, width)  13.4 us
    ppermute x4, starting transfers between devices, passed_along(): return lax.ppermute(x, axis, pairs)  13.2 us
    slice x1, local copies, waits for them, and re-layouts, shards(): gathered[:, 3]  7.58 us
  transfers between devices with their start and end apart: 5, of which 2 were waited for; matrix products, arithmetic and copies ran while one was open for 4% of the time, Pallas kernels for 0%

profile of v2, /device:TPU:27, one launch (start us, length us, event | category | flops | bytes accessed | tf_op | source)
XLA Modules:
  0.0 325.2 jit_solution(467999867151239208)
XLA Ops:
  6.5 0.0 reduce-scatter.2.cloned.1.call-start
  6.5 0.9 pad_maximum_fusion.1
  7.6 0.7 copy.26
  8.2 179.9 %shard_map.82 = bf16[64,50,1024]{2,1,0:T(8,128)(2,1)} custom-call(bf16[50,1024]{1,0:T(8,128)(2,1)} %bitcast.36), custom_call_target="tpu_custom_call" | custom-call | tf_op jit(solution)/shard_map/pallas_call | solution.py:67
  188.2 0.0 copy-start
  188.2 13.4 %reshape.76 = bf16[3200,4,256]{2,1,0:T(4,128)(2,1)} reshape(bf16[64,50,1024]{2,1,0:T(8,128)(2,1)} %shard_map.82) | data formatting | bytes 13107200 | tf_op jit(solution)/shard_map/reshape | solution.py:99
  201.6 0.0 copy-done
  201.6 1.5 copy.15
  203.1 0.5 multiply_reduce_fusion
  203.6 0.0 copy-done.6
  203.6 0.0 copy-start.4
  203.6 0.0 copy-start.2
  203.6 5.4 %fusion.1 = f32[256,3,256]{0,2,1:T(8,128)S(1)} fusion(bf16[3200,3,256]{2,1,0:T(4,128)(2,1)} %bitcast.31, f32[3200]{0:T(1024)S(1)} %copy-done.6, f32[256]{0:T(256)S(1)} %add_rsqrt_fusion.2, bf16[256,3200]{0,1:T(8,128)(2,1)S(1)} %copy.15), kind=kOutput, calls=%fused_computation.1 | convolution fusion | flops 1261568000 | bytes 7353856 | tf_op jit(solution)/shard_map/td,dch->tch/dot_general | solution.py:100
  209.0 0.1 multiply_reduce_fusion.1
  209.1 18.8 %all-reduce = (f32[256]{0:T(256)S(1)}, f32[256]{0:T(256)S(1)}) all-reduce(f32[256]{0:T(256)S(1)} %get-tuple-element.6, f32[256]{0:T(256)S(1)} %get-tuple-element.5), channel_id=1, replica_groups=mesh['seq'=64,'tp'=8] {'tp'}, use_global_device_ids=true, to_apply=%region_2.0 | all-reduce | flops 512 | bytes 4096 | tf_op jit(solution)/shard_map/psum | solution.py:109
  227.9 0.0 copy-done.4
  227.9 0.1 fusion.38
  228.0 4.6 %collective-permute-start = (bf16[256,2,256]{0,2,1:T(8,128)(2,1)S(1)}, bf16[256,2,256]{0,2,1:T(8,128)(2,1)}, u32[]{:S(2)}, u32[]{:S(2)}) collective-permute-start(bf16[256,2,256]{0,2,1:T(8,128)(2,1)S(1)} %pad_maximum_fusion), channel_id=1, source_target_pairs={{0,16},{8,24},{16,32},{24,40},{32,48},{40,56},{48,64},{56,72},{64,... | collective-permute-start | bytes 786440 | tf_op jit(solution)/shard_map/ppermute | solution.py:20
  232.7 4.7 %collective-permute-start.1 = (bf16[256,2,256]{0,2,1:T(8,128)(2,1)S(1)}, bf16[256,2,256]{0,2,1:T(8,128)(2,1)}, u32[]{:S(2)}, u32[]{:S(2)}) collective-permute-start(bf16[256,2,256]{0,2,1:T(8,128)(2,1)S(1)} %pad_maximum_fusion), channel_id=1, source_target_pairs={{0,8},{8,16},{16,24},{24,32},{32,40},{40,48},{48,56},{56,64},{64,7... | collective-permute-start | bytes 786440 | tf_op jit(solution)/shard_map/ppermute | solution.py:20
  237.4 1.9 collective-permute-start.2
  239.4 1.9 collective-permute-start.3
  241.3 0.0 copy-done.2
  241.3 0.1 dynamic_slice.10
  241.4 0.1 fusion.27
  241.5 0.3 broadcast_compare_fusion
  241.7 0.0 copy-start.5
  241.7 7.6 %slice.29 = bf16[3200,1,256]{2,1,0:T(2,128)(2,1)} slice(bf16[3200,4,256]{2,1,0:T(4,128)(2,1)} %reshape.76), slice={[0:3200], [3:4], [0:256]} | slice | bytes 3276800 | tf_op jit(solution)/shard_map/slice | solution.py:145
  249.3 0.1 copy.19
  249.5 0.0 copy-done.5
  249.5 0.8 multiply_convert_fusion.1
  250.2 0.0 collective-permute-done
  250.2 1.0 constant_dynamic-update-slice_fusion.4
  251.2 0.0 collective-permute-done.1
  251.2 1.0 constant_dynamic-update-slice_fusion.3
  252.2 0.0 collective-permute-done.2
  252.3 0.0 copy-start.1
  252.3 2.2 collective-permute-done.3
  254.5 0.1 fusion.37
  254.6 0.0 copy-done.1
  254.6 1.4 fusion.39
  256.0 1.4 fusion.23
  257.4 4.2 %fusion.9 = f32[256,3200]{0,1:T(8,128)} fusion(bf16[256,256]{0,1:T(8,128)(2,1)S(1)} %bitcast.38, bf16[3200,1,256]{2,1,0:T(2,128)(2,1)} %slice.29), kind=kOutput, calls=%fused_computation.11 | convolution fusion | flops 419430400 | bytes 5046272 | tf_op jit(solution)/shard_map/th,dh->td/dot_general | solution.py:144
  261.6 0.0 reduce-scatter.2.cloned.1.call-update
  261.6 0.0 copy-start.3
  261.6 1.9 convert_element_type.28
  263.6 52.8 %reduce-scatter.2.cloned.1.call-done = f32[256,400]{0,1:T(8,128)} async-done(((f32[256,3200]{0,1:T(8,128)}), f32[256,400]{0,1:T(8,128)}) %reduce-scatter.2.cloned.1.call-update) | async-done | bytes 409616 | tf_op jit(solution)/shard_map/reduce_scatter | solution.py:147
  316.4 0.0 copy-done.3
  316.4 1.9 add_convert_fusion
  (11 shorter events, 0.2 us)
Async XLA Ops:
  6.5 309.8 %reduce-scatter.2.cloned.1.call-start = ((), (), s32[]{:S(2)}) async-start(), calls=%async_computation.1 | async-start | bytes 3686400 | tf_op jit(solution)/shard_map/reduce_scatter | solution.py:147
  188.2 13.4 %copy-start = (bf16[256,3200]{1,0:T(8,128)(2,1)S(1)}, bf16[256,3200]{1,0:T(8,128)(2,1)}, u32[]{:S(2)}) copy-start(bf16[256,3200]{1,0:T(8,128)(2,1)} %param.8) | copy-start | bytes 4915204
  201.6 2.0 copy-start.6
  203.6 24.3 %copy-start.4 = (f32[256]{0:T(256)S(1)}, f32[256]{0:T(256)}, u32[]{:S(2)}) copy-start(f32[256]{0:T(256)} %param.12) | copy-start | bytes 3076
  203.6 37.7 %copy-start.2 = (s32[16384]{0:T(1024)S(1)}, s32[16384]{0:T(1024)}, u32[]{:S(2)}) copy-start(s32[16384]{0:T(1024)} %param.15) | copy-start | bytes 196612
  228.0 22.2 %collective-permute-start = (bf16[256,2,256]{0,2,1:T(8,128)(2,1)S(1)}, bf16[256,2,256]{0,2,1:T(8,128)(2,1)}, u32[]{:S(2)}, u32[]{:S(2)}) collective-permute-start(bf16[256,2,256]{0,2,1:T(8,128)(2,1)S(1)} %pad_maximum_fusion), channel_id=1, source_target_pairs={{0,16},{8,24},{16,32},{24,40},{32,48},{40,56},{48,64},{56,72},{64,... | collective-permute-start | bytes 786440 | tf_op jit(solution)/shard_map/ppermute | solution.py:20
  232.7 18.5 %collective-permute-start.1 = (bf16[256,2,256]{0,2,1:T(8,128)(2,1)S(1)}, bf16[256,2,256]{0,2,1:T(8,128)(2,1)}, u32[]{:S(2)}, u32[]{:S(2)}) collective-permute-start(bf16[256,2,256]{0,2,1:T(8,128)(2,1)S(1)} %pad_maximum_fusion), channel_id=1, source_target_pairs={{0,8},{8,16},{16,24},{24,32},{32,40},{40,48},{48,56},{56,64},{64,7... | collective-permute-start | bytes 786440 | tf_op jit(solution)/shard_map/ppermute | solution.py:20
  237.4 14.8 %collective-permute-start.2 = (bf16[256,2,256]{0,2,1:T(8,128)(2,1)S(1)}, bf16[256,2,256]{0,2,1:T(8,128)(2,1)S(1)}, u32[]{:S(2)}, u32[]{:S(2)}) collective-permute-start(bf16[256,2,256]{0,2,1:T(8,128)(2,1)S(1)} %pad_maximum_fusion), channel_id=1, source_target_pairs={{8,0},{16,8},{24,16},{32,24},{40,32},{48,40},{56,48},{64,56},{72,6... | collective-permute-start | bytes 786440 | tf_op jit(solution)/shard_map/ppermute | solution.py:20
  239.4 15.1 %collective-permute-start.3 = (bf16[256,2,256]{0,2,1:T(8,128)(2,1)S(1)}, bf16[256,2,256]{0,2,1:T(8,128)(2,1)S(1)}, u32[]{:S(2)}, u32[]{:S(2)}) collective-permute-start(bf16[256,2,256]{0,2,1:T(8,128)(2,1)S(1)} %pad_maximum_fusion), channel_id=1, source_target_pairs={{16,0},{24,8},{32,16},{40,24},{48,32},{56,40},{64,48},{72,56},{80,... | collective-permute-start | bytes 786440 | tf_op jit(solution)/shard_map/ppermute | solution.py:20
  241.7 7.7 %copy-start.5 = (f32[256]{0:T(256)S(1)}, f32[256]{0:T(256)}, u32[]{:S(2)}) copy-start(f32[256]{0:T(256)} %param.11) | copy-start | bytes 3076
  252.3 2.3 copy-start.1
  261.6 54.8 %copy-start.3 = (f32[400]{0:T(512)S(1)}, f32[400]{0:T(512)}, u32[]{:S(2)}) copy-start(f32[400]{0:T(512)} %param.14) | copy-start | bytes 4804
Sparse Core Ops, SparseCore 0:
  261.7 54.6 reduce-scatter.1

commit v3 on v2

--- a/solution.py
+++ b/solution.py
@@ -20,46 +20,90 @@
     return lax.ppermute(x, axis, pairs)
 
 
-def gather_kernel(n, x_ref, out_ref, send_sem, recv_sem, local_sem):
+def gather_kernel(n, x_ref, out_ref, pair_sems, row_sems, ring_sems, local_sem):
     me = lax.axis_index("seq")
     tp = lax.axis_index("tp")
     mesh_id = pl.DeviceIdType.MESH
+    pair, row = 2, 4
+    slab = pair * row
+    rings = n // slab
+    low = me % pair
+    across = (me // pair) % row
+    ring = me // slab
+    partner = me - low + (1 - low)
+    row_peers = [ring * slab + ((across + k) % row) * pair + low for k in range(1, row)]
+    ahead = ((ring + 1) % rings) * slab + me % slab
+    behind = ((ring + rings - 1) % rings) * slab + me % slab
+
     barrier = pltpu.get_barrier_semaphore()
-
-    def greet(k, carry):
-        peer = lax.rem(me + k, n)
+    for peer in [partner, ahead, behind] + row_peers:
         pl.semaphore_signal(barrier, inc=1, device_id=(peer, tp), device_id_type=mesh_id)
-        return carry
-
-    lax.fori_loop(1, n, greet, 0)
-    pl.semaphore_wait(barrier, n - 1)
+    pl.semaphore_wait(barrier, 3 + len(row_peers))
+
     local = pltpu.make_async_copy(x_ref, out_ref.at[me], local_sem)
     local.start()
-
-    def remote(k):
-        peer = lax.rem(me + k, n)
-        return pltpu.make_async_remote_copy(
-            src_ref=x_ref,
-            dst_ref=out_ref.at[me],
-            send_sem=send_sem.at[k],
-            recv_sem=recv_sem.at[k],
+    first = pltpu.make_async_remote_copy(
+        src_ref=x_ref,
+        dst_ref=out_ref.at[me],
+        send_sem=pair_sems.at[0],
+        recv_sem=pair_sems.at[1],
+        device_id=(partner, tp),
+        device_id_type=mesh_id,
+    )
+    first.start()
+    local.wait()
+    first.wait_send()
+    first.wait_recv()
+
+    base = me - low
+    second = []
+    for k, peer in enumerate(row_peers):
+        copy = pltpu.make_async_remote_copy(
+            src_ref=out_ref.at[pl.ds(base, pair)],
+            dst_ref=out_ref.at[pl.ds(base, pair)],
+            send_sem=row_sems.at[0, k],
+            recv_sem=row_sems.at[1, k],
             device_id=(peer, tp),
             device_id_type=mesh_id,
         )
-
-    def send(k, carry):
-        remote(k).start()
-        return carry
-
-    def finish(k, carry):
-        copy = remote(k)
+        copy.start()
+        second.append(copy)
+    for copy in second:
         copy.wait_send()
         copy.wait_recv()
+
+    half = slab // 2
+
+    def step(t, carry):
+        forward = (ring - t + rings) % rings
+        backward = (ring + t) % rings
+        window_f = out_ref.at[pl.ds(forward * slab, half)]
+        window_b = out_ref.at[pl.ds(backward * slab + half, half)]
+        to_ahead = pltpu.make_async_remote_copy(
+            src_ref=window_f,
+            dst_ref=window_f,
+            send_sem=ring_sems.at[0, 0, t],
+            recv_sem=ring_sems.at[1, 0, t],
+            device_id=(ahead, tp),
+            device_id_type=mesh_id,
+        )
+        to_behind = pltpu.make_async_remote_copy(
+            src_ref=window_b,
+            dst_ref=window_b,
+            send_sem=ring_sems.at[0, 1, t],
+            recv_sem=ring_sems.at[1, 1, t],
+            device_id=(behind, tp),
+            device_id_type=mesh_id,
+        )
+        to_ahead.start()
+        to_behind.start()
+        to_ahead.wait_send()
+        to_behind.wait_send()
+        to_ahead.wait_recv()
+        to_behind.wait_recv()
         return carry
 
-    lax.fori_loop(1, n, send, 0)
-    lax.fori_loop(1, n, finish, 0)
-    local.wait()
+    lax.fori_loop(0, rings - 1, step, 0)
 
 
 def gather_seq(block):
@@ -70,8 +114,9 @@
         in_specs=[pl.BlockSpec(memory_space=pl.ANY)],
         out_specs=pl.BlockSpec(memory_space=pl.ANY),
         scratch_shapes=[
-            pltpu.SemaphoreType.DMA((n,)),
-            pltpu.SemaphoreType.DMA((n,)),
+            pltpu.SemaphoreType.DMA((2,)),
+            pltpu.SemaphoreType.DMA((2, 3)),
+            pltpu.SemaphoreType.DMA((2, 2, n // 8)),
             pltpu.SemaphoreType.DMA(()),
         ],
         compiler_params=pltpu.CompilerParams(collective_id=0, has_side_effects=True),

time: 326 us -> 240 us (0.74)
  the two profiles are of different devices: /device:TPU:27 before, /device:TPU:31 now
where the time goes in v3:
time: 240 us
  Pallas kernels  101 us (42%)
  waiting for transfers between devices  53.6 us (22%)
  local copies, waits for them, and re-layouts  25.6 us (11%)
  blocking collectives  16 us (7%)
  between operations  13.6 us (6%)
  matrix products  12.3 us (5%)
  starting transfers between devices  10.6 us (4%)
  other arithmetic  6.57 us (3%)
    pallas_call x1, Pallas kernels, gather_seq(): pl.pallas_call(functools.partial(gather_kernel, n), out_shape=jax.ShapeDt...  101 us
    reduce_scatter x1, waiting for transfers between devices, shards(): projected = lax.psum_scatter(terms, 'tp', scatter_dimension=1, tiled=True)  52.5 us
    psum x1, blocking collectives, shards(): lax.psum((jnp.sum(query * query, axis=-1), jnp.sum(keys * keys, axis=-1))...  16 us
    reshape x1, local copies, waits for them, and re-layouts, shards(): gather_seq(stacked.reshape(rows, kinds * width)).reshape(-1, kinds, width)  13.4 us
    ppermute x4, starting transfers between devices, passed_along(): return lax.ppermute(x, axis, pairs)  10.6 us
    slice x1, local copies, waits for them, and re-layouts, shards(): gathered[:, 3]  7.58 us
    dot_general x1, matrix products, shards(): jnp.einsum('td,dch->tch', normed, gathered[:, :3], preferred_element_type...  5.35 us
  transfers between devices with their start and end apart: 5, of which 2 were waited for; matrix products, arithmetic and copies ran while one was open for 5% of the time, Pallas kernels for 0%

profile of v3, /device:TPU:31, one launch (start us, length us, event | category | flops | bytes accessed | tf_op | source)
XLA Modules:
  0.0 239.5 jit_solution(9309216862838792235)
XLA Ops:
  6.5 0.0 reduce-scatter.2.cloned.1.call-start
  6.5 0.9 pad_maximum_fusion.1
  7.6 0.7 copy.26
  8.2 101.2 %shard_map.82 = bf16[64,50,1024]{2,1,0:T(8,128)(2,1)} custom-call(bf16[50,1024]{1,0:T(8,128)(2,1)} %bitcast.36), custom_call_target="tpu_custom_call" | custom-call | tf_op jit(solution)/shard_map/pallas_call | solution.py:111
  109.4 0.0 copy-start
  109.4 13.4 %reshape.76 = bf16[3200,4,256]{2,1,0:T(4,128)(2,1)} reshape(bf16[64,50,1024]{2,1,0:T(8,128)(2,1)} %shard_map.82) | data formatting | bytes 13107200 | tf_op jit(solution)/shard_map/reshape | solution.py:144
  122.9 0.0 copy-done
  122.9 1.5 copy.15
  124.4 0.5 multiply_reduce_fusion
  124.8 0.0 copy-done.6
  124.8 0.0 copy-start.4
  124.8 0.0 copy-start.2
  124.9 5.4 %fusion.1 = f32[256,3,256]{0,2,1:T(8,128)S(1)} fusion(bf16[3200,3,256]{2,1,0:T(4,128)(2,1)} %bitcast.31, f32[3200]{0:T(1024)S(1)} %copy-done.6, f32[256]{0:T(256)S(1)} %add_rsqrt_fusion.2, bf16[256,3200]{0,1:T(8,128)(2,1)S(1)} %copy.15), kind=kOutput, calls=%fused_computation.1 | convolution fusion | flops 1261568000 | bytes 7353856 | tf_op jit(solution)/shard_map/td,dch->tch/dot_general | solution.py:145
  130.2 0.1 multiply_reduce_fusion.1
  130.3 16.0 %all-reduce = (f32[256]{0:T(256)S(1)}, f32[256]{0:T(256)S(1)}) all-reduce(f32[256]{0:T(256)S(1)} %get-tuple-element.6, f32[256]{0:T(256)S(1)} %get-tuple-element.5), channel_id=1, replica_groups=mesh['seq'=64,'tp'=8] {'tp'}, use_global_device_ids=true, to_apply=%region_2.0 | all-reduce | flops 512 | bytes 4096 | tf_op jit(solution)/shard_map/psum | solution.py:154
  146.4 0.0 copy-done.4
  146.4 0.1 fusion.38
  146.5 1.9 collective-permute-start
  148.4 1.9 collective-permute-start.1
  150.4 3.4 %collective-permute-start.2 = (bf16[256,2,256]{0,2,1:T(8,128)(2,1)S(1)}, bf16[256,2,256]{0,2,1:T(8,128)(2,1)S(1)}, u32[]{:S(2)}, u32[]{:S(2)}) collective-permute-start(bf16[256,2,256]{0,2,1:T(8,128)(2,1)S(1)} %pad_maximum_fusion), channel_id=1, source_target_pairs={{8,0},{16,8},{24,16},{32,24},{40,32},{48,40},{56,48},{64,56},{72,6... | collective-permute-start | bytes 786440 | tf_op jit(solution)/shard_map/ppermute | solution.py:20
  153.7 3.4 %collective-permute-start.3 = (bf16[256,2,256]{0,2,1:T(8,128)(2,1)S(1)}, bf16[256,2,256]{0,2,1:T(8,128)(2,1)S(1)}, u32[]{:S(2)}, u32[]{:S(2)}) collective-permute-start(bf16[256,2,256]{0,2,1:T(8,128)(2,1)S(1)} %pad_maximum_fusion), channel_id=1, source_target_pairs={{16,0},{24,8},{32,16},{40,24},{48,32},{56,40},{64,48},{72,56},{80,... | collective-permute-start | bytes 786440 | tf_op jit(solution)/shard_map/ppermute | solution.py:20
  157.1 0.0 copy-done.2
  157.1 0.1 dynamic_slice.10
  157.2 0.1 fusion.27
  157.3 0.3 broadcast_compare_fusion
  157.5 0.0 copy-start.5
  157.6 7.6 %slice.29 = bf16[3200,1,256]{2,1,0:T(2,128)(2,1)} slice(bf16[3200,4,256]{2,1,0:T(4,128)(2,1)} %reshape.76), slice={[0:3200], [3:4], [0:256]} | slice | bytes 3276800 | tf_op jit(solution)/shard_map/slice | solution.py:190
  165.1 0.1 copy.19
  165.3 0.0 copy-done.5
  165.3 0.8 multiply_convert_fusion.1
  166.0 0.0 collective-permute-done
  166.0 1.0 constant_dynamic-update-slice_fusion.4
  167.0 0.0 collective-permute-done.1
  167.0 1.0 constant_dynamic-update-slice_fusion.3
  168.0 0.0 collective-permute-done.2
  168.1 0.0 copy-start.1
  168.1 1.0 collective-permute-done.3
  169.1 0.1 fusion.37
  169.2 0.0 copy-done.1
  169.2 1.4 fusion.39
  170.6 1.4 fusion.23
  172.0 4.2 %fusion.9 = f32[256,3200]{0,1:T(8,128)} fusion(bf16[256,256]{0,1:T(8,128)(2,1)S(1)} %bitcast.38, bf16[3200,1,256]{2,1,0:T(2,128)(2,1)} %slice.29), kind=kOutput, calls=%fused_computation.11 | convolution fusion | flops 419430400 | bytes 5046272 | tf_op jit(solution)/shard_map/th,dh->td/dot_general | solution.py:189
  176.2 0.0 reduce-scatter.2.cloned.1.call-update
  176.3 0.0 copy-start.3
  176.3 1.9 convert_element_type.28
  178.2 52.5 %reduce-scatter.2.cloned.1.call-done = f32[256,400]{0,1:T(8,128)} async-done(((f32[256,3200]{0,1:T(8,128)}), f32[256,400]{0,1:T(8,128)}) %reduce-scatter.2.cloned.1.call-update) | async-done | bytes 409616 | tf_op jit(solution)/shard_map/reduce_scatter | solution.py:192
  230.7 0.0 copy-done.3
  230.7 1.9 add_convert_fusion
  (11 shorter events, 0.2 us)
Async XLA Ops:
  6.5 224.2 %reduce-scatter.2.cloned.1.call-start = ((), (), s32[]{:S(2)}) async-start(), calls=%async_computation.1 | async-start | bytes 3686400 | tf_op jit(solution)/shard_map/reduce_scatter | solution.py:192
  109.4 13.4 %copy-start = (bf16[256,3200]{1,0:T(8,128)(2,1)S(1)}, bf16[256,3200]{1,0:T(8,128)(2,1)}, u32[]{:S(2)}) copy-start(bf16[256,3200]{1,0:T(8,128)(2,1)} %param.8) | copy-start | bytes 4915204
  122.9 2.0 copy-start.6
  124.8 21.5 %copy-start.4 = (f32[256]{0:T(256)S(1)}, f32[256]{0:T(256)}, u32[]{:S(2)}) copy-start(f32[256]{0:T(256)} %param.12) | copy-start | bytes 3076
  124.8 32.3 %copy-start.2 = (s32[16384]{0:T(1024)S(1)}, s32[16384]{0:T(1024)}, u32[]{:S(2)}) copy-start(s32[16384]{0:T(1024)} %param.15) | copy-start | bytes 196612
  146.5 19.5 %collective-permute-start = (bf16[256,2,256]{0,2,1:T(8,128)(2,1)S(1)}, bf16[256,2,256]{0,2,1:T(8,128)(2,1)}, u32[]{:S(2)}, u32[]{:S(2)}) collective-permute-start(bf16[256,2,256]{0,2,1:T(8,128)(2,1)S(1)} %pad_maximum_fusion), channel_id=1, source_target_pairs={{0,16},{8,24},{16,32},{24,40},{32,48},{40,56},{48,64},{56,72},{64,... | collective-permute-start | bytes 786440 | tf_op jit(solution)/shard_map/ppermute | solution.py:20
  148.4 18.6 %collective-permute-start.1 = (bf16[256,2,256]{0,2,1:T(8,128)(2,1)S(1)}, bf16[256,2,256]{0,2,1:T(8,128)(2,1)}, u32[]{:S(2)}, u32[]{:S(2)}) collective-permute-start(bf16[256,2,256]{0,2,1:T(8,128)(2,1)S(1)} %pad_maximum_fusion), channel_id=1, source_target_pairs={{0,8},{8,16},{16,24},{24,32},{32,40},{40,48},{48,56},{56,64},{64,7... | collective-permute-start | bytes 786440 | tf_op jit(solution)/shard_map/ppermute | solution.py:20
  150.4 17.7 %collective-permute-start.2 = (bf16[256,2,256]{0,2,1:T(8,128)(2,1)S(1)}, bf16[256,2,256]{0,2,1:T(8,128)(2,1)S(1)}, u32[]{:S(2)}, u32[]{:S(2)}) collective-permute-start(bf16[256,2,256]{0,2,1:T(8,128)(2,1)S(1)} %pad_maximum_fusion), channel_id=1, source_target_pairs={{8,0},{16,8},{24,16},{32,24},{40,32},{48,40},{56,48},{64,56},{72,6... | collective-permute-start | bytes 786440 | tf_op jit(solution)/shard_map/ppermute | solution.py:20
  153.7 15.4 %collective-permute-start.3 = (bf16[256,2,256]{0,2,1:T(8,128)(2,1)S(1)}, bf16[256,2,256]{0,2,1:T(8,128)(2,1)S(1)}, u32[]{:S(2)}, u32[]{:S(2)}) collective-permute-start(bf16[256,2,256]{0,2,1:T(8,128)(2,1)S(1)} %pad_maximum_fusion), channel_id=1, source_target_pairs={{16,0},{24,8},{32,16},{40,24},{48,32},{56,40},{64,48},{72,56},{80,... | collective-permute-start | bytes 786440 | tf_op jit(solution)/shard_map/ppermute | solution.py:20
  157.5 7.7 %copy-start.5 = (f32[256]{0:T(256)S(1)}, f32[256]{0:T(256)}, u32[]{:S(2)}) copy-start(f32[256]{0:T(256)} %param.11) | copy-start | bytes 3076
  168.1 1.2 copy-start.1
  176.3 54.5 %copy-start.3 = (f32[400]{0:T(512)S(1)}, f32[400]{0:T(512)}, u32[]{:S(2)}) copy-start(f32[400]{0:T(512)} %param.14) | copy-start | bytes 4804
Sparse Core Ops, SparseCore 0:
  176.4 54.2 reduce-scatter.1

commit v4 on v3

--- a/solution.py
+++ b/solution.py
@@ -186,10 +186,14 @@
     context = (
         (summed / jnp.transpose(total)[:, :, None]).reshape(count, local_width).astype(jnp.bfloat16)
     )
+    blank = jnp.zeros_like(context)
+    widened_context = jnp.stack([blank, blank, blank, context], axis=1)
     terms = jnp.einsum(
-        "th,dh->td", context, gathered[:, 3], preferred_element_type=jnp.float32
-    )
-    projected = lax.psum_scatter(terms, "tp", scatter_dimension=1, tiled=True)
+        "tkh,dkh->td", widened_context, gathered, preferred_element_type=jnp.float32
+    )
+    projected = lax.psum_scatter(
+        terms.astype(jnp.bfloat16), "tp", scatter_dimension=1, tiled=True
+    ).astype(jnp.float32)
     share = layer_scale.shape[0]
     residual = lax.dynamic_slice_in_dim(source, lax.axis_index("tp") * share, share, 1)
     return (residual + layer_scale * projected).astype(jnp.bfloat16)

time: 240 us -> 232 us (0.967)
  the two profiles are of different devices: /device:TPU:31 before, /device:TPU:23 now
where the time goes in v4:
time: 232 us
  Pallas kernels  101 us (44%)
  waiting for transfers between devices  47.7 us (21%)
  local copies, waits for them, and re-layouts  18.1 us (8%)
  blocking collectives  16.9 us (7%)
  matrix products  15.9 us (7%)
  between operations  13.6 us (6%)
  starting transfers between devices  11.5 us (5%)
  other arithmetic  6.64 us (3%)
    pallas_call x1, Pallas kernels, gather_seq(): pl.pallas_call(functools.partial(gather_kernel, n), out_shape=jax.ShapeDt...  101 us
    reduce_scatter x1, waiting for transfers between devices, shards(): lax.psum_scatter(terms.astype(jnp.bfloat16), 'tp', scatter_dimension=1, t...  43.1 us
    psum x1, blocking collectives, shards(): lax.psum((jnp.sum(query * query, axis=-1), jnp.sum(keys * keys, axis=-1))...  16.9 us
    reshape x1, local copies, waits for them, and re-layouts, shards(): gather_seq(stacked.reshape(rows, kinds * width)).reshape(-1, kinds, width)  13.4 us
    ppermute x4, starting transfers between devices, passed_along(): return lax.ppermute(x, axis, pairs)  11.5 us
    dot_general x1, matrix products, shards(): jnp.einsum('tkh,dkh->td', widened_context, gathered, preferred_element_ty...  6.02 us
    dot_general x1, matrix products, shards(): jnp.einsum('td,dch->tch', normed, gathered[:, :3], preferred_element_type...  5.33 us
  transfers between devices with their start and end apart: 5, of which 3 were waited for; matrix products, arithmetic and copies ran while one was open for 2% of the time, Pallas kernels for 0%

profile of v4, /device:TPU:23, one launch (start us, length us, event | category | flops | bytes accessed | tf_op | source)
XLA Modules:
  0.0 231.5 jit_solution(16808457261632579381)
XLA Ops:
  6.5 0.0 reduce-scatter.2.cloned.1.call-start
  6.5 0.9 pad_maximum_fusion.1
  7.6 0.7 copy.29
  8.2 101.2 %shard_map.82 = bf16[64,50,1024]{2,1,0:T(8,128)(2,1)} custom-call(bf16[50,1024]{1,0:T(8,128)(2,1)} %bitcast.37), custom_call_target="tpu_custom_call" | custom-call | tf_op jit(solution)/shard_map/pallas_call | solution.py:111
  109.4 0.0 copy-start
  109.4 13.4 %reshape.86 = bf16[3200,4,256]{2,1,0:T(4,128)(2,1)} reshape(bf16[64,50,1024]{2,1,0:T(8,128)(2,1)} %shard_map.82) | data formatting | bytes 13107200 | tf_op jit(solution)/shard_map/reshape | solution.py:144
  122.9 0.0 copy-done
  122.9 0.0 copy-start.5
  122.9 1.5 copy.17
  124.4 0.5 multiply_reduce_fusion
  124.8 0.0 copy-done.5
  124.8 0.0 copy-start.3
  124.8 5.3 %fusion.9 = f32[256,3,256]{0,2,1:T(8,128)S(1)} fusion(bf16[3200,3,256]{2,1,0:T(4,128)(2,1)} %bitcast.32, f32[3200]{0:T(1024)S(1)} %copy-done.5, f32[256]{0:T(256)S(1)} %add_rsqrt_fusion.2, bf16[256,3200]{0,1:T(8,128)(2,1)S(1)} %copy.17), kind=kOutput, calls=%fused_computation.5 | convolution fusion | flops 1261568000 | bytes 7353856 | tf_op jit(solution)/shard_map/td,dch->tch/dot_general | solution.py:145
  130.2 0.0 copy-start.1
  130.2 0.0 copy-start.4
  130.2 0.1 multiply_reduce_fusion.1
  130.3 16.9 %all-reduce = (f32[256]{0:T(256)S(1)}, f32[256]{0:T(256)S(1)}) all-reduce(f32[256]{0:T(256)S(1)} %get-tuple-element.6, f32[256]{0:T(256)S(1)} %get-tuple-element.5), channel_id=1, replica_groups=mesh['seq'=64,'tp'=8] {'tp'}, use_global_device_ids=true, to_apply=%region_2.0 | all-reduce | flops 512 | bytes 4096 | tf_op jit(solution)/shard_map/psum | solution.py:154
  147.2 0.0 copy-done.3
  147.2 0.1 fusion.47
  147.4 1.9 collective-permute-start
  149.3 2.3 collective-permute-start.1
  151.6 3.9 %collective-permute-start.2 = (bf16[256,2,256]{0,2,1:T(8,128)(2,1)S(1)}, bf16[256,2,256]{0,2,1:T(8,128)(2,1)S(1)}, u32[]{:S(2)}, u32[]{:S(2)}) collective-permute-start(bf16[256,2,256]{0,2,1:T(8,128)(2,1)S(1)} %pad_maximum_fusion), channel_id=1, source_target_pairs={{8,0},{16,8},{24,16},{32,24},{40,32},{48,40},{56,48},{64,56},{72,6... | collective-permute-start | bytes 786440 | tf_op jit(solution)/shard_map/ppermute | solution.py:20
  155.5 3.4 %collective-permute-start.3 = (bf16[256,2,256]{0,2,1:T(8,128)(2,1)S(1)}, bf16[256,2,256]{0,2,1:T(8,128)(2,1)S(1)}, u32[]{:S(2)}, u32[]{:S(2)}) collective-permute-start(bf16[256,2,256]{0,2,1:T(8,128)(2,1)S(1)} %pad_maximum_fusion), channel_id=1, source_target_pairs={{16,0},{24,8},{32,16},{40,24},{48,32},{56,40},{64,48},{72,56},{80,... | collective-permute-start | bytes 786440 | tf_op jit(solution)/shard_map/ppermute | solution.py:20
  158.9 0.1 copy.21
  159.0 0.0 copy-done.1
  159.0 0.1 dynamic_slice.10
  159.1 0.1 fusion.35
  159.2 0.3 broadcast_compare_fusion
  159.5 0.0 copy-done.4
  159.5 0.8 multiply_convert_fusion.1
  160.2 0.1 pad_maximum_fusion.2
  160.3 2.7 %collective-permute-done = bf16[256,2,256]{0,2,1:T(8,128)(2,1)} collective-permute-done((bf16[256,2,256]{0,2,1:T(8,128)(2,1)S(1)}, bf16[256,2,256]{0,2,1:T(8,128)(2,1)}, u32[]{:S(2)}, u32[]{:S(2)}) %collective-permute-start) | collective-permute-done | bytes 262176 | tf_op jit(solution)/shard_map/ppermute | solution.py:20
  163.0 1.0 constant_dynamic-update-slice_fusion.4
  164.0 0.0 collective-permute-done.1
  164.0 1.0 constant_dynamic-update-slice_fusion.3
  165.0 0.0 collective-permute-done.2
  165.0 1.9 collective-permute-done.3
  166.9 0.1 fusion.46
  167.0 2.3 fusion.48
  169.3 2.3 fusion.28
  171.5 0.1 copy.23
  171.6 6.0 %fusion.6 = bf16[256,3200]{0,1:T(8,128)(2,1)} fusion(bf16[3200,4,256]{2,1,0:T(4,128)(2,1)} %reshape.86, bf16[256,1,256]{2,0,1:T(8,128)(2,1)S(1)} %copy.23, bf16[4]{0:T(256)(128)(2,1)S(1)} %pad_maximum_fusion.2), kind=kOutput, calls=%fused_computation.4 | convolution fusion | flops 1678802944 | bytes 8323080 | tf_op jit(solution)/shard_map/tkh,dkh->td/dot_general | solution.py:191
  177.7 0.0 reduce-scatter.2.cloned.1.call-update
  177.7 0.0 copy-start.2
  177.7 1.9 convert_element_type.41
  179.6 43.1 %reduce-scatter.2.cloned.1.call-done = bf16[256,400]{0,1:T(8,128)(2,1)} async-done(((bf16[256,3200]{0,1:T(8,128)(2,1)}), bf16[256,400]{0,1:T(8,128)(2,1)}) %reduce-scatter.2.cloned.1.call-update) | async-done | bytes 204816 | tf_op jit(solution)/shard_map/reduce_scatter | solution.py:194
  222.8 0.0 copy-done.2
  222.8 1.9 add_convert_fusion
  (11 shorter events, 0.2 us)
Async XLA Ops:
  6.5 216.2 %reduce-scatter.2.cloned.1.call-start = ((), (), s32[]{:S(2)}) async-start(), calls=%async_computation.1 | async-start | bytes 1843200 | tf_op jit(solution)/shard_map/reduce_scatter | solution.py:194
  109.4 13.4 %copy-start = (bf16[256,3200]{1,0:T(8,128)(2,1)S(1)}, bf16[256,3200]{1,0:T(8,128)(2,1)}, u32[]{:S(2)}) copy-start(bf16[256,3200]{1,0:T(8,128)(2,1)} %param.8) | copy-start | bytes 4915204
  122.9 2.0 copy-start.5
  124.8 22.4 %copy-start.3 = (f32[256]{0:T(256)S(1)}, f32[256]{0:T(256)}, u32[]{:S(2)}) copy-start(f32[256]{0:T(256)} %param.12) | copy-start | bytes 3076
  130.2 28.8 %copy-start.1 = (s32[16384]{0:T(1024)S(1)}, s32[16384]{0:T(1024)}, u32[]{:S(2)}) copy-start(s32[16384]{0:T(1024)} %param.15) | copy-start | bytes 196612
  130.2 29.3 %copy-start.4 = (f32[256]{0:T(256)S(1)}, f32[256]{0:T(256)}, u32[]{:S(2)}) copy-start(f32[256]{0:T(256)} %param.11) | copy-start | bytes 3076
  147.4 15.6 %collective-permute-start = (bf16[256,2,256]{0,2,1:T(8,128)(2,1)S(1)}, bf16[256,2,256]{0,2,1:T(8,128)(2,1)}, u32[]{:S(2)}, u32[]{:S(2)}) collective-permute-start(bf16[256,2,256]{0,2,1:T(8,128)(2,1)S(1)} %pad_maximum_fusion), channel_id=1, source_target_pairs={{0,16},{8,24},{16,32},{24,40},{32,48},{40,56},{48,64},{56,72},{64,... | collective-permute-start | bytes 786440 | tf_op jit(solution)/shard_map/ppermute | solution.py:20
  149.3 14.7 %collective-permute-start.1 = (bf16[256,2,256]{0,2,1:T(8,128)(2,1)S(1)}, bf16[256,2,256]{0,2,1:T(8,128)(2,1)}, u32[]{:S(2)}, u32[]{:S(2)}) collective-permute-start(bf16[256,2,256]{0,2,1:T(8,128)(2,1)S(1)} %pad_maximum_fusion), channel_id=1, source_target_pairs={{0,8},{8,16},{16,24},{24,32},{32,40},{40,48},{48,56},{56,64},{64,7... | collective-permute-start | bytes 786440 | tf_op jit(solution)/shard_map/ppermute | solution.py:20
  151.6 13.3 %collective-permute-start.2 = (bf16[256,2,256]{0,2,1:T(8,128)(2,1)S(1)}, bf16[256,2,256]{0,2,1:T(8,128)(2,1)S(1)}, u32[]{:S(2)}, u32[]{:S(2)}) collective-permute-start(bf16[256,2,256]{0,2,1:T(8,128)(2,1)S(1)} %pad_maximum_fusion), channel_id=1, source_target_pairs={{8,0},{16,8},{24,16},{32,24},{40,32},{48,40},{56,48},{64,56},{72,6... | collective-permute-start | bytes 786440 | tf_op jit(solution)/shard_map/ppermute | solution.py:20
  155.5 11.4 %collective-permute-start.3 = (bf16[256,2,256]{0,2,1:T(8,128)(2,1)S(1)}, bf16[256,2,256]{0,2,1:T(8,128)(2,1)S(1)}, u32[]{:S(2)}, u32[]{:S(2)}) collective-permute-start(bf16[256,2,256]{0,2,1:T(8,128)(2,1)S(1)} %pad_maximum_fusion), channel_id=1, source_target_pairs={{16,0},{24,8},{32,16},{40,24},{48,32},{56,40},{64,48},{72,56},{80,... | collective-permute-start | bytes 786440 | tf_op jit(solution)/shard_map/ppermute | solution.py:20
  177.7 45.1 %copy-start.2 = (f32[400]{0:T(512)S(1)}, f32[400]{0:T(512)}, u32[]{:S(2)}) copy-start(f32[400]{0:T(512)} %param.14) | copy-start | bytes 4804
Sparse Core Ops, SparseCore 0:
  177.8 44.9 reduce-scatter.1

commit v5 on v4

--- a/solution.py
+++ b/solution.py
@@ -141,7 +141,7 @@
     heads = local_width // HEAD_DIM
     stacked = jnp.concatenate([qkv_weight, jnp.transpose(out_weight)[:, None, :]], axis=1)
     rows, kinds, width = stacked.shape
-    gathered = gather_seq(stacked.reshape(rows, kinds * width)).reshape(-1, kinds, width)
+    gathered = gather_seq(stacked).reshape(-1, kinds, width)
     joined = jnp.einsum(
         "td,dch->tch",
         normed,

time: 232 us -> 211 us (0.909)
  the two profiles are of different devices: /device:TPU:23 before, /device:TPU:31 now
where the time goes in v5:
time: 211 us
  Pallas kernels  92.5 us (44%)
  waiting for transfers between devices  50.1 us (24%)
  blocking collectives  16 us (8%)
  matrix products  15.9 us (8%)
  between operations  13.6 us (6%)
  starting transfers between devices  10.6 us (5%)
  other arithmetic  6.47 us (3%)
  local copies, waits for them, and re-layouts  5.51 us (3%)
    pallas_call x1, Pallas kernels, gather_seq(): pl.pallas_call(functools.partial(gather_kernel, n), out_shape=jax.ShapeDt...  92.5 us
    reduce_scatter x1, waiting for transfers between devices, shards(): lax.psum_scatter(terms.astype(jnp.bfloat16), 'tp', scatter_dimension=1, t...  41.5 us
    psum x1, blocking collectives, shards(): lax.psum((jnp.sum(query * query, axis=-1), jnp.sum(keys * keys, axis=-1))...  16 us
    ppermute x4, starting transfers between devices, passed_along(): return lax.ppermute(x, axis, pairs)  10.6 us
    ppermute x4, waiting for transfers between devices, passed_along(): return lax.ppermute(x, axis, pairs)  8.58 us
    dot_general x1, matrix products, shards(): jnp.einsum('tkh,dkh->td', widened_context, gathered, preferred_element_ty...  6.02 us
    dot_general x1, matrix products, shards(): jnp.einsum('td,dch->tch', normed, gathered[:, :3], preferred_element_type...  5.33 us
    unnamed x19, local copies, waits for them, and re-layouts  5.05 us
  transfers between devices with their start and end apart: 5, of which 3 were waited for; matrix products, arithmetic and copies ran while one was open for 3% of the time, Pallas kernels for 0%

profile of v5, /device:TPU:31, one launch (start us, length us, event | category | flops | bytes accessed | tf_op | source)
XLA Modules:
  0.0 210.7 jit_solution(13861594882785794623)
XLA Ops:
  6.5 0.0 copy-start
  6.5 0.0 copy-start.2
  6.5 0.0 reduce-scatter.2.cloned.1.call-start
  6.5 3.0 %copy.17 = bf16[256,3200]{0,1:T(8,128)(2,1)S(1)} copy(bf16[256,3200]{1,0:T(8,128)(2,1)} %param.8) | data formatting | bytes 3276800 | tf_op args[0]
  9.6 0.5 multiply_reduce_fusion
  10.0 0.0 copy-done
  10.1 0.0 copy-done.2
  10.1 0.8 pad_maximum_fusion.1.x_ref
  10.9 0.0 copy-start.6
  10.9 92.5 %shard_map.82 = bf16[64,50,4,256]{3,2,1,0:T(4,128)(2,1)} custom-call(bf16[50,4,256]{2,1,0:T(4,128)(2,1)} %pad_maximum_fusion.1.x_ref), custom_call_target="tpu_custom_call" | custom-call | tf_op jit(solution)/shard_map/pallas_call | solution.py:111
  103.4 0.0 copy-done.6
  103.4 0.0 copy-start.4
  103.5 5.3 %fusion.9 = f32[256,3,256]{0,2,1:T(8,128)S(1)} fusion(bf16[3200,3,256]{2,1,0:T(4,128)(2,1)} %bitcast.30, f32[3200]{0:T(1024)S(1)} %copy-done.6, f32[256]{0:T(256)S(1)} %add_rsqrt_fusion.2, bf16[256,3200]{0,1:T(8,128)(2,1)S(1)} %copy.17), kind=kOutput, calls=%fused_computation.5 | convolution fusion | flops 1261568000 | bytes 7353856 | tf_op jit(solution)/shard_map/td,dch->tch/dot_general | solution.py:145
  108.8 0.0 copy-start.1
  108.8 0.0 copy-start.5
  108.8 0.1 multiply_reduce_fusion.1
  108.9 16.0 %all-reduce = (f32[256]{0:T(256)S(1)}, f32[256]{0:T(256)S(1)}) all-reduce(f32[256]{0:T(256)S(1)} %get-tuple-element.6, f32[256]{0:T(256)S(1)} %get-tuple-element.5), channel_id=1, replica_groups=mesh['seq'=64,'tp'=8] {'tp'}, use_global_device_ids=true, to_apply=%region_2.0 | all-reduce | flops 512 | bytes 4096 | tf_op jit(solution)/shard_map/psum | solution.py:154
  124.9 0.0 copy-done.4
  124.9 0.1 fusion.47
  125.1 1.9 collective-permute-start
  127.0 1.9 collective-permute-start.1
  128.9 3.4 %collective-permute-start.2 = (bf16[256,2,256]{0,2,1:T(8,128)(2,1)S(1)}, bf16[256,2,256]{0,2,1:T(8,128)(2,1)S(1)}, u32[]{:S(2)}, u32[]{:S(2)}) collective-permute-start(bf16[256,2,256]{0,2,1:T(8,128)(2,1)S(1)} %pad_maximum_fusion), channel_id=1, source_target_pairs={{8,0},{16,8},{24,16},{32,24},{40,32},{48,40},{56,48},{64,56},{72,6... | collective-permute-start | bytes 786440 | tf_op jit(solution)/shard_map/ppermute | solution.py:20
  132.3 3.4 %collective-permute-start.3 = (bf16[256,2,256]{0,2,1:T(8,128)(2,1)S(1)}, bf16[256,2,256]{0,2,1:T(8,128)(2,1)S(1)}, u32[]{:S(2)}, u32[]{:S(2)}) collective-permute-start(bf16[256,2,256]{0,2,1:T(8,128)(2,1)S(1)} %pad_maximum_fusion), channel_id=1, source_target_pairs={{16,0},{24,8},{32,16},{40,24},{48,32},{56,40},{64,48},{72,56},{80,... | collective-permute-start | bytes 786440 | tf_op jit(solution)/shard_map/ppermute | solution.py:20
  135.7 0.1 copy.22
  135.8 0.0 copy-done.1
  135.8 0.1 dynamic_slice.10
  135.9 0.1 fusion.35
  136.0 0.3 broadcast_compare_fusion
  136.3 0.0 copy-done.5
  136.3 0.8 multiply_convert_fusion.1
  137.0 0.1 pad_maximum_fusion.2
  137.1 0.0 collective-permute-done
  137.1 1.0 constant_dynamic-update-slice_fusion.4
  138.1 0.0 collective-permute-done.1
  138.1 1.0 constant_dynamic-update-slice_fusion.3
  139.1 2.7 %collective-permute-done.2 = bf16[256,2,256]{0,2,1:T(8,128)(2,1)S(1)} collective-permute-done((bf16[256,2,256]{0,2,1:T(8,128)(2,1)S(1)}, bf16[256,2,256]{0,2,1:T(8,128)(2,1)S(1)}, u32[]{:S(2)}, u32[]{:S(2)}) %collective-permute-start.2) | collective-permute-done | bytes 262176 | tf_op jit(solution)/shard_map/ppermute | solution.py:20
  141.8 5.9 %collective-permute-done.3 = bf16[256,2,256]{0,2,1:T(8,128)(2,1)S(1)} collective-permute-done((bf16[256,2,256]{0,2,1:T(8,128)(2,1)S(1)}, bf16[256,2,256]{0,2,1:T(8,128)(2,1)S(1)}, u32[]{:S(2)}, u32[]{:S(2)}) %collective-permute-start.3) | collective-permute-done | bytes 262176 | tf_op jit(solution)/shard_map/ppermute | solution.py:20
  147.7 0.1 fusion.46
  147.8 2.3 %fusion.48 = f32[2,256]{1,0:T(2,128)S(1)} fusion(bf16[256,2,128]{2,0,1:T(8,128)(2,1)} %multiply_convert_fusion.1, bf16[1280,2,128]{0,2,1:T(8,128)(2,1)S(1)} %bitcast.33, pred[256,1280]{1,0:T(8,128)(4,1)S(1)} %broadcast_compare_fusion), kind=kOutput, calls=%fused_computation.59 | convolution fusion | flops 171050240 | bytes 1116160 | tf_op jit(solution)/shard_map/sub | solution.py:182
  150.1 2.3 %fusion.28 = bf16[256,2,128]{0,2,1:T(8,128)(2,1)S(1)} fusion(bf16[1280,2,128]{0,2,1:T(8,128)(2,1)S(1)} %bitcast.35, pred[256,1280]{1,0:T(8,128)(4,1)S(1)} %broadcast_compare_fusion, bf16[256,2,128]{2,0,1:T(8,128)(2,1)} %multiply_convert_fusion.1, bf16[1280,2,128]{0,2,1:T(8,128)(2,1)S(1)} %bitcast.34, f32[256,2]{0,1:T(2,128)S(1)} %bitcast.39), kind=kOutput, calls=%fused_computation.22 | convolution fusion | flops 338953984 | bytes 1902592 | tf_op jit(solution)/shard_map/hqk,khd->qhd/dot_general | solution.py:185
  152.4 0.1 copy.24
  152.5 6.0 %fusion.6 = bf16[256,3200]{0,1:T(8,128)(2,1)} fusion(bf16[3200,4,256]{2,1,0:T(4,128)(2,1)} %bitcast.31, bf16[256,1,256]{2,0,1:T(8,128)(2,1)S(1)} %copy.24, bf16[4]{0:T(256)(128)(2,1)S(1)} %pad_maximum_fusion.2), kind=kOutput, calls=%fused_computation.4 | convolution fusion | flops 1678802944 | bytes 8323080 | tf_op jit(solution)/shard_map/tkh,dkh->td/dot_general | solution.py:191
  158.5 0.0 reduce-scatter.2.cloned.1.call-update
  158.5 0.0 copy-start.3
  158.5 1.9 convert_element_type.41
  160.5 41.5 %reduce-scatter.2.cloned.1.call-done = bf16[256,400]{0,1:T(8,128)(2,1)} async-done(((bf16[256,3200]{0,1:T(8,128)(2,1)}), bf16[256,400]{0,1:T(8,128)(2,1)}) %reduce-scatter.2.cloned.1.call-update) | async-done | bytes 204816 | tf_op jit(solution)/shard_map/reduce_scatter | solution.py:194
  201.9 0.0 copy-done.3
  202.0 1.9 add_convert_fusion
  (11 shorter events, 0.2 us)
Async XLA Ops:
  6.5 3.5 %copy-start = (bf16[50,3,256]{2,0,1:T(8,128)(2,1)S(1)}, bf16[50,3,256]{2,0,1:T(8,128)(2,1)}, u32[]{:S(2)}) copy-start(bf16[50,3,256]{2,0,1:T(8,128)(2,1)} %param.10) | copy-start | bytes 230404
  6.5 3.5 %copy-start.2 = (bf16[256,50]{0,1:T(8,128)(2,1)S(1)}, bf16[256,50]{0,1:T(8,128)(2,1)}, u32[]{:S(2)}) copy-start(bf16[256,50]{0,1:T(8,128)(2,1)} %param.13) | copy-start | bytes 76804
  6.5 195.4 %reduce-scatter.2.cloned.1.call-start = ((), (), s32[]{:S(2)}) async-start(), calls=%async_computation.1 | async-start | bytes 1843200 | tf_op jit(solution)/shard_map/reduce_scatter | solution.py:194
  10.9 92.5 %copy-start.6 = (f32[3200]{0:T(1024)S(1)}, f32[3200]{0:T(1024)}, u32[]{:S(2)}) copy-start(f32[3200]{0:T(1024)} %param.9) | copy-start | bytes 38404
  103.4 21.5 %copy-start.4 = (f32[256]{0:T(256)S(1)}, f32[256]{0:T(256)}, u32[]{:S(2)}) copy-start(f32[256]{0:T(256)} %param.12) | copy-start | bytes 3076
  108.8 27.0 %copy-start.1 = (s32[16384]{0:T(1024)S(1)}, s32[16384]{0:T(1024)}, u32[]{:S(2)}) copy-start(s32[16384]{0:T(1024)} %param.15) | copy-start | bytes 196612
  108.8 27.5 %copy-start.5 = (f32[256]{0:T(256)S(1)}, f32[256]{0:T(256)}, u32[]{:S(2)}) copy-start(f32[256]{0:T(256)} %param.11) | copy-start | bytes 3076
  125.1 12.0 %collective-permute-start = (bf16[256,2,256]{0,2,1:T(8,128)(2,1)S(1)}, bf16[256,2,256]{0,2,1:T(8,128)(2,1)}, u32[]{:S(2)}, u32[]{:S(2)}) collective-permute-start(bf16[256,2,256]{0,2,1:T(8,128)(2,1)S(1)} %pad_maximum_fusion), channel_id=1, source_target_pairs={{0,16},{8,24},{16,32},{24,40},{32,48},{40,56},{48,64},{56,72},{64,... | collective-permute-start | bytes 786440 | tf_op jit(solution)/shard_map/ppermute | solution.py:20
  127.0 11.1 %collective-permute-start.1 = (bf16[256,2,256]{0,2,1:T(8,128)(2,1)S(1)}, bf16[256,2,256]{0,2,1:T(8,128)(2,1)}, u32[]{:S(2)}, u32[]{:S(2)}) collective-permute-start(bf16[256,2,256]{0,2,1:T(8,128)(2,1)S(1)} %pad_maximum_fusion), channel_id=1, source_target_pairs={{0,8},{8,16},{16,24},{24,32},{32,40},{40,48},{48,56},{56,64},{64,7... | collective-permute-start | bytes 786440 | tf_op jit(solution)/shard_map/ppermute | solution.py:20
  128.9 12.8 %collective-permute-start.2 = (bf16[256,2,256]{0,2,1:T(8,128)(2,1)S(1)}, bf16[256,2,256]{0,2,1:T(8,128)(2,1)S(1)}, u32[]{:S(2)}, u32[]{:S(2)}) collective-permute-start(bf16[256,2,256]{0,2,1:T(8,128)(2,1)S(1)} %pad_maximum_fusion), channel_id=1, source_target_pairs={{8,0},{16,8},{24,16},{32,24},{40,32},{48,40},{56,48},{64,56},{72,6... | collective-permute-start | bytes 786440 | tf_op jit(solution)/shard_map/ppermute | solution.py:20
  132.3 15.4 %collective-permute-start.3 = (bf16[256,2,256]{0,2,1:T(8,128)(2,1)S(1)}, bf16[256,2,256]{0,2,1:T(8,128)(2,1)S(1)}, u32[]{:S(2)}, u32[]{:S(2)}) collective-permute-start(bf16[256,2,256]{0,2,1:T(8,128)(2,1)S(1)} %pad_maximum_fusion), channel_id=1, source_target_pairs={{16,0},{24,8},{32,16},{40,24},{48,32},{56,40},{64,48},{72,56},{80,... | collective-permute-start | bytes 786440 | tf_op jit(solution)/shard_map/ppermute | solution.py:20
  158.5 43.4 %copy-start.3 = (f32[400]{0:T(512)S(1)}, f32[400]{0:T(512)}, u32[]{:S(2)}) copy-start(f32[400]{0:T(512)} %param.14) | copy-start | bytes 4804
Sparse Core Ops, SparseCore 0:
  158.6 43.2 reduce-scatter.1

commit v6 on v5

--- a/solution.py
+++ b/solution.py
@@ -120,6 +120,57 @@
             pltpu.SemaphoreType.DMA(()),
         ],
         compiler_params=pltpu.CompilerParams(collective_id=0, has_side_effects=True),
+    )(block)
+
+
+def scatter_kernel(chips, x_ref, out_ref, send_sem, recv_sem, local_sem):
+    seq = lax.axis_index("seq")
+    tp = lax.axis_index("tp")
+    mesh_id = pl.DeviceIdType.MESH
+    core = tp % 2
+    mine = tp // 2
+    owners = [(mine + k) % chips for k in range(1, chips)]
+
+    barrier = pltpu.get_barrier_semaphore()
+    for owner in owners:
+        pl.semaphore_signal(
+            barrier, inc=1, device_id=(seq, owner * 2 + core), device_id_type=mesh_id
+        )
+    pl.semaphore_wait(barrier, chips - 1)
+
+    local = pltpu.make_async_copy(x_ref.at[mine], out_ref.at[mine], local_sem)
+    local.start()
+    copies = []
+    for k, owner in enumerate(owners):
+        copy = pltpu.make_async_remote_copy(
+            src_ref=x_ref.at[owner],
+            dst_ref=out_ref.at[mine],
+            send_sem=send_sem.at[k],
+            recv_sem=recv_sem.at[k],
+            device_id=(seq, owner * 2 + core),
+            device_id_type=mesh_id,
+        )
+        copy.start()
+        copies.append(copy)
+    for copy in copies:
+        copy.wait_send()
+        copy.wait_recv()
+    local.wait()
+
+
+def scatter_chips(block):
+    chips = block.shape[0]
+    return pl.pallas_call(
+        functools.partial(scatter_kernel, chips),
+        out_shape=jax.ShapeDtypeStruct(block.shape, block.dtype),
+        in_specs=[pl.BlockSpec(memory_space=pl.ANY)],
+        out_specs=pl.BlockSpec(memory_space=pl.ANY),
+        scratch_shapes=[
+            pltpu.SemaphoreType.DMA((chips,)),
+            pltpu.SemaphoreType.DMA((chips,)),
+            pltpu.SemaphoreType.DMA(()),
+        ],
+        compiler_params=pltpu.CompilerParams(collective_id=1, has_side_effects=True),
     )(block)
 
 
@@ -188,12 +239,18 @@
     )
     blank = jnp.zeros_like(context)
     widened_context = jnp.stack([blank, blank, blank, context], axis=1)
+    parts = lax.axis_size("tp")
+    chips = parts // 2
+    core = lax.axis_index("tp") % 2
+    by_owner = gathered.reshape(chips, 2, -1, *gathered.shape[1:])
     terms = jnp.einsum(
-        "tkh,dkh->td", widened_context, gathered, preferred_element_type=jnp.float32
-    )
-    projected = lax.psum_scatter(
-        terms.astype(jnp.bfloat16), "tp", scatter_dimension=1, tiled=True
-    ).astype(jnp.float32)
+        "tkh,ycdkh->cytd", widened_context, by_owner, preferred_element_type=jnp.float32
+    )
+    outgoing = lax.dynamic_index_in_dim(terms, 1 - core, 0, keepdims=False)
+    kept = lax.dynamic_index_in_dim(terms, core, 0, keepdims=False)
+    incoming = lax.ppermute(outgoing, "tp", [(i, i ^ 1) for i in range(parts)])
+    chip_sums = (kept + incoming).astype(jnp.bfloat16)
+    projected = jnp.sum(scatter_chips(chip_sums).astype(jnp.float32), axis=0)
     share = layer_scale.shape[0]
     residual = lax.dynamic_slice_in_dim(source, lax.axis_index("tp") * share, share, 1)
     return (residual + layer_scale * projected).astype(jnp.bfloat16)

time: 211 us -> 197 us (0.934)
  the two profiles are of different devices: /device:TPU:31 before, /device:TPU:15 now
where the time goes in v6:
time: 197 us; the launch traced here: 196 us
  Pallas kernels  121 us (61%)
  blocking collectives  17.3 us (9%)
  matrix products  14.5 us (7%)
  starting transfers between devices  13 us (7%)
  local copies, waits for them, and re-layouts  11.6 us (6%)
  other arithmetic  10.1 us (5%)
  waiting for transfers between devices  8.58 us (4%)
    pallas_call x1, Pallas kernels, gather_seq(): pl.pallas_call(functools.partial(gather_kernel, n), out_shape=jax.ShapeDt...  92.5 us
    pallas_call x1, Pallas kernels, scatter_chips(): pl.pallas_call(functools.partial(scatter_kernel, chips), out_shape=jax.Sh...  28.4 us
    psum x1, blocking collectives, shards(): lax.psum((jnp.sum(query * query, axis=-1), jnp.sum(keys * keys, axis=-1))...  17.3 us
    ppermute x4, starting transfers between devices, passed_along(): return lax.ppermute(x, axis, pairs)  10.6 us
    ppermute x4, waiting for transfers between devices, passed_along(): return lax.ppermute(x, axis, pairs)  8.57 us
    dot_general x1, matrix products, shards(): jnp.einsum('td,dch->tch', normed, gathered[:, :3], preferred_element_type...  5.07 us
    dot_general x1, matrix products, shards(): jnp.einsum('tkh,ycdkh->cytd', widened_context, by_owner, preferred_elemen...  4.85 us
    unnamed x17, local copies, waits for them, and re-layouts  4.75 us
  transfers between devices with their start and end apart: 5, of which 2 were waited for; matrix products, arithmetic and copies ran while one was open for 4% of the time, Pallas kernels for 0%

profile of v6, /device:TPU:15, one launch (start us, length us, event | category | flops | bytes accessed | tf_op | source)
XLA Modules:
  0.0 196.2 jit_solution(11604017689243251782)
XLA Ops:
  0.0 0.9 copy.30
  0.9 0.8 copy.31
  1.7 0.8 pad_maximum_fusion.1.x_ref
  2.5 92.5 %shard_map.82 = bf16[64,50,4,256]{3,2,1,0:T(4,128)(2,1)} custom-call(bf16[50,4,256]{2,1,0:T(4,128)(2,1)} %pad_maximum_fusion.1.x_ref), custom_call_target="tpu_custom_call" | custom-call | tf_op jit(solution)/shard_map/pallas_call | solution.py:111
  95.0 0.0 copy-done
  95.0 0.4 multiply_reduce_fusion
  95.4 0.0 copy-done.5
  95.4 0.0 copy-start.3
  95.5 5.1 %fusion.3 = f32[256,3,256]{0,2,1:T(8,128)S(1)} fusion(bf16[3200,3,256]{2,1,0:T(4,128)(2,1)} %bitcast.45, f32[3200]{0:T(1024)S(1)} %copy-done.5, f32[256]{0:T(256)S(1)} %add_rsqrt_fusion.2, bf16[256,3200]{1,0:T(8,128)(2,1)S(1)} %copy-done), kind=kOutput, calls=%fused_computation.3 | convolution fusion | flops 1261568000 | bytes 7353856 | tf_op jit(solution)/shard_map/td,dch->tch/dot_general | solution.py:196
  100.5 0.0 copy-start.1
  100.6 0.0 copy-start.4
  100.6 0.1 multiply_reduce_fusion.1
  100.6 17.3 %all-reduce = (f32[256]{0:T(256)S(1)}, f32[256]{0:T(256)S(1)}) all-reduce(f32[256]{0:T(256)S(1)} %get-tuple-element.6, f32[256]{0:T(256)S(1)} %get-tuple-element.5), channel_id=1, replica_groups=mesh['seq'=64,'tp'=8] {'tp'}, use_global_device_ids=true, to_apply=%region_2.0 | all-reduce | flops 512 | bytes 4096 | tf_op jit(solution)/shard_map/psum | solution.py:205
  117.9 0.0 copy-done.3
  117.9 0.1 fusion.44
  118.1 1.9 collective-permute-start
  120.0 1.9 collective-permute-start.1
  121.9 3.4 %collective-permute-start.2 = (bf16[256,2,256]{0,2,1:T(8,128)(2,1)S(1)}, bf16[256,2,256]{0,2,1:T(8,128)(2,1)S(1)}, u32[]{:S(2)}, u32[]{:S(2)}) collective-permute-start(bf16[256,2,256]{0,2,1:T(8,128)(2,1)S(1)} %pad_maximum_fusion), channel_id=1, source_target_pairs={{8,0},{16,8},{24,16},{32,24},{40,32},{48,40},{56,48},{64,56},{72,6... | collective-permute-start | bytes 786440 | tf_op jit(solution)/shard_map/ppermute | solution.py:20
  125.3 3.4 %collective-permute-start.3 = (bf16[256,2,256]{0,2,1:T(8,128)(2,1)S(1)}, bf16[256,2,256]{0,2,1:T(8,128)(2,1)S(1)}, u32[]{:S(2)}, u32[]{:S(2)}) collective-permute-start(bf16[256,2,256]{0,2,1:T(8,128)(2,1)S(1)} %pad_maximum_fusion), channel_id=1, source_target_pairs={{16,0},{24,8},{32,16},{40,24},{48,32},{56,40},{64,48},{72,56},{80,... | collective-permute-start | bytes 786440 | tf_op jit(solution)/shard_map/ppermute | solution.py:20
  128.7 0.1 copy.33
  128.8 0.0 copy-done.1
  128.8 0.1 dynamic_slice.17
  128.9 0.1 fusion.32
  129.0 0.3 broadcast_compare_fusion
  129.3 0.8 multiply_convert_fusion.1
  130.0 0.1 pad_maximum_fusion.2
  130.1 0.0 collective-permute-done
  130.1 1.0 constant_dynamic-update-slice_fusion.4
  131.1 0.0 collective-permute-done.1
  131.1 1.0 constant_dynamic-update-slice_fusion.3
  132.1 2.0 %collective-permute-done.2 = bf16[256,2,256]{0,2,1:T(8,128)(2,1)S(1)} collective-permute-done((bf16[256,2,256]{0,2,1:T(8,128)(2,1)S(1)}, bf16[256,2,256]{0,2,1:T(8,128)(2,1)S(1)}, u32[]{:S(2)}, u32[]{:S(2)}) %collective-permute-start.2) | collective-permute-done | bytes 262176 | tf_op jit(solution)/shard_map/ppermute | solution.py:20
  134.1 6.6 %collective-permute-done.3 = bf16[256,2,256]{0,2,1:T(8,128)(2,1)S(1)} collective-permute-done((bf16[256,2,256]{0,2,1:T(8,128)(2,1)S(1)}, bf16[256,2,256]{0,2,1:T(8,128)(2,1)S(1)}, u32[]{:S(2)}, u32[]{:S(2)}) %collective-permute-start.3) | collective-permute-done | bytes 262176 | tf_op jit(solution)/shard_map/ppermute | solution.py:20
  140.7 0.1 fusion.43
  140.8 2.3 %fusion.45 = f32[2,256]{1,0:T(2,128)S(1)} fusion(bf16[256,2,128]{2,0,1:T(8,128)(2,1)} %multiply_convert_fusion.1, bf16[1280,2,128]{0,2,1:T(8,128)(2,1)S(1)} %bitcast.48, pred[256,1280]{1,0:T(8,128)(4,1)S(1)} %broadcast_compare_fusion), kind=kOutput, calls=%fused_computation.63 | convolution fusion | flops 171050240 | bytes 1116160 | tf_op jit(solution)/shard_map/sub | solution.py:233
  143.1 2.3 %fusion.26 = bf16[256,2,128]{0,2,1:T(8,128)(2,1)S(1)} fusion(bf16[1280,2,128]{0,2,1:T(8,128)(2,1)S(1)} %bitcast.50, pred[256,1280]{1,0:T(8,128)(4,1)S(1)} %broadcast_compare_fusion, bf16[256,2,128]{2,0,1:T(8,128)(2,1)} %multiply_convert_fusion.1, bf16[1280,2,128]{0,2,1:T(8,128)(2,1)S(1)} %bitcast.49, f32[256,2]{0,1:T(2,128)S(1)} %bitcast.54), kind=kOutput, calls=%fused_computation.25 | convolution fusion | flops 338953984 | bytes 1902592 | tf_op jit(solution)/shard_map/hqk,khd->qhd/dot_general | solution.py:236
  145.3 0.1 copy.35
  145.4 4.8 %fusion.10 = f32[4,2,400,256]{3,2,1,0:T(8,128)S(1)} fusion(bf16[4,2,400,4,256]{4,3,2,1,0:T(4,128)(2,1)} %bitcast.46, bf16[256,1,256]{2,0,1:T(8,128)(2,1)S(1)} %copy.35, bf16[4]{0:T(256)(128)(2,1)S(1)} %pad_maximum_fusion.2), kind=kOutput, calls=%fused_computation.15 | convolution fusion | flops 1677983744 | bytes 9961480 | tf_op jit(solution)/shard_map/tkh,ycdkh->cytd/dot_general | solution.py:246
  150.3 2.0 constant_dynamic-slice_fusion
  152.3 2.4 %collective-permute-start.4 = (f32[4,256,400]{1,2,0:T(8,128)}, f32[4,256,400]{1,2,0:T(8,128)}, u32[]{:S(2)}, u32[]{:S(2)}) collective-permute-start(f32[4,256,400]{1,2,0:T(8,128)} %get-tuple-element.10), channel_id=1, source_target_pairs={{0,1},{1,0},{2,3},{3,2},{4,5},{5,4},{6,7},{7,6},{8,9},{9,8},{10,11... | collective-permute-start | bytes 4915208 | tf_op jit(solution)/shard_map/ppermute | solution.py:251
  154.7 1.9 convert_element_type.41
  156.6 1.8 copy.44
  158.4 0.0 collective-permute-done.4
  158.4 2.9 %copy.38 = f32[4,256,400]{2,1,0:T(8,128)} copy(f32[4,256,400]{1,2,0:T(8,128)} %collective-permute-done.4) | data formatting | bytes 3276800 | tf_op jit(solution)/shard_map/ppermute | solution.py:251
  161.3 2.9 %fusion.9.x_ref = bf16[4,256,400]{2,1,0:T(8,128)(2,1)} fusion(f32[4,256,400]{2,1,0:T(8,128)} %copy.38, f32[4,1,400,256]{2,3,0,1:T(8,128)S(1)} %copy.44), kind=kLoop, calls=%fused_computation.13 | loop fusion | flops 819200 | bytes 4096000 | tf_op jit(solution)/shard_map/convert_element_type | solution.py:252
  164.2 28.4 %shard_map.83 = bf16[4,256,400]{2,1,0:T(8,128)(2,1)} custom-call(bf16[4,256,400]{2,1,0:T(8,128)(2,1)} %fusion.9.x_ref), custom_call_target="tpu_custom_call" | custom-call | tf_op jit(solution)/shard_map/pallas_call | solution.py:163
  192.6 1.4 convert_reduce_fusion
  194.1 1.3 add_convert_fusion
  195.4 0.8 copy.39
  (14 shorter events, 0.1 us)
Async XLA Ops:
  2.5 92.5 %copy-start = (bf16[256,3200]{1,0:T(8,128)(2,1)S(1)}, bf16[256,3200]{1,0:T(8,128)(2,1)}, u32[]{:S(2)}) copy-start(bf16[256,3200]{1,0:T(8,128)(2,1)} %param.8) | copy-start | bytes 4915204
  2.5 93.0 %copy-start.5 = (f32[3200]{0:T(1024)S(1)}, f32[3200]{0:T(1024)}, u32[]{:S(2)}) copy-start(f32[3200]{0:T(1024)} %param.9) | copy-start | bytes 38404
  95.4 22.5 %copy-start.3 = (f32[256]{0:T(256)S(1)}, f32[256]{0:T(256)}, u32[]{:S(2)}) copy-start(f32[256]{0:T(256)} %param.12) | copy-start | bytes 3076
  100.5 28.3 %copy-start.1 = (s32[16384]{0:T(1024)S(1)}, s32[16384]{0:T(1024)}, u32[]{:S(2)}) copy-start(s32[16384]{0:T(1024)} %param.15) | copy-start | bytes 196612
  100.6 28.7 %copy-start.4 = (f32[256]{0:T(256)S(1)}, f32[256]{0:T(256)}, u32[]{:S(2)}) copy-start(f32[256]{0:T(256)} %param.11) | copy-start | bytes 3076
  118.1 12.0 %collective-permute-start = (bf16[256,2,256]{0,2,1:T(8,128)(2,1)S(1)}, bf16[256,2,256]{0,2,1:T(8,128)(2,1)}, u32[]{:S(2)}, u32[]{:S(2)}) collective-permute-start(bf16[256,2,256]{0,2,1:T(8,128)(2,1)S(1)} %pad_maximum_fusion), channel_id=1, source_target_pairs={{0,16},{8,24},{16,32},{24,40},{32,48},{40,56},{48,64},{56,72},{64,... | collective-permute-start | bytes 786440 | tf_op jit(solution)/shard_map/ppermute | solution.py:20
  120.0 11.1 %collective-permute-start.1 = (bf16[256,2,256]{0,2,1:T(8,128)(2,1)S(1)}, bf16[256,2,256]{0,2,1:T(8,128)(2,1)}, u32[]{:S(2)}, u32[]{:S(2)}) collective-permute-start(bf16[256,2,256]{0,2,1:T(8,128)(2,1)S(1)} %pad_maximum_fusion), channel_id=1, source_target_pairs={{0,8},{8,16},{16,24},{24,32},{32,40},{40,48},{48,56},{56,64},{64,7... | collective-permute-start | bytes 786440 | tf_op jit(solution)/shard_map/ppermute | solution.py:20
  121.9 12.2 %collective-permute-start.2 = (bf16[256,2,256]{0,2,1:T(8,128)(2,1)S(1)}, bf16[256,2,256]{0,2,1:T(8,128)(2,1)S(1)}, u32[]{:S(2)}, u32[]{:S(2)}) collective-permute-start(bf16[256,2,256]{0,2,1:T(8,128)(2,1)S(1)} %pad_maximum_fusion), channel_id=1, source_target_pairs={{8,0},{16,8},{24,16},{32,24},{40,32},{48,40},{56,48},{64,56},{72,6... | collective-permute-start | bytes 786440 | tf_op jit(solution)/shard_map/ppermute | solution.py:20
  125.3 15.4 %collective-permute-start.3 = (bf16[256,2,256]{0,2,1:T(8,128)(2,1)S(1)}, bf16[256,2,256]{0,2,1:T(8,128)(2,1)S(1)}, u32[]{:S(2)}, u32[]{:S(2)}) collective-permute-start(bf16[256,2,256]{0,2,1:T(8,128)(2,1)S(1)} %pad_maximum_fusion), channel_id=1, source_target_pairs={{16,0},{24,8},{32,16},{40,24},{48,32},{56,40},{64,48},{72,56},{80,... | collective-permute-start | bytes 786440 | tf_op jit(solution)/shard_map/ppermute | solution.py:20
  152.3 6.2 %collective-permute-start.4 = (f32[4,256,400]{1,2,0:T(8,128)}, f32[4,256,400]{1,2,0:T(8,128)}, u32[]{:S(2)}, u32[]{:S(2)}) collective-permute-start(f32[4,256,400]{1,2,0:T(8,128)} %get-tuple-element.10), channel_id=1, source_target_pairs={{0,1},{1,0},{2,3},{3,2},{4,5},{5,4},{6,7},{7,6},{8,9},{9,8},{10,11... | collective-permute-start | bytes 4915208 | tf_op jit(solution)/shard_map/ppermute | solution.py:251
  164.2 29.9 %copy-start.2 = (f32[400]{0:T(512)S(1)}, f32[400]{0:T(512)}, u32[]{:S(2)}) copy-start(f32[400]{0:T(512)} %param.14) | copy-start | bytes 4804

commit v7 on v6

--- a/solution.py
+++ b/solution.py
@@ -171,6 +171,71 @@
             pltpu.SemaphoreType.DMA(()),
         ],
         compiler_params=pltpu.CompilerParams(collective_id=1, has_side_effects=True),
+    )(block)
+
+
+def exchange_kernel(axis, offsets, x_ref, out_ref, send_sem, recv_sem, local_sem):
+    size = lax.axis_size(axis)
+    me = lax.axis_index(axis)
+    seq = lax.axis_index("seq")
+    tp = lax.axis_index("tp")
+    mesh_id = pl.DeviceIdType.MESH
+
+    def device(position):
+        return (position, tp) if axis == "seq" else (seq, position)
+
+    def slot(entry):
+        return me if entry is None else entry
+
+    peers = [lax.rem(me + offset + size, size) for offset, _ in offsets]
+    barrier = pltpu.get_barrier_semaphore()
+    for peer in peers:
+        pl.semaphore_signal(barrier, inc=1, device_id=device(peer), device_id_type=mesh_id)
+    pl.semaphore_wait(barrier, len(peers))
+
+    own = offsets_own_slot(offsets, me)
+    local = pltpu.make_async_copy(x_ref, out_ref.at[own], local_sem)
+    local.start()
+    copies = []
+    for k, ((_, entry), peer) in enumerate(zip(offsets, peers)):
+        copy = pltpu.make_async_remote_copy(
+            src_ref=x_ref,
+            dst_ref=out_ref.at[slot(entry)],
+            send_sem=send_sem.at[k],
+            recv_sem=recv_sem.at[k],
+            device_id=device(peer),
+            device_id_type=mesh_id,
+        )
+        copy.start()
+        copies.append(copy)
+    for copy in copies:
+        copy.wait_send()
+        copy.wait_recv()
+    local.wait()
+
+
+def offsets_own_slot(offsets, me):
+    slots = [entry for _, entry in offsets]
+    if None in slots:
+        return me
+    return len(offsets) // 2
+
+
+def exchange(block, axis, offsets, slots, collective_id):
+    count = len(offsets)
+    return pl.pallas_call(
+        functools.partial(exchange_kernel, axis, offsets),
+        out_shape=jax.ShapeDtypeStruct((slots,) + block.shape, block.dtype),
+        in_specs=[pl.BlockSpec(memory_space=pl.ANY)],
+        out_specs=pl.BlockSpec(memory_space=pl.ANY),
+        scratch_shapes=[
+            pltpu.SemaphoreType.DMA((count,)),
+            pltpu.SemaphoreType.DMA((count,)),
+            pltpu.SemaphoreType.DMA(()),
+        ],
+        compiler_params=pltpu.CompilerParams(
+            collective_id=collective_id, has_side_effects=True
+        ),
     )(block)
 
 
@@ -202,9 +267,10 @@
     query = joined[:, 0]
     keys = joined[:, 1]
     values = joined[:, 2]
-    query_sq, key_sq = lax.psum(
-        (jnp.sum(query * query, axis=-1), jnp.sum(keys * keys, axis=-1)), "tp"
-    )
+    parts = lax.axis_size("tp")
+    squares = jnp.stack([jnp.sum(query * query, axis=-1), jnp.sum(keys * keys, axis=-1)])
+    everyone = [(k, None) for k in range(1, parts)]
+    query_sq, key_sq = jnp.sum(exchange(squares, "tp", everyone, parts, 2), axis=0)
     full_width = local_width * lax.axis_size("tp")
     query_normed = (query * lax.rsqrt(query_sq / full_width + eps)[:, None] * q_gain).astype(
         jnp.bfloat16
@@ -213,13 +279,8 @@
         jnp.bfloat16
     )
     paired = jnp.stack([key_normed, values.astype(jnp.bfloat16)], axis=1)
-    pieces = []
-    for offset in (2, 1, 0, -1, -2):
-        if offset == 0:
-            pieces.append(paired)
-        else:
-            pieces.append(passed_along(paired, "seq", offset))
-    widened = jnp.concatenate(pieces, axis=0)
+    halo = [(2, 0), (1, 1), (-1, 3), (-2, 4)]
+    widened = exchange(paired, "seq", halo, 5, 3).reshape(5 * count, *paired.shape[1:])
     position = lax.axis_index("seq")
     outside = jnp.full((2 * count,), -1, jnp.int32)
     seg_pad = jnp.concatenate([outside, segment_ids, outside], axis=0)
@@ -239,7 +300,6 @@
     )
     blank = jnp.zeros_like(context)
     widened_context = jnp.stack([blank, blank, blank, context], axis=1)
-    parts = lax.axis_size("tp")
     chips = parts // 2
     core = lax.axis_index("tp") % 2
     by_owner = gathered.reshape(chips, 2, -1, *gathered.shape[1:])

time: 197 us -> 208 us (1.056)
  the two profiles are of different devices: /device:TPU:15 before, /device:TPU:1 now
where the time goes in v7:
time: 208 us; the launch traced here: 207 us
  Pallas kernels  154 us (74%)
  local copies, waits for them, and re-layouts  21.3 us (10%)
  matrix products  15.1 us (7%)
  other arithmetic  14.1 us (7%)
  starting transfers between devices  2.88 us (1%)
    pallas_call x1, Pallas kernels, gather_seq(): pl.pallas_call(functools.partial(gather_kernel, n), out_shape=jax.ShapeDt...  89.4 us
    pallas_call x2, Pallas kernels, exchange(): pl.pallas_call(functools.partial(exchange_kernel, axis, offsets), out_sha...  34.6 us
    pallas_call x1, Pallas kernels, scatter_chips(): pl.pallas_call(functools.partial(scatter_kernel, chips), out_shape=jax.Sh...  29.6 us
    unnamed x22, local copies, waits for them, and re-layouts  5.86 us
    dot_general x1, matrix products, shards(): jnp.einsum('td,dch->tch', normed, gathered[:, :3], preferred_element_type...  5.07 us
    slice x1, local copies, waits for them, and re-layouts, shards(): key_heads = widened[:, 0].reshape(5 * count, heads, HEAD_DIM)  5.06 us
    dot_general x1, matrix products, shards(): jnp.einsum('tkh,ycdkh->cytd', widened_context, by_owner, preferred_elemen...  4.85 us
  transfers between devices with their start and end apart: 1, of which 0 were waited for; matrix products, arithmetic and copies ran while one was open for 2% of the time, Pallas kernels for 0%

profile of v7, /device:TPU:1, one launch (start us, length us, event | category | flops | bytes accessed | tf_op | source)
XLA Modules:
  0.0 207.2 jit_solution(8226069486189066382)
XLA Ops:
  0.0 0.8 copy.51
  0.8 0.9 copy.50
  1.7 0.8 pad_maximum_fusion.1.x_ref
  2.5 89.4 %shard_map.82 = bf16[64,50,4,256]{3,2,1,0:T(4,128)(2,1)} custom-call(bf16[50,4,256]{2,1,0:T(4,128)(2,1)} %pad_maximum_fusion.1.x_ref), custom_call_target="tpu_custom_call" | custom-call | tf_op jit(solution)/shard_map/pallas_call | solution.py:111
  91.9 0.0 copy-done
  91.9 0.4 multiply_reduce_fusion
  92.3 0.0 copy-done.7
  92.3 5.1 %fusion.3 = f32[256,3,256]{0,2,1:T(8,128)S(1)} fusion(bf16[3200,3,256]{2,1,0:T(4,128)(2,1)} %bitcast.51, f32[3200]{0:T(1024)S(1)} %copy-done.7, f32[256]{0:T(256)S(1)} %add_rsqrt_fusion, bf16[256,3200]{1,0:T(8,128)(2,1)S(1)} %copy-done), kind=kOutput, calls=%fused_computation.3 | convolution fusion | flops 1261568000 | bytes 7353856 | tf_op jit(solution)/shard_map/td,dch->tch/dot_general | solution.py:261
  97.4 0.0 copy-start.5
  97.5 0.1 fusion.48
  97.5 0.1 copy.74
  97.6 0.2 copy.71
  97.9 0.2 copy.70
  98.0 1.0 multiply_reduce_fusion.1
  99.1 0.6 pad_maximum_fusion.2.x_ref
  99.6 15.5 %shard_map.83 = f32[8,2,256]{2,1,0:T(2,128)} custom-call(f32[2,256]{1,0:T(2,128)} %pad_maximum_fusion.2.x_ref), custom_call_target="tpu_custom_call" | custom-call | tf_op jit(solution)/shard_map/pallas_call | solution.py:226
  115.1 0.7 reduce_sum.57
  115.9 0.0 copy-done.5
  115.9 0.3 multiply_convert_fusion.2
  116.3 1.3 pad_maximum_fusion.x_ref
  117.6 19.1 %shard_map.84 = bf16[5,256,2,256]{3,2,1,0:T(2,128)(2,1)} custom-call(bf16[256,2,256]{2,1,0:T(2,128)(2,1)} %pad_maximum_fusion.x_ref), custom_call_target="tpu_custom_call" | custom-call | tf_op jit(solution)/shard_map/pallas_call | solution.py:226
  136.6 5.1 %fusion.47 = (bf16[1280,1,256]{2,1,0:T(2,128)(2,1)S(1)}, bf16[1280,1,256]{2,1,0:T(2,128)(2,1)}) fusion(bf16[1280,2,256]{2,1,0:T(2,128)(2,1)} %bitcast.50), kind=kLoop, calls=%fused_computation.60 | loop fusion | bytes 2621440 | tf_op jit(solution)/shard_map/slice | solution.py:290
  141.7 3.7 %copy.57 = bf16[1280,1,256]{0,2,1:T(8,128)(2,1)} copy(bf16[1280,1,256]{2,1,0:T(2,128)(2,1)} %get-tuple-element.8) | data formatting | bytes 1310720 | tf_op jit(solution)/shard_map/slice | solution.py:291
  145.4 0.1 copy.58
  145.5 2.6 %copy.72 = bf16[1280,1,256]{0,2,1:T(8,128)(2,1)} copy(bf16[1280,1,256]{2,1,0:T(2,128)(2,1)S(1)} %get-tuple-element.7) | data formatting | bytes 1310720
  148.1 0.1 dynamic_slice.17
  148.2 0.1 fusion.32
  148.3 1.0 broadcast_compare_fusion
  149.2 0.0 copy-done.6
  149.2 0.1 multiply_convert_fusion.1
  149.4 2.7 %fusion.49 = f32[2,256]{1,0:T(2,128)S(1)} fusion(bf16[256,2,128]{2,0,1:T(8,128)(2,1)S(1)} %multiply_convert_fusion.1, bf16[1280,2,128]{0,2,1:T(8,128)(2,1)} %bitcast.55, pred[256,1280]{1,0:T(8,128)(4,1)} %broadcast_compare_fusion), kind=kOutput, calls=%fused_computation.62 | convolution fusion | flops 171050240 | bytes 1116160 | tf_op jit(solution)/shard_map/sub | solution.py:294
  152.1 0.0 copy-done.1
  152.1 2.4 %fusion.26 = bf16[256,2,128]{0,2,1:T(8,128)(2,1)S(1)} fusion(bf16[1280,2,128]{0,2,1:T(8,128)(2,1)S(1)} %bitcast.54, pred[256,1280]{1,0:T(8,128)(4,1)} %broadcast_compare_fusion, bf16[256,2,128]{2,0,1:T(8,128)(2,1)S(1)} %multiply_convert_fusion.1, bf16[1280,2,128]{0,2,1:T(8,128)(2,1)S(1)} %bitcast.56, f32[256,2]{0,1:T(2,128)S(1)} %bitcast.64), kind=kOutput, calls=%fused_computation.25 | convolution fusion | flops 338953984 | bytes 1902592 | tf_op jit(solution)/shard_map/hqk,khd->qhd/dot_general | solution.py:297
  154.6 0.1 copy.61
  154.7 0.1 pad_maximum_fusion.3
  154.8 4.8 %fusion.10 = f32[4,2,400,256]{3,2,1,0:T(8,128)S(1)} fusion(bf16[4,2,400,4,256]{4,3,2,1,0:T(4,128)(2,1)} %bitcast.52, bf16[256,1,256]{2,0,1:T(8,128)(2,1)S(1)} %copy.61, bf16[4]{0:T(256)(128)(2,1)S(1)} %pad_maximum_fusion.3), kind=kOutput, calls=%fused_computation.15 | convolution fusion | flops 1677983744 | bytes 9961480 | tf_op jit(solution)/shard_map/tkh,ycdkh->cytd/dot_general | solution.py:306
  159.6 2.0 constant_dynamic-slice_fusion
  161.6 2.9 %collective-permute-start = (f32[4,256,400]{1,2,0:T(8,128)}, f32[4,256,400]{1,2,0:T(8,128)}, u32[]{:S(2)}, u32[]{:S(2)}) collective-permute-start(f32[4,256,400]{1,2,0:T(8,128)} %get-tuple-element.6), channel_id=1, source_target_pairs={{0,1},{1,0},{2,3},{3,2},{4,5},{5,4},{6,7},{7,6},{8,9},{9,8},{10,11... | collective-permute-start | bytes 4915208 | tf_op jit(solution)/shard_map/ppermute | solution.py:311
  164.5 1.9 convert_element_type.41
  166.4 1.8 copy.73
  168.2 0.0 collective-permute-done
  168.3 2.8 %copy.64 = f32[4,256,400]{2,1,0:T(8,128)} copy(f32[4,256,400]{1,2,0:T(8,128)} %collective-permute-done) | data formatting | bytes 3276800 | tf_op jit(solution)/shard_map/ppermute | solution.py:311
  171.1 3.0 %fusion.9.x_ref = bf16[4,256,400]{2,1,0:T(8,128)(2,1)} fusion(f32[4,256,400]{2,1,0:T(8,128)} %copy.64, f32[4,1,400,256]{2,3,0,1:T(8,128)S(1)} %copy.73), kind=kLoop, calls=%fused_computation.13 | loop fusion | flops 819200 | bytes 4096000 | tf_op jit(solution)/shard_map/convert_element_type | solution.py:312
  174.1 29.6 %shard_map.85 = bf16[4,256,400]{2,1,0:T(8,128)(2,1)} custom-call(bf16[4,256,400]{2,1,0:T(8,128)(2,1)} %fusion.9.x_ref), custom_call_target="tpu_custom_call" | custom-call | tf_op jit(solution)/shard_map/pallas_call | solution.py:163
  203.7 1.4 convert_reduce_fusion
  205.1 0.0 copy-done.4
  205.1 1.3 add_convert_fusion
  206.4 0.8 copy.65
  (14 shorter events, 0.1 us)
Async XLA Ops:
  2.5 89.4 %copy-start = (bf16[256,3200]{1,0:T(8,128)(2,1)S(1)}, bf16[256,3200]{1,0:T(8,128)(2,1)}, u32[]{:S(2)}) copy-start(bf16[256,3200]{1,0:T(8,128)(2,1)} %param.8) | copy-start | bytes 4915204
  2.5 89.9 %copy-start.7 = (f32[3200]{0:T(1024)S(1)}, f32[3200]{0:T(1024)}, u32[]{:S(2)}) copy-start(f32[3200]{0:T(1024)} %param.9) | copy-start | bytes 38404
  97.4 18.5 %copy-start.5 = (f32[256]{0:T(256)S(1)}, f32[256]{0:T(256)}, u32[]{:S(2)}) copy-start(f32[256]{0:T(256)} %param.12) | copy-start | bytes 3076
  141.7 6.4 %copy-start.3 = (s32[16384]{0:T(1024)S(1)}, s32[16384]{0:T(1024)}, u32[]{:S(2)}) copy-start(s32[16384]{0:T(1024)} %param.15) | copy-start | bytes 196612
  141.7 7.6 %copy-start.6 = (f32[256]{0:T(256)S(1)}, f32[256]{0:T(256)}, u32[]{:S(2)}) copy-start(f32[256]{0:T(256)} %param.11) | copy-start | bytes 3076
  149.4 2.8 %copy-start.1 = (bf16[1280,1,256]{0,2,1:T(8,128)(2,1)S(1)}, bf16[1280,1,256]{0,2,1:T(8,128)(2,1)}, u32[]{:S(2)}) copy-start(bf16[1280,1,256]{0,2,1:T(8,128)(2,1)} %copy.57) | copy-start | bytes 1966084
  149.4 2.8 %copy-start.2 = (bf16[1280,1,256]{0,2,1:T(8,128)(2,1)S(1)}, bf16[1280,1,256]{0,2,1:T(8,128)(2,1)}, u32[]{:S(2)}) copy-start(bf16[1280,1,256]{0,2,1:T(8,128)(2,1)} %copy.72) | copy-start | bytes 1966084
  161.6 6.6 %collective-permute-start = (f32[4,256,400]{1,2,0:T(8,128)}, f32[4,256,400]{1,2,0:T(8,128)}, u32[]{:S(2)}, u32[]{:S(2)}) collective-permute-start(f32[4,256,400]{1,2,0:T(8,128)} %get-tuple-element.6), channel_id=1, source_target_pairs={{0,1},{1,0},{2,3},{3,2},{4,5},{5,4},{6,7},{7,6},{8,9},{9,8},{10,11... | collective-permute-start | bytes 4915208 | tf_op jit(solution)/shard_map/ppermute | solution.py:311
  174.1 31.1 %copy-start.4 = (f32[400]{0:T(512)S(1)}, f32[400]{0:T(512)}, u32[]{:S(2)}) copy-start(f32[400]{0:T(512)} %param.14) | copy-start | bytes 4804

commit v8 on v6

--- a/solution.py
+++ b/solution.py
@@ -20,103 +20,137 @@
     return lax.ppermute(x, axis, pairs)
 
 
-def gather_kernel(n, x_ref, out_ref, pair_sems, row_sems, ring_sems, local_sem):
+def gather_kernel(x_ref, out_ref, pair_sems, row_sems, lane_sems, ring_sems, cross_sems, local_sem):
+    rings, slab = out_ref.shape[0], out_ref.shape[1]
+    pair = 2
+    row = slab // pair
+    lanes = out_ref.shape[-1] // 2
+    first_lanes, second_lanes = pl.ds(0, lanes), pl.ds(lanes, lanes)
     me = lax.axis_index("seq")
     tp = lax.axis_index("tp")
     mesh_id = pl.DeviceIdType.MESH
-    pair, row = 2, 4
-    slab = pair * row
-    rings = n // slab
-    low = me % pair
-    across = (me // pair) % row
     ring = me // slab
-    partner = me - low + (1 - low)
-    row_peers = [ring * slab + ((across + k) % row) * pair + low for k in range(1, row)]
-    ahead = ((ring + 1) % rings) * slab + me % slab
-    behind = ((ring + rings - 1) % rings) * slab + me % slab
+    spot = me % slab
+    low = spot % pair
+    across = spot // pair
+    base = spot - low
+
+    def device(r, s):
+        return (r * slab + s, tp)
+
+    ahead = (ring + 1) % rings
+    behind = (ring + rings - 1) % rings
+    partner = base + 1 - low
+    row_spots = [((across + k) % row) * pair + low for k in range(1, row)]
+    right = ((across + 1) % row) * pair + low
+    left = ((across + row - 1) % row) * pair + low
 
     barrier = pltpu.get_barrier_semaphore()
-    for peer in [partner, ahead, behind] + row_peers:
-        pl.semaphore_signal(barrier, inc=1, device_id=(peer, tp), device_id_type=mesh_id)
-    pl.semaphore_wait(barrier, 3 + len(row_peers))
-
-    local = pltpu.make_async_copy(x_ref, out_ref.at[me], local_sem)
+    targets = [device(ring, partner), device(ahead, spot), device(behind, spot)]
+    targets += [device(ring, s) for s in row_spots]
+    for target in targets:
+        pl.semaphore_signal(barrier, inc=1, device_id=target, device_id_type=mesh_id)
+    pl.semaphore_wait(barrier, len(targets))
+
+    def remote(window, target, sems, index):
+        return pltpu.make_async_remote_copy(
+            src_ref=window,
+            dst_ref=window,
+            send_sem=sems.at[(0,) + index],
+            recv_sem=sems.at[(1,) + index],
+            device_id=target,
+            device_id_type=mesh_id,
+        )
+
+    def finish(copies):
+        for copy in copies:
+            copy.wait_send()
+            copy.wait_recv()
+
+    local = pltpu.make_async_copy(x_ref, out_ref.at[ring, spot], local_sem)
     local.start()
-    first = pltpu.make_async_remote_copy(
+    swap = pltpu.make_async_remote_copy(
         src_ref=x_ref,
-        dst_ref=out_ref.at[me],
+        dst_ref=out_ref.at[ring, spot],
         send_sem=pair_sems.at[0],
         recv_sem=pair_sems.at[1],
-        device_id=(partner, tp),
+        device_id=device(ring, partner),
         device_id_type=mesh_id,
     )
-    first.start()
+    swap.start()
     local.wait()
-    first.wait_send()
-    first.wait_recv()
-
-    base = me - low
-    second = []
-    for k, peer in enumerate(row_peers):
-        copy = pltpu.make_async_remote_copy(
-            src_ref=out_ref.at[pl.ds(base, pair)],
-            dst_ref=out_ref.at[pl.ds(base, pair)],
-            send_sem=row_sems.at[0, k],
-            recv_sem=row_sems.at[1, k],
-            device_id=(peer, tp),
-            device_id_type=mesh_id,
-        )
+    finish([swap])
+
+    pair_a = out_ref.at[ring, pl.ds(base, pair), :, :, first_lanes]
+    rows_a = [remote(pair_a, device(ring, s), row_sems, (k,)) for k, s in enumerate(row_spots)]
+    for copy in rows_a:
         copy.start()
-        second.append(copy)
-    for copy in second:
-        copy.wait_send()
-        copy.wait_recv()
+    for t in range(rings - 1):
+        cw = out_ref.at[(ring - t + rings) % rings, base, :, :, second_lanes]
+        ccw = out_ref.at[(ring + t) % rings, base + 1, :, :, second_lanes]
+        step = [
+            remote(cw, device(ahead, spot), lane_sems, (0, t)),
+            remote(ccw, device(behind, spot), lane_sems, (1, t)),
+        ]
+        for copy in step:
+            copy.start()
+        finish(step)
+    finish(rows_a)
 
     half = slab // 2
-
-    def step(t, carry):
-        forward = (ring - t + rings) % rings
-        backward = (ring + t) % rings
-        window_f = out_ref.at[pl.ds(forward * slab, half)]
-        window_b = out_ref.at[pl.ds(backward * slab + half, half)]
-        to_ahead = pltpu.make_async_remote_copy(
-            src_ref=window_f,
-            dst_ref=window_f,
-            send_sem=ring_sems.at[0, 0, t],
-            recv_sem=ring_sems.at[1, 0, t],
-            device_id=(ahead, tp),
-            device_id_type=mesh_id,
-        )
-        to_behind = pltpu.make_async_remote_copy(
-            src_ref=window_b,
-            dst_ref=window_b,
-            send_sem=ring_sems.at[0, 1, t],
-            recv_sem=ring_sems.at[1, 1, t],
-            device_id=(behind, tp),
-            device_id_type=mesh_id,
-        )
-        to_ahead.start()
-        to_behind.start()
-        to_ahead.wait_send()
-        to_behind.wait_send()
-        to_ahead.wait_recv()
-        to_behind.wait_recv()
-        return carry
-
-    lax.fori_loop(0, rings - 1, step, 0)
-
-
-def gather_seq(block):
-    n = lax.axis_size("seq")
+    mid = rings // 2
+    cross = [
+        remote(out_ref.at[:, pl.ds(base, pair), :, :, second_lanes], device(ring, right), cross_sems, (0, 0)),
+        remote(out_ref.at[:, pl.ds(base, pair), :, :, second_lanes], device(ring, left), cross_sems, (1, 0)),
+    ]
+    for copy in cross:
+        copy.start()
+    onward = None
+    for t in range(rings - 1):
+        cw = out_ref.at[(ring - t + rings) % rings, pl.ds(0, half), :, :, first_lanes]
+        ccw = out_ref.at[(ring + t) % rings, pl.ds(half, half), :, :, first_lanes]
+        step = [
+            remote(cw, device(ahead, spot), ring_sems, (0, t)),
+            remote(ccw, device(behind, spot), ring_sems, (1, t)),
+        ]
+        for copy in step:
+            copy.start()
+        finish(step)
+        if t == 2:
+            finish(cross)
+            from_left = ((across + row - 1) % row) * pair
+            from_right = ((across + 1) % row) * pair
+            onward = [
+                remote(
+                    out_ref.at[pl.ds(0, mid), pl.ds(from_left, pair), :, :, second_lanes],
+                    device(ring, right),
+                    cross_sems,
+                    (0, 1),
+                ),
+                remote(
+                    out_ref.at[pl.ds(mid, mid), pl.ds(from_right, pair), :, :, second_lanes],
+                    device(ring, left),
+                    cross_sems,
+                    (1, 1),
+                ),
+            ]
+            for copy in onward:
+                copy.start()
+    finish(onward)
+
+
+def gather_seq(block, rings, slab):
     return pl.pallas_call(
-        functools.partial(gather_kernel, n),
-        out_shape=jax.ShapeDtypeStruct((n,) + block.shape, block.dtype),
+        gather_kernel,
+        out_shape=jax.ShapeDtypeStruct((rings, slab) + block.shape, block.dtype),
         in_specs=[pl.BlockSpec(memory_space=pl.ANY)],
         out_specs=pl.BlockSpec(memory_space=pl.ANY),
         scratch_shapes=[
             pltpu.SemaphoreType.DMA((2,)),
-            pltpu.SemaphoreType.DMA((2, 3)),
-            pltpu.SemaphoreType.DMA((2, 2, n // 8)),
+            pltpu.SemaphoreType.DMA((2, slab // 2 - 1)),
+            pltpu.SemaphoreType.DMA((2, 2, rings - 1)),
+            pltpu.SemaphoreType.DMA((2, 2, rings - 1)),
+            pltpu.SemaphoreType.DMA((2, 2, 2)),
             pltpu.SemaphoreType.DMA(()),
         ],
         compiler_params=pltpu.CompilerParams(collective_id=0, has_side_effects=True),
@@ -192,7 +226,8 @@
     heads = local_width // HEAD_DIM
     stacked = jnp.concatenate([qkv_weight, jnp.transpose(out_weight)[:, None, :]], axis=1)
     rows, kinds, width = stacked.shape
-    gathered = gather_seq(stacked).reshape(-1, kinds, width)
+    slab = 8
+    gathered = gather_seq(stacked, lax.axis_size("seq") // slab, slab).reshape(-1, kinds, width)
     joined = jnp.einsum(
         "td,dch->tch",
         normed,

time: 197 us -> 190 us (0.964)
  the two profiles are of different devices: /device:TPU:15 before, /device:TPU:79 now
where the time goes in v8:
time: 190 us; the launch traced here: 189 us
  Pallas kernels  102 us (54%)
  blocking collectives  25.5 us (13%)
  starting transfers between devices  14.8 us (8%)
  matrix products  14.5 us (8%)
  local copies, waits for them, and re-layouts  11.6 us (6%)
  other arithmetic  10.1 us (5%)
  waiting for transfers between devices  10 us (5%)
    pallas_call x1, Pallas kernels, gather_seq(): pl.pallas_call(gather_kernel, out_shape=jax.ShapeDtypeStruct((rings, slab...  74.7 us
    pallas_call x1, Pallas kernels, scatter_chips(): pl.pallas_call(functools.partial(scatter_kernel, chips), out_shape=jax.Sh...  27.6 us
    psum x1, blocking collectives, shards(): lax.psum((jnp.sum(query * query, axis=-1), jnp.sum(keys * keys, axis=-1))...  25.5 us
    ppermute x4, starting transfers between devices, passed_along(): return lax.ppermute(x, axis, pairs)  12.4 us
    ppermute x4, waiting for transfers between devices, passed_along(): return lax.ppermute(x, axis, pairs)  10 us
    dot_general x1, matrix products, shards(): jnp.einsum('td,dch->tch', normed, gathered[:, :3], preferred_element_type...  5.08 us
    dot_general x1, matrix products, shards(): jnp.einsum('tkh,ycdkh->cytd', widened_context, by_owner, preferred_elemen...  4.85 us
    unnamed x17, local copies, waits for them, and re-layouts  4.75 us
  transfers between devices with their start and end apart: 5, of which 2 were waited for; matrix products, arithmetic and copies ran while one was open for 4% of the time, Pallas kernels for 0%

profile of v8, /device:TPU:79, one launch (start us, length us, event | category | flops | bytes accessed | tf_op | source)
XLA Modules:
  0.0 189.1 jit_solution(8489026037729933604)
XLA Ops:
  0.0 0.9 copy.30
  0.9 0.8 copy.31
  1.7 0.8 pad_maximum_fusion.1.x_ref
  2.5 74.7 %shard_map.82 = bf16[8,8,50,4,256]{4,3,2,1,0:T(4,128)(2,1)} custom-call(bf16[50,4,256]{2,1,0:T(4,128)(2,1)} %pad_maximum_fusion.1.x_ref), custom_call_target="tpu_custom_call" | custom-call | tf_op jit(solution)/shard_map/pallas_call | solution.py:143
  77.2 0.0 copy-done
  77.2 0.4 multiply_reduce_fusion
  77.6 0.0 copy-done.5
  77.6 0.0 copy-start.3
  77.6 5.1 %fusion.3 = f32[256,3,256]{0,2,1:T(8,128)S(1)} fusion(bf16[3200,3,256]{2,1,0:T(4,128)(2,1)} %bitcast.45, f32[3200]{0:T(1024)S(1)} %copy-done.5, f32[256]{0:T(256)S(1)} %add_rsqrt_fusion.2, bf16[256,3200]{1,0:T(8,128)(2,1)S(1)} %copy-done), kind=kOutput, calls=%fused_computation.3 | convolution fusion | flops 1261568000 | bytes 7353856 | tf_op jit(solution)/shard_map/td,dch->tch/dot_general | solution.py:231
  82.7 0.0 copy-start.1
  82.7 0.0 copy-start.4
  82.7 0.1 multiply_reduce_fusion.1
  82.8 25.5 %all-reduce = (f32[256]{0:T(256)S(1)}, f32[256]{0:T(256)S(1)}) all-reduce(f32[256]{0:T(256)S(1)} %get-tuple-element.6, f32[256]{0:T(256)S(1)} %get-tuple-element.5), channel_id=1, replica_groups=mesh['seq'=64,'tp'=8] {'tp'}, use_global_device_ids=true, to_apply=%region_2.0 | all-reduce | flops 512 | bytes 4096 | tf_op jit(solution)/shard_map/psum | solution.py:240
  108.3 0.1 fusion.44
  108.5 4.4 %collective-permute-start = (bf16[256,2,256]{0,2,1:T(8,128)(2,1)S(1)}, bf16[256,2,256]{0,2,1:T(8,128)(2,1)}, u32[]{:S(2)}, u32[]{:S(2)}) collective-permute-start(bf16[256,2,256]{0,2,1:T(8,128)(2,1)S(1)} %pad_maximum_fusion), channel_id=1, source_target_pairs={{0,16},{8,24},{16,32},{24,40},{32,48},{40,56},{48,64},{56,72},{64,... | collective-permute-start | bytes 786440 | tf_op jit(solution)/shard_map/ppermute | solution.py:20
  112.9 2.8 %collective-permute-start.1 = (bf16[256,2,256]{0,2,1:T(8,128)(2,1)S(1)}, bf16[256,2,256]{0,2,1:T(8,128)(2,1)}, u32[]{:S(2)}, u32[]{:S(2)}) collective-permute-start(bf16[256,2,256]{0,2,1:T(8,128)(2,1)S(1)} %pad_maximum_fusion), channel_id=1, source_target_pairs={{0,8},{8,16},{16,24},{24,32},{32,40},{40,48},{48,56},{56,64},{64,7... | collective-permute-start | bytes 786440 | tf_op jit(solution)/shard_map/ppermute | solution.py:20
  115.6 2.5 %collective-permute-start.2 = (bf16[256,2,256]{0,2,1:T(8,128)(2,1)S(1)}, bf16[256,2,256]{0,2,1:T(8,128)(2,1)S(1)}, u32[]{:S(2)}, u32[]{:S(2)}) collective-permute-start(bf16[256,2,256]{0,2,1:T(8,128)(2,1)S(1)} %pad_maximum_fusion), channel_id=1, source_target_pairs={{8,0},{16,8},{24,16},{32,24},{40,32},{48,40},{56,48},{64,56},{72,6... | collective-permute-start | bytes 786440 | tf_op jit(solution)/shard_map/ppermute | solution.py:20
  118.2 2.7 %collective-permute-start.3 = (bf16[256,2,256]{0,2,1:T(8,128)(2,1)S(1)}, bf16[256,2,256]{0,2,1:T(8,128)(2,1)S(1)}, u32[]{:S(2)}, u32[]{:S(2)}) collective-permute-start(bf16[256,2,256]{0,2,1:T(8,128)(2,1)S(1)} %pad_maximum_fusion), channel_id=1, source_target_pairs={{16,0},{24,8},{32,16},{40,24},{48,32},{56,40},{64,48},{72,56},{80,... | collective-permute-start | bytes 786440 | tf_op jit(solution)/shard_map/ppermute | solution.py:20
  120.9 0.1 copy.33
  121.1 0.0 copy-done.1
  121.1 0.1 dynamic_slice.17
  121.2 0.1 fusion.32
  121.3 0.3 broadcast_compare_fusion
  121.5 0.0 copy-done.4
  121.5 0.8 multiply_convert_fusion.1
  122.3 0.1 pad_maximum_fusion.2
  122.4 0.0 collective-permute-done
  122.4 1.0 constant_dynamic-update-slice_fusion.4
  123.4 0.0 collective-permute-done.1
  123.4 1.0 constant_dynamic-update-slice_fusion.3
  124.4 3.1 %collective-permute-done.2 = bf16[256,2,256]{0,2,1:T(8,128)(2,1)S(1)} collective-permute-done((bf16[256,2,256]{0,2,1:T(8,128)(2,1)S(1)}, bf16[256,2,256]{0,2,1:T(8,128)(2,1)S(1)}, u32[]{:S(2)}, u32[]{:S(2)}) %collective-permute-start.2) | collective-permute-done | bytes 262176 | tf_op jit(solution)/shard_map/ppermute | solution.py:20
  127.5 6.9 %collective-permute-done.3 = bf16[256,2,256]{0,2,1:T(8,128)(2,1)S(1)} collective-permute-done((bf16[256,2,256]{0,2,1:T(8,128)(2,1)S(1)}, bf16[256,2,256]{0,2,1:T(8,128)(2,1)S(1)}, u32[]{:S(2)}, u32[]{:S(2)}) %collective-permute-start.3) | collective-permute-done | bytes 262176 | tf_op jit(solution)/shard_map/ppermute | solution.py:20
  134.4 0.1 fusion.43
  134.5 2.3 %fusion.45 = f32[2,256]{1,0:T(2,128)S(1)} fusion(bf16[256,2,128]{2,0,1:T(8,128)(2,1)} %multiply_convert_fusion.1, bf16[1280,2,128]{0,2,1:T(8,128)(2,1)S(1)} %bitcast.48, pred[256,1280]{1,0:T(8,128)(4,1)S(1)} %broadcast_compare_fusion), kind=kOutput, calls=%fused_computation.63 | convolution fusion | flops 171050240 | bytes 1116160 | tf_op jit(solution)/shard_map/sub | solution.py:268
  136.8 2.3 %fusion.26 = bf16[256,2,128]{0,2,1:T(8,128)(2,1)S(1)} fusion(bf16[1280,2,128]{0,2,1:T(8,128)(2,1)S(1)} %bitcast.50, pred[256,1280]{1,0:T(8,128)(4,1)S(1)} %broadcast_compare_fusion, bf16[256,2,128]{2,0,1:T(8,128)(2,1)} %multiply_convert_fusion.1, bf16[1280,2,128]{0,2,1:T(8,128)(2,1)S(1)} %bitcast.49, f32[256,2]{0,1:T(2,128)S(1)} %bitcast.54), kind=kOutput, calls=%fused_computation.25 | convolution fusion | flops 338953984 | bytes 1902592 | tf_op jit(solution)/shard_map/hqk,khd->qhd/dot_general | solution.py:271
  139.1 0.1 copy.35
  139.2 4.8 %fusion.10 = f32[4,2,400,256]{3,2,1,0:T(8,128)S(1)} fusion(bf16[4,2,400,4,256]{4,3,2,1,0:T(4,128)(2,1)} %bitcast.46, bf16[256,1,256]{2,0,1:T(8,128)(2,1)S(1)} %copy.35, bf16[4]{0:T(256)(128)(2,1)S(1)} %pad_maximum_fusion.2), kind=kOutput, calls=%fused_computation.15 | convolution fusion | flops 1677983744 | bytes 9961480 | tf_op jit(solution)/shard_map/tkh,ycdkh->cytd/dot_general | solution.py:281
  144.0 2.0 %constant_dynamic-slice_fusion = (f32[4,1,400,256]{3,2,1,0:T(8,128)}, f32[4,256,400]{1,2,0:T(8,128)}) fusion(f32[4,2,400,256]{3,2,1,0:T(8,128)S(1)} %fusion.10, s32[]{:T(128)S(6)} %select_n.36, s32[]{:T(128)S(6)} %select_n.37), kind=kLoop, calls=%fused_computation.51 | loop fusion | bytes 6553608 | tf_op jit(solution)/shard_map/dynamic-slice
  146.0 2.4 %collective-permute-start.4 = (f32[4,256,400]{1,2,0:T(8,128)}, f32[4,256,400]{1,2,0:T(8,128)}, u32[]{:S(2)}, u32[]{:S(2)}) collective-permute-start(f32[4,256,400]{1,2,0:T(8,128)} %get-tuple-element.10), channel_id=1, source_target_pairs={{0,1},{1,0},{2,3},{3,2},{4,5},{5,4},{6,7},{7,6},{8,9},{9,8},{10,11... | collective-permute-start | bytes 4915208 | tf_op jit(solution)/shard_map/ppermute | solution.py:286
  148.4 1.9 %convert_element_type.41 = f32[256,3200]{1,0:T(8,128)} convert(bf16[256,3200]{1,0:T(8,128)(2,1)S(1)} %copy-done) | non-fusion elementwise | flops 819200 | bytes 4915200 | tf_op jit(solution)/shard_map/convert_element_type | solution.py:221
  150.3 1.8 copy.44
  152.1 0.0 collective-permute-done.4
  152.1 2.9 %copy.38 = f32[4,256,400]{2,1,0:T(8,128)} copy(f32[4,256,400]{1,2,0:T(8,128)} %collective-permute-done.4) | data formatting | bytes 3276800 | tf_op jit(solution)/shard_map/ppermute | solution.py:286
  155.0 2.9 %fusion.9.x_ref = bf16[4,256,400]{2,1,0:T(8,128)(2,1)} fusion(f32[4,256,400]{2,1,0:T(8,128)} %copy.38, f32[4,1,400,256]{2,3,0,1:T(8,128)S(1)} %copy.44), kind=kLoop, calls=%fused_computation.13 | loop fusion | flops 819200 | bytes 4096000 | tf_op jit(solution)/shard_map/convert_element_type | solution.py:287
  157.9 27.6 %shard_map.83 = bf16[4,256,400]{2,1,0:T(8,128)(2,1)} custom-call(bf16[4,256,400]{2,1,0:T(8,128)(2,1)} %fusion.9.x_ref), custom_call_target="tpu_custom_call" | custom-call | tf_op jit(solution)/shard_map/pallas_call | solution.py:197
  185.5 1.4 convert_reduce_fusion
  187.0 1.3 add_convert_fusion
  188.3 0.8 copy.39
  (14 shorter events, 0.1 us)
Async XLA Ops:
  2.5 74.7 %copy-start = (bf16[256,3200]{1,0:T(8,128)(2,1)S(1)}, bf16[256,3200]{1,0:T(8,128)(2,1)}, u32[]{:S(2)}) copy-start(bf16[256,3200]{1,0:T(8,128)(2,1)} %param.8) | copy-start | bytes 4915204
  2.5 75.1 %copy-start.5 = (f32[3200]{0:T(1024)S(1)}, f32[3200]{0:T(1024)}, u32[]{:S(2)}) copy-start(f32[3200]{0:T(1024)} %param.9) | copy-start | bytes 38404
  77.6 30.7 %copy-start.3 = (f32[256]{0:T(256)S(1)}, f32[256]{0:T(256)}, u32[]{:S(2)}) copy-start(f32[256]{0:T(256)} %param.12) | copy-start | bytes 3076
  82.7 38.4 %copy-start.1 = (s32[16384]{0:T(1024)S(1)}, s32[16384]{0:T(1024)}, u32[]{:S(2)}) copy-start(s32[16384]{0:T(1024)} %param.15) | copy-start | bytes 196612
  82.7 38.8 %copy-start.4 = (f32[256]{0:T(256)S(1)}, f32[256]{0:T(256)}, u32[]{:S(2)}) copy-start(f32[256]{0:T(256)} %param.11) | copy-start | bytes 3076
  108.5 13.9 %collective-permute-start = (bf16[256,2,256]{0,2,1:T(8,128)(2,1)S(1)}, bf16[256,2,256]{0,2,1:T(8,128)(2,1)}, u32[]{:S(2)}, u32[]{:S(2)}) collective-permute-start(bf16[256,2,256]{0,2,1:T(8,128)(2,1)S(1)} %pad_maximum_fusion), channel_id=1, source_target_pairs={{0,16},{8,24},{16,32},{24,40},{32,48},{40,56},{48,64},{56,72},{64,... | collective-permute-start | bytes 786440 | tf_op jit(solution)/shard_map/ppermute | solution.py:20
  112.9 10.5 %collective-permute-start.1 = (bf16[256,2,256]{0,2,1:T(8,128)(2,1)S(1)}, bf16[256,2,256]{0,2,1:T(8,128)(2,1)}, u32[]{:S(2)}, u32[]{:S(2)}) collective-permute-start(bf16[256,2,256]{0,2,1:T(8,128)(2,1)S(1)} %pad_maximum_fusion), channel_id=1, source_target_pairs={{0,8},{8,16},{16,24},{24,32},{32,40},{40,48},{48,56},{56,64},{64,7... | collective-permute-start | bytes 786440 | tf_op jit(solution)/shard_map/ppermute | solution.py:20
  115.6 11.8 %collective-permute-start.2 = (bf16[256,2,256]{0,2,1:T(8,128)(2,1)S(1)}, bf16[256,2,256]{0,2,1:T(8,128)(2,1)S(1)}, u32[]{:S(2)}, u32[]{:S(2)}) collective-permute-start(bf16[256,2,256]{0,2,1:T(8,128)(2,1)S(1)} %pad_maximum_fusion), channel_id=1, source_target_pairs={{8,0},{16,8},{24,16},{32,24},{40,32},{48,40},{56,48},{64,56},{72,6... | collective-permute-start | bytes 786440 | tf_op jit(solution)/shard_map/ppermute | solution.py:20
  118.2 16.2 %collective-permute-start.3 = (bf16[256,2,256]{0,2,1:T(8,128)(2,1)S(1)}, bf16[256,2,256]{0,2,1:T(8,128)(2,1)S(1)}, u32[]{:S(2)}, u32[]{:S(2)}) collective-permute-start(bf16[256,2,256]{0,2,1:T(8,128)(2,1)S(1)} %pad_maximum_fusion), channel_id=1, source_target_pairs={{16,0},{24,8},{32,16},{40,24},{48,32},{56,40},{64,48},{72,56},{80,... | collective-permute-start | bytes 786440 | tf_op jit(solution)/shard_map/ppermute | solution.py:20
  146.0 6.1 %collective-permute-start.4 = (f32[4,256,400]{1,2,0:T(8,128)}, f32[4,256,400]{1,2,0:T(8,128)}, u32[]{:S(2)}, u32[]{:S(2)}) collective-permute-start(f32[4,256,400]{1,2,0:T(8,128)} %get-tuple-element.10), channel_id=1, source_target_pairs={{0,1},{1,0},{2,3},{3,2},{4,5},{5,4},{6,7},{7,6},{8,9},{9,8},{10,11... | collective-permute-start | bytes 4915208 | tf_op jit(solution)/shard_map/ppermute | solution.py:286
  157.9 29.0 %copy-start.2 = (f32[400]{0:T(512)S(1)}, f32[400]{0:T(512)}, u32[]{:S(2)}) copy-start(f32[400]{0:T(512)} %param.14) | copy-start | bytes 4804

commit v9 on v8

--- a/solution.py
+++ b/solution.py
@@ -157,31 +157,47 @@
     )(block)
 
 
-def scatter_kernel(chips, x_ref, out_ref, send_sem, recv_sem, local_sem):
+def scatter_kernel(terms_ref, out_ref, mine, incoming, sums, send_sem, recv_sem, local_sems):
+    chips = out_ref.shape[0]
     seq = lax.axis_index("seq")
     tp = lax.axis_index("tp")
     mesh_id = pl.DeviceIdType.MESH
     core = tp % 2
-    mine = tp // 2
-    owners = [(mine + k) % chips for k in range(1, chips)]
+    here = tp // 2
+    owners = [(here + k) % chips for k in range(1, chips)]
+    targets = [(seq, tp + 1 - 2 * core)] + [(seq, owner * 2 + core) for owner in owners]
 
     barrier = pltpu.get_barrier_semaphore()
-    for owner in owners:
-        pl.semaphore_signal(
-            barrier, inc=1, device_id=(seq, owner * 2 + core), device_id_type=mesh_id
-        )
-    pl.semaphore_wait(barrier, chips - 1)
-
-    local = pltpu.make_async_copy(x_ref.at[mine], out_ref.at[mine], local_sem)
+    for target in targets:
+        pl.semaphore_signal(barrier, inc=1, device_id=target, device_id_type=mesh_id)
+    pl.semaphore_wait(barrier, len(targets))
+
+    keep = pltpu.make_async_copy(terms_ref.at[core], mine, local_sems.at[0])
+    keep.start()
+    swap = pltpu.make_async_remote_copy(
+        src_ref=terms_ref.at[1 - core],
+        dst_ref=incoming,
+        send_sem=send_sem.at[0],
+        recv_sem=recv_sem.at[0],
+        device_id=targets[0],
+        device_id_type=mesh_id,
+    )
+    swap.start()
+    keep.wait()
+    swap.wait_send()
+    swap.wait_recv()
+    sums[...] = (mine[...] + incoming[...]).astype(sums.dtype)
+
+    local = pltpu.make_async_copy(sums.at[here], out_ref.at[here], local_sems.at[1])
     local.start()
     copies = []
     for k, owner in enumerate(owners):
         copy = pltpu.make_async_remote_copy(
-            src_ref=x_ref.at[owner],
-            dst_ref=out_ref.at[mine],
-            send_sem=send_sem.at[k],
-            recv_sem=recv_sem.at[k],
-            device_id=(seq, owner * 2 + core),
+            src_ref=sums.at[owner],
+            dst_ref=out_ref.at[here],
+            send_sem=send_sem.at[k + 1],
+            recv_sem=recv_sem.at[k + 1],
+            device_id=targets[k + 1],
             device_id_type=mesh_id,
         )
         copy.start()
@@ -192,20 +208,24 @@
     local.wait()
 
 
-def scatter_chips(block):
-    chips = block.shape[0]
+def scatter_chips(terms):
+    block = terms.shape[1:]
+    chips = block[0]
     return pl.pallas_call(
-        functools.partial(scatter_kernel, chips),
-        out_shape=jax.ShapeDtypeStruct(block.shape, block.dtype),
+        scatter_kernel,
+        out_shape=jax.ShapeDtypeStruct(block, jnp.bfloat16),
         in_specs=[pl.BlockSpec(memory_space=pl.ANY)],
         out_specs=pl.BlockSpec(memory_space=pl.ANY),
         scratch_shapes=[
+            pltpu.VMEM(block, jnp.float32),
+            pltpu.VMEM(block, jnp.float32),
+            pltpu.VMEM(block, jnp.bfloat16),
             pltpu.SemaphoreType.DMA((chips,)),
             pltpu.SemaphoreType.DMA((chips,)),
-            pltpu.SemaphoreType.DMA(()),
+            pltpu.SemaphoreType.DMA((2,)),
         ],
         compiler_params=pltpu.CompilerParams(collective_id=1, has_side_effects=True),
-    )(block)
+    )(terms)
 
 
 def masked_scores(query, keys, query_seg, key_seg):
@@ -276,16 +296,11 @@
     widened_context = jnp.stack([blank, blank, blank, context], axis=1)
     parts = lax.axis_size("tp")
     chips = parts // 2
-    core = lax.axis_index("tp") % 2
     by_owner = gathered.reshape(chips, 2, -1, *gathered.shape[1:])
     terms = jnp.einsum(
         "tkh,ycdkh->cytd", widened_context, by_owner, preferred_element_type=jnp.float32
     )
-    outgoing = lax.dynamic_index_in_dim(terms, 1 - core, 0, keepdims=False)
-    kept = lax.dynamic_index_in_dim(terms, core, 0, keepdims=False)
-    incoming = lax.ppermute(outgoing, "tp", [(i, i ^ 1) for i in range(parts)])
-    chip_sums = (kept + incoming).astype(jnp.bfloat16)
-    projected = jnp.sum(scatter_chips(chip_sums).astype(jnp.float32), axis=0)
+    projected = jnp.sum(scatter_chips(terms).astype(jnp.float32), axis=0)
     share = layer_scale.shape[0]
     residual = lax.dynamic_slice_in_dim(source, lax.axis_index("tp") * share, share, 1)
     return (residual + layer_scale * projected).astype(jnp.bfloat16)

time: 190 us -> 181 us (0.953)
  the two profiles are of different devices: /device:TPU:79 before, /device:TPU:9 now
where the time goes in v9:
time: 181 us
  Pallas kernels  110 us (61%)
  blocking collectives  25.2 us (14%)
  matrix products  15.1 us (8%)
  starting transfers between devices  10 us (6%)
  waiting for transfers between devices  7.34 us (4%)
  other arithmetic  6.68 us (4%)
  local copies, waits for them, and re-layouts  5.9 us (3%)
    pallas_call x1, Pallas kernels, gather_seq(): pl.pallas_call(gather_kernel, out_shape=jax.ShapeDtypeStruct((rings, slab...  79.4 us
    pallas_call x1, Pallas kernels, scatter_chips(): pl.pallas_call(scatter_kernel, out_shape=jax.ShapeDtypeStruct(block, jnp....  30.9 us
    psum x1, blocking collectives, shards(): lax.psum((jnp.sum(query * query, axis=-1), jnp.sum(keys * keys, axis=-1))...  25.2 us
    ppermute x4, starting transfers between devices, passed_along(): return lax.ppermute(x, axis, pairs)  10 us
    ppermute x4, waiting for transfers between devices, passed_along(): return lax.ppermute(x, axis, pairs)  7.34 us
    dot_general x1, matrix products, shards(): jnp.einsum('tkh,ycdkh->cytd', widened_context, by_owner, preferred_elemen...  7.28 us
    dot_general x1, matrix products, shards(): jnp.einsum('td,dch->tch', normed, gathered[:, :3], preferred_element_type...  5.08 us
    unnamed x16, local copies, waits for them, and re-layouts  3.86 us
  transfers between devices with their start and end apart: 4, of which 2 were waited for; matrix products, arithmetic and copies ran while one was open for 3% of the time, Pallas kernels for 0%

profile of v9, /device:TPU:9, one launch (start us, length us, event | category | flops | bytes accessed | tf_op | source)
XLA Modules:
  0.0 180.8 jit_solution(9040131109036523094)
XLA Ops:
  0.0 0.9 copy.28
  0.9 0.8 copy.29
  1.7 0.8 pad_maximum_fusion.1.x_ref
  2.5 0.0 copy-start
  2.5 0.0 copy-start.5
  2.5 79.4 %shard_map.82 = bf16[8,8,50,4,256]{4,3,2,1,0:T(4,128)(2,1)} custom-call(bf16[50,4,256]{2,1,0:T(4,128)(2,1)} %pad_maximum_fusion.1.x_ref), custom_call_target="tpu_custom_call" | custom-call | tf_op jit(solution)/shard_map/pallas_call | solution.py:143
  81.9 0.0 copy-done
  81.9 0.4 multiply_reduce_fusion
  82.3 0.0 copy-done.5
  82.4 0.0 copy-start.3
  82.4 5.1 %fusion.3 = f32[256,3,256]{0,2,1:T(8,128)S(1)} fusion(bf16[3200,3,256]{2,1,0:T(4,128)(2,1)} %bitcast.34, f32[3200]{0:T(1024)S(1)} %copy-done.5, f32[256]{0:T(256)S(1)} %add_rsqrt_fusion.2, bf16[256,3200]{1,0:T(8,128)(2,1)S(1)} %copy-done), kind=kOutput, calls=%fused_computation.3 | convolution fusion | flops 1261568000 | bytes 7353856 | tf_op jit(solution)/shard_map/td,dch->tch/dot_general | solution.py:251
  87.5 0.0 copy-start.1
  87.5 0.0 copy-start.4
  87.5 0.1 multiply_reduce_fusion.1
  87.6 25.2 %all-reduce = (f32[256]{0:T(256)S(1)}, f32[256]{0:T(256)S(1)}) all-reduce(f32[256]{0:T(256)S(1)} %get-tuple-element.6, f32[256]{0:T(256)S(1)} %get-tuple-element.5), channel_id=1, replica_groups=mesh['seq'=64,'tp'=8] {'tp'}, use_global_device_ids=true, to_apply=%region_2.0 | all-reduce | flops 512 | bytes 4096 | tf_op jit(solution)/shard_map/psum | solution.py:260
  112.7 0.0 copy-done.3
  112.7 0.1 fusion.43
  112.9 2.8 %collective-permute-start = (bf16[256,2,256]{0,2,1:T(8,128)(2,1)S(1)}, bf16[256,2,256]{0,2,1:T(8,128)(2,1)}, u32[]{:S(2)}, u32[]{:S(2)}) collective-permute-start(bf16[256,2,256]{0,2,1:T(8,128)(2,1)S(1)} %pad_maximum_fusion), channel_id=1, source_target_pairs={{0,16},{8,24},{16,32},{24,40},{32,48},{40,56},{48,64},{56,72},{64,... | collective-permute-start | bytes 786440 | tf_op jit(solution)/shard_map/ppermute | solution.py:20
  115.7 1.9 %collective-permute-start.1 = (bf16[256,2,256]{0,2,1:T(8,128)(2,1)S(1)}, bf16[256,2,256]{0,2,1:T(8,128)(2,1)}, u32[]{:S(2)}, u32[]{:S(2)}) collective-permute-start(bf16[256,2,256]{0,2,1:T(8,128)(2,1)S(1)} %pad_maximum_fusion), channel_id=1, source_target_pairs={{0,8},{8,16},{16,24},{24,32},{32,40},{40,48},{48,56},{56,64},{64,7... | collective-permute-start | bytes 786440 | tf_op jit(solution)/shard_map/ppermute | solution.py:20
  117.6 4.1 %collective-permute-start.2 = (bf16[256,2,256]{0,2,1:T(8,128)(2,1)S(1)}, bf16[256,2,256]{0,2,1:T(8,128)(2,1)}, u32[]{:S(2)}, u32[]{:S(2)}) collective-permute-start(bf16[256,2,256]{0,2,1:T(8,128)(2,1)S(1)} %pad_maximum_fusion), channel_id=1, source_target_pairs={{8,0},{16,8},{24,16},{32,24},{40,32},{48,40},{56,48},{64,56},{72,6... | collective-permute-start | bytes 786440 | tf_op jit(solution)/shard_map/ppermute | solution.py:20
  121.6 1.3 collective-permute-start.3
  123.0 0.1 copy.31
  123.1 0.0 copy-done.1
  123.1 0.1 dynamic_slice.10
  123.2 0.1 fusion.31
  123.3 0.3 broadcast_compare_fusion
  123.5 0.0 copy-done.4
  123.5 0.1 multiply_convert_fusion.1
  123.6 2.0 %convert_element_type.38 = f32[256,3200]{1,0:T(8,128)} convert(bf16[256,3200]{1,0:T(8,128)(2,1)S(1)} %copy-done) | non-fusion elementwise | flops 819200 | bytes 4915200 | tf_op jit(solution)/shard_map/convert_element_type | solution.py:241
  125.7 0.1 pad_maximum_fusion.2
  125.8 0.0 collective-permute-done
  125.8 1.0 constant_dynamic-update-slice_fusion.4
  126.7 0.0 collective-permute-done.1
  126.7 1.0 constant_dynamic-update-slice_fusion.3
  127.7 1.8 %collective-permute-done.2 = bf16[256,2,256]{0,2,1:T(8,128)(2,1)} collective-permute-done((bf16[256,2,256]{0,2,1:T(8,128)(2,1)S(1)}, bf16[256,2,256]{0,2,1:T(8,128)(2,1)}, u32[]{:S(2)}, u32[]{:S(2)}) %collective-permute-start.2) | collective-permute-done | bytes 262176 | tf_op jit(solution)/shard_map/ppermute | solution.py:20
  129.6 1.0 constant_dynamic-update-slice_fusion.1
  130.5 5.5 %collective-permute-done.3 = bf16[256,2,256]{0,2,1:T(8,128)(2,1)S(1)} collective-permute-done((bf16[256,2,256]{0,2,1:T(8,128)(2,1)S(1)}, bf16[256,2,256]{0,2,1:T(8,128)(2,1)S(1)}, u32[]{:S(2)}, u32[]{:S(2)}) %collective-permute-start.3) | collective-permute-done | bytes 262176 | tf_op jit(solution)/shard_map/ppermute | solution.py:20
  136.1 0.1 fusion.42
  136.2 1.4 fusion.44
  137.6 1.4 fusion.25
  138.9 0.1 copy.33
  139.0 7.3 %fusion.9.terms_ref = f32[2,4,256,400]{3,2,1,0:T(8,128)} fusion(bf16[4,2,400,4,256]{4,3,2,1,0:T(4,128)(2,1)} %bitcast.35, bf16[256,1,256]{2,0,1:T(8,128)(2,1)S(1)} %copy.33, bf16[4]{0:T(256)(128)(2,1)S(1)} %pad_maximum_fusion.2), kind=kOutput, calls=%fused_computation.12 | convolution fusion | flops 1677983744 | bytes 9961480 | tf_op jit(solution)/shard_map/tkh,ycdkh->cytd/dot_general | solution.py:300
  146.3 0.0 copy-start.2
  146.3 30.9 %shard_map.83 = bf16[4,256,400]{2,1,0:T(8,128)(2,1)} custom-call(f32[2,4,256,400]{3,2,1,0:T(8,128)} %fusion.9.terms_ref), custom_call_target="tpu_custom_call" | custom-call | tf_op jit(solution)/shard_map/pallas_call | solution.py:214
  177.2 1.4 convert_reduce_fusion
  178.7 0.0 copy-done.2
  178.7 1.3 add_convert_fusion
  180.0 0.8 copy.36
  (8 shorter events, 0.1 us)
Async XLA Ops:
  2.5 79.4 %copy-start = (bf16[256,3200]{1,0:T(8,128)(2,1)S(1)}, bf16[256,3200]{1,0:T(8,128)(2,1)}, u32[]{:S(2)}) copy-start(bf16[256,3200]{1,0:T(8,128)(2,1)} %param.8) | copy-start | bytes 4915204
  2.5 79.9 %copy-start.5 = (f32[3200]{0:T(1024)S(1)}, f32[3200]{0:T(1024)}, u32[]{:S(2)}) copy-start(f32[3200]{0:T(1024)} %param.9) | copy-start | bytes 38404
  82.4 30.4 %copy-start.3 = (f32[256]{0:T(256)S(1)}, f32[256]{0:T(256)}, u32[]{:S(2)}) copy-start(f32[256]{0:T(256)} %param.12) | copy-start | bytes 3076
  87.5 35.6 %copy-start.1 = (s32[16384]{0:T(1024)S(1)}, s32[16384]{0:T(1024)}, u32[]{:S(2)}) copy-start(s32[16384]{0:T(1024)} %param.15) | copy-start | bytes 196612
  87.5 36.1 %copy-start.4 = (f32[256]{0:T(256)S(1)}, f32[256]{0:T(256)}, u32[]{:S(2)}) copy-start(f32[256]{0:T(256)} %param.11) | copy-start | bytes 3076
  112.9 12.9 %collective-permute-start = (bf16[256,2,256]{0,2,1:T(8,128)(2,1)S(1)}, bf16[256,2,256]{0,2,1:T(8,128)(2,1)}, u32[]{:S(2)}, u32[]{:S(2)}) collective-permute-start(bf16[256,2,256]{0,2,1:T(8,128)(2,1)S(1)} %pad_maximum_fusion), channel_id=1, source_target_pairs={{0,16},{8,24},{16,32},{24,40},{32,48},{40,56},{48,64},{56,72},{64,... | collective-permute-start | bytes 786440 | tf_op jit(solution)/shard_map/ppermute | solution.py:20
  115.7 11.1 %collective-permute-start.1 = (bf16[256,2,256]{0,2,1:T(8,128)(2,1)S(1)}, bf16[256,2,256]{0,2,1:T(8,128)(2,1)}, u32[]{:S(2)}, u32[]{:S(2)}) collective-permute-start(bf16[256,2,256]{0,2,1:T(8,128)(2,1)S(1)} %pad_maximum_fusion), channel_id=1, source_target_pairs={{0,8},{8,16},{16,24},{24,32},{32,40},{40,48},{48,56},{56,64},{64,7... | collective-permute-start | bytes 786440 | tf_op jit(solution)/shard_map/ppermute | solution.py:20
  117.6 12.0 %collective-permute-start.2 = (bf16[256,2,256]{0,2,1:T(8,128)(2,1)S(1)}, bf16[256,2,256]{0,2,1:T(8,128)(2,1)}, u32[]{:S(2)}, u32[]{:S(2)}) collective-permute-start(bf16[256,2,256]{0,2,1:T(8,128)(2,1)S(1)} %pad_maximum_fusion), channel_id=1, source_target_pairs={{8,0},{16,8},{24,16},{32,24},{40,32},{48,40},{56,48},{64,56},{72,6... | collective-permute-start | bytes 786440 | tf_op jit(solution)/shard_map/ppermute | solution.py:20
  121.6 14.4 %collective-permute-start.3 = (bf16[256,2,256]{0,2,1:T(8,128)(2,1)S(1)}, bf16[256,2,256]{0,2,1:T(8,128)(2,1)S(1)}, u32[]{:S(2)}, u32[]{:S(2)}) collective-permute-start(bf16[256,2,256]{0,2,1:T(8,128)(2,1)S(1)} %pad_maximum_fusion), channel_id=1, source_target_pairs={{16,0},{24,8},{32,16},{40,24},{48,32},{56,40},{64,48},{72,56},{80,... | collective-permute-start | bytes 786440 | tf_op jit(solution)/shard_map/ppermute | solution.py:20
  146.3 32.3 %copy-start.2 = (f32[400]{0:T(512)S(1)}, f32[400]{0:T(512)}, u32[]{:S(2)}) copy-start(f32[400]{0:T(512)} %param.14) | copy-start | bytes 4804

commit v10 on v9

--- a/solution.py
+++ b/solution.py
@@ -228,6 +228,71 @@
     )(terms)
 
 
+def exchange_kernel(axis, offsets, x_ref, out_ref, send_sem, recv_sem, local_sem):
+    size = lax.axis_size(axis)
+    me = lax.axis_index(axis)
+    seq = lax.axis_index("seq")
+    tp = lax.axis_index("tp")
+    mesh_id = pl.DeviceIdType.MESH
+
+    def device(position):
+        return (position, tp) if axis == "seq" else (seq, position)
+
+    def slot(entry):
+        return me if entry is None else entry
+
+    peers = [lax.rem(me + offset + size, size) for offset, _ in offsets]
+    barrier = pltpu.get_barrier_semaphore()
+    for peer in peers:
+        pl.semaphore_signal(barrier, inc=1, device_id=device(peer), device_id_type=mesh_id)
+    pl.semaphore_wait(barrier, len(peers))
+
+    own = offsets_own_slot(offsets, me)
+    local = pltpu.make_async_copy(x_ref, out_ref.at[own], local_sem)
+    local.start()
+    copies = []
+    for k, ((_, entry), peer) in enumerate(zip(offsets, peers)):
+        copy = pltpu.make_async_remote_copy(
+            src_ref=x_ref,
+            dst_ref=out_ref.at[slot(entry)],
+            send_sem=send_sem.at[k],
+            recv_sem=recv_sem.at[k],
+            device_id=device(peer),
+            device_id_type=mesh_id,
+        )
+        copy.start()
+        copies.append(copy)
+    for copy in copies:
+        copy.wait_send()
+        copy.wait_recv()
+    local.wait()
+
+
+def offsets_own_slot(offsets, me):
+    slots = [entry for _, entry in offsets]
+    if None in slots:
+        return me
+    return len(offsets) // 2
+
+
+def exchange(block, axis, offsets, slots, collective_id):
+    count = len(offsets)
+    return pl.pallas_call(
+        functools.partial(exchange_kernel, axis, offsets),
+        out_shape=jax.ShapeDtypeStruct((slots,) + block.shape, block.dtype),
+        in_specs=[pl.BlockSpec(memory_space=pl.ANY)],
+        out_specs=pl.BlockSpec(memory_space=pl.ANY),
+        scratch_shapes=[
+            pltpu.SemaphoreType.DMA((count,)),
+            pltpu.SemaphoreType.DMA((count,)),
+            pltpu.SemaphoreType.DMA(()),
+        ],
+        compiler_params=pltpu.CompilerParams(
+            collective_id=collective_id, has_side_effects=True
+        ),
+    )(block)
+
+
 def masked_scores(query, keys, query_seg, key_seg):
     scores = jnp.einsum(
         "qhd,khd->hqk", query, keys, preferred_element_type=jnp.float32
@@ -257,9 +322,10 @@
     query = joined[:, 0]
     keys = joined[:, 1]
     values = joined[:, 2]
-    query_sq, key_sq = lax.psum(
-        (jnp.sum(query * query, axis=-1), jnp.sum(keys * keys, axis=-1)), "tp"
-    )
+    parts = lax.axis_size("tp")
+    squares = jnp.stack([jnp.sum(query * query, axis=-1), jnp.sum(keys * keys, axis=-1)])
+    everyone = [(k, None) for k in range(1, parts)]
+    query_sq, key_sq = jnp.sum(exchange(squares, "tp", everyone, parts, 2), axis=0)
     full_width = local_width * lax.axis_size("tp")
     query_normed = (query * lax.rsqrt(query_sq / full_width + eps)[:, None] * q_gain).astype(
         jnp.bfloat16
@@ -294,7 +360,6 @@
     )
     blank = jnp.zeros_like(context)
     widened_context = jnp.stack([blank, blank, blank, context], axis=1)
-    parts = lax.axis_size("tp")
     chips = parts // 2
     by_owner = gathered.reshape(chips, 2, -1, *gathered.shape[1:])
     terms = jnp.einsum(

time: 181 us -> 178 us (0.983)
  the two profiles are of different devices: /device:TPU:9 before, /device:TPU:22 now
where the time goes in v10:
time: 178 us; the launch traced here: 177 us
  Pallas kernels  132 us (74%)
  matrix products  15.1 us (8%)
  starting transfers between devices  12.6 us (7%)
  other arithmetic  8 us (4%)
  local copies, waits for them, and re-layouts  5.9 us (3%)
  waiting for transfers between devices  3.8 us (2%)
    pallas_call x1, Pallas kernels, gather_seq(): pl.pallas_call(gather_kernel, out_shape=jax.ShapeDtypeStruct((rings, slab...  88 us
    pallas_call x1, Pallas kernels, scatter_chips(): pl.pallas_call(scatter_kernel, out_shape=jax.ShapeDtypeStruct(block, jnp....  34.9 us
    ppermute x4, starting transfers between devices, passed_along(): return lax.ppermute(x, axis, pairs)  12.6 us
    pallas_call x1, Pallas kernels, exchange(): pl.pallas_call(functools.partial(exchange_kernel, axis, offsets), out_sha...  8.82 us
    dot_general x1, matrix products, shards(): jnp.einsum('tkh,ycdkh->cytd', widened_context, by_owner, preferred_elemen...  7.28 us
    dot_general x1, matrix products, shards(): jnp.einsum('td,dch->tch', normed, gathered[:, :3], preferred_element_type...  5.07 us
    unnamed x16, local copies, waits for them, and re-layouts  3.86 us
    ppermute x4, waiting for transfers between devices, passed_along(): return lax.ppermute(x, axis, pairs)  3.8 us
  transfers between devices with their start and end apart: 4, of which 3 were waited for; matrix products, arithmetic and copies ran while one was open for 3% of the time, Pallas kernels for 0%

profile of v10, /device:TPU:22, one launch (start us, length us, event | category | flops | bytes accessed | tf_op | source)
XLA Modules:
  0.0 177.4 jit_solution(17176078610604011534)
XLA Ops:
  0.0 0.9 copy.28
  0.9 0.8 copy.29
  1.7 0.8 pad_maximum_fusion.1.x_ref
  2.5 0.0 copy-start
  2.5 88.0 %shard_map.82 = bf16[8,8,50,4,256]{4,3,2,1,0:T(4,128)(2,1)} custom-call(bf16[50,4,256]{2,1,0:T(4,128)(2,1)} %pad_maximum_fusion.1.x_ref), custom_call_target="tpu_custom_call" | custom-call | tf_op jit(solution)/shard_map/pallas_call | solution.py:143
  90.5 0.0 copy-done
  90.5 0.4 multiply_reduce_fusion
  90.9 0.0 copy-done.5
  90.9 0.0 copy-start.3
  90.9 5.1 %fusion.3 = f32[256,3,256]{0,2,1:T(8,128)S(1)} fusion(bf16[3200,3,256]{2,1,0:T(4,128)(2,1)} %bitcast.38, f32[3200]{0:T(1024)S(1)} %copy-done.5, f32[256]{0:T(256)S(1)} %add_rsqrt_fusion, bf16[256,3200]{1,0:T(8,128)(2,1)S(1)} %copy-done), kind=kOutput, calls=%fused_computation.3 | convolution fusion | flops 1261568000 | bytes 7353856 | tf_op jit(solution)/shard_map/td,dch->tch/dot_general | solution.py:316
  96.0 0.0 copy-start.1
  96.0 0.0 copy-start.4
  96.0 0.1 multiply_reduce_fusion.2
  96.1 0.6 pad_maximum_fusion.2.x_ref
  96.7 8.8 %shard_map.83 = f32[8,2,256]{2,1,0:T(2,128)} custom-call(f32[2,256]{1,0:T(2,128)} %pad_maximum_fusion.2.x_ref), custom_call_target="tpu_custom_call" | custom-call | tf_op jit(solution)/shard_map/pallas_call | solution.py:280
  105.5 0.7 reduce_sum.57
  106.3 0.0 copy-done.3
  106.3 0.1 fusion.47
  106.4 3.9 %collective-permute-start = (bf16[256,2,256]{0,2,1:T(8,128)(2,1)S(1)}, bf16[256,2,256]{0,2,1:T(8,128)(2,1)}, u32[]{:S(2)}, u32[]{:S(2)}) collective-permute-start(bf16[256,2,256]{0,2,1:T(8,128)(2,1)S(1)} %pad_maximum_fusion), channel_id=1, source_target_pairs={{0,16},{8,24},{16,32},{24,40},{32,48},{40,56},{48,64},{56,72},{64,... | collective-permute-start | bytes 786440 | tf_op jit(solution)/shard_map/ppermute | solution.py:20
  110.4 2.1 %collective-permute-start.1 = (bf16[256,2,256]{0,2,1:T(8,128)(2,1)S(1)}, bf16[256,2,256]{0,2,1:T(8,128)(2,1)}, u32[]{:S(2)}, u32[]{:S(2)}) collective-permute-start(bf16[256,2,256]{0,2,1:T(8,128)(2,1)S(1)} %pad_maximum_fusion), channel_id=1, source_target_pairs={{0,8},{8,16},{16,24},{24,32},{32,40},{40,48},{48,56},{56,64},{64,7... | collective-permute-start | bytes 786440 | tf_op jit(solution)/shard_map/ppermute | solution.py:20
  112.4 4.7 %collective-permute-start.2 = (bf16[256,2,256]{0,2,1:T(8,128)(2,1)S(1)}, bf16[256,2,256]{0,2,1:T(8,128)(2,1)}, u32[]{:S(2)}, u32[]{:S(2)}) collective-permute-start(bf16[256,2,256]{0,2,1:T(8,128)(2,1)S(1)} %pad_maximum_fusion), channel_id=1, source_target_pairs={{8,0},{16,8},{24,16},{32,24},{40,32},{48,40},{56,48},{64,56},{72,6... | collective-permute-start | bytes 786440 | tf_op jit(solution)/shard_map/ppermute | solution.py:20
  117.1 1.9 %collective-permute-start.3 = (bf16[256,2,256]{0,2,1:T(8,128)(2,1)S(1)}, bf16[256,2,256]{0,2,1:T(8,128)(2,1)S(1)}, u32[]{:S(2)}, u32[]{:S(2)}) collective-permute-start(bf16[256,2,256]{0,2,1:T(8,128)(2,1)S(1)} %pad_maximum_fusion), channel_id=1, source_target_pairs={{16,0},{24,8},{32,16},{40,24},{48,32},{56,40},{64,48},{72,56},{80,... | collective-permute-start | bytes 786440 | tf_op jit(solution)/shard_map/ppermute | solution.py:20
  119.1 0.1 copy.31
  119.2 0.0 copy-done.1
  119.2 0.1 dynamic_slice.10
  119.3 0.1 fusion.31
  119.4 0.3 broadcast_compare_fusion
  119.6 0.0 copy-done.4
  119.7 0.1 multiply_convert_fusion.1
  119.8 2.0 %convert_element_type.38 = f32[256,3200]{1,0:T(8,128)} convert(bf16[256,3200]{1,0:T(8,128)(2,1)S(1)} %copy-done) | non-fusion elementwise | flops 819200 | bytes 4915200 | tf_op jit(solution)/shard_map/convert_element_type | solution.py:306
  121.8 0.1 pad_maximum_fusion.3
  121.9 0.4 collective-permute-done
  122.3 1.0 constant_dynamic-update-slice_fusion.4
  123.3 0.0 collective-permute-done.1
  123.3 1.0 constant_dynamic-update-slice_fusion.3
  124.3 1.6 collective-permute-done.2
  125.8 1.0 constant_dynamic-update-slice_fusion.1
  126.8 1.8 %collective-permute-done.3 = bf16[256,2,256]{0,2,1:T(8,128)(2,1)S(1)} collective-permute-done((bf16[256,2,256]{0,2,1:T(8,128)(2,1)S(1)}, bf16[256,2,256]{0,2,1:T(8,128)(2,1)S(1)}, u32[]{:S(2)}, u32[]{:S(2)}) %collective-permute-start.3) | collective-permute-done | bytes 262176 | tf_op jit(solution)/shard_map/ppermute | solution.py:20
  128.6 0.1 fusion.46
  128.7 1.4 fusion.48
  130.1 1.4 fusion.25
  131.5 0.1 copy.33
  131.6 7.3 %fusion.9.terms_ref = f32[2,4,256,400]{3,2,1,0:T(8,128)} fusion(bf16[4,2,400,4,256]{4,3,2,1,0:T(4,128)(2,1)} %bitcast.39, bf16[256,1,256]{2,0,1:T(8,128)(2,1)S(1)} %copy.33, bf16[4]{0:T(256)(128)(2,1)S(1)} %pad_maximum_fusion.3), kind=kOutput, calls=%fused_computation.12 | convolution fusion | flops 1677983744 | bytes 9961480 | tf_op jit(solution)/shard_map/tkh,ycdkh->cytd/dot_general | solution.py:365
  138.9 34.9 %shard_map.84 = bf16[4,256,400]{2,1,0:T(8,128)(2,1)} custom-call(f32[2,4,256,400]{3,2,1,0:T(8,128)} %fusion.9.terms_ref), custom_call_target="tpu_custom_call" | custom-call | tf_op jit(solution)/shard_map/pallas_call | solution.py:214
  173.8 1.4 convert_reduce_fusion
  175.2 0.0 copy-done.2
  175.2 1.3 add_convert_fusion
  176.5 0.8 copy.36
  (10 shorter events, 0.1 us)
Async XLA Ops:
  2.5 88.0 %copy-start = (bf16[256,3200]{1,0:T(8,128)(2,1)S(1)}, bf16[256,3200]{1,0:T(8,128)(2,1)}, u32[]{:S(2)}) copy-start(bf16[256,3200]{1,0:T(8,128)(2,1)} %param.8) | copy-start | bytes 4915204
  2.5 88.4 %copy-start.5 = (f32[3200]{0:T(1024)S(1)}, f32[3200]{0:T(1024)}, u32[]{:S(2)}) copy-start(f32[3200]{0:T(1024)} %param.9) | copy-start | bytes 38404
  90.9 15.4 %copy-start.3 = (f32[256]{0:T(256)S(1)}, f32[256]{0:T(256)}, u32[]{:S(2)}) copy-start(f32[256]{0:T(256)} %param.12) | copy-start | bytes 3076
  96.0 23.2 %copy-start.1 = (s32[16384]{0:T(1024)S(1)}, s32[16384]{0:T(1024)}, u32[]{:S(2)}) copy-start(s32[16384]{0:T(1024)} %param.15) | copy-start | bytes 196612
  96.0 23.6 %copy-start.4 = (f32[256]{0:T(256)S(1)}, f32[256]{0:T(256)}, u32[]{:S(2)}) copy-start(f32[256]{0:T(256)} %param.11) | copy-start | bytes 3076
  106.4 15.8 %collective-permute-start = (bf16[256,2,256]{0,2,1:T(8,128)(2,1)S(1)}, bf16[256,2,256]{0,2,1:T(8,128)(2,1)}, u32[]{:S(2)}, u32[]{:S(2)}) collective-permute-start(bf16[256,2,256]{0,2,1:T(8,128)(2,1)S(1)} %pad_maximum_fusion), channel_id=1, source_target_pairs={{0,16},{8,24},{16,32},{24,40},{32,48},{40,56},{48,64},{56,72},{64,... | collective-permute-start | bytes 786440 | tf_op jit(solution)/shard_map/ppermute | solution.py:20
  110.4 12.9 %collective-permute-start.1 = (bf16[256,2,256]{0,2,1:T(8,128)(2,1)S(1)}, bf16[256,2,256]{0,2,1:T(8,128)(2,1)}, u32[]{:S(2)}, u32[]{:S(2)}) collective-permute-start(bf16[256,2,256]{0,2,1:T(8,128)(2,1)S(1)} %pad_maximum_fusion), channel_id=1, source_target_pairs={{0,8},{8,16},{16,24},{24,32},{32,40},{40,48},{48,56},{56,64},{64,7... | collective-permute-start | bytes 786440 | tf_op jit(solution)/shard_map/ppermute | solution.py:20
  112.4 13.4 %collective-permute-start.2 = (bf16[256,2,256]{0,2,1:T(8,128)(2,1)S(1)}, bf16[256,2,256]{0,2,1:T(8,128)(2,1)}, u32[]{:S(2)}, u32[]{:S(2)}) collective-permute-start(bf16[256,2,256]{0,2,1:T(8,128)(2,1)S(1)} %pad_maximum_fusion), channel_id=1, source_target_pairs={{8,0},{16,8},{24,16},{32,24},{40,32},{48,40},{56,48},{64,56},{72,6... | collective-permute-start | bytes 786440 | tf_op jit(solution)/shard_map/ppermute | solution.py:20
  117.1 11.5 %collective-permute-start.3 = (bf16[256,2,256]{0,2,1:T(8,128)(2,1)S(1)}, bf16[256,2,256]{0,2,1:T(8,128)(2,1)S(1)}, u32[]{:S(2)}, u32[]{:S(2)}) collective-permute-start(bf16[256,2,256]{0,2,1:T(8,128)(2,1)S(1)} %pad_maximum_fusion), channel_id=1, source_target_pairs={{16,0},{24,8},{32,16},{40,24},{48,32},{56,40},{64,48},{72,56},{80,... | collective-permute-start | bytes 786440 | tf_op jit(solution)/shard_map/ppermute | solution.py:20
  138.9 36.3 %copy-start.2 = (f32[400]{0:T(512)S(1)}, f32[400]{0:T(512)}, u32[]{:S(2)}) copy-start(f32[400]{0:T(512)} %param.14) | copy-start | bytes 4804

commit v11 on v10

--- a/solution.py
+++ b/solution.py
@@ -85,9 +85,12 @@
     rows_a = [remote(pair_a, device(ring, s), row_sems, (k,)) for k, s in enumerate(row_spots)]
     for copy in rows_a:
         copy.start()
-    for t in range(rings - 1):
-        cw = out_ref.at[(ring - t + rings) % rings, base, :, :, second_lanes]
-        ccw = out_ref.at[(ring + t) % rings, base + 1, :, :, second_lanes]
+    for t in range(rings // 2):
+        last = t == rings // 2 - 1
+        cw_spots = pl.ds(base, 1 if last else pair)
+        ccw_spots = pl.ds(base + 1 if last else base, 1 if last else pair)
+        cw = out_ref.at[(ring - t + rings) % rings, cw_spots, :, :, second_lanes]
+        ccw = out_ref.at[(ring + t) % rings, ccw_spots, :, :, second_lanes]
         step = [
             remote(cw, device(ahead, spot), lane_sems, (0, t)),
             remote(ccw, device(behind, spot), lane_sems, (1, t)),
@@ -106,9 +109,12 @@
     for copy in cross:
         copy.start()
     onward = None
-    for t in range(rings - 1):
-        cw = out_ref.at[(ring - t + rings) % rings, pl.ds(0, half), :, :, first_lanes]
-        ccw = out_ref.at[(ring + t) % rings, pl.ds(half, half), :, :, first_lanes]
+    for t in range(rings // 2):
+        last = t == rings // 2 - 1
+        cw_spots = pl.ds(0, half if last else slab)
+        ccw_spots = pl.ds(half if last else 0, half if last else slab)
+        cw = out_ref.at[(ring - t + rings) % rings, cw_spots, :, :, first_lanes]
+        ccw = out_ref.at[(ring + t) % rings, ccw_spots, :, :, first_lanes]
         step = [
             remote(cw, device(ahead, spot), ring_sems, (0, t)),
             remote(ccw, device(behind, spot), ring_sems, (1, t)),
@@ -116,7 +122,7 @@
         for copy in step:
             copy.start()
         finish(step)
-        if t == 2:
+        if t == 1:
             finish(cross)
             from_left = ((across + row - 1) % row) * pair
             from_right = ((across + 1) % row) * pair
@@ -148,8 +154,8 @@
         scratch_shapes=[
             pltpu.SemaphoreType.DMA((2,)),
             pltpu.SemaphoreType.DMA((2, slab // 2 - 1)),
-            pltpu.SemaphoreType.DMA((2, 2, rings - 1)),
-            pltpu.SemaphoreType.DMA((2, 2, rings - 1)),
+            pltpu.SemaphoreType.DMA((2, 2, rings // 2)),
+            pltpu.SemaphoreType.DMA((2, 2, rings // 2)),
             pltpu.SemaphoreType.DMA((2, 2, 2)),
             pltpu.SemaphoreType.DMA(()),
         ],

time: 178 us -> 159 us (0.89)
  Pallas kernels: 132 us -> 112 us
    pallas_call x1, Pallas kernels: 88 us -> 68.7 us  [gather_seq(): pl.pallas_call(gather_kernel, out_shape=jax.ShapeDtypeStruct((rings, slab...]
  transfers between devices with their start and end apart: 4 -> 4, of which waited for: 3 -> 2; matrix products, arithmetic and copies ran while one was open for 3% -> 4% of each run, Pallas kernels for 0% -> 0%
where the time goes in v11:
time: 159 us; the launch traced here: 158 us
  Pallas kernels  112 us (70%)
  matrix products  15.1 us (9%)
  starting transfers between devices  13 us (8%)
  other arithmetic  8 us (5%)
  local copies, waits for them, and re-layouts  5.9 us (4%)
  waiting for transfers between devices  3.8 us (2%)
    pallas_call x1, Pallas kernels, gather_seq(): pl.pallas_call(gather_kernel, out_shape=jax.ShapeDtypeStruct((rings, slab...  68.7 us
    pallas_call x1, Pallas kernels, scatter_chips(): pl.pallas_call(scatter_kernel, out_shape=jax.ShapeDtypeStruct(block, jnp....  34.9 us
    ppermute x4, starting transfers between devices, passed_along(): return lax.ppermute(x, axis, pairs)  13 us
    pallas_call x1, Pallas kernels, exchange(): pl.pallas_call(functools.partial(exchange_kernel, axis, offsets), out_sha...  8.81 us
    dot_general x1, matrix products, shards(): jnp.einsum('tkh,ycdkh->cytd', widened_context, by_owner, preferred_elemen...  7.29 us
    dot_general x1, matrix products, shards(): jnp.einsum('td,dch->tch', normed, gathered[:, :3], preferred_element_type...  5.08 us
    unnamed x16, local copies, waits for them, and re-layouts  3.86 us
    ppermute x4, waiting for transfers between devices, passed_along(): return lax.ppermute(x, axis, pairs)  3.8 us
  transfers between devices with their start and end apart: 4, of which 2 were waited for; matrix products, arithmetic and copies ran while one was open for 4% of the time, Pallas kernels for 0%

profile of v11, /device:TPU:22, one launch (start us, length us, event | category | flops | bytes accessed | tf_op | source)
XLA Modules:
  0.0 158.4 jit_solution(1709718932247595206)
XLA Ops:
  0.0 0.9 copy.28
  0.9 0.8 copy.29
  1.7 0.8 pad_maximum_fusion.1.x_ref
  2.5 0.0 copy-start
  2.5 68.7 %shard_map.82 = bf16[8,8,50,4,256]{4,3,2,1,0:T(4,128)(2,1)} custom-call(bf16[50,4,256]{2,1,0:T(4,128)(2,1)} %pad_maximum_fusion.1.x_ref), custom_call_target="tpu_custom_call" | custom-call | tf_op jit(solution)/shard_map/pallas_call | solution.py:149
  71.2 0.0 copy-done
  71.2 0.4 multiply_reduce_fusion
  71.6 0.0 copy-done.5
  71.6 0.0 copy-start.3
  71.6 5.1 %fusion.3 = f32[256,3,256]{0,2,1:T(8,128)S(1)} fusion(bf16[3200,3,256]{2,1,0:T(4,128)(2,1)} %bitcast.38, f32[3200]{0:T(1024)S(1)} %copy-done.5, f32[256]{0:T(256)S(1)} %add_rsqrt_fusion, bf16[256,3200]{1,0:T(8,128)(2,1)S(1)} %copy-done), kind=kOutput, calls=%fused_computation.3 | convolution fusion | flops 1261568000 | bytes 7353856 | tf_op jit(solution)/shard_map/td,dch->tch/dot_general | solution.py:322
  76.7 0.0 copy-start.1
  76.7 0.0 copy-start.4
  76.7 0.1 multiply_reduce_fusion.2
  76.8 0.6 pad_maximum_fusion.2.x_ref
  77.4 8.8 %shard_map.83 = f32[8,2,256]{2,1,0:T(2,128)} custom-call(f32[2,256]{1,0:T(2,128)} %pad_maximum_fusion.2.x_ref), custom_call_target="tpu_custom_call" | custom-call | tf_op jit(solution)/shard_map/pallas_call | solution.py:286
  86.2 0.7 reduce_sum.57
  86.9 0.0 copy-done.3
  87.0 0.1 fusion.47
  87.1 4.3 %collective-permute-start = (bf16[256,2,256]{0,2,1:T(8,128)(2,1)S(1)}, bf16[256,2,256]{0,2,1:T(8,128)(2,1)}, u32[]{:S(2)}, u32[]{:S(2)}) collective-permute-start(bf16[256,2,256]{0,2,1:T(8,128)(2,1)S(1)} %pad_maximum_fusion), channel_id=1, source_target_pairs={{0,16},{8,24},{16,32},{24,40},{32,48},{40,56},{48,64},{56,72},{64,... | collective-permute-start | bytes 786440 | tf_op jit(solution)/shard_map/ppermute | solution.py:20
  91.4 1.9 %collective-permute-start.1 = (bf16[256,2,256]{0,2,1:T(8,128)(2,1)S(1)}, bf16[256,2,256]{0,2,1:T(8,128)(2,1)}, u32[]{:S(2)}, u32[]{:S(2)}) collective-permute-start(bf16[256,2,256]{0,2,1:T(8,128)(2,1)S(1)} %pad_maximum_fusion), channel_id=1, source_target_pairs={{0,8},{8,16},{16,24},{24,32},{32,40},{40,48},{48,56},{56,64},{64,7... | collective-permute-start | bytes 786440 | tf_op jit(solution)/shard_map/ppermute | solution.py:20
  93.4 4.8 %collective-permute-start.2 = (bf16[256,2,256]{0,2,1:T(8,128)(2,1)S(1)}, bf16[256,2,256]{0,2,1:T(8,128)(2,1)}, u32[]{:S(2)}, u32[]{:S(2)}) collective-permute-start(bf16[256,2,256]{0,2,1:T(8,128)(2,1)S(1)} %pad_maximum_fusion), channel_id=1, source_target_pairs={{8,0},{16,8},{24,16},{32,24},{40,32},{48,40},{56,48},{64,56},{72,6... | collective-permute-start | bytes 786440 | tf_op jit(solution)/shard_map/ppermute | solution.py:20
  98.2 1.9 %collective-permute-start.3 = (bf16[256,2,256]{0,2,1:T(8,128)(2,1)S(1)}, bf16[256,2,256]{0,2,1:T(8,128)(2,1)S(1)}, u32[]{:S(2)}, u32[]{:S(2)}) collective-permute-start(bf16[256,2,256]{0,2,1:T(8,128)(2,1)S(1)} %pad_maximum_fusion), channel_id=1, source_target_pairs={{16,0},{24,8},{32,16},{40,24},{48,32},{56,40},{64,48},{72,56},{80,... | collective-permute-start | bytes 786440 | tf_op jit(solution)/shard_map/ppermute | solution.py:20
  100.1 0.1 copy.31
  100.3 0.0 copy-done.1
  100.3 0.1 dynamic_slice.10
  100.4 0.1 fusion.31
  100.4 0.3 broadcast_compare_fusion
  100.7 0.0 copy-done.4
  100.7 0.1 multiply_convert_fusion.1
  100.8 2.0 %convert_element_type.38 = f32[256,3200]{1,0:T(8,128)} convert(bf16[256,3200]{1,0:T(8,128)(2,1)S(1)} %copy-done) | non-fusion elementwise | flops 819200 | bytes 4915200 | tf_op jit(solution)/shard_map/convert_element_type | solution.py:312
  102.9 0.1 pad_maximum_fusion.3
  102.9 0.0 collective-permute-done
  102.9 1.0 constant_dynamic-update-slice_fusion.4
  103.9 0.0 collective-permute-done.1
  103.9 1.0 constant_dynamic-update-slice_fusion.3
  104.9 2.6 %collective-permute-done.2 = bf16[256,2,256]{0,2,1:T(8,128)(2,1)} collective-permute-done((bf16[256,2,256]{0,2,1:T(8,128)(2,1)S(1)}, bf16[256,2,256]{0,2,1:T(8,128)(2,1)}, u32[]{:S(2)}, u32[]{:S(2)}) %collective-permute-start.2) | collective-permute-done | bytes 262176 | tf_op jit(solution)/shard_map/ppermute | solution.py:20
  107.6 1.0 constant_dynamic-update-slice_fusion.1
  108.5 1.2 collective-permute-done.3
  109.7 0.1 fusion.46
  109.8 1.4 fusion.48
  111.2 1.4 fusion.25
  112.6 0.1 copy.33
  112.7 7.3 %fusion.9.terms_ref = f32[2,4,256,400]{3,2,1,0:T(8,128)} fusion(bf16[4,2,400,4,256]{4,3,2,1,0:T(4,128)(2,1)} %bitcast.39, bf16[256,1,256]{2,0,1:T(8,128)(2,1)S(1)} %copy.33, bf16[4]{0:T(256)(128)(2,1)S(1)} %pad_maximum_fusion.3), kind=kOutput, calls=%fused_computation.12 | convolution fusion | flops 1677983744 | bytes 9961480 | tf_op jit(solution)/shard_map/tkh,ycdkh->cytd/dot_general | solution.py:371
  120.0 34.9 %shard_map.84 = bf16[4,256,400]{2,1,0:T(8,128)(2,1)} custom-call(f32[2,4,256,400]{3,2,1,0:T(8,128)} %fusion.9.terms_ref), custom_call_target="tpu_custom_call" | custom-call | tf_op jit(solution)/shard_map/pallas_call | solution.py:220
  154.8 1.4 convert_reduce_fusion
  156.3 0.0 copy-done.2
  156.3 1.3 add_convert_fusion
  157.6 0.8 copy.36
  (10 shorter events, 0.1 us)
Async XLA Ops:
  2.5 68.7 %copy-start = (bf16[256,3200]{1,0:T(8,128)(2,1)S(1)}, bf16[256,3200]{1,0:T(8,128)(2,1)}, u32[]{:S(2)}) copy-start(bf16[256,3200]{1,0:T(8,128)(2,1)} %param.8) | copy-start | bytes 4915204
  2.5 69.1 %copy-start.5 = (f32[3200]{0:T(1024)S(1)}, f32[3200]{0:T(1024)}, u32[]{:S(2)}) copy-start(f32[3200]{0:T(1024)} %param.9) | copy-start | bytes 38404
  71.6 15.4 %copy-start.3 = (f32[256]{0:T(256)S(1)}, f32[256]{0:T(256)}, u32[]{:S(2)}) copy-start(f32[256]{0:T(256)} %param.12) | copy-start | bytes 3076
  76.7 23.6 %copy-start.1 = (s32[16384]{0:T(1024)S(1)}, s32[16384]{0:T(1024)}, u32[]{:S(2)}) copy-start(s32[16384]{0:T(1024)} %param.15) | copy-start | bytes 196612
  76.7 24.0 %copy-start.4 = (f32[256]{0:T(256)S(1)}, f32[256]{0:T(256)}, u32[]{:S(2)}) copy-start(f32[256]{0:T(256)} %param.11) | copy-start | bytes 3076
  87.1 15.8 %collective-permute-start = (bf16[256,2,256]{0,2,1:T(8,128)(2,1)S(1)}, bf16[256,2,256]{0,2,1:T(8,128)(2,1)}, u32[]{:S(2)}, u32[]{:S(2)}) collective-permute-start(bf16[256,2,256]{0,2,1:T(8,128)(2,1)S(1)} %pad_maximum_fusion), channel_id=1, source_target_pairs={{0,16},{8,24},{16,32},{24,40},{32,48},{40,56},{48,64},{56,72},{64,... | collective-permute-start | bytes 786440 | tf_op jit(solution)/shard_map/ppermute | solution.py:20
  91.4 12.5 %collective-permute-start.1 = (bf16[256,2,256]{0,2,1:T(8,128)(2,1)S(1)}, bf16[256,2,256]{0,2,1:T(8,128)(2,1)}, u32[]{:S(2)}, u32[]{:S(2)}) collective-permute-start(bf16[256,2,256]{0,2,1:T(8,128)(2,1)S(1)} %pad_maximum_fusion), channel_id=1, source_target_pairs={{0,8},{8,16},{16,24},{24,32},{32,40},{40,48},{48,56},{56,64},{64,7... | collective-permute-start | bytes 786440 | tf_op jit(solution)/shard_map/ppermute | solution.py:20
  93.4 14.2 %collective-permute-start.2 = (bf16[256,2,256]{0,2,1:T(8,128)(2,1)S(1)}, bf16[256,2,256]{0,2,1:T(8,128)(2,1)}, u32[]{:S(2)}, u32[]{:S(2)}) collective-permute-start(bf16[256,2,256]{0,2,1:T(8,128)(2,1)S(1)} %pad_maximum_fusion), channel_id=1, source_target_pairs={{8,0},{16,8},{24,16},{32,24},{40,32},{48,40},{56,48},{64,56},{72,6... | collective-permute-start | bytes 786440 | tf_op jit(solution)/shard_map/ppermute | solution.py:20
  98.2 11.5 %collective-permute-start.3 = (bf16[256,2,256]{0,2,1:T(8,128)(2,1)S(1)}, bf16[256,2,256]{0,2,1:T(8,128)(2,1)S(1)}, u32[]{:S(2)}, u32[]{:S(2)}) collective-permute-start(bf16[256,2,256]{0,2,1:T(8,128)(2,1)S(1)} %pad_maximum_fusion), channel_id=1, source_target_pairs={{16,0},{24,8},{32,16},{40,24},{48,32},{56,40},{64,48},{72,56},{80,... | collective-permute-start | bytes 786440 | tf_op jit(solution)/shard_map/ppermute | solution.py:20
  120.0 36.3 %copy-start.2 = (f32[400]{0:T(512)S(1)}, f32[400]{0:T(512)}, u32[]{:S(2)}) copy-start(f32[400]{0:T(512)} %param.14) | copy-start | bytes 4804

commit v12 on v11

--- a/solution.py
+++ b/solution.py
@@ -163,54 +163,65 @@
     )(block)
 
 
-def scatter_kernel(terms_ref, out_ref, mine, incoming, sums, send_sem, recv_sem, local_sems):
+def scatter_kernel(terms_ref, out_ref, mine, incoming, sums, transit, send_sem, recv_sem, local_sems):
     chips = out_ref.shape[0]
+    rows = out_ref.shape[1] // 2
     seq = lax.axis_index("seq")
     tp = lax.axis_index("tp")
     mesh_id = pl.DeviceIdType.MESH
     core = tp % 2
     here = tp // 2
-    owners = [(here + k) % chips for k in range(1, chips)]
-    targets = [(seq, tp + 1 - 2 * core)] + [(seq, owner * 2 + core) for owner in owners]
-
+    up = (here + 1) % chips
+    far = (here + 2) % chips
+    down = (here + chips - 1) % chips
+
+    def device(chip):
+        return (seq, chip * 2 + core)
+
+    targets = [(seq, tp + 1 - 2 * core), device(up), device(far), device(down)]
     barrier = pltpu.get_barrier_semaphore()
     for target in targets:
         pl.semaphore_signal(barrier, inc=1, device_id=target, device_id_type=mesh_id)
     pl.semaphore_wait(barrier, len(targets))
 
+    def remote(src, dst, target, k):
+        return pltpu.make_async_remote_copy(
+            src_ref=src,
+            dst_ref=dst,
+            send_sem=send_sem.at[k],
+            recv_sem=recv_sem.at[k],
+            device_id=target,
+            device_id_type=mesh_id,
+        )
+
     keep = pltpu.make_async_copy(terms_ref.at[core], mine, local_sems.at[0])
     keep.start()
-    swap = pltpu.make_async_remote_copy(
-        src_ref=terms_ref.at[1 - core],
-        dst_ref=incoming,
-        send_sem=send_sem.at[0],
-        recv_sem=recv_sem.at[0],
-        device_id=targets[0],
-        device_id_type=mesh_id,
-    )
+    swap = remote(terms_ref.at[1 - core], incoming, targets[0], 0)
     swap.start()
     keep.wait()
     swap.wait_send()
     swap.wait_recv()
     sums[...] = (mine[...] + incoming[...]).astype(sums.dtype)
 
+    top, bottom = pl.ds(0, rows), pl.ds(rows, rows)
     local = pltpu.make_async_copy(sums.at[here], out_ref.at[here], local_sems.at[1])
     local.start()
-    copies = []
-    for k, owner in enumerate(owners):
-        copy = pltpu.make_async_remote_copy(
-            src_ref=sums.at[owner],
-            dst_ref=out_ref.at[here],
-            send_sem=send_sem.at[k + 1],
-            recv_sem=recv_sem.at[k + 1],
-            device_id=targets[k + 1],
-            device_id_type=mesh_id,
-        )
+    direct = remote(sums.at[far, top], out_ref.at[here, top], device(far), 1)
+    to_up = remote(sums.at[up], out_ref.at[here], device(up), 2)
+    to_down = remote(sums.at[down], out_ref.at[here], device(down), 3)
+    hand = remote(sums.at[far, bottom], transit, device(down), 4)
+    copies = [direct, to_up, to_down, hand]
+    for copy in copies:
         copy.start()
-        copies.append(copy)
-    for copy in copies:
+    hand.wait_recv()
+    onward = remote(transit, out_ref.at[up, bottom], device(down), 5)
+    onward.start()
+    hand.wait_send()
+    for copy in [direct, to_up, to_down]:
         copy.wait_send()
         copy.wait_recv()
+    onward.wait_send()
+    onward.wait_recv()
     local.wait()
 
 
@@ -226,8 +237,9 @@
             pltpu.VMEM(block, jnp.float32),
             pltpu.VMEM(block, jnp.float32),
             pltpu.VMEM(block, jnp.bfloat16),
-            pltpu.SemaphoreType.DMA((chips,)),
-            pltpu.SemaphoreType.DMA((chips,)),
+            pltpu.VMEM((block[1] // 2,) + block[2:], jnp.bfloat16),
+            pltpu.SemaphoreType.DMA((6,)),
+            pltpu.SemaphoreType.DMA((6,)),
             pltpu.SemaphoreType.DMA((2,)),
         ],
         compiler_params=pltpu.CompilerParams(collective_id=1, has_side_effects=True),

time: 159 us -> 166 us (1.044)
  the two profiles are of different devices: /device:TPU:22 before, /device:TPU:15 now
where the time goes in v12:
time: 166 us; the launch traced here: 165 us
  Pallas kernels  116 us (70%)
  matrix products  15.1 us (9%)
  starting transfers between devices  12 us (7%)
  waiting for transfers between devices  8.36 us (5%)
  other arithmetic  8 us (5%)
  local copies, waits for them, and re-layouts  5.9 us (4%)
    pallas_call x1, Pallas kernels, gather_seq(): pl.pallas_call(gather_kernel, out_shape=jax.ShapeDtypeStruct((rings, slab...  62.6 us
    pallas_call x1, Pallas kernels, scatter_chips(): pl.pallas_call(scatter_kernel, out_shape=jax.ShapeDtypeStruct(block, jnp....  38.6 us
    pallas_call x1, Pallas kernels, exchange(): pl.pallas_call(functools.partial(exchange_kernel, axis, offsets), out_sha...  14.5 us
    ppermute x4, starting transfers between devices, passed_along(): return lax.ppermute(x, axis, pairs)  12 us
    ppermute x4, waiting for transfers between devices, passed_along(): return lax.ppermute(x, axis, pairs)  8.36 us
    dot_general x1, matrix products, shards(): jnp.einsum('tkh,ycdkh->cytd', widened_context, by_owner, preferred_elemen...  7.28 us
    dot_general x1, matrix products, shards(): jnp.einsum('td,dch->tch', normed, gathered[:, :3], preferred_element_type...  5.08 us
    unnamed x16, local copies, waits for them, and re-layouts  3.86 us
  transfers between devices with their start and end apart: 4, of which 2 were waited for; matrix products, arithmetic and copies ran while one was open for 3% of the time, Pallas kernels for 0%

profile of v12, /device:TPU:15, one launch (start us, length us, event | category | flops | bytes accessed | tf_op | source)
XLA Modules:
  0.0 165.3 jit_solution(4697973740953418282)
XLA Ops:
  0.0 0.9 copy.28
  0.9 0.8 copy.29
  1.7 0.8 pad_maximum_fusion.1.x_ref
  2.5 0.0 copy-start
  2.5 62.6 %shard_map.82 = bf16[8,8,50,4,256]{4,3,2,1,0:T(4,128)(2,1)} custom-call(bf16[50,4,256]{2,1,0:T(4,128)(2,1)} %pad_maximum_fusion.1.x_ref), custom_call_target="tpu_custom_call" | custom-call | tf_op jit(solution)/shard_map/pallas_call | solution.py:149
  65.1 0.0 copy-done
  65.1 0.4 multiply_reduce_fusion
  65.5 0.0 copy-done.5
  65.5 0.0 copy-start.3
  65.5 5.1 %fusion.3 = f32[256,3,256]{0,2,1:T(8,128)S(1)} fusion(bf16[3200,3,256]{2,1,0:T(4,128)(2,1)} %bitcast.38, f32[3200]{0:T(1024)S(1)} %copy-done.5, f32[256]{0:T(256)S(1)} %add_rsqrt_fusion, bf16[256,3200]{1,0:T(8,128)(2,1)S(1)} %copy-done), kind=kOutput, calls=%fused_computation.3 | convolution fusion | flops 1261568000 | bytes 7353856 | tf_op jit(solution)/shard_map/td,dch->tch/dot_general | solution.py:334
  70.6 0.0 copy-start.1
  70.6 0.0 copy-start.4
  70.6 0.1 multiply_reduce_fusion.2
  70.7 0.6 pad_maximum_fusion.2.x_ref
  71.3 14.5 %shard_map.83 = f32[8,2,256]{2,1,0:T(2,128)} custom-call(f32[2,256]{1,0:T(2,128)} %pad_maximum_fusion.2.x_ref), custom_call_target="tpu_custom_call" | custom-call | tf_op jit(solution)/shard_map/pallas_call | solution.py:298
  85.8 0.7 reduce_sum.57
  86.5 0.0 copy-done.3
  86.5 0.1 fusion.47
  86.7 2.9 %collective-permute-start = (bf16[256,2,256]{0,2,1:T(8,128)(2,1)S(1)}, bf16[256,2,256]{0,2,1:T(8,128)(2,1)}, u32[]{:S(2)}, u32[]{:S(2)}) collective-permute-start(bf16[256,2,256]{0,2,1:T(8,128)(2,1)S(1)} %pad_maximum_fusion), channel_id=1, source_target_pairs={{0,16},{8,24},{16,32},{24,40},{32,48},{40,56},{48,64},{56,72},{64,... | collective-permute-start | bytes 786440 | tf_op jit(solution)/shard_map/ppermute | solution.py:20
  89.6 4.5 %collective-permute-start.1 = (bf16[256,2,256]{0,2,1:T(8,128)(2,1)S(1)}, bf16[256,2,256]{0,2,1:T(8,128)(2,1)}, u32[]{:S(2)}, u32[]{:S(2)}) collective-permute-start(bf16[256,2,256]{0,2,1:T(8,128)(2,1)S(1)} %pad_maximum_fusion), channel_id=1, source_target_pairs={{0,8},{8,16},{16,24},{24,32},{32,40},{40,48},{48,56},{56,64},{64,7... | collective-permute-start | bytes 786440 | tf_op jit(solution)/shard_map/ppermute | solution.py:20
  94.1 1.9 %collective-permute-start.2 = (bf16[256,2,256]{0,2,1:T(8,128)(2,1)S(1)}, bf16[256,2,256]{0,2,1:T(8,128)(2,1)}, u32[]{:S(2)}, u32[]{:S(2)}) collective-permute-start(bf16[256,2,256]{0,2,1:T(8,128)(2,1)S(1)} %pad_maximum_fusion), channel_id=1, source_target_pairs={{8,0},{16,8},{24,16},{32,24},{40,32},{48,40},{56,48},{64,56},{72,6... | collective-permute-start | bytes 786440 | tf_op jit(solution)/shard_map/ppermute | solution.py:20
  96.0 2.7 %collective-permute-start.3 = (bf16[256,2,256]{0,2,1:T(8,128)(2,1)S(1)}, bf16[256,2,256]{0,2,1:T(8,128)(2,1)S(1)}, u32[]{:S(2)}, u32[]{:S(2)}) collective-permute-start(bf16[256,2,256]{0,2,1:T(8,128)(2,1)S(1)} %pad_maximum_fusion), channel_id=1, source_target_pairs={{16,0},{24,8},{32,16},{40,24},{48,32},{56,40},{64,48},{72,56},{80,... | collective-permute-start | bytes 786440 | tf_op jit(solution)/shard_map/ppermute | solution.py:20
  98.8 0.1 copy.31
  98.9 0.0 copy-done.1
  98.9 0.1 dynamic_slice.10
  99.0 0.1 fusion.31
  99.1 0.3 broadcast_compare_fusion
  99.3 0.0 copy-done.4
  99.3 0.1 multiply_convert_fusion.1
  99.4 2.0 %convert_element_type.38 = f32[256,3200]{1,0:T(8,128)} convert(bf16[256,3200]{1,0:T(8,128)(2,1)S(1)} %copy-done) | non-fusion elementwise | flops 819200 | bytes 4915200 | tf_op jit(solution)/shard_map/convert_element_type | solution.py:324
  101.5 0.1 pad_maximum_fusion.3
  101.6 0.0 collective-permute-done
  101.6 1.0 constant_dynamic-update-slice_fusion.4
  102.5 0.0 collective-permute-done.1
  102.5 1.0 constant_dynamic-update-slice_fusion.3
  103.5 2.5 %collective-permute-done.2 = bf16[256,2,256]{0,2,1:T(8,128)(2,1)} collective-permute-done((bf16[256,2,256]{0,2,1:T(8,128)(2,1)S(1)}, bf16[256,2,256]{0,2,1:T(8,128)(2,1)}, u32[]{:S(2)}, u32[]{:S(2)}) %collective-permute-start.2) | collective-permute-done | bytes 262176 | tf_op jit(solution)/shard_map/ppermute | solution.py:20
  106.0 1.0 constant_dynamic-update-slice_fusion.1
  107.0 5.9 %collective-permute-done.3 = bf16[256,2,256]{0,2,1:T(8,128)(2,1)S(1)} collective-permute-done((bf16[256,2,256]{0,2,1:T(8,128)(2,1)S(1)}, bf16[256,2,256]{0,2,1:T(8,128)(2,1)S(1)}, u32[]{:S(2)}, u32[]{:S(2)}) %collective-permute-start.3) | collective-permute-done | bytes 262176 | tf_op jit(solution)/shard_map/ppermute | solution.py:20
  112.9 0.1 fusion.46
  113.0 1.4 fusion.48
  114.4 1.4 fusion.25
  115.8 0.1 copy.33
  115.9 7.3 %fusion.9.terms_ref = f32[2,4,256,400]{3,2,1,0:T(8,128)} fusion(bf16[4,2,400,4,256]{4,3,2,1,0:T(4,128)(2,1)} %bitcast.39, bf16[256,1,256]{2,0,1:T(8,128)(2,1)S(1)} %copy.33, bf16[4]{0:T(256)(128)(2,1)S(1)} %pad_maximum_fusion.3), kind=kOutput, calls=%fused_computation.12 | convolution fusion | flops 1677983744 | bytes 9961480 | tf_op jit(solution)/shard_map/tkh,ycdkh->cytd/dot_general | solution.py:383
  123.2 38.6 %shard_map.84 = bf16[4,256,400]{2,1,0:T(8,128)(2,1)} custom-call(f32[2,4,256,400]{3,2,1,0:T(8,128)} %fusion.9.terms_ref), custom_call_target="tpu_custom_call" | custom-call | tf_op jit(solution)/shard_map/pallas_call | solution.py:231
  161.7 1.4 convert_reduce_fusion
  163.2 0.0 copy-done.2
  163.2 1.3 add_convert_fusion
  164.5 0.8 copy.36
  (10 shorter events, 0.1 us)
Async XLA Ops:
  2.5 62.6 %copy-start = (bf16[256,3200]{1,0:T(8,128)(2,1)S(1)}, bf16[256,3200]{1,0:T(8,128)(2,1)}, u32[]{:S(2)}) copy-start(bf16[256,3200]{1,0:T(8,128)(2,1)} %param.8) | copy-start | bytes 4915204
  2.5 63.0 %copy-start.5 = (f32[3200]{0:T(1024)S(1)}, f32[3200]{0:T(1024)}, u32[]{:S(2)}) copy-start(f32[3200]{0:T(1024)} %param.9) | copy-start | bytes 38404
  65.5 21.0 %copy-start.3 = (f32[256]{0:T(256)S(1)}, f32[256]{0:T(256)}, u32[]{:S(2)}) copy-start(f32[256]{0:T(256)} %param.12) | copy-start | bytes 3076
  70.6 28.3 %copy-start.1 = (s32[16384]{0:T(1024)S(1)}, s32[16384]{0:T(1024)}, u32[]{:S(2)}) copy-start(s32[16384]{0:T(1024)} %param.15) | copy-start | bytes 196612
  70.6 28.7 %copy-start.4 = (f32[256]{0:T(256)S(1)}, f32[256]{0:T(256)}, u32[]{:S(2)}) copy-start(f32[256]{0:T(256)} %param.11) | copy-start | bytes 3076
  86.7 14.9 %collective-permute-start = (bf16[256,2,256]{0,2,1:T(8,128)(2,1)S(1)}, bf16[256,2,256]{0,2,1:T(8,128)(2,1)}, u32[]{:S(2)}, u32[]{:S(2)}) collective-permute-start(bf16[256,2,256]{0,2,1:T(8,128)(2,1)S(1)} %pad_maximum_fusion), channel_id=1, source_target_pairs={{0,16},{8,24},{16,32},{24,40},{32,48},{40,56},{48,64},{56,72},{64,... | collective-permute-start | bytes 786440 | tf_op jit(solution)/shard_map/ppermute | solution.py:20
  89.6 13.0 %collective-permute-start.1 = (bf16[256,2,256]{0,2,1:T(8,128)(2,1)S(1)}, bf16[256,2,256]{0,2,1:T(8,128)(2,1)}, u32[]{:S(2)}, u32[]{:S(2)}) collective-permute-start(bf16[256,2,256]{0,2,1:T(8,128)(2,1)S(1)} %pad_maximum_fusion), channel_id=1, source_target_pairs={{0,8},{8,16},{16,24},{24,32},{32,40},{40,48},{48,56},{56,64},{64,7... | collective-permute-start | bytes 786440 | tf_op jit(solution)/shard_map/ppermute | solution.py:20
  94.1 11.9 %collective-permute-start.2 = (bf16[256,2,256]{0,2,1:T(8,128)(2,1)S(1)}, bf16[256,2,256]{0,2,1:T(8,128)(2,1)}, u32[]{:S(2)}, u32[]{:S(2)}) collective-permute-start(bf16[256,2,256]{0,2,1:T(8,128)(2,1)S(1)} %pad_maximum_fusion), channel_id=1, source_target_pairs={{8,0},{16,8},{24,16},{32,24},{40,32},{48,40},{56,48},{64,56},{72,6... | collective-permute-start | bytes 786440 | tf_op jit(solution)/shard_map/ppermute | solution.py:20
  96.0 16.8 %collective-permute-start.3 = (bf16[256,2,256]{0,2,1:T(8,128)(2,1)S(1)}, bf16[256,2,256]{0,2,1:T(8,128)(2,1)S(1)}, u32[]{:S(2)}, u32[]{:S(2)}) collective-permute-start(bf16[256,2,256]{0,2,1:T(8,128)(2,1)S(1)} %pad_maximum_fusion), channel_id=1, source_target_pairs={{16,0},{24,8},{32,16},{40,24},{48,32},{56,40},{64,48},{72,56},{80,... | collective-permute-start | bytes 786440 | tf_op jit(solution)/shard_map/ppermute | solution.py:20
  123.1 40.0 %copy-start.2 = (f32[400]{0:T(512)S(1)}, f32[400]{0:T(512)}, u32[]{:S(2)}) copy-start(f32[400]{0:T(512)} %param.14) | copy-start | bytes 4804

commit v13 on v11

--- a/solution.py
+++ b/solution.py
@@ -192,7 +192,8 @@
     keep.wait()
     swap.wait_send()
     swap.wait_recv()
-    sums[...] = (mine[...] + incoming[...]).astype(sums.dtype)
+    total = mine[...].astype(jnp.float32) + incoming[...].astype(jnp.float32)
+    sums[...] = total.astype(sums.dtype)
 
     local = pltpu.make_async_copy(sums.at[here], out_ref.at[here], local_sems.at[1])
     local.start()
@@ -223,8 +224,8 @@
         in_specs=[pl.BlockSpec(memory_space=pl.ANY)],
         out_specs=pl.BlockSpec(memory_space=pl.ANY),
         scratch_shapes=[
-            pltpu.VMEM(block, jnp.float32),
-            pltpu.VMEM(block, jnp.float32),
+            pltpu.VMEM(block, terms.dtype),
+            pltpu.VMEM(block, terms.dtype),
             pltpu.VMEM(block, jnp.bfloat16),
             pltpu.SemaphoreType.DMA((chips,)),
             pltpu.SemaphoreType.DMA((chips,)),
@@ -371,7 +372,9 @@
     terms = jnp.einsum(
         "tkh,ycdkh->cytd", widened_context, by_owner, preferred_element_type=jnp.float32
     )
-    projected = jnp.sum(scatter_chips(terms).astype(jnp.float32), axis=0)
+    projected = jnp.sum(
+        scatter_chips(terms.astype(jnp.bfloat16)).astype(jnp.float32), axis=0
+    )
     share = layer_scale.shape[0]
     residual = lax.dynamic_slice_in_dim(source, lax.axis_index("tp") * share, share, 1)
     return (residual + layer_scale * projected).astype(jnp.bfloat16)

time: 159 us -> 158 us (level)
  matrix products: 15.1 us -> 12.7 us
  local copies, waits for them, and re-layouts: 5.9 us -> 8.27 us
    dot_general x1, matrix products: 7.29 us -> 4.85 us  [shards(): jnp.einsum('tkh,ycdkh->cytd', widened_context, by_owner, preferred_elemen...]
    convert_element_type x0 -> x1, local copies, waits for them, and re-layouts: none -> 2.37 us  [shards(): terms.astype(jnp.bfloat16)]
where the time goes in v13:
time: 158 us; the launch traced here: 157 us
  Pallas kernels  111 us (70%)
  starting transfers between devices  13 us (8%)
  matrix products  12.7 us (8%)
  local copies, waits for them, and re-layouts  8.27 us (5%)
  other arithmetic  7.94 us (5%)
  waiting for transfers between devices  3.86 us (2%)
    pallas_call x1, Pallas kernels, gather_seq(): pl.pallas_call(gather_kernel, out_shape=jax.ShapeDtypeStruct((rings, slab...  68.7 us
    pallas_call x1, Pallas kernels, scatter_chips(): pl.pallas_call(scatter_kernel, out_shape=jax.ShapeDtypeStruct(block, jnp....  33.4 us
    ppermute x4, starting transfers between devices, passed_along(): return lax.ppermute(x, axis, pairs)  13 us
    pallas_call x1, Pallas kernels, exchange(): pl.pallas_call(functools.partial(exchange_kernel, axis, offsets), out_sha...  8.81 us
    dot_general x1, matrix products, shards(): jnp.einsum('td,dch->tch', normed, gathered[:, :3], preferred_element_type...  5.07 us
    dot_general x1, matrix products, shards(): jnp.einsum('tkh,ycdkh->cytd', widened_context, by_owner, preferred_elemen...  4.85 us
    ppermute x4, waiting for transfers between devices, passed_along(): return lax.ppermute(x, axis, pairs)  3.86 us
    unnamed x16, local copies, waits for them, and re-layouts  3.86 us
  transfers between devices with their start and end apart: 4, of which 2 were waited for; matrix products, arithmetic and copies ran while one was open for 4% of the time, Pallas kernels for 0%

profile of v13, /device:TPU:22, one launch (start us, length us, event | category | flops | bytes accessed | tf_op | source)
XLA Modules:
  0.0 156.9 jit_solution(11254945247738263094)
XLA Ops:
  0.0 0.9 copy.37
  0.9 0.8 copy.38
  1.7 0.8 pad_maximum_fusion.1.x_ref
  2.5 68.7 %shard_map.82 = bf16[8,8,50,4,256]{4,3,2,1,0:T(4,128)(2,1)} custom-call(bf16[50,4,256]{2,1,0:T(4,128)(2,1)} %pad_maximum_fusion.1.x_ref), custom_call_target="tpu_custom_call" | custom-call | tf_op jit(solution)/shard_map/pallas_call | solution.py:149
  71.2 0.0 copy-done
  71.2 0.4 multiply_reduce_fusion
  71.6 0.0 copy-done.5
  71.6 0.0 copy-start.3
  71.6 5.1 %fusion.3 = f32[256,3,256]{0,2,1:T(8,128)S(1)} fusion(bf16[3200,3,256]{2,1,0:T(4,128)(2,1)} %bitcast.41, f32[3200]{0:T(1024)S(1)} %copy-done.5, f32[256]{0:T(256)S(1)} %add_rsqrt_fusion, bf16[256,3200]{1,0:T(8,128)(2,1)S(1)} %copy-done), kind=kOutput, calls=%fused_computation.3 | convolution fusion | flops 1261568000 | bytes 7353856 | tf_op jit(solution)/shard_map/td,dch->tch/dot_general | solution.py:323
  76.7 0.0 copy-start.1
  76.7 0.0 copy-start.4
  76.7 0.1 multiply_reduce_fusion.2
  76.8 0.6 pad_maximum_fusion.2.x_ref
  77.4 8.8 %shard_map.83 = f32[8,2,256]{2,1,0:T(2,128)} custom-call(f32[2,256]{1,0:T(2,128)} %pad_maximum_fusion.2.x_ref), custom_call_target="tpu_custom_call" | custom-call | tf_op jit(solution)/shard_map/pallas_call | solution.py:287
  86.2 0.7 reduce_sum.57
  86.9 0.0 copy-done.3
  86.9 0.1 fusion.46
  87.1 4.3 %collective-permute-start = (bf16[256,2,256]{0,2,1:T(8,128)(2,1)S(1)}, bf16[256,2,256]{0,2,1:T(8,128)(2,1)}, u32[]{:S(2)}, u32[]{:S(2)}) collective-permute-start(bf16[256,2,256]{0,2,1:T(8,128)(2,1)S(1)} %pad_maximum_fusion), channel_id=1, source_target_pairs={{0,16},{8,24},{16,32},{24,40},{32,48},{40,56},{48,64},{56,72},{64,... | collective-permute-start | bytes 786440 | tf_op jit(solution)/shard_map/ppermute | solution.py:20
  91.4 1.9 %collective-permute-start.1 = (bf16[256,2,256]{0,2,1:T(8,128)(2,1)S(1)}, bf16[256,2,256]{0,2,1:T(8,128)(2,1)}, u32[]{:S(2)}, u32[]{:S(2)}) collective-permute-start(bf16[256,2,256]{0,2,1:T(8,128)(2,1)S(1)} %pad_maximum_fusion), channel_id=1, source_target_pairs={{0,8},{8,16},{16,24},{24,32},{32,40},{40,48},{48,56},{56,64},{64,7... | collective-permute-start | bytes 786440 | tf_op jit(solution)/shard_map/ppermute | solution.py:20
  93.4 4.8 %collective-permute-start.2 = (bf16[256,2,256]{0,2,1:T(8,128)(2,1)S(1)}, bf16[256,2,256]{0,2,1:T(8,128)(2,1)}, u32[]{:S(2)}, u32[]{:S(2)}) collective-permute-start(bf16[256,2,256]{0,2,1:T(8,128)(2,1)S(1)} %pad_maximum_fusion), channel_id=1, source_target_pairs={{8,0},{16,8},{24,16},{32,24},{40,32},{48,40},{56,48},{64,56},{72,6... | collective-permute-start | bytes 786440 | tf_op jit(solution)/shard_map/ppermute | solution.py:20
  98.2 1.9 %collective-permute-start.3 = (bf16[256,2,256]{0,2,1:T(8,128)(2,1)S(1)}, bf16[256,2,256]{0,2,1:T(8,128)(2,1)S(1)}, u32[]{:S(2)}, u32[]{:S(2)}) collective-permute-start(bf16[256,2,256]{0,2,1:T(8,128)(2,1)S(1)} %pad_maximum_fusion), channel_id=1, source_target_pairs={{16,0},{24,8},{32,16},{40,24},{48,32},{56,40},{64,48},{72,56},{80,... | collective-permute-start | bytes 786440 | tf_op jit(solution)/shard_map/ppermute | solution.py:20
  100.1 0.1 copy.40
  100.3 0.0 copy-done.1
  100.3 0.1 dynamic_slice.10
  100.3 0.1 fusion.30
  100.4 0.3 broadcast_compare_fusion
  100.7 0.0 copy-done.4
  100.7 0.1 multiply_convert_fusion.1
  100.8 2.0 %convert_element_type.43 = f32[256,3200]{1,0:T(8,128)} convert(bf16[256,3200]{1,0:T(8,128)(2,1)S(1)} %copy-done) | non-fusion elementwise | flops 819200 | bytes 4915200 | tf_op jit(solution)/shard_map/convert_element_type | solution.py:313
  102.8 0.1 pad_maximum_fusion.3
  102.9 0.0 collective-permute-done
  102.9 1.0 constant_dynamic-update-slice_fusion.4
  103.8 0.0 collective-permute-done.1
  103.8 1.0 constant_dynamic-update-slice_fusion.3
  104.8 2.7 %collective-permute-done.2 = bf16[256,2,256]{0,2,1:T(8,128)(2,1)} collective-permute-done((bf16[256,2,256]{0,2,1:T(8,128)(2,1)S(1)}, bf16[256,2,256]{0,2,1:T(8,128)(2,1)}, u32[]{:S(2)}, u32[]{:S(2)}) %collective-permute-start.2) | collective-permute-done | bytes 262176 | tf_op jit(solution)/shard_map/ppermute | solution.py:20
  107.5 1.0 constant_dynamic-update-slice_fusion.1
  108.5 1.2 collective-permute-done.3
  109.7 0.1 fusion.45
  109.8 1.4 fusion.47
  111.2 1.4 fusion.24
  112.6 0.1 copy.42
  112.7 4.8 %bitcast_convert_fusion = bf16[4,2,400,256]{3,2,1,0:T(8,128)(2,1)S(1)} fusion(bf16[4,2,400,4,256]{4,3,2,1,0:T(4,128)(2,1)} %bitcast.42, bf16[256,1,256]{2,0,1:T(8,128)(2,1)S(1)} %copy.42, bf16[4]{0:T(256)(128)(2,1)S(1)} %pad_maximum_fusion.3), kind=kOutput, calls=%fused_computation.8 | convolution fusion | flops 1678802944 | bytes 8323080 | tf_op jit(solution)/shard_map/tkh,ycdkh->cytd/dot_general | solution.py:372
  117.5 2.4 %copy.44 = bf16[4,2,400,256]{2,3,0,1:T(8,128)(2,1)} copy(bf16[4,2,400,256]{3,2,1,0:T(8,128)(2,1)S(1)} %bitcast_convert_fusion) | data formatting | bytes 3276800 | tf_op jit(solution)/shard_map/convert_element_type | solution.py:376
  119.9 33.4 %shard_map.84 = bf16[4,256,400]{2,1,0:T(8,128)(2,1)} custom-call(bf16[2,4,256,400]{3,2,1,0:T(8,128)(2,1)} %bitcast.40), custom_call_target="tpu_custom_call" | custom-call | tf_op jit(solution)/shard_map/pallas_call | solution.py:221
  153.3 1.4 convert_reduce_fusion
  154.8 0.0 copy-done.2
  154.8 1.3 add_convert_fusion
  156.1 0.8 copy.45
  (11 shorter events, 0.1 us)
Async XLA Ops:
  2.5 68.7 %copy-start = (bf16[256,3200]{1,0:T(8,128)(2,1)S(1)}, bf16[256,3200]{1,0:T(8,128)(2,1)}, u32[]{:S(2)}) copy-start(bf16[256,3200]{1,0:T(8,128)(2,1)} %param.8) | copy-start | bytes 4915204
  2.5 69.1 %copy-start.5 = (f32[3200]{0:T(1024)S(1)}, f32[3200]{0:T(1024)}, u32[]{:S(2)}) copy-start(f32[3200]{0:T(1024)} %param.9) | copy-start | bytes 38404
  71.6 15.4 %copy-start.3 = (f32[256]{0:T(256)S(1)}, f32[256]{0:T(256)}, u32[]{:S(2)}) copy-start(f32[256]{0:T(256)} %param.12) | copy-start | bytes 3076
  76.7 23.6 %copy-start.1 = (s32[16384]{0:T(1024)S(1)}, s32[16384]{0:T(1024)}, u32[]{:S(2)}) copy-start(s32[16384]{0:T(1024)} %param.15) | copy-start | bytes 196612
  76.7 24.0 %copy-start.4 = (f32[256]{0:T(256)S(1)}, f32[256]{0:T(256)}, u32[]{:S(2)}) copy-start(f32[256]{0:T(256)} %param.11) | copy-start | bytes 3076
  87.1 15.8 %collective-permute-start = (bf16[256,2,256]{0,2,1:T(8,128)(2,1)S(1)}, bf16[256,2,256]{0,2,1:T(8,128)(2,1)}, u32[]{:S(2)}, u32[]{:S(2)}) collective-permute-start(bf16[256,2,256]{0,2,1:T(8,128)(2,1)S(1)} %pad_maximum_fusion), channel_id=1, source_target_pairs={{0,16},{8,24},{16,32},{24,40},{32,48},{40,56},{48,64},{56,72},{64,... | collective-permute-start | bytes 786440 | tf_op jit(solution)/shard_map/ppermute | solution.py:20
  91.4 12.4 %collective-permute-start.1 = (bf16[256,2,256]{0,2,1:T(8,128)(2,1)S(1)}, bf16[256,2,256]{0,2,1:T(8,128)(2,1)}, u32[]{:S(2)}, u32[]{:S(2)}) collective-permute-start(bf16[256,2,256]{0,2,1:T(8,128)(2,1)S(1)} %pad_maximum_fusion), channel_id=1, source_target_pairs={{0,8},{8,16},{16,24},{24,32},{32,40},{40,48},{48,56},{56,64},{64,7... | collective-permute-start | bytes 786440 | tf_op jit(solution)/shard_map/ppermute | solution.py:20
  93.4 14.2 %collective-permute-start.2 = (bf16[256,2,256]{0,2,1:T(8,128)(2,1)S(1)}, bf16[256,2,256]{0,2,1:T(8,128)(2,1)}, u32[]{:S(2)}, u32[]{:S(2)}) collective-permute-start(bf16[256,2,256]{0,2,1:T(8,128)(2,1)S(1)} %pad_maximum_fusion), channel_id=1, source_target_pairs={{8,0},{16,8},{24,16},{32,24},{40,32},{48,40},{56,48},{64,56},{72,6... | collective-permute-start | bytes 786440 | tf_op jit(solution)/shard_map/ppermute | solution.py:20
  98.2 11.5 %collective-permute-start.3 = (bf16[256,2,256]{0,2,1:T(8,128)(2,1)S(1)}, bf16[256,2,256]{0,2,1:T(8,128)(2,1)S(1)}, u32[]{:S(2)}, u32[]{:S(2)}) collective-permute-start(bf16[256,2,256]{0,2,1:T(8,128)(2,1)S(1)} %pad_maximum_fusion), channel_id=1, source_target_pairs={{16,0},{24,8},{32,16},{40,24},{48,32},{56,40},{64,48},{72,56},{80,... | collective-permute-start | bytes 786440 | tf_op jit(solution)/shard_map/ppermute | solution.py:20
  119.9 34.9 %copy-start.2 = (f32[400]{0:T(512)S(1)}, f32[400]{0:T(512)}, u32[]{:S(2)}) copy-start(f32[400]{0:T(512)} %param.14) | copy-start | bytes 4804

commit v14 on v13

--- a/solution.py
+++ b/solution.py
@@ -24,8 +24,9 @@
     rings, slab = out_ref.shape[0], out_ref.shape[1]
     pair = 2
     row = slab // pair
-    lanes = out_ref.shape[-1] // 2
-    first_lanes, second_lanes = pl.ds(0, lanes), pl.ds(lanes, lanes)
+    rows = out_ref.shape[2]
+    split = (rows * 3 + 7) // 8
+    first_rows, second_rows = pl.ds(0, split), pl.ds(split, rows - split)
     me = lax.axis_index("seq")
     tp = lax.axis_index("tp")
     mesh_id = pl.DeviceIdType.MESH
@@ -81,7 +82,7 @@
     local.wait()
     finish([swap])
 
-    pair_a = out_ref.at[ring, pl.ds(base, pair), :, :, first_lanes]
+    pair_a = out_ref.at[ring, pl.ds(base, pair), first_rows]
     rows_a = [remote(pair_a, device(ring, s), row_sems, (k,)) for k, s in enumerate(row_spots)]
     for copy in rows_a:
         copy.start()
@@ -89,8 +90,8 @@
         last = t == rings // 2 - 1
         cw_spots = pl.ds(base, 1 if last else pair)
         ccw_spots = pl.ds(base + 1 if last else base, 1 if last else pair)
-        cw = out_ref.at[(ring - t + rings) % rings, cw_spots, :, :, second_lanes]
-        ccw = out_ref.at[(ring + t) % rings, ccw_spots, :, :, second_lanes]
+        cw = out_ref.at[(ring - t + rings) % rings, cw_spots, second_rows]
+        ccw = out_ref.at[(ring + t) % rings, ccw_spots, second_rows]
         step = [
             remote(cw, device(ahead, spot), lane_sems, (0, t)),
             remote(ccw, device(behind, spot), lane_sems, (1, t)),
@@ -103,8 +104,8 @@
     half = slab // 2
     mid = rings // 2
     cross = [
-        remote(out_ref.at[:, pl.ds(base, pair), :, :, second_lanes], device(ring, right), cross_sems, (0, 0)),
-        remote(out_ref.at[:, pl.ds(base, pair), :, :, second_lanes], device(ring, left), cross_sems, (1, 0)),
+        remote(out_ref.at[:, pl.ds(base, pair), second_rows], device(ring, right), cross_sems, (0, 0)),
+        remote(out_ref.at[:, pl.ds(base, pair), second_rows], device(ring, left), cross_sems, (1, 0)),
     ]
     for copy in cross:
         copy.start()
@@ -113,8 +114,8 @@
         last = t == rings // 2 - 1
         cw_spots = pl.ds(0, half if last else slab)
         ccw_spots = pl.ds(half if last else 0, half if last else slab)
-        cw = out_ref.at[(ring - t + rings) % rings, cw_spots, :, :, first_lanes]
-        ccw = out_ref.at[(ring + t) % rings, ccw_spots, :, :, first_lanes]
+        cw = out_ref.at[(ring - t + rings) % rings, cw_spots, first_rows]
+        ccw = out_ref.at[(ring + t) % rings, ccw_spots, first_rows]
         step = [
             remote(cw, device(ahead, spot), ring_sems, (0, t)),
             remote(ccw, device(behind, spot), ring_sems, (1, t)),
@@ -128,13 +129,13 @@
             from_right = ((across + 1) % row) * pair
             onward = [
                 remote(
-                    out_ref.at[pl.ds(0, mid), pl.ds(from_left, pair), :, :, second_lanes],
+                    out_ref.at[pl.ds(0, mid), pl.ds(from_left, pair), second_rows],
                     device(ring, right),
                     cross_sems,
                     (0, 1),
                 ),
                 remote(
-                    out_ref.at[pl.ds(mid, mid), pl.ds(from_right, pair), :, :, second_lanes],
+                    out_ref.at[pl.ds(mid, mid), pl.ds(from_right, pair), second_rows],
                     device(ring, left),
                     cross_sems,
                     (1, 1),

time: 158 us -> 157 us (level)
  transfers between devices with their start and end apart: 4 -> 4, of which waited for: 2 -> 3; matrix products, arithmetic and copies ran while one was open for 4% -> 4% of each run, Pallas kernels for 0% -> 0%
where the time goes in v14:
time: 157 us
  Pallas kernels  112 us (71%)
  matrix products  12.7 us (8%)
  starting transfers between devices  12.6 us (8%)
  local copies, waits for them, and re-layouts  8.27 us (5%)
  other arithmetic  7.94 us (5%)
  waiting for transfers between devices  3.43 us (2%)
    pallas_call x1, Pallas kernels, gather_seq(): pl.pallas_call(gather_kernel, out_shape=jax.ShapeDtypeStruct((rings, slab...  69.4 us
    pallas_call x1, Pallas kernels, scatter_chips(): pl.pallas_call(scatter_kernel, out_shape=jax.ShapeDtypeStruct(block, jnp....  33.4 us
    ppermute x4, starting transfers between devices, passed_along(): return lax.ppermute(x, axis, pairs)  12.6 us
    pallas_call x1, Pallas kernels, exchange(): pl.pallas_call(functools.partial(exchange_kernel, axis, offsets), out_sha...  8.82 us
    dot_general x1, matrix products, shards(): jnp.einsum('td,dch->tch', normed, gathered[:, :3], preferred_element_type...  5.07 us
    dot_general x1, matrix products, shards(): jnp.einsum('tkh,ycdkh->cytd', widened_context, by_owner, preferred_elemen...  4.85 us
    unnamed x16, local copies, waits for them, and re-layouts  3.86 us
    ppermute x4, waiting for transfers between devices, passed_along(): return lax.ppermute(x, axis, pairs)  3.43 us
  transfers between devices with their start and end apart: 4, of which 3 were waited for; matrix products, arithmetic and copies ran while one was open for 4% of the time, Pallas kernels for 0%

profile of v14, /device:TPU:22, one launch (start us, length us, event | category | flops | bytes accessed | tf_op | source)
XLA Modules:
  0.0 156.8 jit_solution(10450617662958347232)
XLA Ops:
  0.0 0.9 copy.37
  0.9 0.8 copy.38
  1.7 0.8 pad_maximum_fusion.1.x_ref
  2.5 69.4 %shard_map.82 = bf16[8,8,50,4,256]{4,3,2,1,0:T(4,128)(2,1)} custom-call(bf16[50,4,256]{2,1,0:T(4,128)(2,1)} %pad_maximum_fusion.1.x_ref), custom_call_target="tpu_custom_call" | custom-call | tf_op jit(solution)/shard_map/pallas_call | solution.py:150
  71.9 0.0 copy-done
  71.9 0.4 multiply_reduce_fusion
  72.3 0.0 copy-done.5
  72.3 0.0 copy-start.3
  72.3 5.1 %fusion.3 = f32[256,3,256]{0,2,1:T(8,128)S(1)} fusion(bf16[3200,3,256]{2,1,0:T(4,128)(2,1)} %bitcast.41, f32[3200]{0:T(1024)S(1)} %copy-done.5, f32[256]{0:T(256)S(1)} %add_rsqrt_fusion, bf16[256,3200]{1,0:T(8,128)(2,1)S(1)} %copy-done), kind=kOutput, calls=%fused_computation.3 | convolution fusion | flops 1261568000 | bytes 7353856 | tf_op jit(solution)/shard_map/td,dch->tch/dot_general | solution.py:324
  77.4 0.0 copy-start.1
  77.4 0.0 copy-start.4
  77.4 0.1 multiply_reduce_fusion.2
  77.5 0.6 pad_maximum_fusion.2.x_ref
  78.1 8.8 %shard_map.83 = f32[8,2,256]{2,1,0:T(2,128)} custom-call(f32[2,256]{1,0:T(2,128)} %pad_maximum_fusion.2.x_ref), custom_call_target="tpu_custom_call" | custom-call | tf_op jit(solution)/shard_map/pallas_call | solution.py:288
  86.9 0.7 reduce_sum.57
  87.7 0.0 copy-done.3
  87.7 0.1 fusion.46
  87.8 3.5 %collective-permute-start = (bf16[256,2,256]{0,2,1:T(8,128)(2,1)S(1)}, bf16[256,2,256]{0,2,1:T(8,128)(2,1)}, u32[]{:S(2)}, u32[]{:S(2)}) collective-permute-start(bf16[256,2,256]{0,2,1:T(8,128)(2,1)S(1)} %pad_maximum_fusion), channel_id=1, source_target_pairs={{0,16},{8,24},{16,32},{24,40},{32,48},{40,56},{48,64},{56,72},{64,... | collective-permute-start | bytes 786440 | tf_op jit(solution)/shard_map/ppermute | solution.py:20
  91.3 2.9 %collective-permute-start.1 = (bf16[256,2,256]{0,2,1:T(8,128)(2,1)S(1)}, bf16[256,2,256]{0,2,1:T(8,128)(2,1)}, u32[]{:S(2)}, u32[]{:S(2)}) collective-permute-start(bf16[256,2,256]{0,2,1:T(8,128)(2,1)S(1)} %pad_maximum_fusion), channel_id=1, source_target_pairs={{0,8},{8,16},{16,24},{24,32},{32,40},{40,48},{48,56},{56,64},{64,7... | collective-permute-start | bytes 786440 | tf_op jit(solution)/shard_map/ppermute | solution.py:20
  94.2 3.9 %collective-permute-start.2 = (bf16[256,2,256]{0,2,1:T(8,128)(2,1)S(1)}, bf16[256,2,256]{0,2,1:T(8,128)(2,1)}, u32[]{:S(2)}, u32[]{:S(2)}) collective-permute-start(bf16[256,2,256]{0,2,1:T(8,128)(2,1)S(1)} %pad_maximum_fusion), channel_id=1, source_target_pairs={{8,0},{16,8},{24,16},{32,24},{40,32},{48,40},{56,48},{64,56},{72,6... | collective-permute-start | bytes 786440 | tf_op jit(solution)/shard_map/ppermute | solution.py:20
  98.1 2.4 %collective-permute-start.3 = (bf16[256,2,256]{0,2,1:T(8,128)(2,1)S(1)}, bf16[256,2,256]{0,2,1:T(8,128)(2,1)S(1)}, u32[]{:S(2)}, u32[]{:S(2)}) collective-permute-start(bf16[256,2,256]{0,2,1:T(8,128)(2,1)S(1)} %pad_maximum_fusion), channel_id=1, source_target_pairs={{16,0},{24,8},{32,16},{40,24},{48,32},{56,40},{64,48},{72,56},{80,... | collective-permute-start | bytes 786440 | tf_op jit(solution)/shard_map/ppermute | solution.py:20
  100.4 0.1 copy.40
  100.6 0.0 copy-done.1
  100.6 0.1 dynamic_slice.10
  100.7 0.1 fusion.30
  100.8 0.3 broadcast_compare_fusion
  101.0 0.0 copy-done.4
  101.0 0.1 multiply_convert_fusion.1
  101.1 2.0 %convert_element_type.43 = f32[256,3200]{1,0:T(8,128)} convert(bf16[256,3200]{1,0:T(8,128)(2,1)S(1)} %copy-done) | non-fusion elementwise | flops 819200 | bytes 4915200 | tf_op jit(solution)/shard_map/convert_element_type | solution.py:314
  103.1 0.1 pad_maximum_fusion.3
  103.2 0.6 collective-permute-done
  103.8 1.0 constant_dynamic-update-slice_fusion.4
  104.7 0.0 collective-permute-done.1
  104.7 1.0 constant_dynamic-update-slice_fusion.3
  105.7 1.8 %collective-permute-done.2 = bf16[256,2,256]{0,2,1:T(8,128)(2,1)} collective-permute-done((bf16[256,2,256]{0,2,1:T(8,128)(2,1)S(1)}, bf16[256,2,256]{0,2,1:T(8,128)(2,1)}, u32[]{:S(2)}, u32[]{:S(2)}) %collective-permute-start.2) | collective-permute-done | bytes 262176 | tf_op jit(solution)/shard_map/ppermute | solution.py:20
  107.5 1.0 constant_dynamic-update-slice_fusion.1
  108.5 1.1 collective-permute-done.3
  109.6 0.1 fusion.45
  109.7 1.4 fusion.47
  111.1 1.4 fusion.24
  112.5 0.1 copy.42
  112.6 4.8 %bitcast_convert_fusion = bf16[4,2,400,256]{3,2,1,0:T(8,128)(2,1)S(1)} fusion(bf16[4,2,400,4,256]{4,3,2,1,0:T(4,128)(2,1)} %bitcast.42, bf16[256,1,256]{2,0,1:T(8,128)(2,1)S(1)} %copy.42, bf16[4]{0:T(256)(128)(2,1)S(1)} %pad_maximum_fusion.3), kind=kOutput, calls=%fused_computation.8 | convolution fusion | flops 1678802944 | bytes 8323080 | tf_op jit(solution)/shard_map/tkh,ycdkh->cytd/dot_general | solution.py:373
  117.4 2.4 %copy.44 = bf16[4,2,400,256]{2,3,0,1:T(8,128)(2,1)} copy(bf16[4,2,400,256]{3,2,1,0:T(8,128)(2,1)S(1)} %bitcast_convert_fusion) | data formatting | bytes 3276800 | tf_op jit(solution)/shard_map/convert_element_type | solution.py:377
  119.8 33.4 %shard_map.84 = bf16[4,256,400]{2,1,0:T(8,128)(2,1)} custom-call(bf16[2,4,256,400]{3,2,1,0:T(8,128)(2,1)} %bitcast.40), custom_call_target="tpu_custom_call" | custom-call | tf_op jit(solution)/shard_map/pallas_call | solution.py:222
  153.2 1.4 convert_reduce_fusion
  154.7 0.0 copy-done.2
  154.7 1.3 add_convert_fusion
  156.0 0.8 copy.45
  (11 shorter events, 0.1 us)
Async XLA Ops:
  2.5 69.4 %copy-start = (bf16[256,3200]{1,0:T(8,128)(2,1)S(1)}, bf16[256,3200]{1,0:T(8,128)(2,1)}, u32[]{:S(2)}) copy-start(bf16[256,3200]{1,0:T(8,128)(2,1)} %param.8) | copy-start | bytes 4915204
  2.5 69.8 %copy-start.5 = (f32[3200]{0:T(1024)S(1)}, f32[3200]{0:T(1024)}, u32[]{:S(2)}) copy-start(f32[3200]{0:T(1024)} %param.9) | copy-start | bytes 38404
  72.3 15.4 %copy-start.3 = (f32[256]{0:T(256)S(1)}, f32[256]{0:T(256)}, u32[]{:S(2)}) copy-start(f32[256]{0:T(256)} %param.12) | copy-start | bytes 3076
  77.4 23.2 %copy-start.1 = (s32[16384]{0:T(1024)S(1)}, s32[16384]{0:T(1024)}, u32[]{:S(2)}) copy-start(s32[16384]{0:T(1024)} %param.15) | copy-start | bytes 196612
  77.4 23.6 %copy-start.4 = (f32[256]{0:T(256)S(1)}, f32[256]{0:T(256)}, u32[]{:S(2)}) copy-start(f32[256]{0:T(256)} %param.11) | copy-start | bytes 3076
  87.8 15.9 %collective-permute-start = (bf16[256,2,256]{0,2,1:T(8,128)(2,1)S(1)}, bf16[256,2,256]{0,2,1:T(8,128)(2,1)}, u32[]{:S(2)}, u32[]{:S(2)}) collective-permute-start(bf16[256,2,256]{0,2,1:T(8,128)(2,1)S(1)} %pad_maximum_fusion), channel_id=1, source_target_pairs={{0,16},{8,24},{16,32},{24,40},{32,48},{40,56},{48,64},{56,72},{64,... | collective-permute-start | bytes 786440 | tf_op jit(solution)/shard_map/ppermute | solution.py:20
  91.3 13.4 %collective-permute-start.1 = (bf16[256,2,256]{0,2,1:T(8,128)(2,1)S(1)}, bf16[256,2,256]{0,2,1:T(8,128)(2,1)}, u32[]{:S(2)}, u32[]{:S(2)}) collective-permute-start(bf16[256,2,256]{0,2,1:T(8,128)(2,1)S(1)} %pad_maximum_fusion), channel_id=1, source_target_pairs={{0,8},{8,16},{16,24},{24,32},{32,40},{40,48},{48,56},{56,64},{64,7... | collective-permute-start | bytes 786440 | tf_op jit(solution)/shard_map/ppermute | solution.py:20
  94.2 13.3 %collective-permute-start.2 = (bf16[256,2,256]{0,2,1:T(8,128)(2,1)S(1)}, bf16[256,2,256]{0,2,1:T(8,128)(2,1)}, u32[]{:S(2)}, u32[]{:S(2)}) collective-permute-start(bf16[256,2,256]{0,2,1:T(8,128)(2,1)S(1)} %pad_maximum_fusion), channel_id=1, source_target_pairs={{8,0},{16,8},{24,16},{32,24},{40,32},{48,40},{56,48},{64,56},{72,6... | collective-permute-start | bytes 786440 | tf_op jit(solution)/shard_map/ppermute | solution.py:20
  98.1 11.5 %collective-permute-start.3 = (bf16[256,2,256]{0,2,1:T(8,128)(2,1)S(1)}, bf16[256,2,256]{0,2,1:T(8,128)(2,1)S(1)}, u32[]{:S(2)}, u32[]{:S(2)}) collective-permute-start(bf16[256,2,256]{0,2,1:T(8,128)(2,1)S(1)} %pad_maximum_fusion), channel_id=1, source_target_pairs={{16,0},{24,8},{32,16},{40,24},{48,32},{56,40},{64,48},{72,56},{80,... | collective-permute-start | bytes 786440 | tf_op jit(solution)/shard_map/ppermute | solution.py:20
  119.8 34.9 %copy-start.2 = (f32[400]{0:T(512)S(1)}, f32[400]{0:T(512)}, u32[]{:S(2)}) copy-start(f32[400]{0:T(512)} %param.14) | copy-start | bytes 4804

commit v15 on v14

--- a/solution.py
+++ b/solution.py
@@ -330,6 +330,10 @@
     query = joined[:, 0]
     keys = joined[:, 1]
     values = joined[:, 2]
+    values_low = values.astype(jnp.bfloat16)
+    value_pieces = {
+        offset: passed_along(values_low, "seq", offset) for offset in (2, 1, -1, -2)
+    }
     parts = lax.axis_size("tp")
     squares = jnp.stack([jnp.sum(query * query, axis=-1), jnp.sum(keys * keys, axis=-1)])
     everyone = [(k, None) for k in range(1, parts)]
@@ -341,22 +345,25 @@
     key_normed = (keys * lax.rsqrt(key_sq / full_width + eps)[:, None] * k_gain).astype(
         jnp.bfloat16
     )
-    paired = jnp.stack([key_normed, values.astype(jnp.bfloat16)], axis=1)
-    pieces = []
+    key_pieces = []
+    value_list = []
     for offset in (2, 1, 0, -1, -2):
         if offset == 0:
-            pieces.append(paired)
+            key_pieces.append(key_normed)
+            value_list.append(values_low)
         else:
-            pieces.append(passed_along(paired, "seq", offset))
-    widened = jnp.concatenate(pieces, axis=0)
+            key_pieces.append(passed_along(key_normed, "seq", offset))
+            value_list.append(value_pieces[offset])
+    wide_keys = jnp.concatenate(key_pieces, axis=0)
+    wide_values = jnp.concatenate(value_list, axis=0)
     position = lax.axis_index("seq")
     outside = jnp.full((2 * count,), -1, jnp.int32)
     seg_pad = jnp.concatenate([outside, segment_ids, outside], axis=0)
     key_seg = lax.dynamic_slice_in_dim(seg_pad, position * count, 5 * count, 0)
     query_seg = lax.dynamic_slice_in_dim(segment_ids, position * count, count, 0)
     query_heads = query_normed.reshape(count, heads, HEAD_DIM)
-    key_heads = widened[:, 0].reshape(5 * count, heads, HEAD_DIM)
-    value_heads = widened[:, 1].reshape(5 * count, heads, HEAD_DIM)
+    key_heads = wide_keys.reshape(5 * count, heads, HEAD_DIM)
+    value_heads = wide_values.reshape(5 * count, heads, HEAD_DIM)
     scores, mask = masked_scores(query_heads, key_heads, query_seg, key_seg)
     peak = jnp.max(scores, axis=-1, keepdims=True)
     weights = jnp.where(mask, jnp.exp(scores - peak), 0.0)

time: 157 us -> 174 us (1.11)
  the two profiles are of different devices: /device:TPU:22 before, /device:TPU:15 now
where the time goes in v15:
time: 174 us; the launch traced here: 173 us
  Pallas kernels  116 us (67%)
  starting transfers between devices  22.9 us (13%)
  matrix products  12.7 us (7%)
  local copies, waits for them, and re-layouts  9.88 us (6%)
  other arithmetic  8.04 us (5%)
  waiting for transfers between devices  3.67 us (2%)
    pallas_call x1, Pallas kernels, gather_seq(): pl.pallas_call(gather_kernel, out_shape=jax.ShapeDtypeStruct((rings, slab...  63.2 us
    pallas_call x1, Pallas kernels, scatter_chips(): pl.pallas_call(scatter_kernel, out_shape=jax.ShapeDtypeStruct(block, jnp....  35.4 us
    ppermute x8, starting transfers between devices, passed_along(): return lax.ppermute(x, axis, pairs)  22.9 us
    pallas_call x1, Pallas kernels, exchange(): pl.pallas_call(functools.partial(exchange_kernel, axis, offsets), out_sha...  17 us
    unnamed x20, local copies, waits for them, and re-layouts  5.56 us
    dot_general x1, matrix products, shards(): jnp.einsum('td,dch->tch', normed, gathered[:, :3], preferred_element_type...  5.1 us
    dot_general x1, matrix products, shards(): jnp.einsum('tkh,ycdkh->cytd', widened_context, by_owner, preferred_elemen...  4.85 us
    ppermute x8, waiting for transfers between devices, passed_along(): return lax.ppermute(x, axis, pairs)  3.67 us
  transfers between devices with their start and end apart: 8, of which 3 were waited for; matrix products, arithmetic and copies ran while one was open for 6% of the time, Pallas kernels for 10%

profile of v15, /device:TPU:15, one launch (start us, length us, event | category | flops | bytes accessed | tf_op | source)
XLA Modules:
  0.0 173.1 jit_solution(3935751281424606524)
XLA Ops:
  0.0 0.8 copy.38
  0.8 0.9 copy.37
  1.7 0.8 pad_maximum_fusion.x_ref
  2.5 63.2 %shard_map.82 = bf16[8,8,50,4,256]{4,3,2,1,0:T(4,128)(2,1)} custom-call(bf16[50,4,256]{2,1,0:T(4,128)(2,1)} %pad_maximum_fusion.x_ref), custom_call_target="tpu_custom_call" | custom-call | tf_op jit(solution)/shard_map/pallas_call | solution.py:150
  65.7 0.4 multiply_reduce_fusion
  66.1 0.0 copy-start.2
  66.1 0.0 copy-start.1
  66.1 0.0 copy-start.4
  66.1 5.1 %fusion.3 = f32[256,3,256]{0,2,1:T(8,128)S(1)} fusion(bf16[3200,3,256]{2,1,0:T(4,128)(2,1)} %bitcast.53, f32[3200]{0:T(1024)S(1)} %copy-done.5, f32[256]{0:T(256)S(1)} %add_rsqrt_fusion, bf16[256,3200]{1,0:T(8,128)(2,1)S(1)} %copy-done), kind=kOutput, calls=%fused_computation.3 | convolution fusion | flops 1261568000 | bytes 7353856 | tf_op jit(solution)/shard_map/td,dch->tch/dot_general | solution.py:324
  71.3 2.0 %collective-permute-start = (bf16[256,256]{0,1:T(8,128)(2,1)S(1)}, bf16[256,256]{0,1:T(8,128)(2,1)}, u32[]{:S(2)}, u32[]{:S(2)}) collective-permute-start(bf16[256,256]{0,1:T(8,128)(2,1)S(1)} %fusion.29), channel_id=1, source_target_pairs={{0,16},{8,24},{16,32},{24,40},{32,48},{40,56},{48,64},{56,72},{64,... | collective-permute-start | bytes 393224 | tf_op jit(solution)/shard_map/ppermute | solution.py:20
  73.2 1.9 %collective-permute-start.1 = (bf16[256,256]{0,1:T(8,128)(2,1)S(1)}, bf16[256,256]{0,1:T(8,128)(2,1)}, u32[]{:S(2)}, u32[]{:S(2)}) collective-permute-start(bf16[256,256]{0,1:T(8,128)(2,1)S(1)} %fusion.29), channel_id=1, source_target_pairs={{0,8},{8,16},{16,24},{24,32},{32,40},{40,48},{48,56},{56,64},{64,7... | collective-permute-start | bytes 393224 | tf_op jit(solution)/shard_map/ppermute | solution.py:20
  75.2 3.4 %collective-permute-start.2 = (bf16[256,256]{0,1:T(8,128)(2,1)S(1)}, bf16[256,256]{0,1:T(8,128)(2,1)}, u32[]{:S(2)}, u32[]{:S(2)}) collective-permute-start(bf16[256,256]{0,1:T(8,128)(2,1)S(1)} %fusion.29), channel_id=1, source_target_pairs={{8,0},{16,8},{24,16},{32,24},{40,32},{48,40},{56,48},{64,56},{72,6... | collective-permute-start | bytes 393224 | tf_op jit(solution)/shard_map/ppermute | solution.py:20
  78.5 0.1 multiply_reduce_fusion.2
  78.7 0.6 pad_maximum_fusion.1.x_ref
  79.2 17.0 %shard_map.83 = f32[8,2,256]{2,1,0:T(2,128)} custom-call(f32[2,256]{1,0:T(2,128)} %pad_maximum_fusion.1.x_ref), custom_call_target="tpu_custom_call" | custom-call | tf_op jit(solution)/shard_map/pallas_call | solution.py:288
  96.2 0.7 reduce_sum.57
  97.0 0.1 multiply_convert_fusion.1
  97.1 3.1 %collective-permute-start.4 = (bf16[256,256]{0,1:T(8,128)(2,1)S(1)}, bf16[256,256]{0,1:T(8,128)(2,1)}, u32[]{:S(2)}, u32[]{:S(2)}) collective-permute-start(bf16[256,256]{0,1:T(8,128)(2,1)S(1)} %multiply_convert_fusion.1), channel_id=1, source_target_pairs={{0,16},{8,24},{16,32},{24,40},{32,48},{40,56},{48,64},{56,72},{64,... | collective-permute-start | bytes 393224 | tf_op jit(solution)/shard_map/ppermute | solution.py:20
  100.2 5.3 %collective-permute-start.5 = (bf16[256,256]{0,1:T(8,128)(2,1)S(1)}, bf16[256,256]{0,1:T(8,128)(2,1)}, u32[]{:S(2)}, u32[]{:S(2)}) collective-permute-start(bf16[256,256]{0,1:T(8,128)(2,1)S(1)} %multiply_convert_fusion.1), channel_id=1, source_target_pairs={{0,8},{8,16},{16,24},{24,32},{32,40},{40,48},{48,56},{56,64},{64,7... | collective-permute-start | bytes 393224 | tf_op jit(solution)/shard_map/ppermute | solution.py:20
  105.6 0.1 copy.40
  105.7 0.1 dynamic_slice.10
  105.8 0.1 fusion.31
  105.9 0.3 broadcast_compare_fusion
  106.2 0.1 multiply_convert_fusion.2
  106.3 0.1 pad_maximum_fusion.2
  106.4 2.0 %convert_element_type.44 = f32[256,3200]{1,0:T(8,128)} convert(bf16[256,3200]{1,0:T(8,128)(2,1)S(1)} %copy-done) | non-fusion elementwise | flops 819200 | bytes 4915200 | tf_op jit(solution)/shard_map/convert_element_type | solution.py:314
  108.3 0.0 collective-permute-done.4
  108.3 2.2 %collective-permute-start.6 = (bf16[256,256]{0,1:T(8,128)(2,1)S(1)}, bf16[256,256]{0,1:T(8,128)(2,1)S(1)}, u32[]{:S(2)}, u32[]{:S(2)}) collective-permute-start(bf16[256,256]{0,1:T(8,128)(2,1)S(1)} %multiply_convert_fusion.1), channel_id=1, source_target_pairs={{8,0},{16,8},{24,16},{32,24},{40,32},{48,40},{56,48},{64,56},{72,6... | collective-permute-start | bytes 393224 | tf_op jit(solution)/shard_map/ppermute | solution.py:20
  110.5 0.9 constant_dynamic-update-slice_fusion.9
  111.4 3.1 %collective-permute-start.7 = (bf16[256,256]{0,1:T(8,128)(2,1)S(1)}, bf16[256,256]{0,1:T(8,128)(2,1)S(1)}, u32[]{:S(2)}, u32[]{:S(2)}) collective-permute-start(bf16[256,256]{0,1:T(8,128)(2,1)S(1)} %multiply_convert_fusion.1), channel_id=1, source_target_pairs={{16,0},{24,8},{32,16},{40,24},{48,32},{56,40},{64,48},{72,56},{80,... | collective-permute-start | bytes 393224 | tf_op jit(solution)/shard_map/ppermute | solution.py:20
  114.5 0.9 constant_dynamic-update-slice_fusion.8
  115.5 0.1 constant_dynamic-update-slice_fusion.7
  115.6 2.0 %collective-permute-done.6 = bf16[256,256]{0,1:T(8,128)(2,1)S(1)} collective-permute-done((bf16[256,256]{0,1:T(8,128)(2,1)S(1)}, bf16[256,256]{0,1:T(8,128)(2,1)S(1)}, u32[]{:S(2)}, u32[]{:S(2)}) %collective-permute-start.6) | collective-permute-done | bytes 131104 | tf_op jit(solution)/shard_map/ppermute | solution.py:20
  117.6 1.9 %collective-permute-start.3 = (bf16[256,256]{0,1:T(8,128)(2,1)S(1)}, bf16[256,256]{0,1:T(8,128)(2,1)S(1)}, u32[]{:S(2)}, u32[]{:S(2)}) collective-permute-start(bf16[256,256]{0,1:T(8,128)(2,1)S(1)} %fusion.29), channel_id=1, source_target_pairs={{16,0},{24,8},{32,16},{40,24},{48,32},{56,40},{64,48},{72,56},{80,... | collective-permute-start | bytes 393224 | tf_op jit(solution)/shard_map/ppermute | solution.py:20
  119.5 1.1 collective-permute-done.7
  120.7 1.4 fusion.46
  122.1 0.9 constant_dynamic-update-slice_fusion.4
  123.0 0.9 constant_dynamic-update-slice_fusion.3
  124.0 0.9 constant_dynamic-update-slice_fusion.1
  124.9 0.5 collective-permute-done.3
  125.4 1.4 fusion.24
  126.8 0.1 copy.42
  126.9 4.8 %bitcast_convert_fusion = bf16[4,2,400,256]{3,2,1,0:T(8,128)(2,1)S(1)} fusion(bf16[4,2,400,4,256]{4,3,2,1,0:T(4,128)(2,1)} %bitcast.54, bf16[256,1,256]{2,0,1:T(8,128)(2,1)S(1)} %copy.42, bf16[4]{0:T(256)(128)(2,1)S(1)} %pad_maximum_fusion.2), kind=kOutput, calls=%fused_computation.8 | convolution fusion | flops 1678802944 | bytes 8323080 | tf_op jit(solution)/shard_map/tkh,ycdkh->cytd/dot_general | solution.py:380
  131.7 2.4 %copy.44 = bf16[4,2,400,256]{2,3,0,1:T(8,128)(2,1)} copy(bf16[4,2,400,256]{3,2,1,0:T(8,128)(2,1)S(1)} %bitcast_convert_fusion) | data formatting | bytes 3276800 | tf_op jit(solution)/shard_map/convert_element_type | solution.py:384
  134.1 35.4 %shard_map.84 = bf16[4,256,400]{2,1,0:T(8,128)(2,1)} custom-call(bf16[2,4,256,400]{3,2,1,0:T(8,128)(2,1)} %bitcast.52), custom_call_target="tpu_custom_call" | custom-call | tf_op jit(solution)/shard_map/pallas_call | solution.py:222
  169.5 1.4 convert_reduce_fusion
  171.0 1.3 add_convert_fusion
  172.3 0.8 copy.45
  (23 shorter events, 0.2 us)
Async XLA Ops:
  2.5 63.2 %copy-start = (bf16[256,3200]{1,0:T(8,128)(2,1)S(1)}, bf16[256,3200]{1,0:T(8,128)(2,1)}, u32[]{:S(2)}) copy-start(bf16[256,3200]{1,0:T(8,128)(2,1)} %param.8) | copy-start | bytes 4915204
  2.5 63.6 %copy-start.5 = (f32[3200]{0:T(1024)S(1)}, f32[3200]{0:T(1024)}, u32[]{:S(2)}) copy-start(f32[3200]{0:T(1024)} %param.9) | copy-start | bytes 38404
  66.1 30.9 %copy-start.2 = (f32[256]{0:T(256)S(1)}, f32[256]{0:T(256)}, u32[]{:S(2)}) copy-start(f32[256]{0:T(256)} %param.12) | copy-start | bytes 3076
  66.1 39.6 %copy-start.1 = (s32[16384]{0:T(1024)S(1)}, s32[16384]{0:T(1024)}, u32[]{:S(2)}) copy-start(s32[16384]{0:T(1024)} %param.15) | copy-start | bytes 196612
  66.1 40.0 %copy-start.4 = (f32[256]{0:T(256)S(1)}, f32[256]{0:T(256)}, u32[]{:S(2)}) copy-start(f32[256]{0:T(256)} %param.11) | copy-start | bytes 3076
  71.3 50.8 %collective-permute-start = (bf16[256,256]{0,1:T(8,128)(2,1)S(1)}, bf16[256,256]{0,1:T(8,128)(2,1)}, u32[]{:S(2)}, u32[]{:S(2)}) collective-permute-start(bf16[256,256]{0,1:T(8,128)(2,1)S(1)} %fusion.29), channel_id=1, source_target_pairs={{0,16},{8,24},{16,32},{24,40},{32,48},{40,56},{48,64},{56,72},{64,... | collective-permute-start | bytes 393224 | tf_op jit(solution)/shard_map/ppermute | solution.py:20
  73.2 49.7 %collective-permute-start.1 = (bf16[256,256]{0,1:T(8,128)(2,1)S(1)}, bf16[256,256]{0,1:T(8,128)(2,1)}, u32[]{:S(2)}, u32[]{:S(2)}) collective-permute-start(bf16[256,256]{0,1:T(8,128)(2,1)S(1)} %fusion.29), channel_id=1, source_target_pairs={{0,8},{8,16},{16,24},{24,32},{32,40},{40,48},{48,56},{56,64},{64,7... | collective-permute-start | bytes 393224 | tf_op jit(solution)/shard_map/ppermute | solution.py:20
  75.2 48.8 %collective-permute-start.2 = (bf16[256,256]{0,1:T(8,128)(2,1)S(1)}, bf16[256,256]{0,1:T(8,128)(2,1)}, u32[]{:S(2)}, u32[]{:S(2)}) collective-permute-start(bf16[256,256]{0,1:T(8,128)(2,1)S(1)} %fusion.29), channel_id=1, source_target_pairs={{8,0},{16,8},{24,16},{32,24},{40,32},{48,40},{56,48},{64,56},{72,6... | collective-permute-start | bytes 393224 | tf_op jit(solution)/shard_map/ppermute | solution.py:20
  97.1 11.2 %collective-permute-start.4 = (bf16[256,256]{0,1:T(8,128)(2,1)S(1)}, bf16[256,256]{0,1:T(8,128)(2,1)}, u32[]{:S(2)}, u32[]{:S(2)}) collective-permute-start(bf16[256,256]{0,1:T(8,128)(2,1)S(1)} %multiply_convert_fusion.1), channel_id=1, source_target_pairs={{0,16},{8,24},{16,32},{24,40},{32,48},{40,56},{48,64},{56,72},{64,... | collective-permute-start | bytes 393224 | tf_op jit(solution)/shard_map/ppermute | solution.py:20
  100.2 11.2 %collective-permute-start.5 = (bf16[256,256]{0,1:T(8,128)(2,1)S(1)}, bf16[256,256]{0,1:T(8,128)(2,1)}, u32[]{:S(2)}, u32[]{:S(2)}) collective-permute-start(bf16[256,256]{0,1:T(8,128)(2,1)S(1)} %multiply_convert_fusion.1), channel_id=1, source_target_pairs={{0,8},{8,16},{16,24},{24,32},{32,40},{40,48},{48,56},{56,64},{64,7... | collective-permute-start | bytes 393224 | tf_op jit(solution)/shard_map/ppermute | solution.py:20
  108.3 9.3 %collective-permute-start.6 = (bf16[256,256]{0,1:T(8,128)(2,1)S(1)}, bf16[256,256]{0,1:T(8,128)(2,1)S(1)}, u32[]{:S(2)}, u32[]{:S(2)}) collective-permute-start(bf16[256,256]{0,1:T(8,128)(2,1)S(1)} %multiply_convert_fusion.1), channel_id=1, source_target_pairs={{8,0},{16,8},{24,16},{32,24},{40,32},{48,40},{56,48},{64,56},{72,6... | collective-permute-start | bytes 393224 | tf_op jit(solution)/shard_map/ppermute | solution.py:20
  111.4 9.2 %collective-permute-start.7 = (bf16[256,256]{0,1:T(8,128)(2,1)S(1)}, bf16[256,256]{0,1:T(8,128)(2,1)S(1)}, u32[]{:S(2)}, u32[]{:S(2)}) collective-permute-start(bf16[256,256]{0,1:T(8,128)(2,1)S(1)} %multiply_convert_fusion.1), channel_id=1, source_target_pairs={{16,0},{24,8},{32,16},{40,24},{48,32},{56,40},{64,48},{72,56},{80,... | collective-permute-start | bytes 393224 | tf_op jit(solution)/shard_map/ppermute | solution.py:20
  117.6 7.8 %collective-permute-start.3 = (bf16[256,256]{0,1:T(8,128)(2,1)S(1)}, bf16[256,256]{0,1:T(8,128)(2,1)S(1)}, u32[]{:S(2)}, u32[]{:S(2)}) collective-permute-start(bf16[256,256]{0,1:T(8,128)(2,1)S(1)} %fusion.29), channel_id=1, source_target_pairs={{16,0},{24,8},{32,16},{40,24},{48,32},{56,40},{64,48},{72,56},{80,... | collective-permute-start | bytes 393224 | tf_op jit(solution)/shard_map/ppermute | solution.py:20
  134.1 36.9 %copy-start.3 = (f32[400]{0:T(512)S(1)}, f32[400]{0:T(512)}, u32[]{:S(2)}) copy-start(f32[400]{0:T(512)} %param.14) | copy-start | bytes 4804

commit v16 on v13

--- a/solution.py
+++ b/solution.py
@@ -370,10 +370,10 @@
     chips = parts // 2
     by_owner = gathered.reshape(chips, 2, -1, *gathered.shape[1:])
     terms = jnp.einsum(
-        "tkh,ycdkh->cytd", widened_context, by_owner, preferred_element_type=jnp.float32
-    )
-    projected = jnp.sum(
-        scatter_chips(terms.astype(jnp.bfloat16)).astype(jnp.float32), axis=0
+        "tkh,ycdkh->cydt", widened_context, by_owner, preferred_element_type=jnp.float32
+    )
+    projected = jnp.transpose(
+        jnp.sum(scatter_chips(terms.astype(jnp.bfloat16)).astype(jnp.float32), axis=0)
     )
     share = layer_scale.shape[0]
     residual = lax.dynamic_slice_in_dim(source, lax.axis_index("tp") * share, share, 1)

time: 158 us -> 153 us (0.968)
  the two profiles are of different devices: /device:TPU:22 before, /device:TPU:15 now
where the time goes in v16:
time: 153 us; the launch traced here: 152 us
  Pallas kernels  102 us (67%)
  matrix products  14.1 us (9%)
  starting transfers between devices  12 us (8%)
  other arithmetic  8.39 us (5%)
  waiting for transfers between devices  8.39 us (5%)
  local copies, waits for them, and re-layouts  6.46 us (4%)
    pallas_call x1, Pallas kernels, gather_seq(): pl.pallas_call(gather_kernel, out_shape=jax.ShapeDtypeStruct((rings, slab...  62.6 us
    pallas_call x1, Pallas kernels, scatter_chips(): pl.pallas_call(scatter_kernel, out_shape=jax.ShapeDtypeStruct(block, jnp....  25.3 us
    pallas_call x1, Pallas kernels, exchange(): pl.pallas_call(functools.partial(exchange_kernel, axis, offsets), out_sha...  14.5 us
    ppermute x4, starting transfers between devices, passed_along(): return lax.ppermute(x, axis, pairs)  12 us
    ppermute x4, waiting for transfers between devices, passed_along(): return lax.ppermute(x, axis, pairs)  8.39 us
    dot_general x1, matrix products, shards(): jnp.einsum('tkh,ycdkh->cydt', widened_context, by_owner, preferred_elemen...  6.02 us
    unnamed x19, local copies, waits for them, and re-layouts  6 us
    dot_general x1, matrix products, shards(): jnp.einsum('td,dch->tch', normed, gathered[:, :3], preferred_element_type...  5.33 us
  transfers between devices with their start and end apart: 4, of which 2 were waited for; matrix products, arithmetic and copies ran while one was open for 4% of the time, Pallas kernels for 0%

profile of v16, /device:TPU:15, one launch (start us, length us, event | category | flops | bytes accessed | tf_op | source)
XLA Modules:
  0.0 152.0 jit_solution(314006574501952952)
XLA Ops:
  0.0 0.0 copy-start
  0.0 0.0 copy-start.2
  0.0 3.0 %copy.18 = bf16[256,3200]{0,1:T(8,128)(2,1)S(1)} copy(bf16[256,3200]{1,0:T(8,128)(2,1)} %param.8) | data formatting | bytes 3276800 | tf_op args[0]
  3.0 0.5 multiply_reduce_fusion
  3.5 0.0 copy-done
  3.6 0.0 copy-done.2
  3.6 0.8 pad_maximum_fusion.1.x_ref
  4.4 62.6 %shard_map.82 = bf16[8,8,50,4,256]{4,3,2,1,0:T(4,128)(2,1)} custom-call(bf16[50,4,256]{2,1,0:T(4,128)(2,1)} %pad_maximum_fusion.1.x_ref), custom_call_target="tpu_custom_call" | custom-call | tf_op jit(solution)/shard_map/pallas_call | solution.py:149
  66.9 0.0 copy-done.6
  67.0 0.0 copy-start.4
  67.0 5.3 %fusion.3 = f32[256,3,256]{0,2,1:T(8,128)S(1)} fusion(bf16[3200,3,256]{2,1,0:T(4,128)(2,1)} %bitcast.44, f32[3200]{0:T(1024)S(1)} %copy-done.6, f32[256]{0:T(256)S(1)} %add_rsqrt_fusion, bf16[256,3200]{0,1:T(8,128)(2,1)S(1)} %copy.18), kind=kOutput, calls=%fused_computation.3 | convolution fusion | flops 1261568000 | bytes 7353856 | tf_op jit(solution)/shard_map/td,dch->tch/dot_general | solution.py:323
  72.3 0.0 copy-start.1
  72.3 0.0 copy-start.5
  72.3 0.1 multiply_reduce_fusion.2
  72.4 0.6 pad_maximum_fusion.2.x_ref
  73.0 14.5 %shard_map.83 = f32[8,2,256]{2,1,0:T(2,128)} custom-call(f32[2,256]{1,0:T(2,128)} %pad_maximum_fusion.2.x_ref), custom_call_target="tpu_custom_call" | custom-call | tf_op jit(solution)/shard_map/pallas_call | solution.py:287
  87.5 0.7 reduce_sum.57
  88.2 0.0 copy-done.4
  88.3 0.1 fusion.50
  88.4 2.9 %collective-permute-start = (bf16[256,2,256]{0,2,1:T(8,128)(2,1)S(1)}, bf16[256,2,256]{0,2,1:T(8,128)(2,1)}, u32[]{:S(2)}, u32[]{:S(2)}) collective-permute-start(bf16[256,2,256]{0,2,1:T(8,128)(2,1)S(1)} %pad_maximum_fusion), channel_id=1, source_target_pairs={{0,16},{8,24},{16,32},{24,40},{32,48},{40,56},{48,64},{56,72},{64,... | collective-permute-start | bytes 786440 | tf_op jit(solution)/shard_map/ppermute | solution.py:20
  91.3 4.5 %collective-permute-start.1 = (bf16[256,2,256]{0,2,1:T(8,128)(2,1)S(1)}, bf16[256,2,256]{0,2,1:T(8,128)(2,1)}, u32[]{:S(2)}, u32[]{:S(2)}) collective-permute-start(bf16[256,2,256]{0,2,1:T(8,128)(2,1)S(1)} %pad_maximum_fusion), channel_id=1, source_target_pairs={{0,8},{8,16},{16,24},{24,32},{32,40},{40,48},{48,56},{56,64},{64,7... | collective-permute-start | bytes 786440 | tf_op jit(solution)/shard_map/ppermute | solution.py:20
  95.8 1.9 %collective-permute-start.2 = (bf16[256,2,256]{0,2,1:T(8,128)(2,1)S(1)}, bf16[256,2,256]{0,2,1:T(8,128)(2,1)}, u32[]{:S(2)}, u32[]{:S(2)}) collective-permute-start(bf16[256,2,256]{0,2,1:T(8,128)(2,1)S(1)} %pad_maximum_fusion), channel_id=1, source_target_pairs={{8,0},{16,8},{24,16},{32,24},{40,32},{48,40},{56,48},{64,56},{72,6... | collective-permute-start | bytes 786440 | tf_op jit(solution)/shard_map/ppermute | solution.py:20
  97.8 2.7 %collective-permute-start.3 = (bf16[256,2,256]{0,2,1:T(8,128)(2,1)S(1)}, bf16[256,2,256]{0,2,1:T(8,128)(2,1)S(1)}, u32[]{:S(2)}, u32[]{:S(2)}) collective-permute-start(bf16[256,2,256]{0,2,1:T(8,128)(2,1)S(1)} %pad_maximum_fusion), channel_id=1, source_target_pairs={{16,0},{24,8},{32,16},{40,24},{48,32},{56,40},{64,48},{72,56},{80,... | collective-permute-start | bytes 786440 | tf_op jit(solution)/shard_map/ppermute | solution.py:20
  100.5 0.1 copy.23
  100.6 0.0 copy-done.1
  100.6 0.1 dynamic_slice.10
  100.7 0.1 fusion.34
  100.8 0.3 broadcast_compare_fusion
  101.0 0.0 copy-done.5
  101.0 0.1 multiply_convert_fusion.1
  101.2 2.0 %convert_element_type.43 = f32[256,3200]{0,1:T(8,128)} convert(bf16[256,3200]{0,1:T(8,128)(2,1)S(1)} %copy.18) | non-fusion elementwise | flops 819200 | bytes 4915200 | tf_op jit(solution)/shard_map/convert_element_type | solution.py:313
  103.2 0.1 pad_maximum_fusion.3
  103.2 0.0 collective-permute-done
  103.2 1.0 constant_dynamic-update-slice_fusion.4
  104.2 0.0 collective-permute-done.1
  104.2 1.0 constant_dynamic-update-slice_fusion.3
  105.2 2.5 %collective-permute-done.2 = bf16[256,2,256]{0,2,1:T(8,128)(2,1)} collective-permute-done((bf16[256,2,256]{0,2,1:T(8,128)(2,1)S(1)}, bf16[256,2,256]{0,2,1:T(8,128)(2,1)}, u32[]{:S(2)}, u32[]{:S(2)}) %collective-permute-start.2) | collective-permute-done | bytes 262176 | tf_op jit(solution)/shard_map/ppermute | solution.py:20
  107.7 1.0 constant_dynamic-update-slice_fusion.1
  108.7 5.9 %collective-permute-done.3 = bf16[256,2,256]{0,2,1:T(8,128)(2,1)S(1)} collective-permute-done((bf16[256,2,256]{0,2,1:T(8,128)(2,1)S(1)}, bf16[256,2,256]{0,2,1:T(8,128)(2,1)S(1)}, u32[]{:S(2)}, u32[]{:S(2)}) %collective-permute-start.3) | collective-permute-done | bytes 262176 | tf_op jit(solution)/shard_map/ppermute | solution.py:20
  114.6 0.1 fusion.49
  114.7 1.4 fusion.51
  116.1 1.4 fusion.27
  117.5 0.1 copy.25
  117.6 6.0 %fusion.16.terms_ref = bf16[2,4,400,256]{3,2,1,0:T(8,128)(2,1)} fusion(bf16[4,2,400,4,256]{4,3,2,1,0:T(4,128)(2,1)} %bitcast.45, bf16[256,1,256]{2,0,1:T(8,128)(2,1)S(1)} %copy.25, bf16[4]{0:T(256)(128)(2,1)S(1)} %pad_maximum_fusion.3), kind=kOutput, calls=%fused_computation.18 | convolution fusion | flops 1678802944 | bytes 8323080 | tf_op jit(solution)/shard_map/tkh,ycdkh->cydt/dot_general | solution.py:372
  123.6 25.3 %shard_map.84 = bf16[4,400,256]{2,1,0:T(8,128)(2,1)} custom-call(bf16[2,4,400,256]{3,2,1,0:T(8,128)(2,1)} %fusion.16.terms_ref), custom_call_target="tpu_custom_call" | custom-call | tf_op jit(solution)/shard_map/pallas_call | solution.py:221
  148.9 1.3 convert_reduce_fusion
  150.2 0.0 copy-done.3
  150.2 1.8 %fusion.31 = bf16[256,400]{0,1:T(8,128)(2,1)} fusion(f32[400,256]{1,0:T(8,128)S(1)} %convert_reduce_fusion, f32[256,3200]{0,1:T(8,128)} %convert_element_type.43, s32[]{:T(128)S(6)} %select_n.16, f32[400]{0:T(512)S(1)} %copy-done.3), kind=kLoop, calls=%fused_computation.28 | loop fusion | flops 307200 | bytes 1025604 | tf_op jit(solution)/shard_map/convert_element_type | solution.py:380
  (12 shorter events, 0.2 us)
Async XLA Ops:
  0.0 3.5 %copy-start = (bf16[50,3,256]{2,0,1:T(8,128)(2,1)S(1)}, bf16[50,3,256]{2,0,1:T(8,128)(2,1)}, u32[]{:S(2)}) copy-start(bf16[50,3,256]{2,0,1:T(8,128)(2,1)} %param.10) | copy-start | bytes 230404
  0.0 3.6 %copy-start.2 = (bf16[256,50]{0,1:T(8,128)(2,1)S(1)}, bf16[256,50]{0,1:T(8,128)(2,1)}, u32[]{:S(2)}) copy-start(bf16[256,50]{0,1:T(8,128)(2,1)} %param.13) | copy-start | bytes 76804
  4.4 62.6 %copy-start.6 = (f32[3200]{0:T(1024)S(1)}, f32[3200]{0:T(1024)}, u32[]{:S(2)}) copy-start(f32[3200]{0:T(1024)} %param.9) | copy-start | bytes 38404
  67.0 21.3 %copy-start.4 = (f32[256]{0:T(256)S(1)}, f32[256]{0:T(256)}, u32[]{:S(2)}) copy-start(f32[256]{0:T(256)} %param.12) | copy-start | bytes 3076
  72.3 28.3 %copy-start.1 = (s32[16384]{0:T(1024)S(1)}, s32[16384]{0:T(1024)}, u32[]{:S(2)}) copy-start(s32[16384]{0:T(1024)} %param.15) | copy-start | bytes 196612
  72.3 28.7 %copy-start.5 = (f32[256]{0:T(256)S(1)}, f32[256]{0:T(256)}, u32[]{:S(2)}) copy-start(f32[256]{0:T(256)} %param.11) | copy-start | bytes 3076
  88.4 14.8 %collective-permute-start = (bf16[256,2,256]{0,2,1:T(8,128)(2,1)S(1)}, bf16[256,2,256]{0,2,1:T(8,128)(2,1)}, u32[]{:S(2)}, u32[]{:S(2)}) collective-permute-start(bf16[256,2,256]{0,2,1:T(8,128)(2,1)S(1)} %pad_maximum_fusion), channel_id=1, source_target_pairs={{0,16},{8,24},{16,32},{24,40},{32,48},{40,56},{48,64},{56,72},{64,... | collective-permute-start | bytes 786440 | tf_op jit(solution)/shard_map/ppermute | solution.py:20
  91.3 12.9 %collective-permute-start.1 = (bf16[256,2,256]{0,2,1:T(8,128)(2,1)S(1)}, bf16[256,2,256]{0,2,1:T(8,128)(2,1)}, u32[]{:S(2)}, u32[]{:S(2)}) collective-permute-start(bf16[256,2,256]{0,2,1:T(8,128)(2,1)S(1)} %pad_maximum_fusion), channel_id=1, source_target_pairs={{0,8},{8,16},{16,24},{24,32},{32,40},{40,48},{48,56},{56,64},{64,7... | collective-permute-start | bytes 786440 | tf_op jit(solution)/shard_map/ppermute | solution.py:20
  95.8 11.9 %collective-permute-start.2 = (bf16[256,2,256]{0,2,1:T(8,128)(2,1)S(1)}, bf16[256,2,256]{0,2,1:T(8,128)(2,1)}, u32[]{:S(2)}, u32[]{:S(2)}) collective-permute-start(bf16[256,2,256]{0,2,1:T(8,128)(2,1)S(1)} %pad_maximum_fusion), channel_id=1, source_target_pairs={{8,0},{16,8},{24,16},{32,24},{40,32},{48,40},{56,48},{64,56},{72,6... | collective-permute-start | bytes 786440 | tf_op jit(solution)/shard_map/ppermute | solution.py:20
  97.8 16.8 %collective-permute-start.3 = (bf16[256,2,256]{0,2,1:T(8,128)(2,1)S(1)}, bf16[256,2,256]{0,2,1:T(8,128)(2,1)S(1)}, u32[]{:S(2)}, u32[]{:S(2)}) collective-permute-start(bf16[256,2,256]{0,2,1:T(8,128)(2,1)S(1)} %pad_maximum_fusion), channel_id=1, source_target_pairs={{16,0},{24,8},{32,16},{40,24},{48,32},{56,40},{64,48},{72,56},{80,... | collective-permute-start | bytes 786440 | tf_op jit(solution)/shard_map/ppermute | solution.py:20
  123.6 26.6 %copy-start.3 = (f32[400]{0:T(512)S(1)}, f32[400]{0:T(512)}, u32[]{:S(2)}) copy-start(f32[400]{0:T(512)} %param.14) | copy-start | bytes 4804

commit v17 on v16

--- a/solution.py
+++ b/solution.py
@@ -16,7 +16,7 @@
 
 def passed_along(x, axis, by):
     size = lax.axis_size(axis)
-    pairs = [(i, i + by) for i in range(size) if 0 <= i + by < size]
+    pairs = [(i, (i + by) % size) for i in range(size)]
     return lax.ppermute(x, axis, pairs)
 
 

time: 153 us -> 154 us (level)
  the two profiles are of different devices: /device:TPU:15 before, /device:TPU:16 now
where the time goes in v17:
time: 154 us
  Pallas kernels  107 us (69%)
  starting transfers between devices  15.9 us (10%)
  matrix products  14.1 us (9%)
  other arithmetic  8.39 us (5%)
  local copies, waits for them, and re-layouts  6.46 us (4%)
    pallas_call x1, Pallas kernels, gather_seq(): pl.pallas_call(gather_kernel, out_shape=jax.ShapeDtypeStruct((rings, slab...  70.6 us
    pallas_call x1, Pallas kernels, scatter_chips(): pl.pallas_call(scatter_kernel, out_shape=jax.ShapeDtypeStruct(block, jnp....  28.1 us
    ppermute x4, starting transfers between devices, passed_along(): return lax.ppermute(x, axis, pairs)  15.9 us
    pallas_call x1, Pallas kernels, exchange(): pl.pallas_call(functools.partial(exchange_kernel, axis, offsets), out_sha...  8.79 us
    dot_general x1, matrix products, shards(): jnp.einsum('tkh,ycdkh->cydt', widened_context, by_owner, preferred_elemen...  6.02 us
    unnamed x19, local copies, waits for them, and re-layouts  6 us
    dot_general x1, matrix products, shards(): jnp.einsum('td,dch->tch', normed, gathered[:, :3], preferred_element_type...  5.33 us
  transfers between devices with their start and end apart: 4, of which 2 were waited for; matrix products, arithmetic and copies ran while one was open for 4% of the time, Pallas kernels for 0%

profile of v17, /device:TPU:16, one launch (start us, length us, event | category | flops | bytes accessed | tf_op | source)
XLA Modules:
  0.0 153.7 jit_solution(3109977159028827386)
XLA Ops:
  0.0 0.0 copy-start
  0.0 3.0 %copy.18 = bf16[256,3200]{0,1:T(8,128)(2,1)S(1)} copy(bf16[256,3200]{1,0:T(8,128)(2,1)} %param.8) | data formatting | bytes 3276800 | tf_op args[0]
  3.0 0.5 multiply_reduce_fusion
  3.5 0.0 copy-done
  3.6 0.0 copy-done.2
  3.6 0.8 pad_maximum_fusion.1.x_ref
  4.4 0.0 copy-start.6
  4.4 70.6 %shard_map.82 = bf16[8,8,50,4,256]{4,3,2,1,0:T(4,128)(2,1)} custom-call(bf16[50,4,256]{2,1,0:T(4,128)(2,1)} %pad_maximum_fusion.1.x_ref), custom_call_target="tpu_custom_call" | custom-call | tf_op jit(solution)/shard_map/pallas_call | solution.py:149
  75.0 0.0 copy-done.6
  75.0 0.0 copy-start.4
  75.0 5.3 %fusion.3 = f32[256,3,256]{0,2,1:T(8,128)S(1)} fusion(bf16[3200,3,256]{2,1,0:T(4,128)(2,1)} %bitcast.44, f32[3200]{0:T(1024)S(1)} %copy-done.6, f32[256]{0:T(256)S(1)} %add_rsqrt_fusion, bf16[256,3200]{0,1:T(8,128)(2,1)S(1)} %copy.18), kind=kOutput, calls=%fused_computation.3 | convolution fusion | flops 1261568000 | bytes 7353856 | tf_op jit(solution)/shard_map/td,dch->tch/dot_general | solution.py:323
  80.3 0.0 copy-start.1
  80.3 0.0 copy-start.5
  80.3 0.1 multiply_reduce_fusion.2
  80.4 0.6 pad_maximum_fusion.2.x_ref
  81.0 8.8 %shard_map.83 = f32[8,2,256]{2,1,0:T(2,128)} custom-call(f32[2,256]{1,0:T(2,128)} %pad_maximum_fusion.2.x_ref), custom_call_target="tpu_custom_call" | custom-call | tf_op jit(solution)/shard_map/pallas_call | solution.py:287
  89.8 0.7 reduce_sum.57
  90.6 0.0 copy-done.4
  90.6 0.1 fusion.50
  90.7 3.2 %collective-permute-start = (bf16[256,2,256]{0,2,1:T(8,128)(2,1)S(1)}, bf16[256,2,256]{0,2,1:T(8,128)(2,1)}, u32[]{:S(2)}, u32[]{:S(2)}) collective-permute-start(bf16[256,2,256]{0,2,1:T(8,128)(2,1)S(1)} %pad_maximum_fusion), channel_id=1, source_target_pairs={{0,16},{8,24},{16,32},{24,40},{32,48},{40,56},{48,64},{56,72},{64,... | collective-permute-start | bytes 786440 | tf_op jit(solution)/shard_map/ppermute | solution.py:20
  94.0 3.1 %collective-permute-start.1 = (bf16[256,2,256]{0,2,1:T(8,128)(2,1)S(1)}, bf16[256,2,256]{0,2,1:T(8,128)(2,1)}, u32[]{:S(2)}, u32[]{:S(2)}) collective-permute-start(bf16[256,2,256]{0,2,1:T(8,128)(2,1)S(1)} %pad_maximum_fusion), channel_id=1, source_target_pairs={{0,8},{8,16},{16,24},{24,32},{32,40},{40,48},{48,56},{56,64},{64,7... | collective-permute-start | bytes 786440 | tf_op jit(solution)/shard_map/ppermute | solution.py:20
  97.0 7.0 %collective-permute-start.2 = (bf16[256,2,256]{0,2,1:T(8,128)(2,1)S(1)}, bf16[256,2,256]{0,2,1:T(8,128)(2,1)}, u32[]{:S(2)}, u32[]{:S(2)}) collective-permute-start(bf16[256,2,256]{0,2,1:T(8,128)(2,1)S(1)} %pad_maximum_fusion), channel_id=1, source_target_pairs={{0,504},{8,0},{16,8},{24,16},{32,24},{40,32},{48,40},{56,48},{64,5... | collective-permute-start | bytes 786440 | tf_op jit(solution)/shard_map/ppermute | solution.py:20
  104.0 2.6 %collective-permute-start.3 = (bf16[256,2,256]{0,2,1:T(8,128)(2,1)S(1)}, bf16[256,2,256]{0,2,1:T(8,128)(2,1)S(1)}, u32[]{:S(2)}, u32[]{:S(2)}) collective-permute-start(bf16[256,2,256]{0,2,1:T(8,128)(2,1)S(1)} %pad_maximum_fusion), channel_id=1, source_target_pairs={{0,496},{8,504},{16,0},{24,8},{32,16},{40,24},{48,32},{56,40},{64,... | collective-permute-start | bytes 786440 | tf_op jit(solution)/shard_map/ppermute | solution.py:20
  106.7 0.1 copy.23
  106.8 0.0 copy-done.1
  106.8 0.1 dynamic_slice.10
  106.9 0.1 fusion.34
  107.0 0.3 broadcast_compare_fusion
  107.2 0.0 copy-done.5
  107.2 0.1 multiply_convert_fusion.1
  107.4 2.0 %convert_element_type.43 = f32[256,3200]{0,1:T(8,128)} convert(bf16[256,3200]{0,1:T(8,128)(2,1)S(1)} %copy.18) | non-fusion elementwise | flops 819200 | bytes 4915200 | tf_op jit(solution)/shard_map/convert_element_type | solution.py:313
  109.4 0.1 pad_maximum_fusion.3
  109.4 0.5 collective-permute-done
  110.0 1.0 constant_dynamic-update-slice_fusion.4
  110.9 0.0 collective-permute-done.1
  111.0 1.0 constant_dynamic-update-slice_fusion.3
  112.0 0.0 collective-permute-done.2
  112.0 1.0 constant_dynamic-update-slice_fusion.1
  112.9 0.5 collective-permute-done.3
  113.4 0.1 fusion.49
  113.5 1.4 fusion.51
  114.9 1.4 fusion.27
  116.3 0.1 copy.25
  116.4 6.0 %fusion.16.terms_ref = bf16[2,4,400,256]{3,2,1,0:T(8,128)(2,1)} fusion(bf16[4,2,400,4,256]{4,3,2,1,0:T(4,128)(2,1)} %bitcast.45, bf16[256,1,256]{2,0,1:T(8,128)(2,1)S(1)} %copy.25, bf16[4]{0:T(256)(128)(2,1)S(1)} %pad_maximum_fusion.3), kind=kOutput, calls=%fused_computation.18 | convolution fusion | flops 1678802944 | bytes 8323080 | tf_op jit(solution)/shard_map/tkh,ycdkh->cydt/dot_general | solution.py:372
  122.4 28.1 %shard_map.84 = bf16[4,400,256]{2,1,0:T(8,128)(2,1)} custom-call(bf16[2,4,400,256]{3,2,1,0:T(8,128)(2,1)} %fusion.16.terms_ref), custom_call_target="tpu_custom_call" | custom-call | tf_op jit(solution)/shard_map/pallas_call | solution.py:221
  150.6 1.3 convert_reduce_fusion
  151.9 0.0 copy-done.3
  151.9 1.8 %fusion.31 = bf16[256,400]{0,1:T(8,128)(2,1)} fusion(f32[400,256]{1,0:T(8,128)S(1)} %convert_reduce_fusion, f32[256,3200]{0,1:T(8,128)} %convert_element_type.43, s32[]{:T(128)S(6)} %select_n.16, f32[400]{0:T(512)S(1)} %copy-done.3), kind=kLoop, calls=%fused_computation.28 | loop fusion | flops 307200 | bytes 1025604 | tf_op jit(solution)/shard_map/convert_element_type | solution.py:380
  (12 shorter events, 0.2 us)
Async XLA Ops:
  0.0 3.5 %copy-start = (bf16[50,3,256]{2,0,1:T(8,128)(2,1)S(1)}, bf16[50,3,256]{2,0,1:T(8,128)(2,1)}, u32[]{:S(2)}) copy-start(bf16[50,3,256]{2,0,1:T(8,128)(2,1)} %param.10) | copy-start | bytes 230404
  0.0 3.6 %copy-start.2 = (bf16[256,50]{0,1:T(8,128)(2,1)S(1)}, bf16[256,50]{0,1:T(8,128)(2,1)}, u32[]{:S(2)}) copy-start(bf16[256,50]{0,1:T(8,128)(2,1)} %param.13) | copy-start | bytes 76804
  4.4 70.6 %copy-start.6 = (f32[3200]{0:T(1024)S(1)}, f32[3200]{0:T(1024)}, u32[]{:S(2)}) copy-start(f32[3200]{0:T(1024)} %param.9) | copy-start | bytes 38404
  75.0 15.6 %copy-start.4 = (f32[256]{0:T(256)S(1)}, f32[256]{0:T(256)}, u32[]{:S(2)}) copy-start(f32[256]{0:T(256)} %param.12) | copy-start | bytes 3076
  80.3 26.5 %copy-start.1 = (s32[16384]{0:T(1024)S(1)}, s32[16384]{0:T(1024)}, u32[]{:S(2)}) copy-start(s32[16384]{0:T(1024)} %param.15) | copy-start | bytes 196612
  80.3 26.9 %copy-start.5 = (f32[256]{0:T(256)S(1)}, f32[256]{0:T(256)}, u32[]{:S(2)}) copy-start(f32[256]{0:T(256)} %param.11) | copy-start | bytes 3076
  90.7 19.3 %collective-permute-start = (bf16[256,2,256]{0,2,1:T(8,128)(2,1)S(1)}, bf16[256,2,256]{0,2,1:T(8,128)(2,1)}, u32[]{:S(2)}, u32[]{:S(2)}) collective-permute-start(bf16[256,2,256]{0,2,1:T(8,128)(2,1)S(1)} %pad_maximum_fusion), channel_id=1, source_target_pairs={{0,16},{8,24},{16,32},{24,40},{32,48},{40,56},{48,64},{56,72},{64,... | collective-permute-start | bytes 786440 | tf_op jit(solution)/shard_map/ppermute | solution.py:20
  94.0 17.0 %collective-permute-start.1 = (bf16[256,2,256]{0,2,1:T(8,128)(2,1)S(1)}, bf16[256,2,256]{0,2,1:T(8,128)(2,1)}, u32[]{:S(2)}, u32[]{:S(2)}) collective-permute-start(bf16[256,2,256]{0,2,1:T(8,128)(2,1)S(1)} %pad_maximum_fusion), channel_id=1, source_target_pairs={{0,8},{8,16},{16,24},{24,32},{32,40},{40,48},{48,56},{56,64},{64,7... | collective-permute-start | bytes 786440 | tf_op jit(solution)/shard_map/ppermute | solution.py:20
  97.0 14.9 %collective-permute-start.2 = (bf16[256,2,256]{0,2,1:T(8,128)(2,1)S(1)}, bf16[256,2,256]{0,2,1:T(8,128)(2,1)}, u32[]{:S(2)}, u32[]{:S(2)}) collective-permute-start(bf16[256,2,256]{0,2,1:T(8,128)(2,1)S(1)} %pad_maximum_fusion), channel_id=1, source_target_pairs={{0,504},{8,0},{16,8},{24,16},{32,24},{40,32},{48,40},{56,48},{64,5... | collective-permute-start | bytes 786440 | tf_op jit(solution)/shard_map/ppermute | solution.py:20
  104.0 9.4 %collective-permute-start.3 = (bf16[256,2,256]{0,2,1:T(8,128)(2,1)S(1)}, bf16[256,2,256]{0,2,1:T(8,128)(2,1)S(1)}, u32[]{:S(2)}, u32[]{:S(2)}) collective-permute-start(bf16[256,2,256]{0,2,1:T(8,128)(2,1)S(1)} %pad_maximum_fusion), channel_id=1, source_target_pairs={{0,496},{8,504},{16,0},{24,8},{32,16},{40,24},{48,32},{56,40},{64,... | collective-permute-start | bytes 786440 | tf_op jit(solution)/shard_map/ppermute | solution.py:20
  122.4 29.4 %copy-start.3 = (f32[400]{0:T(512)S(1)}, f32[400]{0:T(512)}, u32[]{:S(2)}) copy-start(f32[400]{0:T(512)} %param.14) | copy-start | bytes 4804

commit v18 on v16

--- a/solution.py
+++ b/solution.py
@@ -170,49 +170,57 @@
     mesh_id = pl.DeviceIdType.MESH
     core = tp % 2
     here = tp // 2
-    owners = [(here + k) % chips for k in range(1, chips)]
-    targets = [(seq, tp + 1 - 2 * core)] + [(seq, owner * 2 + core) for owner in owners]
+    partner = (seq, tp + 1 - 2 * core)
+    order = [(here + k) % chips for k in (2, 1, 3, 0)]
+
+    def device(chip):
+        return (seq, chip * 2 + core)
 
     barrier = pltpu.get_barrier_semaphore()
-    for target in targets:
+    for target in [partner] + [device(owner) for owner in order[:3]]:
         pl.semaphore_signal(barrier, inc=1, device_id=target, device_id_type=mesh_id)
-    pl.semaphore_wait(barrier, len(targets))
-
-    keep = pltpu.make_async_copy(terms_ref.at[core], mine, local_sems.at[0])
-    keep.start()
-    swap = pltpu.make_async_remote_copy(
-        src_ref=terms_ref.at[1 - core],
-        dst_ref=incoming,
-        send_sem=send_sem.at[0],
-        recv_sem=recv_sem.at[0],
-        device_id=targets[0],
-        device_id_type=mesh_id,
-    )
-    swap.start()
-    keep.wait()
-    swap.wait_send()
-    swap.wait_recv()
-    total = mine[...].astype(jnp.float32) + incoming[...].astype(jnp.float32)
-    sums[...] = total.astype(sums.dtype)
-
-    local = pltpu.make_async_copy(sums.at[here], out_ref.at[here], local_sems.at[1])
-    local.start()
-    copies = []
-    for k, owner in enumerate(owners):
-        copy = pltpu.make_async_remote_copy(
-            src_ref=sums.at[owner],
-            dst_ref=out_ref.at[here],
-            send_sem=send_sem.at[k + 1],
-            recv_sem=recv_sem.at[k + 1],
-            device_id=targets[k + 1],
+    pl.semaphore_wait(barrier, 4)
+
+    arrivals = []
+    for k, owner in enumerate(order):
+        keep = pltpu.make_async_copy(terms_ref.at[core, owner], mine.at[owner], local_sems.at[k])
+        swap = pltpu.make_async_remote_copy(
+            src_ref=terms_ref.at[1 - core, owner],
+            dst_ref=incoming.at[owner],
+            send_sem=send_sem.at[k],
+            recv_sem=recv_sem.at[k],
+            device_id=partner,
             device_id_type=mesh_id,
         )
+        keep.start()
+        swap.start()
+        arrivals.append((keep, swap))
+
+    outgoing = []
+    for k, owner in enumerate(order):
+        keep, swap = arrivals[k]
+        keep.wait()
+        swap.wait_send()
+        swap.wait_recv()
+        total = mine[owner].astype(jnp.float32) + incoming[owner].astype(jnp.float32)
+        sums[owner] = total.astype(sums.dtype)
+        if k < 3:
+            copy = pltpu.make_async_remote_copy(
+                src_ref=sums.at[owner],
+                dst_ref=out_ref.at[here],
+                send_sem=send_sem.at[4 + k],
+                recv_sem=recv_sem.at[4 + k],
+                device_id=device(owner),
+                device_id_type=mesh_id,
+            )
+        else:
+            copy = pltpu.make_async_copy(sums.at[owner], out_ref.at[here], local_sems.at[4])
         copy.start()
-        copies.append(copy)
-    for copy in copies:
+        outgoing.append(copy)
+    for copy in outgoing[:3]:
         copy.wait_send()
         copy.wait_recv()
-    local.wait()
+    outgoing[3].wait()
 
 
 def scatter_chips(terms):
@@ -227,9 +235,9 @@
             pltpu.VMEM(block, terms.dtype),
             pltpu.VMEM(block, terms.dtype),
             pltpu.VMEM(block, jnp.bfloat16),
-            pltpu.SemaphoreType.DMA((chips,)),
-            pltpu.SemaphoreType.DMA((chips,)),
-            pltpu.SemaphoreType.DMA((2,)),
+            pltpu.SemaphoreType.DMA((7,)),
+            pltpu.SemaphoreType.DMA((7,)),
+            pltpu.SemaphoreType.DMA((5,)),
         ],
         compiler_params=pltpu.CompilerParams(collective_id=1, has_side_effects=True),
     )(terms)

time: 153 us -> 152 us (level)
  no operation moved by 1% of the time
where the time goes in v18:
time: 152 us; the launch traced here: 151 us
  Pallas kernels  101 us (66%)
  matrix products  14.1 us (9%)
  starting transfers between devices  12 us (8%)
  other arithmetic  8.39 us (6%)
  waiting for transfers between devices  8.39 us (6%)
  local copies, waits for them, and re-layouts  6.46 us (4%)
    pallas_call x1, Pallas kernels, gather_seq(): pl.pallas_call(gather_kernel, out_shape=jax.ShapeDtypeStruct((rings, slab...  62.6 us
    pallas_call x1, Pallas kernels, scatter_chips(): pl.pallas_call(scatter_kernel, out_shape=jax.ShapeDtypeStruct(block, jnp....  24.4 us
    pallas_call x1, Pallas kernels, exchange(): pl.pallas_call(functools.partial(exchange_kernel, axis, offsets), out_sha...  14.5 us
    ppermute x4, starting transfers between devices, passed_along(): return lax.ppermute(x, axis, pairs)  12 us
    ppermute x4, waiting for transfers between devices, passed_along(): return lax.ppermute(x, axis, pairs)  8.39 us
    dot_general x1, matrix products, shards(): jnp.einsum('tkh,ycdkh->cydt', widened_context, by_owner, preferred_elemen...  6.02 us
    unnamed x19, local copies, waits for them, and re-layouts  6 us
    dot_general x1, matrix products, shards(): jnp.einsum('td,dch->tch', normed, gathered[:, :3], preferred_element_type...  5.33 us
  transfers between devices with their start and end apart: 4, of which 2 were waited for; matrix products, arithmetic and copies ran while one was open for 4% of the time, Pallas kernels for 0%

profile of v18, /device:TPU:15, one launch (start us, length us, event | category | flops | bytes accessed | tf_op | source)
XLA Modules:
  0.0 151.1 jit_solution(14893995822047917287)
XLA Ops:
  0.0 0.0 copy-start
  0.0 0.0 copy-start.2
  0.0 3.0 %copy.18 = bf16[256,3200]{0,1:T(8,128)(2,1)S(1)} copy(bf16[256,3200]{1,0:T(8,128)(2,1)} %param.8) | data formatting | bytes 3276800 | tf_op args[0]
  3.0 0.5 multiply_reduce_fusion
  3.5 0.0 copy-done
  3.6 0.0 copy-done.2
  3.6 0.8 pad_maximum_fusion.1.x_ref
  4.4 62.6 %shard_map.82 = bf16[8,8,50,4,256]{4,3,2,1,0:T(4,128)(2,1)} custom-call(bf16[50,4,256]{2,1,0:T(4,128)(2,1)} %pad_maximum_fusion.1.x_ref), custom_call_target="tpu_custom_call" | custom-call | tf_op jit(solution)/shard_map/pallas_call | solution.py:149
  66.9 0.0 copy-done.6
  67.0 0.0 copy-start.4
  67.0 5.3 %fusion.3 = f32[256,3,256]{0,2,1:T(8,128)S(1)} fusion(bf16[3200,3,256]{2,1,0:T(4,128)(2,1)} %bitcast.44, f32[3200]{0:T(1024)S(1)} %copy-done.6, f32[256]{0:T(256)S(1)} %add_rsqrt_fusion, bf16[256,3200]{0,1:T(8,128)(2,1)S(1)} %copy.18), kind=kOutput, calls=%fused_computation.3 | convolution fusion | flops 1261568000 | bytes 7353856 | tf_op jit(solution)/shard_map/td,dch->tch/dot_general | solution.py:331
  72.3 0.0 copy-start.1
  72.3 0.0 copy-start.5
  72.3 0.1 multiply_reduce_fusion.2
  72.4 0.6 pad_maximum_fusion.2.x_ref
  73.0 14.5 %shard_map.83 = f32[8,2,256]{2,1,0:T(2,128)} custom-call(f32[2,256]{1,0:T(2,128)} %pad_maximum_fusion.2.x_ref), custom_call_target="tpu_custom_call" | custom-call | tf_op jit(solution)/shard_map/pallas_call | solution.py:295
  87.5 0.7 reduce_sum.57
  88.2 0.0 copy-done.4
  88.3 0.1 fusion.50
  88.4 2.9 %collective-permute-start = (bf16[256,2,256]{0,2,1:T(8,128)(2,1)S(1)}, bf16[256,2,256]{0,2,1:T(8,128)(2,1)}, u32[]{:S(2)}, u32[]{:S(2)}) collective-permute-start(bf16[256,2,256]{0,2,1:T(8,128)(2,1)S(1)} %pad_maximum_fusion), channel_id=1, source_target_pairs={{0,16},{8,24},{16,32},{24,40},{32,48},{40,56},{48,64},{56,72},{64,... | collective-permute-start | bytes 786440 | tf_op jit(solution)/shard_map/ppermute | solution.py:20
  91.3 4.5 %collective-permute-start.1 = (bf16[256,2,256]{0,2,1:T(8,128)(2,1)S(1)}, bf16[256,2,256]{0,2,1:T(8,128)(2,1)}, u32[]{:S(2)}, u32[]{:S(2)}) collective-permute-start(bf16[256,2,256]{0,2,1:T(8,128)(2,1)S(1)} %pad_maximum_fusion), channel_id=1, source_target_pairs={{0,8},{8,16},{16,24},{24,32},{32,40},{40,48},{48,56},{56,64},{64,7... | collective-permute-start | bytes 786440 | tf_op jit(solution)/shard_map/ppermute | solution.py:20
  95.8 1.9 %collective-permute-start.2 = (bf16[256,2,256]{0,2,1:T(8,128)(2,1)S(1)}, bf16[256,2,256]{0,2,1:T(8,128)(2,1)}, u32[]{:S(2)}, u32[]{:S(2)}) collective-permute-start(bf16[256,2,256]{0,2,1:T(8,128)(2,1)S(1)} %pad_maximum_fusion), channel_id=1, source_target_pairs={{8,0},{16,8},{24,16},{32,24},{40,32},{48,40},{56,48},{64,56},{72,6... | collective-permute-start | bytes 786440 | tf_op jit(solution)/shard_map/ppermute | solution.py:20
  97.8 2.7 %collective-permute-start.3 = (bf16[256,2,256]{0,2,1:T(8,128)(2,1)S(1)}, bf16[256,2,256]{0,2,1:T(8,128)(2,1)S(1)}, u32[]{:S(2)}, u32[]{:S(2)}) collective-permute-start(bf16[256,2,256]{0,2,1:T(8,128)(2,1)S(1)} %pad_maximum_fusion), channel_id=1, source_target_pairs={{16,0},{24,8},{32,16},{40,24},{48,32},{56,40},{64,48},{72,56},{80,... | collective-permute-start | bytes 786440 | tf_op jit(solution)/shard_map/ppermute | solution.py:20
  100.5 0.1 copy.23
  100.6 0.0 copy-done.1
  100.6 0.1 dynamic_slice.10
  100.7 0.1 fusion.34
  100.8 0.3 broadcast_compare_fusion
  101.0 0.0 copy-done.5
  101.0 0.1 multiply_convert_fusion.1
  101.2 2.0 %convert_element_type.43 = f32[256,3200]{0,1:T(8,128)} convert(bf16[256,3200]{0,1:T(8,128)(2,1)S(1)} %copy.18) | non-fusion elementwise | flops 819200 | bytes 4915200 | tf_op jit(solution)/shard_map/convert_element_type | solution.py:321
  103.2 0.1 pad_maximum_fusion.3
  103.2 0.0 collective-permute-done
  103.2 1.0 constant_dynamic-update-slice_fusion.4
  104.2 0.0 collective-permute-done.1
  104.2 1.0 constant_dynamic-update-slice_fusion.3
  105.2 2.5 %collective-permute-done.2 = bf16[256,2,256]{0,2,1:T(8,128)(2,1)} collective-permute-done((bf16[256,2,256]{0,2,1:T(8,128)(2,1)S(1)}, bf16[256,2,256]{0,2,1:T(8,128)(2,1)}, u32[]{:S(2)}, u32[]{:S(2)}) %collective-permute-start.2) | collective-permute-done | bytes 262176 | tf_op jit(solution)/shard_map/ppermute | solution.py:20
  107.7 1.0 constant_dynamic-update-slice_fusion.1
  108.7 5.9 %collective-permute-done.3 = bf16[256,2,256]{0,2,1:T(8,128)(2,1)S(1)} collective-permute-done((bf16[256,2,256]{0,2,1:T(8,128)(2,1)S(1)}, bf16[256,2,256]{0,2,1:T(8,128)(2,1)S(1)}, u32[]{:S(2)}, u32[]{:S(2)}) %collective-permute-start.3) | collective-permute-done | bytes 262176 | tf_op jit(solution)/shard_map/ppermute | solution.py:20
  114.6 0.1 fusion.49
  114.7 1.4 fusion.51
  116.1 1.4 fusion.27
  117.5 0.1 copy.25
  117.6 6.0 %fusion.16.terms_ref = bf16[2,4,400,256]{3,2,1,0:T(8,128)(2,1)} fusion(bf16[4,2,400,4,256]{4,3,2,1,0:T(4,128)(2,1)} %bitcast.45, bf16[256,1,256]{2,0,1:T(8,128)(2,1)S(1)} %copy.25, bf16[4]{0:T(256)(128)(2,1)S(1)} %pad_maximum_fusion.3), kind=kOutput, calls=%fused_computation.18 | convolution fusion | flops 1678802944 | bytes 8323080 | tf_op jit(solution)/shard_map/tkh,ycdkh->cydt/dot_general | solution.py:380
  123.6 24.4 %shard_map.84 = bf16[4,400,256]{2,1,0:T(8,128)(2,1)} custom-call(bf16[2,4,400,256]{3,2,1,0:T(8,128)(2,1)} %fusion.16.terms_ref), custom_call_target="tpu_custom_call" | custom-call | tf_op jit(solution)/shard_map/pallas_call | solution.py:229
  148.0 1.3 convert_reduce_fusion
  149.3 0.0 copy-done.3
  149.3 1.8 %fusion.31 = bf16[256,400]{0,1:T(8,128)(2,1)} fusion(f32[400,256]{1,0:T(8,128)S(1)} %convert_reduce_fusion, f32[256,3200]{0,1:T(8,128)} %convert_element_type.43, s32[]{:T(128)S(6)} %select_n.16, f32[400]{0:T(512)S(1)} %copy-done.3), kind=kLoop, calls=%fused_computation.28 | loop fusion | flops 307200 | bytes 1025604 | tf_op jit(solution)/shard_map/convert_element_type | solution.py:388
  (12 shorter events, 0.2 us)
Async XLA Ops:
  0.0 3.5 %copy-start = (bf16[50,3,256]{2,0,1:T(8,128)(2,1)S(1)}, bf16[50,3,256]{2,0,1:T(8,128)(2,1)}, u32[]{:S(2)}) copy-start(bf16[50,3,256]{2,0,1:T(8,128)(2,1)} %param.10) | copy-start | bytes 230404
  0.0 3.6 %copy-start.2 = (bf16[256,50]{0,1:T(8,128)(2,1)S(1)}, bf16[256,50]{0,1:T(8,128)(2,1)}, u32[]{:S(2)}) copy-start(bf16[256,50]{0,1:T(8,128)(2,1)} %param.13) | copy-start | bytes 76804
  4.4 62.6 %copy-start.6 = (f32[3200]{0:T(1024)S(1)}, f32[3200]{0:T(1024)}, u32[]{:S(2)}) copy-start(f32[3200]{0:T(1024)} %param.9) | copy-start | bytes 38404
  67.0 21.3 %copy-start.4 = (f32[256]{0:T(256)S(1)}, f32[256]{0:T(256)}, u32[]{:S(2)}) copy-start(f32[256]{0:T(256)} %param.12) | copy-start | bytes 3076
  72.3 28.3 %copy-start.1 = (s32[16384]{0:T(1024)S(1)}, s32[16384]{0:T(1024)}, u32[]{:S(2)}) copy-start(s32[16384]{0:T(1024)} %param.15) | copy-start | bytes 196612
  72.3 28.7 %copy-start.5 = (f32[256]{0:T(256)S(1)}, f32[256]{0:T(256)}, u32[]{:S(2)}) copy-start(f32[256]{0:T(256)} %param.11) | copy-start | bytes 3076
  88.4 14.8 %collective-permute-start = (bf16[256,2,256]{0,2,1:T(8,128)(2,1)S(1)}, bf16[256,2,256]{0,2,1:T(8,128)(2,1)}, u32[]{:S(2)}, u32[]{:S(2)}) collective-permute-start(bf16[256,2,256]{0,2,1:T(8,128)(2,1)S(1)} %pad_maximum_fusion), channel_id=1, source_target_pairs={{0,16},{8,24},{16,32},{24,40},{32,48},{40,56},{48,64},{56,72},{64,... | collective-permute-start | bytes 786440 | tf_op jit(solution)/shard_map/ppermute | solution.py:20
  91.3 12.9 %collective-permute-start.1 = (bf16[256,2,256]{0,2,1:T(8,128)(2,1)S(1)}, bf16[256,2,256]{0,2,1:T(8,128)(2,1)}, u32[]{:S(2)}, u32[]{:S(2)}) collective-permute-start(bf16[256,2,256]{0,2,1:T(8,128)(2,1)S(1)} %pad_maximum_fusion), channel_id=1, source_target_pairs={{0,8},{8,16},{16,24},{24,32},{32,40},{40,48},{48,56},{56,64},{64,7... | collective-permute-start | bytes 786440 | tf_op jit(solution)/shard_map/ppermute | solution.py:20
  95.8 11.9 %collective-permute-start.2 = (bf16[256,2,256]{0,2,1:T(8,128)(2,1)S(1)}, bf16[256,2,256]{0,2,1:T(8,128)(2,1)}, u32[]{:S(2)}, u32[]{:S(2)}) collective-permute-start(bf16[256,2,256]{0,2,1:T(8,128)(2,1)S(1)} %pad_maximum_fusion), channel_id=1, source_target_pairs={{8,0},{16,8},{24,16},{32,24},{40,32},{48,40},{56,48},{64,56},{72,6... | collective-permute-start | bytes 786440 | tf_op jit(solution)/shard_map/ppermute | solution.py:20
  97.8 16.8 %collective-permute-start.3 = (bf16[256,2,256]{0,2,1:T(8,128)(2,1)S(1)}, bf16[256,2,256]{0,2,1:T(8,128)(2,1)S(1)}, u32[]{:S(2)}, u32[]{:S(2)}) collective-permute-start(bf16[256,2,256]{0,2,1:T(8,128)(2,1)S(1)} %pad_maximum_fusion), channel_id=1, source_target_pairs={{16,0},{24,8},{32,16},{40,24},{48,32},{56,40},{64,48},{72,56},{80,... | collective-permute-start | bytes 786440 | tf_op jit(solution)/shard_map/ppermute | solution.py:20
  123.6 25.7 %copy-start.3 = (f32[400]{0:T(512)S(1)}, f32[400]{0:T(512)}, u32[]{:S(2)}) copy-start(f32[400]{0:T(512)} %param.14) | copy-start | bytes 4804

commit v19 on v18

--- a/solution.py
+++ b/solution.py
@@ -20,7 +20,10 @@
     return lax.ppermute(x, axis, pairs)
 
 
-def gather_kernel(x_ref, out_ref, pair_sems, row_sems, lane_sems, ring_sems, cross_sems, local_sem):
+def gather_kernel(
+    x_ref, tokens_ref, gain_ref, out_ref, normed_ref,
+    pair_sems, row_sems, lane_sems, ring_sems, cross_sems, local_sem,
+):
     rings, slab = out_ref.shape[0], out_ref.shape[1]
     pair = 2
     row = slab // pair
@@ -108,6 +111,12 @@
     ]
     for copy in cross:
         copy.start()
+    source = tokens_ref[...].astype(jnp.float32)
+    power = jnp.mean(source * source, axis=-1, keepdims=True)
+    scaled = source * lax.rsqrt(power + eps) * gain_ref[...]
+    normed_ref[...] = jnp.transpose(scaled.astype(jnp.bfloat16).astype(jnp.float32)).astype(
+        normed_ref.dtype
+    )
     onward = None
     for t in range(rings // 2):
         last = t == rings // 2 - 1
@@ -145,12 +154,22 @@
     finish(onward)
 
 
-def gather_seq(block, rings, slab):
+def gather_seq(block, tokens, gain, rings, slab):
     return pl.pallas_call(
         gather_kernel,
-        out_shape=jax.ShapeDtypeStruct((rings, slab) + block.shape, block.dtype),
-        in_specs=[pl.BlockSpec(memory_space=pl.ANY)],
-        out_specs=pl.BlockSpec(memory_space=pl.ANY),
+        out_shape=(
+            jax.ShapeDtypeStruct((rings, slab) + block.shape, block.dtype),
+            jax.ShapeDtypeStruct(tokens.shape[::-1], jnp.bfloat16),
+        ),
+        in_specs=[
+            pl.BlockSpec(memory_space=pl.ANY),
+            pl.BlockSpec(memory_space=pltpu.VMEM),
+            pl.BlockSpec(memory_space=pltpu.VMEM),
+        ],
+        out_specs=(
+            pl.BlockSpec(memory_space=pl.ANY),
+            pl.BlockSpec(memory_space=pltpu.VMEM),
+        ),
         scratch_shapes=[
             pltpu.SemaphoreType.DMA((2,)),
             pltpu.SemaphoreType.DMA((2, slab // 2 - 1)),
@@ -160,7 +179,7 @@
             pltpu.SemaphoreType.DMA(()),
         ],
         compiler_params=pltpu.CompilerParams(collective_id=0, has_side_effects=True),
-    )(block)
+    )(block, tokens, gain.reshape(1, -1))
 
 
 def scatter_kernel(terms_ref, out_ref, mine, incoming, sums, send_sem, recv_sem, local_sems):
@@ -319,18 +338,18 @@
 def shards(tokens, norm_gain, qkv_weight, q_gain, k_gain, out_weight, layer_scale, segment_ids):
     count = tokens.shape[0]
     source = tokens.astype(jnp.float32)
-    normed = (
-        source * lax.rsqrt(jnp.mean(source * source, axis=-1, keepdims=True) + eps) * norm_gain
-    ).astype(jnp.bfloat16)
     local_width = qkv_weight.shape[2]
     heads = local_width // HEAD_DIM
     stacked = jnp.concatenate([qkv_weight, jnp.transpose(out_weight)[:, None, :]], axis=1)
     rows, kinds, width = stacked.shape
     slab = 8
-    gathered = gather_seq(stacked, lax.axis_size("seq") // slab, slab).reshape(-1, kinds, width)
+    gathered, normed_t = gather_seq(
+        stacked, tokens, norm_gain, lax.axis_size("seq") // slab, slab
+    )
+    gathered = gathered.reshape(-1, kinds, width)
     joined = jnp.einsum(
-        "td,dch->tch",
-        normed,
+        "dt,dch->tch",
+        normed_t,
         gathered[:, :3],
         preferred_element_type=jnp.float32,
     )

time: 152 us -> 153 us (level)
  Pallas kernels: 101 us -> 105 us
  waiting for transfers between devices: 8.39 us -> 11.9 us
  other arithmetic: 8.39 us -> 4.92 us
  local copies, waits for them, and re-layouts: 6.46 us -> 4.8 us
    unnamed x19 -> x13, local copies, waits for them, and re-layouts: 6 us -> 1.14 us
    ppermute x4, waiting for transfers between devices: 8.39 us -> 11.9 us  [passed_along(): return lax.ppermute(x, axis, pairs)]
    pallas_call x1, Pallas kernels: 62.6 us -> 65.7 us  [gather_seq(): pl.pallas_call(gather_kernel, out_shape=(jax.ShapeDtypeStruct((rings, sla...]
    convert_element_type x1 -> x0, other arithmetic: 2 us -> none  [shards(): source = tokens.astype(jnp.float32)]
  transfers between devices with their start and end apart: 4 -> 4, of which waited for: 2 -> 2; matrix products, arithmetic and copies ran while one was open for 4% -> 1% of each run, Pallas kernels for 0% -> 0%
where the time goes in v19:
time: 153 us; the launch traced here: 152 us
  Pallas kernels  105 us (69%)
  matrix products  14.3 us (9%)
  waiting for transfers between devices  11.9 us (8%)
  starting transfers between devices  11.6 us (8%)
  other arithmetic  4.92 us (3%)
  local copies, waits for them, and re-layouts  4.8 us (3%)
    pallas_call x1, Pallas kernels, gather_seq(): pl.pallas_call(gather_kernel, out_shape=(jax.ShapeDtypeStruct((rings, sla...  65.7 us
    pallas_call x1, Pallas kernels, scatter_chips(): pl.pallas_call(scatter_kernel, out_shape=jax.ShapeDtypeStruct(block, jnp....  24.4 us
    pallas_call x1, Pallas kernels, exchange(): pl.pallas_call(functools.partial(exchange_kernel, axis, offsets), out_sha...  14.4 us
    ppermute x4, waiting for transfers between devices, passed_along(): return lax.ppermute(x, axis, pairs)  11.9 us
    ppermute x4, starting transfers between devices, passed_along(): return lax.ppermute(x, axis, pairs)  11.6 us
    dot_general x1, matrix products, shards(): jnp.einsum('tkh,ycdkh->cydt', widened_context, by_owner, preferred_elemen...  6.03 us
    dot_general x1, matrix products, shards(): jnp.einsum('dt,dch->tch', normed_t, gathered[:, :3], preferred_element_ty...  5.41 us
  transfers between devices with their start and end apart: 4, of which 2 were waited for; matrix products, arithmetic and copies ran while one was open for 1% of the time, Pallas kernels for 0%

profile of v19, /device:TPU:15, one launch (start us, length us, event | category | flops | bytes accessed | tf_op | source)
XLA Modules:
  0.0 152.3 jit_solution(5314588949582516814)
XLA Ops:
  0.0 0.9 copy.18
  0.9 0.8 copy.19
  1.7 1.3 reshape.99.gain_ref
  3.0 0.8 pad_maximum_fusion.1.x_ref
  3.8 65.7 %shard_map.82 = (bf16[8,8,50,4,256]{4,3,2,1,0:T(4,128)(2,1)}, bf16[3200,256]{1,0:T(8,128)(2,1)}) custom-call(bf16[50,4,256]{2,1,0:T(4,128)(2,1)} %pad_maximum_fusion.1.x_ref, bf16[256,3200]{1,0:T(8,128)(2,1)} %tokens_ref.1, f32[1,3200]{1,0:T(1,128)} %reshape.99.gain_ref), custom_call_target="tpu_custom_call" | custom-call | tf_op jit(solution)/shard_map/pallas_call | solution.py:158
  69.6 0.0 copy-start.2
  69.6 5.4 %fusion.3 = f32[256,3,256]{0,2,1:T(8,128)S(1)} fusion(bf16[3200,3,256]{2,1,0:T(4,128)(2,1)} %bitcast.55, bf16[3200,256]{1,0:T(8,128)(2,1)} %get-tuple-element.8), kind=kOutput, calls=%fused_computation.3 | convolution fusion | flops 1258291200 | bytes 7340032 | tf_op jit(solution)/shard_map/dt,dch->tch/dot_general | solution.py:350
  75.0 0.0 copy-start
  75.0 0.0 copy-start.3
  75.0 0.1 multiply_reduce_fusion.1
  75.1 0.6 pad_maximum_fusion.2.x_ref
  75.7 14.4 %shard_map.83 = f32[8,2,256]{2,1,0:T(2,128)} custom-call(f32[2,256]{1,0:T(2,128)} %pad_maximum_fusion.2.x_ref), custom_call_target="tpu_custom_call" | custom-call | tf_op jit(solution)/shard_map/pallas_call | solution.py:314
  90.1 0.7 reduce_sum.47
  90.8 0.0 copy-done.2
  90.8 0.1 fusion.46
  91.0 2.9 %collective-permute-start = (bf16[256,2,256]{0,2,1:T(8,128)(2,1)S(1)}, bf16[256,2,256]{0,2,1:T(8,128)(2,1)S(1)}, u32[]{:S(2)}, u32[]{:S(2)}) collective-permute-start(bf16[256,2,256]{0,2,1:T(8,128)(2,1)S(1)} %pad_maximum_fusion), channel_id=1, source_target_pairs={{0,16},{8,24},{16,32},{24,40},{32,48},{40,56},{48,64},{56,72},{64,... | collective-permute-start | bytes 786440 | tf_op jit(solution)/shard_map/ppermute | solution.py:20
  93.9 4.0 %collective-permute-start.1 = (bf16[256,2,256]{0,2,1:T(8,128)(2,1)S(1)}, bf16[256,2,256]{0,2,1:T(8,128)(2,1)S(1)}, u32[]{:S(2)}, u32[]{:S(2)}) collective-permute-start(bf16[256,2,256]{0,2,1:T(8,128)(2,1)S(1)} %pad_maximum_fusion), channel_id=1, source_target_pairs={{0,8},{8,16},{16,24},{24,32},{32,40},{40,48},{48,56},{56,64},{64,7... | collective-permute-start | bytes 786440 | tf_op jit(solution)/shard_map/ppermute | solution.py:20
  98.0 1.9 %collective-permute-start.2 = (bf16[256,2,256]{0,2,1:T(8,128)(2,1)S(1)}, bf16[256,2,256]{0,2,1:T(8,128)(2,1)S(1)}, u32[]{:S(2)}, u32[]{:S(2)}) collective-permute-start(bf16[256,2,256]{0,2,1:T(8,128)(2,1)S(1)} %pad_maximum_fusion), channel_id=1, source_target_pairs={{8,0},{16,8},{24,16},{32,24},{40,32},{48,40},{56,48},{64,56},{72,6... | collective-permute-start | bytes 786440 | tf_op jit(solution)/shard_map/ppermute | solution.py:20
  99.9 2.7 %collective-permute-start.3 = (bf16[256,2,256]{0,2,1:T(8,128)(2,1)S(1)}, bf16[256,2,256]{0,2,1:T(8,128)(2,1)S(1)}, u32[]{:S(2)}, u32[]{:S(2)}) collective-permute-start(bf16[256,2,256]{0,2,1:T(8,128)(2,1)S(1)} %pad_maximum_fusion), channel_id=1, source_target_pairs={{16,0},{24,8},{32,16},{40,24},{48,32},{56,40},{64,48},{72,56},{80,... | collective-permute-start | bytes 786440 | tf_op jit(solution)/shard_map/ppermute | solution.py:20
  102.6 0.1 copy.21
  102.8 0.0 copy-done
  102.8 0.1 dynamic_slice.10
  102.8 0.1 fusion.30
  102.9 0.3 broadcast_compare_fusion
  103.2 0.0 copy-done.3
  103.2 0.1 multiply_convert_fusion
  103.3 1.1 constant_dynamic-slice_fusion
  104.4 0.1 copy.32
  104.6 0.1 pad_maximum_fusion.3
  104.7 0.0 collective-permute-done
  104.7 0.0 collective-permute-done.1
  104.8 5.0 %collective-permute-done.2 = bf16[256,2,256]{0,2,1:T(8,128)(2,1)S(1)} collective-permute-done((bf16[256,2,256]{0,2,1:T(8,128)(2,1)S(1)}, bf16[256,2,256]{0,2,1:T(8,128)(2,1)S(1)}, u32[]{:S(2)}, u32[]{:S(2)}) %collective-permute-start.2) | collective-permute-done | bytes 262176 | tf_op jit(solution)/shard_map/ppermute | solution.py:20
  109.8 6.9 %collective-permute-done.3 = bf16[256,2,256]{0,2,1:T(8,128)(2,1)S(1)} collective-permute-done((bf16[256,2,256]{0,2,1:T(8,128)(2,1)S(1)}, bf16[256,2,256]{0,2,1:T(8,128)(2,1)S(1)}, u32[]{:S(2)}, u32[]{:S(2)}) %collective-permute-start.3) | collective-permute-done | bytes 262176 | tf_op jit(solution)/shard_map/ppermute | solution.py:20
  116.8 0.1 fusion.45
  116.9 1.4 fusion.47
  118.3 1.4 fusion.23
  119.7 0.1 copy.23
  119.8 6.0 %fusion.12.terms_ref = bf16[2,4,400,256]{3,2,1,0:T(8,128)(2,1)} fusion(bf16[4,2,400,4,256]{4,3,2,1,0:T(4,128)(2,1)} %bitcast.56, bf16[256,1,256]{2,0,1:T(8,128)(2,1)S(1)} %copy.23, bf16[4]{0:T(256)(128)(2,1)S(1)} %pad_maximum_fusion.3), kind=kOutput, calls=%fused_computation.13 | convolution fusion | flops 1678802944 | bytes 8323080 | tf_op jit(solution)/shard_map/tkh,ycdkh->cydt/dot_general | solution.py:399
  125.8 0.0 copy-start.1
  125.8 24.4 %shard_map.84 = bf16[4,400,256]{2,1,0:T(8,128)(2,1)} custom-call(bf16[2,4,400,256]{3,2,1,0:T(8,128)(2,1)} %fusion.12.terms_ref), custom_call_target="tpu_custom_call" | custom-call | tf_op jit(solution)/shard_map/pallas_call | solution.py:248
  150.2 1.3 convert_reduce_fusion
  151.5 0.0 copy-done.1
  151.5 0.8 fusion.27
  (10 shorter events, 0.2 us)
Async XLA Ops:
  69.6 21.3 %copy-start.2 = (f32[256]{0:T(256)S(1)}, f32[256]{0:T(256)}, u32[]{:S(2)}) copy-start(f32[256]{0:T(256)} %param.12) | copy-start | bytes 3076
  75.0 27.8 %copy-start = (s32[16384]{0:T(1024)S(1)}, s32[16384]{0:T(1024)}, u32[]{:S(2)}) copy-start(s32[16384]{0:T(1024)} %param.15) | copy-start | bytes 196612
  75.0 28.2 %copy-start.3 = (f32[256]{0:T(256)S(1)}, f32[256]{0:T(256)}, u32[]{:S(2)}) copy-start(f32[256]{0:T(256)} %param.11) | copy-start | bytes 3076
  91.0 13.7 %collective-permute-start = (bf16[256,2,256]{0,2,1:T(8,128)(2,1)S(1)}, bf16[256,2,256]{0,2,1:T(8,128)(2,1)S(1)}, u32[]{:S(2)}, u32[]{:S(2)}) collective-permute-start(bf16[256,2,256]{0,2,1:T(8,128)(2,1)S(1)} %pad_maximum_fusion), channel_id=1, source_target_pairs={{0,16},{8,24},{16,32},{24,40},{32,48},{40,56},{48,64},{56,72},{64,... | collective-permute-start | bytes 786440 | tf_op jit(solution)/shard_map/ppermute | solution.py:20
  93.9 10.8 %collective-permute-start.1 = (bf16[256,2,256]{0,2,1:T(8,128)(2,1)S(1)}, bf16[256,2,256]{0,2,1:T(8,128)(2,1)S(1)}, u32[]{:S(2)}, u32[]{:S(2)}) collective-permute-start(bf16[256,2,256]{0,2,1:T(8,128)(2,1)S(1)} %pad_maximum_fusion), channel_id=1, source_target_pairs={{0,8},{8,16},{16,24},{24,32},{32,40},{40,48},{48,56},{56,64},{64,7... | collective-permute-start | bytes 786440 | tf_op jit(solution)/shard_map/ppermute | solution.py:20
  98.0 11.8 %collective-permute-start.2 = (bf16[256,2,256]{0,2,1:T(8,128)(2,1)S(1)}, bf16[256,2,256]{0,2,1:T(8,128)(2,1)S(1)}, u32[]{:S(2)}, u32[]{:S(2)}) collective-permute-start(bf16[256,2,256]{0,2,1:T(8,128)(2,1)S(1)} %pad_maximum_fusion), channel_id=1, source_target_pairs={{8,0},{16,8},{24,16},{32,24},{40,32},{48,40},{56,48},{64,56},{72,6... | collective-permute-start | bytes 786440 | tf_op jit(solution)/shard_map/ppermute | solution.py:20
  99.9 16.8 %collective-permute-start.3 = (bf16[256,2,256]{0,2,1:T(8,128)(2,1)S(1)}, bf16[256,2,256]{0,2,1:T(8,128)(2,1)S(1)}, u32[]{:S(2)}, u32[]{:S(2)}) collective-permute-start(bf16[256,2,256]{0,2,1:T(8,128)(2,1)S(1)} %pad_maximum_fusion), channel_id=1, source_target_pairs={{16,0},{24,8},{32,16},{40,24},{48,32},{56,40},{64,48},{72,56},{80,... | collective-permute-start | bytes 786440 | tf_op jit(solution)/shard_map/ppermute | solution.py:20
  125.8 25.7 %copy-start.1 = (f32[400]{0:T(512)S(1)}, f32[400]{0:T(512)}, u32[]{:S(2)}) copy-start(f32[400]{0:T(512)} %param.14) | copy-start | bytes 4804

commit v20 on v19

--- a/solution.py
+++ b/solution.py
@@ -111,12 +111,6 @@
     ]
     for copy in cross:
         copy.start()
-    source = tokens_ref[...].astype(jnp.float32)
-    power = jnp.mean(source * source, axis=-1, keepdims=True)
-    scaled = source * lax.rsqrt(power + eps) * gain_ref[...]
-    normed_ref[...] = jnp.transpose(scaled.astype(jnp.bfloat16).astype(jnp.float32)).astype(
-        normed_ref.dtype
-    )
     onward = None
     for t in range(rings // 2):
         last = t == rings // 2 - 1
@@ -130,6 +124,13 @@
         ]
         for copy in step:
             copy.start()
+        if t == 0:
+            source = tokens_ref[...].astype(jnp.float32)
+            power = jnp.mean(source * source, axis=-1, keepdims=True)
+            scaled = source * lax.rsqrt(power + eps) * gain_ref[...]
+            normed_ref[...] = jnp.transpose(scaled.astype(jnp.bfloat16).astype(jnp.float32)).astype(
+                normed_ref.dtype
+            )
         finish(step)
         if t == 1:
             finish(cross)

time: 153 us -> 153 us (level)
  no operation moved by 1% of the time
where the time goes in v20:
time: 153 us; the launch traced here: 152 us
  Pallas kernels  104 us (68%)
  matrix products  14.3 us (9%)
  starting transfers between devices  12 us (8%)
  waiting for transfers between devices  11.9 us (8%)
  other arithmetic  4.92 us (3%)
  local copies, waits for them, and re-layouts  4.8 us (3%)
    pallas_call x1, Pallas kernels, gather_seq(): pl.pallas_call(gather_kernel, out_shape=(jax.ShapeDtypeStruct((rings, sla...  65 us
    pallas_call x1, Pallas kernels, scatter_chips(): pl.pallas_call(scatter_kernel, out_shape=jax.ShapeDtypeStruct(block, jnp....  24.4 us
    pallas_call x1, Pallas kernels, exchange(): pl.pallas_call(functools.partial(exchange_kernel, axis, offsets), out_sha...  14.5 us
    ppermute x4, starting transfers between devices, passed_along(): return lax.ppermute(x, axis, pairs)  12 us
    ppermute x4, waiting for transfers between devices, passed_along(): return lax.ppermute(x, axis, pairs)  11.9 us
    dot_general x1, matrix products, shards(): jnp.einsum('tkh,ycdkh->cydt', widened_context, by_owner, preferred_elemen...  6.02 us
    dot_general x1, matrix products, shards(): jnp.einsum('dt,dch->tch', normed_t, gathered[:, :3], preferred_element_ty...  5.41 us
  transfers between devices with their start and end apart: 4, of which 2 were waited for; matrix products, arithmetic and copies ran while one was open for 1% of the time, Pallas kernels for 0%

profile of v20, /device:TPU:15, one launch (start us, length us, event | category | flops | bytes accessed | tf_op | source)
XLA Modules:
  0.0 152.1 jit_solution(14156746985096116373)
XLA Ops:
  0.0 0.9 copy.18
  0.9 0.8 copy.19
  1.7 1.3 reshape.99.gain_ref
  3.0 0.8 pad_maximum_fusion.1.x_ref
  3.8 65.0 %shard_map.82 = (bf16[8,8,50,4,256]{4,3,2,1,0:T(4,128)(2,1)}, bf16[3200,256]{1,0:T(8,128)(2,1)}) custom-call(bf16[50,4,256]{2,1,0:T(4,128)(2,1)} %pad_maximum_fusion.1.x_ref, bf16[256,3200]{1,0:T(8,128)(2,1)} %tokens_ref.1, f32[1,3200]{1,0:T(1,128)} %reshape.99.gain_ref), custom_call_target="tpu_custom_call" | custom-call | tf_op jit(solution)/shard_map/pallas_call | solution.py:159
  68.8 0.0 copy-start.2
  68.8 5.4 %fusion.3 = f32[256,3,256]{0,2,1:T(8,128)S(1)} fusion(bf16[3200,3,256]{2,1,0:T(4,128)(2,1)} %bitcast.55, bf16[3200,256]{1,0:T(8,128)(2,1)} %get-tuple-element.8), kind=kOutput, calls=%fused_computation.3 | convolution fusion | flops 1258291200 | bytes 7340032 | tf_op jit(solution)/shard_map/dt,dch->tch/dot_general | solution.py:351
  74.3 0.0 copy-start
  74.3 0.0 copy-start.3
  74.3 0.1 multiply_reduce_fusion.1
  74.4 0.6 pad_maximum_fusion.2.x_ref
  75.0 14.5 %shard_map.83 = f32[8,2,256]{2,1,0:T(2,128)} custom-call(f32[2,256]{1,0:T(2,128)} %pad_maximum_fusion.2.x_ref), custom_call_target="tpu_custom_call" | custom-call | tf_op jit(solution)/shard_map/pallas_call | solution.py:315
  89.4 0.7 reduce_sum.47
  90.2 0.0 copy-done.2
  90.2 0.1 fusion.46
  90.3 2.9 %collective-permute-start = (bf16[256,2,256]{0,2,1:T(8,128)(2,1)S(1)}, bf16[256,2,256]{0,2,1:T(8,128)(2,1)S(1)}, u32[]{:S(2)}, u32[]{:S(2)}) collective-permute-start(bf16[256,2,256]{0,2,1:T(8,128)(2,1)S(1)} %pad_maximum_fusion), channel_id=1, source_target_pairs={{0,16},{8,24},{16,32},{24,40},{32,48},{40,56},{48,64},{56,72},{64,... | collective-permute-start | bytes 786440 | tf_op jit(solution)/shard_map/ppermute | solution.py:20
  93.2 4.5 %collective-permute-start.1 = (bf16[256,2,256]{0,2,1:T(8,128)(2,1)S(1)}, bf16[256,2,256]{0,2,1:T(8,128)(2,1)S(1)}, u32[]{:S(2)}, u32[]{:S(2)}) collective-permute-start(bf16[256,2,256]{0,2,1:T(8,128)(2,1)S(1)} %pad_maximum_fusion), channel_id=1, source_target_pairs={{0,8},{8,16},{16,24},{24,32},{32,40},{40,48},{48,56},{56,64},{64,7... | collective-permute-start | bytes 786440 | tf_op jit(solution)/shard_map/ppermute | solution.py:20
  97.7 1.9 %collective-permute-start.2 = (bf16[256,2,256]{0,2,1:T(8,128)(2,1)S(1)}, bf16[256,2,256]{0,2,1:T(8,128)(2,1)S(1)}, u32[]{:S(2)}, u32[]{:S(2)}) collective-permute-start(bf16[256,2,256]{0,2,1:T(8,128)(2,1)S(1)} %pad_maximum_fusion), channel_id=1, source_target_pairs={{8,0},{16,8},{24,16},{32,24},{40,32},{48,40},{56,48},{64,56},{72,6... | collective-permute-start | bytes 786440 | tf_op jit(solution)/shard_map/ppermute | solution.py:20
  99.6 2.7 %collective-permute-start.3 = (bf16[256,2,256]{0,2,1:T(8,128)(2,1)S(1)}, bf16[256,2,256]{0,2,1:T(8,128)(2,1)S(1)}, u32[]{:S(2)}, u32[]{:S(2)}) collective-permute-start(bf16[256,2,256]{0,2,1:T(8,128)(2,1)S(1)} %pad_maximum_fusion), channel_id=1, source_target_pairs={{16,0},{24,8},{32,16},{40,24},{48,32},{56,40},{64,48},{72,56},{80,... | collective-permute-start | bytes 786440 | tf_op jit(solution)/shard_map/ppermute | solution.py:20
  102.4 0.1 copy.21
  102.5 0.0 copy-done
  102.5 0.1 dynamic_slice.10
  102.6 0.1 fusion.30
  102.7 0.3 broadcast_compare_fusion
  102.9 0.0 copy-done.3
  103.0 0.1 multiply_convert_fusion
  103.1 1.1 constant_dynamic-slice_fusion
  104.2 0.1 copy.32
  104.3 0.1 pad_maximum_fusion.3
  104.4 0.0 collective-permute-done
  104.4 0.0 collective-permute-done.1
  104.5 5.0 %collective-permute-done.2 = bf16[256,2,256]{0,2,1:T(8,128)(2,1)S(1)} collective-permute-done((bf16[256,2,256]{0,2,1:T(8,128)(2,1)S(1)}, bf16[256,2,256]{0,2,1:T(8,128)(2,1)S(1)}, u32[]{:S(2)}, u32[]{:S(2)}) %collective-permute-start.2) | collective-permute-done | bytes 262176 | tf_op jit(solution)/shard_map/ppermute | solution.py:20
  109.5 6.9 %collective-permute-done.3 = bf16[256,2,256]{0,2,1:T(8,128)(2,1)S(1)} collective-permute-done((bf16[256,2,256]{0,2,1:T(8,128)(2,1)S(1)}, bf16[256,2,256]{0,2,1:T(8,128)(2,1)S(1)}, u32[]{:S(2)}, u32[]{:S(2)}) %collective-permute-start.3) | collective-permute-done | bytes 262176 | tf_op jit(solution)/shard_map/ppermute | solution.py:20
  116.5 0.1 fusion.45
  116.6 1.4 fusion.47
  118.0 1.4 fusion.23
  119.4 0.1 copy.23
  119.5 6.0 %fusion.12.terms_ref = bf16[2,4,400,256]{3,2,1,0:T(8,128)(2,1)} fusion(bf16[4,2,400,4,256]{4,3,2,1,0:T(4,128)(2,1)} %bitcast.56, bf16[256,1,256]{2,0,1:T(8,128)(2,1)S(1)} %copy.23, bf16[4]{0:T(256)(128)(2,1)S(1)} %pad_maximum_fusion.3), kind=kOutput, calls=%fused_computation.13 | convolution fusion | flops 1678802944 | bytes 8323080 | tf_op jit(solution)/shard_map/tkh,ycdkh->cydt/dot_general | solution.py:400
  125.6 0.0 copy-start.1
  125.6 24.4 %shard_map.84 = bf16[4,400,256]{2,1,0:T(8,128)(2,1)} custom-call(bf16[2,4,400,256]{3,2,1,0:T(8,128)(2,1)} %fusion.12.terms_ref), custom_call_target="tpu_custom_call" | custom-call | tf_op jit(solution)/shard_map/pallas_call | solution.py:249
  150.0 1.3 convert_reduce_fusion
  151.3 0.0 copy-done.1
  151.3 0.8 fusion.27
  (10 shorter events, 0.2 us)
Async XLA Ops:
  68.8 21.4 %copy-start.2 = (f32[256]{0:T(256)S(1)}, f32[256]{0:T(256)}, u32[]{:S(2)}) copy-start(f32[256]{0:T(256)} %param.12) | copy-start | bytes 3076
  74.3 28.2 %copy-start = (s32[16384]{0:T(1024)S(1)}, s32[16384]{0:T(1024)}, u32[]{:S(2)}) copy-start(s32[16384]{0:T(1024)} %param.15) | copy-start | bytes 196612
  74.3 28.7 %copy-start.3 = (f32[256]{0:T(256)S(1)}, f32[256]{0:T(256)}, u32[]{:S(2)}) copy-start(f32[256]{0:T(256)} %param.11) | copy-start | bytes 3076
  90.3 14.1 %collective-permute-start = (bf16[256,2,256]{0,2,1:T(8,128)(2,1)S(1)}, bf16[256,2,256]{0,2,1:T(8,128)(2,1)S(1)}, u32[]{:S(2)}, u32[]{:S(2)}) collective-permute-start(bf16[256,2,256]{0,2,1:T(8,128)(2,1)S(1)} %pad_maximum_fusion), channel_id=1, source_target_pairs={{0,16},{8,24},{16,32},{24,40},{32,48},{40,56},{48,64},{56,72},{64,... | collective-permute-start | bytes 786440 | tf_op jit(solution)/shard_map/ppermute | solution.py:20
  93.2 11.2 %collective-permute-start.1 = (bf16[256,2,256]{0,2,1:T(8,128)(2,1)S(1)}, bf16[256,2,256]{0,2,1:T(8,128)(2,1)S(1)}, u32[]{:S(2)}, u32[]{:S(2)}) collective-permute-start(bf16[256,2,256]{0,2,1:T(8,128)(2,1)S(1)} %pad_maximum_fusion), channel_id=1, source_target_pairs={{0,8},{8,16},{16,24},{24,32},{32,40},{40,48},{48,56},{56,64},{64,7... | collective-permute-start | bytes 786440 | tf_op jit(solution)/shard_map/ppermute | solution.py:20
  97.7 11.8 %collective-permute-start.2 = (bf16[256,2,256]{0,2,1:T(8,128)(2,1)S(1)}, bf16[256,2,256]{0,2,1:T(8,128)(2,1)S(1)}, u32[]{:S(2)}, u32[]{:S(2)}) collective-permute-start(bf16[256,2,256]{0,2,1:T(8,128)(2,1)S(1)} %pad_maximum_fusion), channel_id=1, source_target_pairs={{8,0},{16,8},{24,16},{32,24},{40,32},{48,40},{56,48},{64,56},{72,6... | collective-permute-start | bytes 786440 | tf_op jit(solution)/shard_map/ppermute | solution.py:20
  99.6 16.8 %collective-permute-start.3 = (bf16[256,2,256]{0,2,1:T(8,128)(2,1)S(1)}, bf16[256,2,256]{0,2,1:T(8,128)(2,1)S(1)}, u32[]{:S(2)}, u32[]{:S(2)}) collective-permute-start(bf16[256,2,256]{0,2,1:T(8,128)(2,1)S(1)} %pad_maximum_fusion), channel_id=1, source_target_pairs={{16,0},{24,8},{32,16},{40,24},{48,32},{56,40},{64,48},{72,56},{80,... | collective-permute-start | bytes 786440 | tf_op jit(solution)/shard_map/ppermute | solution.py:20
  125.6 25.7 %copy-start.1 = (f32[400]{0:T(512)S(1)}, f32[400]{0:T(512)}, u32[]{:S(2)}) copy-start(f32[400]{0:T(512)} %param.14) | copy-start | bytes 4804

commit v21 on v18

--- a/solution.py
+++ b/solution.py
@@ -149,7 +149,7 @@
     return pl.pallas_call(
         gather_kernel,
         out_shape=jax.ShapeDtypeStruct((rings, slab) + block.shape, block.dtype),
-        in_specs=[pl.BlockSpec(memory_space=pl.ANY)],
+        in_specs=[pl.BlockSpec(memory_space=pltpu.VMEM)],
         out_specs=pl.BlockSpec(memory_space=pl.ANY),
         scratch_shapes=[
             pltpu.SemaphoreType.DMA((2,)),

time: 152 us -> 157 us (1.033)
  Pallas kernels: 101 us -> 105 us
    pallas_call x1, Pallas kernels: 14.5 us -> 17.6 us  [exchange(): pl.pallas_call(functools.partial(exchange_kernel, axis, offsets), out_sha...]
where the time goes in v21:
time: 157 us; the launch traced here: 156 us
  Pallas kernels  105 us (67%)
  matrix products  14.1 us (9%)
  starting transfers between devices  13.5 us (9%)
  other arithmetic  8.39 us (5%)
  waiting for transfers between devices  7.71 us (5%)
  local copies, waits for them, and re-layouts  6.46 us (4%)
    pallas_call x1, Pallas kernels, gather_seq(): pl.pallas_call(gather_kernel, out_shape=jax.ShapeDtypeStruct((rings, slab...  62.9 us
    pallas_call x1, Pallas kernels, scatter_chips(): pl.pallas_call(scatter_kernel, out_shape=jax.ShapeDtypeStruct(block, jnp....  25 us
    pallas_call x1, Pallas kernels, exchange(): pl.pallas_call(functools.partial(exchange_kernel, axis, offsets), out_sha...  17.6 us
    ppermute x4, starting transfers between devices, passed_along(): return lax.ppermute(x, axis, pairs)  13.5 us
    ppermute x4, waiting for transfers between devices, passed_along(): return lax.ppermute(x, axis, pairs)  7.71 us
    dot_general x1, matrix products, shards(): jnp.einsum('tkh,ycdkh->cydt', widened_context, by_owner, preferred_elemen...  6.02 us
    unnamed x19, local copies, waits for them, and re-layouts  6 us
    dot_general x1, matrix products, shards(): jnp.einsum('td,dch->tch', normed, gathered[:, :3], preferred_element_type...  5.33 us
  transfers between devices with their start and end apart: 4, of which 2 were waited for; matrix products, arithmetic and copies ran while one was open for 4% of the time, Pallas kernels for 0%

profile of v21, /device:TPU:15, one launch (start us, length us, event | category | flops | bytes accessed | tf_op | source)
XLA Modules:
  0.0 155.9 jit_solution(13396621442293594391)
XLA Ops:
  0.0 0.0 copy-start
  0.0 0.0 copy-start.2
  0.0 3.0 %copy.18 = bf16[256,3200]{0,1:T(8,128)(2,1)S(1)} copy(bf16[256,3200]{1,0:T(8,128)(2,1)} %param.8) | data formatting | bytes 3276800 | tf_op args[0]
  3.0 0.5 multiply_reduce_fusion
  3.5 0.0 copy-done
  3.6 0.0 copy-done.2
  3.6 0.8 pad_maximum_fusion.1.x_ref
  4.4 62.9 %shard_map.82 = bf16[8,8,50,4,256]{4,3,2,1,0:T(4,128)(2,1)} custom-call(bf16[50,4,256]{2,1,0:T(4,128)(2,1)} %pad_maximum_fusion.1.x_ref), custom_call_target="tpu_custom_call" | custom-call | tf_op jit(solution)/shard_map/pallas_call | solution.py:149
  67.2 0.0 copy-done.6
  67.2 0.0 copy-start.4
  67.3 5.3 %fusion.3 = f32[256,3,256]{0,2,1:T(8,128)S(1)} fusion(bf16[3200,3,256]{2,1,0:T(4,128)(2,1)} %bitcast.44, f32[3200]{0:T(1024)S(1)} %copy-done.6, f32[256]{0:T(256)S(1)} %add_rsqrt_fusion, bf16[256,3200]{0,1:T(8,128)(2,1)S(1)} %copy.18), kind=kOutput, calls=%fused_computation.3 | convolution fusion | flops 1261568000 | bytes 7353856 | tf_op jit(solution)/shard_map/td,dch->tch/dot_general | solution.py:331
  72.6 0.0 copy-start.1
  72.6 0.0 copy-start.5
  72.6 0.1 multiply_reduce_fusion.2
  72.7 0.6 pad_maximum_fusion.2.x_ref
  73.3 17.6 %shard_map.83 = f32[8,2,256]{2,1,0:T(2,128)} custom-call(f32[2,256]{1,0:T(2,128)} %pad_maximum_fusion.2.x_ref), custom_call_target="tpu_custom_call" | custom-call | tf_op jit(solution)/shard_map/pallas_call | solution.py:295
  90.8 0.7 reduce_sum.57
  91.6 0.0 copy-done.4
  91.6 0.1 fusion.50
  91.8 5.8 %collective-permute-start = (bf16[256,2,256]{0,2,1:T(8,128)(2,1)S(1)}, bf16[256,2,256]{0,2,1:T(8,128)(2,1)}, u32[]{:S(2)}, u32[]{:S(2)}) collective-permute-start(bf16[256,2,256]{0,2,1:T(8,128)(2,1)S(1)} %pad_maximum_fusion), channel_id=1, source_target_pairs={{0,16},{8,24},{16,32},{24,40},{32,48},{40,56},{48,64},{56,72},{64,... | collective-permute-start | bytes 786440 | tf_op jit(solution)/shard_map/ppermute | solution.py:20
  97.6 2.4 %collective-permute-start.1 = (bf16[256,2,256]{0,2,1:T(8,128)(2,1)S(1)}, bf16[256,2,256]{0,2,1:T(8,128)(2,1)}, u32[]{:S(2)}, u32[]{:S(2)}) collective-permute-start(bf16[256,2,256]{0,2,1:T(8,128)(2,1)S(1)} %pad_maximum_fusion), channel_id=1, source_target_pairs={{0,8},{8,16},{16,24},{24,32},{32,40},{40,48},{48,56},{56,64},{64,7... | collective-permute-start | bytes 786440 | tf_op jit(solution)/shard_map/ppermute | solution.py:20
  100.0 2.9 %collective-permute-start.2 = (bf16[256,2,256]{0,2,1:T(8,128)(2,1)S(1)}, bf16[256,2,256]{0,2,1:T(8,128)(2,1)}, u32[]{:S(2)}, u32[]{:S(2)}) collective-permute-start(bf16[256,2,256]{0,2,1:T(8,128)(2,1)S(1)} %pad_maximum_fusion), channel_id=1, source_target_pairs={{8,0},{16,8},{24,16},{32,24},{40,32},{48,40},{56,48},{64,56},{72,6... | collective-permute-start | bytes 786440 | tf_op jit(solution)/shard_map/ppermute | solution.py:20
  102.9 2.4 %collective-permute-start.3 = (bf16[256,2,256]{0,2,1:T(8,128)(2,1)S(1)}, bf16[256,2,256]{0,2,1:T(8,128)(2,1)S(1)}, u32[]{:S(2)}, u32[]{:S(2)}) collective-permute-start(bf16[256,2,256]{0,2,1:T(8,128)(2,1)S(1)} %pad_maximum_fusion), channel_id=1, source_target_pairs={{16,0},{24,8},{32,16},{40,24},{48,32},{56,40},{64,48},{72,56},{80,... | collective-permute-start | bytes 786440 | tf_op jit(solution)/shard_map/ppermute | solution.py:20
  105.3 0.1 copy.23
  105.4 0.0 copy-done.1
  105.4 0.1 dynamic_slice.10
  105.5 0.1 fusion.34
  105.6 0.3 broadcast_compare_fusion
  105.9 0.0 copy-done.5
  105.9 0.1 multiply_convert_fusion.1
  106.0 2.0 %convert_element_type.43 = f32[256,3200]{0,1:T(8,128)} convert(bf16[256,3200]{0,1:T(8,128)(2,1)S(1)} %copy.18) | non-fusion elementwise | flops 819200 | bytes 4915200 | tf_op jit(solution)/shard_map/convert_element_type | solution.py:321
  108.0 0.1 pad_maximum_fusion.3
  108.1 0.0 collective-permute-done
  108.1 1.0 constant_dynamic-update-slice_fusion.4
  109.0 0.0 collective-permute-done.1
  109.0 1.0 constant_dynamic-update-slice_fusion.3
  110.0 2.2 %collective-permute-done.2 = bf16[256,2,256]{0,2,1:T(8,128)(2,1)} collective-permute-done((bf16[256,2,256]{0,2,1:T(8,128)(2,1)S(1)}, bf16[256,2,256]{0,2,1:T(8,128)(2,1)}, u32[]{:S(2)}, u32[]{:S(2)}) %collective-permute-start.2) | collective-permute-done | bytes 262176 | tf_op jit(solution)/shard_map/ppermute | solution.py:20
  112.2 1.0 constant_dynamic-update-slice_fusion.1
  113.2 5.6 %collective-permute-done.3 = bf16[256,2,256]{0,2,1:T(8,128)(2,1)S(1)} collective-permute-done((bf16[256,2,256]{0,2,1:T(8,128)(2,1)S(1)}, bf16[256,2,256]{0,2,1:T(8,128)(2,1)S(1)}, u32[]{:S(2)}, u32[]{:S(2)}) %collective-permute-start.3) | collective-permute-done | bytes 262176 | tf_op jit(solution)/shard_map/ppermute | solution.py:20
  118.7 0.1 fusion.49
  118.8 1.4 fusion.51
  120.2 1.4 fusion.27
  121.6 0.1 copy.25
  121.7 6.0 %fusion.16.terms_ref = bf16[2,4,400,256]{3,2,1,0:T(8,128)(2,1)} fusion(bf16[4,2,400,4,256]{4,3,2,1,0:T(4,128)(2,1)} %bitcast.45, bf16[256,1,256]{2,0,1:T(8,128)(2,1)S(1)} %copy.25, bf16[4]{0:T(256)(128)(2,1)S(1)} %pad_maximum_fusion.3), kind=kOutput, calls=%fused_computation.18 | convolution fusion | flops 1678802944 | bytes 8323080 | tf_op jit(solution)/shard_map/tkh,ycdkh->cydt/dot_general | solution.py:380
  127.8 25.0 %shard_map.84 = bf16[4,400,256]{2,1,0:T(8,128)(2,1)} custom-call(bf16[2,4,400,256]{3,2,1,0:T(8,128)(2,1)} %fusion.16.terms_ref), custom_call_target="tpu_custom_call" | custom-call | tf_op jit(solution)/shard_map/pallas_call | solution.py:229
  152.8 1.3 convert_reduce_fusion
  154.1 0.0 copy-done.3
  154.1 1.8 %fusion.31 = bf16[256,400]{0,1:T(8,128)(2,1)} fusion(f32[400,256]{1,0:T(8,128)S(1)} %convert_reduce_fusion, f32[256,3200]{0,1:T(8,128)} %convert_element_type.43, s32[]{:T(128)S(6)} %select_n.16, f32[400]{0:T(512)S(1)} %copy-done.3), kind=kLoop, calls=%fused_computation.28 | loop fusion | flops 307200 | bytes 1025604 | tf_op jit(solution)/shard_map/convert_element_type | solution.py:388
  (12 shorter events, 0.2 us)
Async XLA Ops:
  0.0 3.5 %copy-start = (bf16[50,3,256]{2,0,1:T(8,128)(2,1)S(1)}, bf16[50,3,256]{2,0,1:T(8,128)(2,1)}, u32[]{:S(2)}) copy-start(bf16[50,3,256]{2,0,1:T(8,128)(2,1)} %param.10) | copy-start | bytes 230404
  0.0 3.6 %copy-start.2 = (bf16[256,50]{0,1:T(8,128)(2,1)S(1)}, bf16[256,50]{0,1:T(8,128)(2,1)}, u32[]{:S(2)}) copy-start(bf16[256,50]{0,1:T(8,128)(2,1)} %param.13) | copy-start | bytes 76804
  4.4 62.9 %copy-start.6 = (f32[3200]{0:T(1024)S(1)}, f32[3200]{0:T(1024)}, u32[]{:S(2)}) copy-start(f32[3200]{0:T(1024)} %param.9) | copy-start | bytes 38404
  67.2 24.4 %copy-start.4 = (f32[256]{0:T(256)S(1)}, f32[256]{0:T(256)}, u32[]{:S(2)}) copy-start(f32[256]{0:T(256)} %param.12) | copy-start | bytes 3076
  72.6 32.8 %copy-start.1 = (s32[16384]{0:T(1024)S(1)}, s32[16384]{0:T(1024)}, u32[]{:S(2)}) copy-start(s32[16384]{0:T(1024)} %param.15) | copy-start | bytes 196612
  72.6 33.3 %copy-start.5 = (f32[256]{0:T(256)S(1)}, f32[256]{0:T(256)}, u32[]{:S(2)}) copy-start(f32[256]{0:T(256)} %param.11) | copy-start | bytes 3076
  91.8 16.3 %collective-permute-start = (bf16[256,2,256]{0,2,1:T(8,128)(2,1)S(1)}, bf16[256,2,256]{0,2,1:T(8,128)(2,1)}, u32[]{:S(2)}, u32[]{:S(2)}) collective-permute-start(bf16[256,2,256]{0,2,1:T(8,128)(2,1)S(1)} %pad_maximum_fusion), channel_id=1, source_target_pairs={{0,16},{8,24},{16,32},{24,40},{32,48},{40,56},{48,64},{56,72},{64,... | collective-permute-start | bytes 786440 | tf_op jit(solution)/shard_map/ppermute | solution.py:20
  97.6 11.5 %collective-permute-start.1 = (bf16[256,2,256]{0,2,1:T(8,128)(2,1)S(1)}, bf16[256,2,256]{0,2,1:T(8,128)(2,1)}, u32[]{:S(2)}, u32[]{:S(2)}) collective-permute-start(bf16[256,2,256]{0,2,1:T(8,128)(2,1)S(1)} %pad_maximum_fusion), channel_id=1, source_target_pairs={{0,8},{8,16},{16,24},{24,32},{32,40},{40,48},{48,56},{56,64},{64,7... | collective-permute-start | bytes 786440 | tf_op jit(solution)/shard_map/ppermute | solution.py:20
  100.0 12.2 %collective-permute-start.2 = (bf16[256,2,256]{0,2,1:T(8,128)(2,1)S(1)}, bf16[256,2,256]{0,2,1:T(8,128)(2,1)}, u32[]{:S(2)}, u32[]{:S(2)}) collective-permute-start(bf16[256,2,256]{0,2,1:T(8,128)(2,1)S(1)} %pad_maximum_fusion), channel_id=1, source_target_pairs={{8,0},{16,8},{24,16},{32,24},{40,32},{48,40},{56,48},{64,56},{72,6... | collective-permute-start | bytes 786440 | tf_op jit(solution)/shard_map/ppermute | solution.py:20
  102.9 15.8 %collective-permute-start.3 = (bf16[256,2,256]{0,2,1:T(8,128)(2,1)S(1)}, bf16[256,2,256]{0,2,1:T(8,128)(2,1)S(1)}, u32[]{:S(2)}, u32[]{:S(2)}) collective-permute-start(bf16[256,2,256]{0,2,1:T(8,128)(2,1)S(1)} %pad_maximum_fusion), channel_id=1, source_target_pairs={{16,0},{24,8},{32,16},{40,24},{48,32},{56,40},{64,48},{72,56},{80,... | collective-permute-start | bytes 786440 | tf_op jit(solution)/shard_map/ppermute | solution.py:20
  127.8 26.3 %copy-start.3 = (f32[400]{0:T(512)S(1)}, f32[400]{0:T(512)}, u32[]{:S(2)}) copy-start(f32[400]{0:T(512)} %param.14) | copy-start | bytes 4804

commit v22 on v18

--- a/solution.py
+++ b/solution.py
@@ -163,8 +163,8 @@
     )(block)
 
 
-def scatter_kernel(terms_ref, out_ref, mine, incoming, sums, send_sem, recv_sem, local_sems):
-    chips = out_ref.shape[0]
+def scatter_kernel(terms_ref, out_ref, mine, incoming, sums, landed, send_sem, recv_sem, local_sems):
+    chips = landed.shape[0]
     seq = lax.axis_index("seq")
     tp = lax.axis_index("tp")
     mesh_id = pl.DeviceIdType.MESH
@@ -207,20 +207,24 @@
         if k < 3:
             copy = pltpu.make_async_remote_copy(
                 src_ref=sums.at[owner],
-                dst_ref=out_ref.at[here],
+                dst_ref=landed.at[here],
                 send_sem=send_sem.at[4 + k],
                 recv_sem=recv_sem.at[4 + k],
                 device_id=device(owner),
                 device_id_type=mesh_id,
             )
         else:
-            copy = pltpu.make_async_copy(sums.at[owner], out_ref.at[here], local_sems.at[4])
+            copy = pltpu.make_async_copy(sums.at[owner], landed.at[here], local_sems.at[4])
         copy.start()
         outgoing.append(copy)
     for copy in outgoing[:3]:
         copy.wait_send()
         copy.wait_recv()
     outgoing[3].wait()
+    total = landed[0].astype(jnp.float32)
+    for chip in range(1, chips):
+        total = total + landed[chip].astype(jnp.float32)
+    out_ref[...] = total
 
 
 def scatter_chips(terms):
@@ -228,12 +232,13 @@
     chips = block[0]
     return pl.pallas_call(
         scatter_kernel,
-        out_shape=jax.ShapeDtypeStruct(block, jnp.bfloat16),
+        out_shape=jax.ShapeDtypeStruct(block[1:], jnp.float32),
         in_specs=[pl.BlockSpec(memory_space=pl.ANY)],
-        out_specs=pl.BlockSpec(memory_space=pl.ANY),
+        out_specs=pl.BlockSpec(memory_space=pltpu.VMEM),
         scratch_shapes=[
             pltpu.VMEM(block, terms.dtype),
             pltpu.VMEM(block, terms.dtype),
+            pltpu.VMEM(block, jnp.bfloat16),
             pltpu.VMEM(block, jnp.bfloat16),
             pltpu.SemaphoreType.DMA((7,)),
             pltpu.SemaphoreType.DMA((7,)),
@@ -380,9 +385,7 @@
     terms = jnp.einsum(
         "tkh,ycdkh->cydt", widened_context, by_owner, preferred_element_type=jnp.float32
     )
-    projected = jnp.transpose(
-        jnp.sum(scatter_chips(terms.astype(jnp.bfloat16)).astype(jnp.float32), axis=0)
-    )
+    projected = jnp.transpose(scatter_chips(terms.astype(jnp.bfloat16)))
     share = layer_scale.shape[0]
     residual = lax.dynamic_slice_in_dim(source, lax.axis_index("tp") * share, share, 1)
     return (residual + layer_scale * projected).astype(jnp.bfloat16)

time: 152 us -> 151 us (level)
  no operation moved by 1% of the time
where the time goes in v22:
time: 151 us
  Pallas kernels  102 us (68%)
  matrix products  14.1 us (9%)
  starting transfers between devices  12 us (8%)
  waiting for transfers between devices  8.39 us (6%)
  other arithmetic  7.22 us (5%)
  local copies, waits for them, and re-layouts  6.47 us (4%)
    pallas_call x1, Pallas kernels, gather_seq(): pl.pallas_call(gather_kernel, out_shape=jax.ShapeDtypeStruct((rings, slab...  62.6 us
    pallas_call x1, Pallas kernels, scatter_chips(): pl.pallas_call(scatter_kernel, out_shape=jax.ShapeDtypeStruct(block[1:],...  25 us
    pallas_call x1, Pallas kernels, exchange(): pl.pallas_call(functools.partial(exchange_kernel, axis, offsets), out_sha...  14.5 us
    ppermute x4, starting transfers between devices, passed_along(): return lax.ppermute(x, axis, pairs)  12 us
    ppermute x4, waiting for transfers between devices, passed_along(): return lax.ppermute(x, axis, pairs)  8.39 us
    dot_general x1, matrix products, shards(): jnp.einsum('tkh,ycdkh->cydt', widened_context, by_owner, preferred_elemen...  6.03 us
    unnamed x19, local copies, waits for them, and re-layouts  6 us
    dot_general x1, matrix products, shards(): jnp.einsum('td,dch->tch', normed, gathered[:, :3], preferred_element_type...  5.33 us
  transfers between devices with their start and end apart: 4, of which 2 were waited for; matrix products, arithmetic and copies ran while one was open for 4% of the time, Pallas kernels for 0%

profile of v22, /device:TPU:15, one launch (start us, length us, event | category | flops | bytes accessed | tf_op | source)
XLA Modules:
  0.0 150.5 jit_solution(10675997303204906023)
XLA Ops:
  0.0 0.0 copy-start
  0.0 0.0 copy-start.2
  0.0 3.0 %copy.18 = bf16[256,3200]{0,1:T(8,128)(2,1)S(1)} copy(bf16[256,3200]{1,0:T(8,128)(2,1)} %param.8) | data formatting | bytes 3276800 | tf_op args[0]
  3.0 0.5 multiply_reduce_fusion
  3.5 0.0 copy-done
  3.6 0.0 copy-done.2
  3.6 0.8 pad_maximum_fusion.1.x_ref
  4.4 62.6 %shard_map.82 = bf16[8,8,50,4,256]{4,3,2,1,0:T(4,128)(2,1)} custom-call(bf16[50,4,256]{2,1,0:T(4,128)(2,1)} %pad_maximum_fusion.1.x_ref), custom_call_target="tpu_custom_call" | custom-call | tf_op jit(solution)/shard_map/pallas_call | solution.py:149
  66.9 0.0 copy-done.6
  67.0 0.0 copy-start.4
  67.0 5.3 %fusion.3 = f32[256,3,256]{0,2,1:T(8,128)S(1)} fusion(bf16[3200,3,256]{2,1,0:T(4,128)(2,1)} %bitcast.44, f32[3200]{0:T(1024)S(1)} %copy-done.6, f32[256]{0:T(256)S(1)} %add_rsqrt_fusion, bf16[256,3200]{0,1:T(8,128)(2,1)S(1)} %copy.18), kind=kOutput, calls=%fused_computation.3 | convolution fusion | flops 1261568000 | bytes 7353856 | tf_op jit(solution)/shard_map/td,dch->tch/dot_general | solution.py:336
  72.3 0.0 copy-start.1
  72.3 0.0 copy-start.5
  72.3 0.1 multiply_reduce_fusion.2
  72.4 0.6 pad_maximum_fusion.2.x_ref
  73.0 14.5 %shard_map.83 = f32[8,2,256]{2,1,0:T(2,128)} custom-call(f32[2,256]{1,0:T(2,128)} %pad_maximum_fusion.2.x_ref), custom_call_target="tpu_custom_call" | custom-call | tf_op jit(solution)/shard_map/pallas_call | solution.py:300
  87.5 0.7 reduce_sum.48
  88.2 0.0 copy-done.4
  88.3 0.1 fusion.50
  88.4 2.9 %collective-permute-start = (bf16[256,2,256]{0,2,1:T(8,128)(2,1)S(1)}, bf16[256,2,256]{0,2,1:T(8,128)(2,1)}, u32[]{:S(2)}, u32[]{:S(2)}) collective-permute-start(bf16[256,2,256]{0,2,1:T(8,128)(2,1)S(1)} %pad_maximum_fusion), channel_id=1, source_target_pairs={{0,16},{8,24},{16,32},{24,40},{32,48},{40,56},{48,64},{56,72},{64,... | collective-permute-start | bytes 786440 | tf_op jit(solution)/shard_map/ppermute | solution.py:20
  91.3 4.5 %collective-permute-start.1 = (bf16[256,2,256]{0,2,1:T(8,128)(2,1)S(1)}, bf16[256,2,256]{0,2,1:T(8,128)(2,1)}, u32[]{:S(2)}, u32[]{:S(2)}) collective-permute-start(bf16[256,2,256]{0,2,1:T(8,128)(2,1)S(1)} %pad_maximum_fusion), channel_id=1, source_target_pairs={{0,8},{8,16},{16,24},{24,32},{32,40},{40,48},{48,56},{56,64},{64,7... | collective-permute-start | bytes 786440 | tf_op jit(solution)/shard_map/ppermute | solution.py:20
  95.8 1.9 %collective-permute-start.2 = (bf16[256,2,256]{0,2,1:T(8,128)(2,1)S(1)}, bf16[256,2,256]{0,2,1:T(8,128)(2,1)}, u32[]{:S(2)}, u32[]{:S(2)}) collective-permute-start(bf16[256,2,256]{0,2,1:T(8,128)(2,1)S(1)} %pad_maximum_fusion), channel_id=1, source_target_pairs={{8,0},{16,8},{24,16},{32,24},{40,32},{48,40},{56,48},{64,56},{72,6... | collective-permute-start | bytes 786440 | tf_op jit(solution)/shard_map/ppermute | solution.py:20
  97.8 2.7 %collective-permute-start.3 = (bf16[256,2,256]{0,2,1:T(8,128)(2,1)S(1)}, bf16[256,2,256]{0,2,1:T(8,128)(2,1)S(1)}, u32[]{:S(2)}, u32[]{:S(2)}) collective-permute-start(bf16[256,2,256]{0,2,1:T(8,128)(2,1)S(1)} %pad_maximum_fusion), channel_id=1, source_target_pairs={{16,0},{24,8},{32,16},{40,24},{48,32},{56,40},{64,48},{72,56},{80,... | collective-permute-start | bytes 786440 | tf_op jit(solution)/shard_map/ppermute | solution.py:20
  100.5 0.1 copy.23
  100.6 0.0 copy-done.1
  100.6 0.1 dynamic_slice.10
  100.7 0.1 fusion.34
  100.8 0.3 broadcast_compare_fusion
  101.0 0.0 copy-done.5
  101.0 0.1 multiply_convert_fusion.1
  101.2 2.0 %convert_element_type.40 = f32[256,3200]{0,1:T(8,128)} convert(bf16[256,3200]{0,1:T(8,128)(2,1)S(1)} %copy.18) | non-fusion elementwise | flops 819200 | bytes 4915200 | tf_op jit(solution)/shard_map/convert_element_type | solution.py:326
  103.2 0.1 pad_maximum_fusion.3
  103.2 0.0 collective-permute-done
  103.2 1.0 constant_dynamic-update-slice_fusion.4
  104.2 0.0 collective-permute-done.1
  104.2 1.0 constant_dynamic-update-slice_fusion.3
  105.2 2.5 %collective-permute-done.2 = bf16[256,2,256]{0,2,1:T(8,128)(2,1)} collective-permute-done((bf16[256,2,256]{0,2,1:T(8,128)(2,1)S(1)}, bf16[256,2,256]{0,2,1:T(8,128)(2,1)}, u32[]{:S(2)}, u32[]{:S(2)}) %collective-permute-start.2) | collective-permute-done | bytes 262176 | tf_op jit(solution)/shard_map/ppermute | solution.py:20
  107.7 1.0 constant_dynamic-update-slice_fusion.1
  108.7 5.9 %collective-permute-done.3 = bf16[256,2,256]{0,2,1:T(8,128)(2,1)S(1)} collective-permute-done((bf16[256,2,256]{0,2,1:T(8,128)(2,1)S(1)}, bf16[256,2,256]{0,2,1:T(8,128)(2,1)S(1)}, u32[]{:S(2)}, u32[]{:S(2)}) %collective-permute-start.3) | collective-permute-done | bytes 262176 | tf_op jit(solution)/shard_map/ppermute | solution.py:20
  114.6 0.1 fusion.49
  114.7 1.4 fusion.51
  116.1 1.4 fusion.27
  117.5 0.1 copy.25
  117.6 0.0 copy-start.3
  117.6 6.0 %fusion.16.terms_ref = bf16[2,4,400,256]{3,2,1,0:T(8,128)(2,1)} fusion(bf16[4,2,400,4,256]{4,3,2,1,0:T(4,128)(2,1)} %bitcast.45, bf16[256,1,256]{2,0,1:T(8,128)(2,1)S(1)} %copy.25, bf16[4]{0:T(256)(128)(2,1)S(1)} %pad_maximum_fusion.3), kind=kOutput, calls=%fused_computation.17 | convolution fusion | flops 1678802944 | bytes 8323080 | tf_op jit(solution)/shard_map/tkh,ycdkh->cydt/dot_general | solution.py:385
  123.6 25.0 %shard_map.84 = f32[400,256]{1,0:T(8,128)} custom-call(bf16[2,4,400,256]{3,2,1,0:T(8,128)(2,1)} %fusion.16.terms_ref), custom_call_target="tpu_custom_call" | custom-call | tf_op jit(solution)/shard_map/pallas_call | solution.py:233
  148.6 0.0 copy-done.3
  148.6 1.9 %fusion.31 = bf16[256,400]{0,1:T(8,128)(2,1)} fusion(f32[400,256]{1,0:T(8,128)} %shard_map.84, f32[256,3200]{0,1:T(8,128)} %convert_element_type.40, s32[]{:T(128)S(6)} %select_n.16, f32[400]{0:T(512)S(1)} %copy-done.3), kind=kLoop, calls=%fused_computation.27 | loop fusion | flops 307200 | bytes 1025604 | tf_op jit(solution)/shard_map/convert_element_type | solution.py:391
  (11 shorter events, 0.2 us)
Async XLA Ops:
  0.0 3.5 %copy-start = (bf16[50,3,256]{2,0,1:T(8,128)(2,1)S(1)}, bf16[50,3,256]{2,0,1:T(8,128)(2,1)}, u32[]{:S(2)}) copy-start(bf16[50,3,256]{2,0,1:T(8,128)(2,1)} %param.10) | copy-start | bytes 230404
  0.0 3.6 %copy-start.2 = (bf16[256,50]{0,1:T(8,128)(2,1)S(1)}, bf16[256,50]{0,1:T(8,128)(2,1)}, u32[]{:S(2)}) copy-start(bf16[256,50]{0,1:T(8,128)(2,1)} %param.13) | copy-start | bytes 76804
  4.4 62.6 %copy-start.6 = (f32[3200]{0:T(1024)S(1)}, f32[3200]{0:T(1024)}, u32[]{:S(2)}) copy-start(f32[3200]{0:T(1024)} %param.9) | copy-start | bytes 38404
  67.0 21.3 %copy-start.4 = (f32[256]{0:T(256)S(1)}, f32[256]{0:T(256)}, u32[]{:S(2)}) copy-start(f32[256]{0:T(256)} %param.12) | copy-start | bytes 3076
  72.3 28.3 %copy-start.1 = (s32[16384]{0:T(1024)S(1)}, s32[16384]{0:T(1024)}, u32[]{:S(2)}) copy-start(s32[16384]{0:T(1024)} %param.15) | copy-start | bytes 196612
  72.3 28.7 %copy-start.5 = (f32[256]{0:T(256)S(1)}, f32[256]{0:T(256)}, u32[]{:S(2)}) copy-start(f32[256]{0:T(256)} %param.11) | copy-start | bytes 3076
  88.4 14.8 %collective-permute-start = (bf16[256,2,256]{0,2,1:T(8,128)(2,1)S(1)}, bf16[256,2,256]{0,2,1:T(8,128)(2,1)}, u32[]{:S(2)}, u32[]{:S(2)}) collective-permute-start(bf16[256,2,256]{0,2,1:T(8,128)(2,1)S(1)} %pad_maximum_fusion), channel_id=1, source_target_pairs={{0,16},{8,24},{16,32},{24,40},{32,48},{40,56},{48,64},{56,72},{64,... | collective-permute-start | bytes 786440 | tf_op jit(solution)/shard_map/ppermute | solution.py:20
  91.3 12.9 %collective-permute-start.1 = (bf16[256,2,256]{0,2,1:T(8,128)(2,1)S(1)}, bf16[256,2,256]{0,2,1:T(8,128)(2,1)}, u32[]{:S(2)}, u32[]{:S(2)}) collective-permute-start(bf16[256,2,256]{0,2,1:T(8,128)(2,1)S(1)} %pad_maximum_fusion), channel_id=1, source_target_pairs={{0,8},{8,16},{16,24},{24,32},{32,40},{40,48},{48,56},{56,64},{64,7... | collective-permute-start | bytes 786440 | tf_op jit(solution)/shard_map/ppermute | solution.py:20
  95.8 11.9 %collective-permute-start.2 = (bf16[256,2,256]{0,2,1:T(8,128)(2,1)S(1)}, bf16[256,2,256]{0,2,1:T(8,128)(2,1)}, u32[]{:S(2)}, u32[]{:S(2)}) collective-permute-start(bf16[256,2,256]{0,2,1:T(8,128)(2,1)S(1)} %pad_maximum_fusion), channel_id=1, source_target_pairs={{8,0},{16,8},{24,16},{32,24},{40,32},{48,40},{56,48},{64,56},{72,6... | collective-permute-start | bytes 786440 | tf_op jit(solution)/shard_map/ppermute | solution.py:20
  97.8 16.8 %collective-permute-start.3 = (bf16[256,2,256]{0,2,1:T(8,128)(2,1)S(1)}, bf16[256,2,256]{0,2,1:T(8,128)(2,1)S(1)}, u32[]{:S(2)}, u32[]{:S(2)}) collective-permute-start(bf16[256,2,256]{0,2,1:T(8,128)(2,1)S(1)} %pad_maximum_fusion), channel_id=1, source_target_pairs={{16,0},{24,8},{32,16},{40,24},{48,32},{56,40},{64,48},{72,56},{80,... | collective-permute-start | bytes 786440 | tf_op jit(solution)/shard_map/ppermute | solution.py:20
  117.6 31.0 %copy-start.3 = (f32[400]{0:T(512)S(1)}, f32[400]{0:T(512)}, u32[]{:S(2)}) copy-start(f32[400]{0:T(512)} %param.14) | copy-start | bytes 4804

commit v23 on v22

--- a/solution.py
+++ b/solution.py
@@ -248,7 +248,7 @@
     )(terms)
 
 
-def exchange_kernel(axis, offsets, x_ref, out_ref, send_sem, recv_sem, local_sem):
+def exchange_kernel(axis, offsets, x_ref, total_ref, out_ref, send_sem, recv_sem, local_sem):
     size = lax.axis_size(axis)
     me = lax.axis_index(axis)
     seq = lax.axis_index("seq")
@@ -286,6 +286,10 @@
         copy.wait_send()
         copy.wait_recv()
     local.wait()
+    total = out_ref[0]
+    for slot in range(1, out_ref.shape[0]):
+        total = total + out_ref[slot]
+    total_ref[...] = total
 
 
 def offsets_own_slot(offsets, me):
@@ -299,10 +303,11 @@
     count = len(offsets)
     return pl.pallas_call(
         functools.partial(exchange_kernel, axis, offsets),
-        out_shape=jax.ShapeDtypeStruct((slots,) + block.shape, block.dtype),
+        out_shape=jax.ShapeDtypeStruct(block.shape, block.dtype),
         in_specs=[pl.BlockSpec(memory_space=pl.ANY)],
-        out_specs=pl.BlockSpec(memory_space=pl.ANY),
+        out_specs=pl.BlockSpec(memory_space=pltpu.VMEM),
         scratch_shapes=[
+            pltpu.VMEM((slots,) + block.shape, block.dtype),
             pltpu.SemaphoreType.DMA((count,)),
             pltpu.SemaphoreType.DMA((count,)),
             pltpu.SemaphoreType.DMA(()),
@@ -345,7 +350,7 @@
     parts = lax.axis_size("tp")
     squares = jnp.stack([jnp.sum(query * query, axis=-1), jnp.sum(keys * keys, axis=-1)])
     everyone = [(k, None) for k in range(1, parts)]
-    query_sq, key_sq = jnp.sum(exchange(squares, "tp", everyone, parts, 2), axis=0)
+    query_sq, key_sq = exchange(squares, "tp", everyone, parts, 2)
     full_width = local_width * lax.axis_size("tp")
     query_normed = (query * lax.rsqrt(query_sq / full_width + eps)[:, None] * q_gain).astype(
         jnp.bfloat16

time: 151 us -> 152 us (level)
  no operation moved by 1% of the time
where the time goes in v23:
time: 152 us; the launch traced here: 151 us
  Pallas kernels  103 us (68%)
  matrix products  14.1 us (9%)
  starting transfers between devices  12 us (8%)
  waiting for transfers between devices  8.39 us (6%)
  other arithmetic  7.23 us (5%)
  local copies, waits for them, and re-layouts  6.47 us (4%)
    pallas_call x1, Pallas kernels, gather_seq(): pl.pallas_call(gather_kernel, out_shape=jax.ShapeDtypeStruct((rings, slab...  62.6 us
    pallas_call x1, Pallas kernels, scatter_chips(): pl.pallas_call(scatter_kernel, out_shape=jax.ShapeDtypeStruct(block[1:],...  25 us
    pallas_call x1, Pallas kernels, exchange(): pl.pallas_call(functools.partial(exchange_kernel, axis, offsets), out_sha...  15 us
    ppermute x4, starting transfers between devices, passed_along(): return lax.ppermute(x, axis, pairs)  12 us
    ppermute x4, waiting for transfers between devices, passed_along(): return lax.ppermute(x, axis, pairs)  8.39 us
    dot_general x1, matrix products, shards(): jnp.einsum('tkh,ycdkh->cydt', widened_context, by_owner, preferred_elemen...  6.03 us
    unnamed x19, local copies, waits for them, and re-layouts  6 us
    dot_general x1, matrix products, shards(): jnp.einsum('td,dch->tch', normed, gathered[:, :3], preferred_element_type...  5.33 us
  transfers between devices with their start and end apart: 4, of which 2 were waited for; matrix products, arithmetic and copies ran while one was open for 4% of the time, Pallas kernels for 0%

profile of v23, /device:TPU:15, one launch (start us, length us, event | category | flops | bytes accessed | tf_op | source)
XLA Modules:
  0.0 151.0 jit_solution(9932211184836350778)
XLA Ops:
  0.0 0.0 copy-start
  0.0 0.0 copy-start.2
  0.0 3.0 %copy.18 = bf16[256,3200]{0,1:T(8,128)(2,1)S(1)} copy(bf16[256,3200]{1,0:T(8,128)(2,1)} %param.8) | data formatting | bytes 3276800 | tf_op args[0]
  3.0 0.5 multiply_reduce_fusion
  3.5 0.0 copy-done
  3.6 0.0 copy-done.2
  3.6 0.8 pad_maximum_fusion.1.x_ref
  4.4 62.6 %shard_map.82 = bf16[8,8,50,4,256]{4,3,2,1,0:T(4,128)(2,1)} custom-call(bf16[50,4,256]{2,1,0:T(4,128)(2,1)} %pad_maximum_fusion.1.x_ref), custom_call_target="tpu_custom_call" | custom-call | tf_op jit(solution)/shard_map/pallas_call | solution.py:149
  66.9 0.0 copy-done.6
  67.0 0.0 copy-start.4
  67.0 5.3 %fusion.3 = f32[256,3,256]{0,2,1:T(8,128)S(1)} fusion(bf16[3200,3,256]{2,1,0:T(4,128)(2,1)} %bitcast.44, f32[3200]{0:T(1024)S(1)} %copy-done.6, f32[256]{0:T(256)S(1)} %add_rsqrt_fusion.2, bf16[256,3200]{0,1:T(8,128)(2,1)S(1)} %copy.18), kind=kOutput, calls=%fused_computation.3 | convolution fusion | flops 1261568000 | bytes 7353856 | tf_op jit(solution)/shard_map/td,dch->tch/dot_general | solution.py:341
  72.3 0.0 copy-start.1
  72.3 0.0 copy-start.5
  72.3 0.1 multiply_reduce_fusion.2
  72.4 0.6 pad_maximum_fusion.2.x_ref
  73.0 15.0 %shard_map.83 = f32[2,256]{1,0:T(2,128)} custom-call(f32[2,256]{1,0:T(2,128)} %pad_maximum_fusion.2.x_ref), custom_call_target="tpu_custom_call" | custom-call | tf_op jit(solution)/shard_map/pallas_call | solution.py:304
  88.0 0.8 add_rsqrt_fusion
  88.7 0.0 copy-done.4
  88.7 0.1 fusion.46
  88.9 2.9 %collective-permute-start = (bf16[256,2,256]{0,2,1:T(8,128)(2,1)S(1)}, bf16[256,2,256]{0,2,1:T(8,128)(2,1)}, u32[]{:S(2)}, u32[]{:S(2)}) collective-permute-start(bf16[256,2,256]{0,2,1:T(8,128)(2,1)S(1)} %pad_maximum_fusion), channel_id=1, source_target_pairs={{0,16},{8,24},{16,32},{24,40},{32,48},{40,56},{48,64},{56,72},{64,... | collective-permute-start | bytes 786440 | tf_op jit(solution)/shard_map/ppermute | solution.py:20
  91.8 4.5 %collective-permute-start.1 = (bf16[256,2,256]{0,2,1:T(8,128)(2,1)S(1)}, bf16[256,2,256]{0,2,1:T(8,128)(2,1)}, u32[]{:S(2)}, u32[]{:S(2)}) collective-permute-start(bf16[256,2,256]{0,2,1:T(8,128)(2,1)S(1)} %pad_maximum_fusion), channel_id=1, source_target_pairs={{0,8},{8,16},{16,24},{24,32},{32,40},{40,48},{48,56},{56,64},{64,7... | collective-permute-start | bytes 786440 | tf_op jit(solution)/shard_map/ppermute | solution.py:20
  96.3 1.9 %collective-permute-start.2 = (bf16[256,2,256]{0,2,1:T(8,128)(2,1)S(1)}, bf16[256,2,256]{0,2,1:T(8,128)(2,1)}, u32[]{:S(2)}, u32[]{:S(2)}) collective-permute-start(bf16[256,2,256]{0,2,1:T(8,128)(2,1)S(1)} %pad_maximum_fusion), channel_id=1, source_target_pairs={{8,0},{16,8},{24,16},{32,24},{40,32},{48,40},{56,48},{64,56},{72,6... | collective-permute-start | bytes 786440 | tf_op jit(solution)/shard_map/ppermute | solution.py:20
  98.2 2.7 %collective-permute-start.3 = (bf16[256,2,256]{0,2,1:T(8,128)(2,1)S(1)}, bf16[256,2,256]{0,2,1:T(8,128)(2,1)S(1)}, u32[]{:S(2)}, u32[]{:S(2)}) collective-permute-start(bf16[256,2,256]{0,2,1:T(8,128)(2,1)S(1)} %pad_maximum_fusion), channel_id=1, source_target_pairs={{16,0},{24,8},{32,16},{40,24},{48,32},{56,40},{64,48},{72,56},{80,... | collective-permute-start | bytes 786440 | tf_op jit(solution)/shard_map/ppermute | solution.py:20
  100.9 0.1 copy.23
  101.1 0.0 copy-done.1
  101.1 0.1 dynamic_slice.10
  101.2 0.1 fusion.34
  101.3 0.3 broadcast_compare_fusion
  101.5 0.0 copy-done.5
  101.5 0.1 multiply_convert_fusion.1
  101.6 2.0 %convert_element_type.40 = f32[256,3200]{0,1:T(8,128)} convert(bf16[256,3200]{0,1:T(8,128)(2,1)S(1)} %copy.18) | non-fusion elementwise | flops 819200 | bytes 4915200 | tf_op jit(solution)/shard_map/convert_element_type | solution.py:331
  103.6 0.1 pad_maximum_fusion.3
  103.7 0.0 collective-permute-done
  103.7 1.0 constant_dynamic-update-slice_fusion.4
  104.7 0.0 collective-permute-done.1
  104.7 1.0 constant_dynamic-update-slice_fusion.3
  105.7 2.5 %collective-permute-done.2 = bf16[256,2,256]{0,2,1:T(8,128)(2,1)} collective-permute-done((bf16[256,2,256]{0,2,1:T(8,128)(2,1)S(1)}, bf16[256,2,256]{0,2,1:T(8,128)(2,1)}, u32[]{:S(2)}, u32[]{:S(2)}) %collective-permute-start.2) | collective-permute-done | bytes 262176 | tf_op jit(solution)/shard_map/ppermute | solution.py:20
  108.2 1.0 constant_dynamic-update-slice_fusion.1
  109.2 5.9 %collective-permute-done.3 = bf16[256,2,256]{0,2,1:T(8,128)(2,1)S(1)} collective-permute-done((bf16[256,2,256]{0,2,1:T(8,128)(2,1)S(1)}, bf16[256,2,256]{0,2,1:T(8,128)(2,1)S(1)}, u32[]{:S(2)}, u32[]{:S(2)}) %collective-permute-start.3) | collective-permute-done | bytes 262176 | tf_op jit(solution)/shard_map/ppermute | solution.py:20
  115.1 0.1 fusion.45
  115.2 1.4 fusion.47
  116.6 1.4 fusion.27
  118.0 0.1 copy.25
  118.1 0.0 copy-start.3
  118.1 6.0 %fusion.16.terms_ref = bf16[2,4,400,256]{3,2,1,0:T(8,128)(2,1)} fusion(bf16[4,2,400,4,256]{4,3,2,1,0:T(4,128)(2,1)} %bitcast.45, bf16[256,1,256]{2,0,1:T(8,128)(2,1)S(1)} %copy.25, bf16[4]{0:T(256)(128)(2,1)S(1)} %pad_maximum_fusion.3), kind=kOutput, calls=%fused_computation.17 | convolution fusion | flops 1678802944 | bytes 8323080 | tf_op jit(solution)/shard_map/tkh,ycdkh->cydt/dot_general | solution.py:390
  124.1 25.0 %shard_map.84 = f32[400,256]{1,0:T(8,128)} custom-call(bf16[2,4,400,256]{3,2,1,0:T(8,128)(2,1)} %fusion.16.terms_ref), custom_call_target="tpu_custom_call" | custom-call | tf_op jit(solution)/shard_map/pallas_call | solution.py:233
  149.1 0.0 copy-done.3
  149.1 1.9 %fusion.31 = bf16[256,400]{0,1:T(8,128)(2,1)} fusion(f32[400,256]{1,0:T(8,128)} %shard_map.84, f32[256,3200]{0,1:T(8,128)} %convert_element_type.40, s32[]{:T(128)S(6)} %select_n.16, f32[400]{0:T(512)S(1)} %copy-done.3), kind=kLoop, calls=%fused_computation.27 | loop fusion | flops 307200 | bytes 1025604 | tf_op jit(solution)/shard_map/convert_element_type | solution.py:396
  (10 shorter events, 0.2 us)
Async XLA Ops:
  0.0 3.5 %copy-start = (bf16[50,3,256]{2,0,1:T(8,128)(2,1)S(1)}, bf16[50,3,256]{2,0,1:T(8,128)(2,1)}, u32[]{:S(2)}) copy-start(bf16[50,3,256]{2,0,1:T(8,128)(2,1)} %param.10) | copy-start | bytes 230404
  0.0 3.6 %copy-start.2 = (bf16[256,50]{0,1:T(8,128)(2,1)S(1)}, bf16[256,50]{0,1:T(8,128)(2,1)}, u32[]{:S(2)}) copy-start(bf16[256,50]{0,1:T(8,128)(2,1)} %param.13) | copy-start | bytes 76804
  4.4 62.6 %copy-start.6 = (f32[3200]{0:T(1024)S(1)}, f32[3200]{0:T(1024)}, u32[]{:S(2)}) copy-start(f32[3200]{0:T(1024)} %param.9) | copy-start | bytes 38404
  67.0 21.8 %copy-start.4 = (f32[256]{0:T(256)S(1)}, f32[256]{0:T(256)}, u32[]{:S(2)}) copy-start(f32[256]{0:T(256)} %param.12) | copy-start | bytes 3076
  72.3 28.8 %copy-start.1 = (s32[16384]{0:T(1024)S(1)}, s32[16384]{0:T(1024)}, u32[]{:S(2)}) copy-start(s32[16384]{0:T(1024)} %param.15) | copy-start | bytes 196612
  72.3 29.2 %copy-start.5 = (f32[256]{0:T(256)S(1)}, f32[256]{0:T(256)}, u32[]{:S(2)}) copy-start(f32[256]{0:T(256)} %param.11) | copy-start | bytes 3076
  88.9 14.8 %collective-permute-start = (bf16[256,2,256]{0,2,1:T(8,128)(2,1)S(1)}, bf16[256,2,256]{0,2,1:T(8,128)(2,1)}, u32[]{:S(2)}, u32[]{:S(2)}) collective-permute-start(bf16[256,2,256]{0,2,1:T(8,128)(2,1)S(1)} %pad_maximum_fusion), channel_id=1, source_target_pairs={{0,16},{8,24},{16,32},{24,40},{32,48},{40,56},{48,64},{56,72},{64,... | collective-permute-start | bytes 786440 | tf_op jit(solution)/shard_map/ppermute | solution.py:20
  91.8 12.9 %collective-permute-start.1 = (bf16[256,2,256]{0,2,1:T(8,128)(2,1)S(1)}, bf16[256,2,256]{0,2,1:T(8,128)(2,1)}, u32[]{:S(2)}, u32[]{:S(2)}) collective-permute-start(bf16[256,2,256]{0,2,1:T(8,128)(2,1)S(1)} %pad_maximum_fusion), channel_id=1, source_target_pairs={{0,8},{8,16},{16,24},{24,32},{32,40},{40,48},{48,56},{56,64},{64,7... | collective-permute-start | bytes 786440 | tf_op jit(solution)/shard_map/ppermute | solution.py:20
  96.3 11.9 %collective-permute-start.2 = (bf16[256,2,256]{0,2,1:T(8,128)(2,1)S(1)}, bf16[256,2,256]{0,2,1:T(8,128)(2,1)}, u32[]{:S(2)}, u32[]{:S(2)}) collective-permute-start(bf16[256,2,256]{0,2,1:T(8,128)(2,1)S(1)} %pad_maximum_fusion), channel_id=1, source_target_pairs={{8,0},{16,8},{24,16},{32,24},{40,32},{48,40},{56,48},{64,56},{72,6... | collective-permute-start | bytes 786440 | tf_op jit(solution)/shard_map/ppermute | solution.py:20
  98.2 16.8 %collective-permute-start.3 = (bf16[256,2,256]{0,2,1:T(8,128)(2,1)S(1)}, bf16[256,2,256]{0,2,1:T(8,128)(2,1)S(1)}, u32[]{:S(2)}, u32[]{:S(2)}) collective-permute-start(bf16[256,2,256]{0,2,1:T(8,128)(2,1)S(1)} %pad_maximum_fusion), channel_id=1, source_target_pairs={{16,0},{24,8},{32,16},{40,24},{48,32},{56,40},{64,48},{72,56},{80,... | collective-permute-start | bytes 786440 | tf_op jit(solution)/shard_map/ppermute | solution.py:20
  118.1 31.0 %copy-start.3 = (f32[400]{0:T(512)S(1)}, f32[400]{0:T(512)}, u32[]{:S(2)}) copy-start(f32[400]{0:T(512)} %param.14) | copy-start | bytes 4804

commit v24 on v22

--- a/solution.py
+++ b/solution.py
@@ -214,16 +214,15 @@
                 device_id_type=mesh_id,
             )
         else:
-            copy = pltpu.make_async_copy(sums.at[owner], landed.at[here], local_sems.at[4])
+            continue
         copy.start()
         outgoing.append(copy)
-    for copy in outgoing[:3]:
+    for copy in outgoing:
         copy.wait_send()
         copy.wait_recv()
-    outgoing[3].wait()
-    total = landed[0].astype(jnp.float32)
+    total = sums[here].astype(jnp.float32)
     for chip in range(1, chips):
-        total = total + landed[chip].astype(jnp.float32)
+        total = total + landed[(here + chip) % chips].astype(jnp.float32)
     out_ref[...] = total
 
 
@@ -242,7 +241,7 @@
             pltpu.VMEM(block, jnp.bfloat16),
             pltpu.SemaphoreType.DMA((7,)),
             pltpu.SemaphoreType.DMA((7,)),
-            pltpu.SemaphoreType.DMA((5,)),
+            pltpu.SemaphoreType.DMA((4,)),
         ],
         compiler_params=pltpu.CompilerParams(collective_id=1, has_side_effects=True),
     )(terms)

time: 151 us -> 151 us (level)
  no operation moved by 1% of the time
where the time goes in v24:
time: 151 us
  Pallas kernels  102 us (68%)
  matrix products  14.1 us (9%)
  starting transfers between devices  12 us (8%)
  waiting for transfers between devices  8.39 us (6%)
  other arithmetic  7.22 us (5%)
  local copies, waits for them, and re-layouts  6.47 us (4%)
    pallas_call x1, Pallas kernels, gather_seq(): pl.pallas_call(gather_kernel, out_shape=jax.ShapeDtypeStruct((rings, slab...  62.6 us
    pallas_call x1, Pallas kernels, scatter_chips(): pl.pallas_call(scatter_kernel, out_shape=jax.ShapeDtypeStruct(block[1:],...  25 us
    pallas_call x1, Pallas kernels, exchange(): pl.pallas_call(functools.partial(exchange_kernel, axis, offsets), out_sha...  14.5 us
    ppermute x4, starting transfers between devices, passed_along(): return lax.ppermute(x, axis, pairs)  12 us
    ppermute x4, waiting for transfers between devices, passed_along(): return lax.ppermute(x, axis, pairs)  8.39 us
    dot_general x1, matrix products, shards(): jnp.einsum('tkh,ycdkh->cydt', widened_context, by_owner, preferred_elemen...  6.03 us
    unnamed x19, local copies, waits for them, and re-layouts  6 us
    dot_general x1, matrix products, shards(): jnp.einsum('td,dch->tch', normed, gathered[:, :3], preferred_element_type...  5.33 us
  transfers between devices with their start and end apart: 4, of which 2 were waited for; matrix products, arithmetic and copies ran while one was open for 4% of the time, Pallas kernels for 0%

profile of v24, /device:TPU:15, one launch (start us, length us, event | category | flops | bytes accessed | tf_op | source)
XLA Modules:
  0.0 150.5 jit_solution(18310761630623574487)
XLA Ops:
  0.0 0.0 copy-start
  0.0 0.0 copy-start.2
  0.0 3.0 %copy.18 = bf16[256,3200]{0,1:T(8,128)(2,1)S(1)} copy(bf16[256,3200]{1,0:T(8,128)(2,1)} %param.8) | data formatting | bytes 3276800 | tf_op args[0]
  3.0 0.5 multiply_reduce_fusion
  3.5 0.0 copy-done
  3.6 0.0 copy-done.2
  3.6 0.8 pad_maximum_fusion.1.x_ref
  4.4 62.6 %shard_map.82 = bf16[8,8,50,4,256]{4,3,2,1,0:T(4,128)(2,1)} custom-call(bf16[50,4,256]{2,1,0:T(4,128)(2,1)} %pad_maximum_fusion.1.x_ref), custom_call_target="tpu_custom_call" | custom-call | tf_op jit(solution)/shard_map/pallas_call | solution.py:149
  66.9 0.0 copy-done.6
  67.0 0.0 copy-start.4
  67.0 5.3 %fusion.3 = f32[256,3,256]{0,2,1:T(8,128)S(1)} fusion(bf16[3200,3,256]{2,1,0:T(4,128)(2,1)} %bitcast.44, f32[3200]{0:T(1024)S(1)} %copy-done.6, f32[256]{0:T(256)S(1)} %add_rsqrt_fusion, bf16[256,3200]{0,1:T(8,128)(2,1)S(1)} %copy.18), kind=kOutput, calls=%fused_computation.3 | convolution fusion | flops 1261568000 | bytes 7353856 | tf_op jit(solution)/shard_map/td,dch->tch/dot_general | solution.py:335
  72.3 0.0 copy-start.1
  72.3 0.0 copy-start.5
  72.3 0.1 multiply_reduce_fusion.2
  72.4 0.6 pad_maximum_fusion.2.x_ref
  73.0 14.5 %shard_map.83 = f32[8,2,256]{2,1,0:T(2,128)} custom-call(f32[2,256]{1,0:T(2,128)} %pad_maximum_fusion.2.x_ref), custom_call_target="tpu_custom_call" | custom-call | tf_op jit(solution)/shard_map/pallas_call | solution.py:299
  87.5 0.7 reduce_sum.48
  88.2 0.0 copy-done.4
  88.3 0.1 fusion.50
  88.4 2.9 %collective-permute-start = (bf16[256,2,256]{0,2,1:T(8,128)(2,1)S(1)}, bf16[256,2,256]{0,2,1:T(8,128)(2,1)}, u32[]{:S(2)}, u32[]{:S(2)}) collective-permute-start(bf16[256,2,256]{0,2,1:T(8,128)(2,1)S(1)} %pad_maximum_fusion), channel_id=1, source_target_pairs={{0,16},{8,24},{16,32},{24,40},{32,48},{40,56},{48,64},{56,72},{64,... | collective-permute-start | bytes 786440 | tf_op jit(solution)/shard_map/ppermute | solution.py:20
  91.3 4.5 %collective-permute-start.1 = (bf16[256,2,256]{0,2,1:T(8,128)(2,1)S(1)}, bf16[256,2,256]{0,2,1:T(8,128)(2,1)}, u32[]{:S(2)}, u32[]{:S(2)}) collective-permute-start(bf16[256,2,256]{0,2,1:T(8,128)(2,1)S(1)} %pad_maximum_fusion), channel_id=1, source_target_pairs={{0,8},{8,16},{16,24},{24,32},{32,40},{40,48},{48,56},{56,64},{64,7... | collective-permute-start | bytes 786440 | tf_op jit(solution)/shard_map/ppermute | solution.py:20
  95.8 1.9 %collective-permute-start.2 = (bf16[256,2,256]{0,2,1:T(8,128)(2,1)S(1)}, bf16[256,2,256]{0,2,1:T(8,128)(2,1)}, u32[]{:S(2)}, u32[]{:S(2)}) collective-permute-start(bf16[256,2,256]{0,2,1:T(8,128)(2,1)S(1)} %pad_maximum_fusion), channel_id=1, source_target_pairs={{8,0},{16,8},{24,16},{32,24},{40,32},{48,40},{56,48},{64,56},{72,6... | collective-permute-start | bytes 786440 | tf_op jit(solution)/shard_map/ppermute | solution.py:20
  97.8 2.7 %collective-permute-start.3 = (bf16[256,2,256]{0,2,1:T(8,128)(2,1)S(1)}, bf16[256,2,256]{0,2,1:T(8,128)(2,1)S(1)}, u32[]{:S(2)}, u32[]{:S(2)}) collective-permute-start(bf16[256,2,256]{0,2,1:T(8,128)(2,1)S(1)} %pad_maximum_fusion), channel_id=1, source_target_pairs={{16,0},{24,8},{32,16},{40,24},{48,32},{56,40},{64,48},{72,56},{80,... | collective-permute-start | bytes 786440 | tf_op jit(solution)/shard_map/ppermute | solution.py:20
  100.5 0.1 copy.23
  100.6 0.0 copy-done.1
  100.6 0.1 dynamic_slice.10
  100.7 0.1 fusion.34
  100.8 0.3 broadcast_compare_fusion
  101.0 0.0 copy-done.5
  101.0 0.1 multiply_convert_fusion.1
  101.2 2.0 %convert_element_type.40 = f32[256,3200]{0,1:T(8,128)} convert(bf16[256,3200]{0,1:T(8,128)(2,1)S(1)} %copy.18) | non-fusion elementwise | flops 819200 | bytes 4915200 | tf_op jit(solution)/shard_map/convert_element_type | solution.py:325
  103.2 0.1 pad_maximum_fusion.3
  103.2 0.0 collective-permute-done
  103.2 1.0 constant_dynamic-update-slice_fusion.4
  104.2 0.0 collective-permute-done.1
  104.2 1.0 constant_dynamic-update-slice_fusion.3
  105.2 2.5 %collective-permute-done.2 = bf16[256,2,256]{0,2,1:T(8,128)(2,1)} collective-permute-done((bf16[256,2,256]{0,2,1:T(8,128)(2,1)S(1)}, bf16[256,2,256]{0,2,1:T(8,128)(2,1)}, u32[]{:S(2)}, u32[]{:S(2)}) %collective-permute-start.2) | collective-permute-done | bytes 262176 | tf_op jit(solution)/shard_map/ppermute | solution.py:20
  107.7 1.0 constant_dynamic-update-slice_fusion.1
  108.7 5.9 %collective-permute-done.3 = bf16[256,2,256]{0,2,1:T(8,128)(2,1)S(1)} collective-permute-done((bf16[256,2,256]{0,2,1:T(8,128)(2,1)S(1)}, bf16[256,2,256]{0,2,1:T(8,128)(2,1)S(1)}, u32[]{:S(2)}, u32[]{:S(2)}) %collective-permute-start.3) | collective-permute-done | bytes 262176 | tf_op jit(solution)/shard_map/ppermute | solution.py:20
  114.6 0.1 fusion.49
  114.7 1.4 fusion.51
  116.1 1.4 fusion.27
  117.5 0.1 copy.25
  117.6 0.0 copy-start.3
  117.6 6.0 %fusion.16.terms_ref = bf16[2,4,400,256]{3,2,1,0:T(8,128)(2,1)} fusion(bf16[4,2,400,4,256]{4,3,2,1,0:T(4,128)(2,1)} %bitcast.45, bf16[256,1,256]{2,0,1:T(8,128)(2,1)S(1)} %copy.25, bf16[4]{0:T(256)(128)(2,1)S(1)} %pad_maximum_fusion.3), kind=kOutput, calls=%fused_computation.17 | convolution fusion | flops 1678802944 | bytes 8323080 | tf_op jit(solution)/shard_map/tkh,ycdkh->cydt/dot_general | solution.py:384
  123.6 25.0 %shard_map.84 = f32[400,256]{1,0:T(8,128)} custom-call(bf16[2,4,400,256]{3,2,1,0:T(8,128)(2,1)} %fusion.16.terms_ref), custom_call_target="tpu_custom_call" | custom-call | tf_op jit(solution)/shard_map/pallas_call | solution.py:232
  148.6 0.0 copy-done.3
  148.6 1.9 %fusion.31 = bf16[256,400]{0,1:T(8,128)(2,1)} fusion(f32[400,256]{1,0:T(8,128)} %shard_map.84, f32[256,3200]{0,1:T(8,128)} %convert_element_type.40, s32[]{:T(128)S(6)} %select_n.16, f32[400]{0:T(512)S(1)} %copy-done.3), kind=kLoop, calls=%fused_computation.27 | loop fusion | flops 307200 | bytes 1025604 | tf_op jit(solution)/shard_map/convert_element_type | solution.py:390
  (11 shorter events, 0.2 us)
Async XLA Ops:
  0.0 3.5 %copy-start = (bf16[50,3,256]{2,0,1:T(8,128)(2,1)S(1)}, bf16[50,3,256]{2,0,1:T(8,128)(2,1)}, u32[]{:S(2)}) copy-start(bf16[50,3,256]{2,0,1:T(8,128)(2,1)} %param.10) | copy-start | bytes 230404
  0.0 3.6 %copy-start.2 = (bf16[256,50]{0,1:T(8,128)(2,1)S(1)}, bf16[256,50]{0,1:T(8,128)(2,1)}, u32[]{:S(2)}) copy-start(bf16[256,50]{0,1:T(8,128)(2,1)} %param.13) | copy-start | bytes 76804
  4.4 62.6 %copy-start.6 = (f32[3200]{0:T(1024)S(1)}, f32[3200]{0:T(1024)}, u32[]{:S(2)}) copy-start(f32[3200]{0:T(1024)} %param.9) | copy-start | bytes 38404
  67.0 21.3 %copy-start.4 = (f32[256]{0:T(256)S(1)}, f32[256]{0:T(256)}, u32[]{:S(2)}) copy-start(f32[256]{0:T(256)} %param.12) | copy-start | bytes 3076
  72.3 28.3 %copy-start.1 = (s32[16384]{0:T(1024)S(1)}, s32[16384]{0:T(1024)}, u32[]{:S(2)}) copy-start(s32[16384]{0:T(1024)} %param.15) | copy-start | bytes 196612
  72.3 28.7 %copy-start.5 = (f32[256]{0:T(256)S(1)}, f32[256]{0:T(256)}, u32[]{:S(2)}) copy-start(f32[256]{0:T(256)} %param.11) | copy-start | bytes 3076
  88.4 14.8 %collective-permute-start = (bf16[256,2,256]{0,2,1:T(8,128)(2,1)S(1)}, bf16[256,2,256]{0,2,1:T(8,128)(2,1)}, u32[]{:S(2)}, u32[]{:S(2)}) collective-permute-start(bf16[256,2,256]{0,2,1:T(8,128)(2,1)S(1)} %pad_maximum_fusion), channel_id=1, source_target_pairs={{0,16},{8,24},{16,32},{24,40},{32,48},{40,56},{48,64},{56,72},{64,... | collective-permute-start | bytes 786440 | tf_op jit(solution)/shard_map/ppermute | solution.py:20
  91.3 12.9 %collective-permute-start.1 = (bf16[256,2,256]{0,2,1:T(8,128)(2,1)S(1)}, bf16[256,2,256]{0,2,1:T(8,128)(2,1)}, u32[]{:S(2)}, u32[]{:S(2)}) collective-permute-start(bf16[256,2,256]{0,2,1:T(8,128)(2,1)S(1)} %pad_maximum_fusion), channel_id=1, source_target_pairs={{0,8},{8,16},{16,24},{24,32},{32,40},{40,48},{48,56},{56,64},{64,7... | collective-permute-start | bytes 786440 | tf_op jit(solution)/shard_map/ppermute | solution.py:20
  95.8 11.9 %collective-permute-start.2 = (bf16[256,2,256]{0,2,1:T(8,128)(2,1)S(1)}, bf16[256,2,256]{0,2,1:T(8,128)(2,1)}, u32[]{:S(2)}, u32[]{:S(2)}) collective-permute-start(bf16[256,2,256]{0,2,1:T(8,128)(2,1)S(1)} %pad_maximum_fusion), channel_id=1, source_target_pairs={{8,0},{16,8},{24,16},{32,24},{40,32},{48,40},{56,48},{64,56},{72,6... | collective-permute-start | bytes 786440 | tf_op jit(solution)/shard_map/ppermute | solution.py:20
  97.8 16.8 %collective-permute-start.3 = (bf16[256,2,256]{0,2,1:T(8,128)(2,1)S(1)}, bf16[256,2,256]{0,2,1:T(8,128)(2,1)S(1)}, u32[]{:S(2)}, u32[]{:S(2)}) collective-permute-start(bf16[256,2,256]{0,2,1:T(8,128)(2,1)S(1)} %pad_maximum_fusion), channel_id=1, source_target_pairs={{16,0},{24,8},{32,16},{40,24},{48,32},{56,40},{64,48},{72,56},{80,... | collective-permute-start | bytes 786440 | tf_op jit(solution)/shard_map/ppermute | solution.py:20
  117.6 31.0 %copy-start.3 = (f32[400]{0:T(512)S(1)}, f32[400]{0:T(512)}, u32[]{:S(2)}) copy-start(f32[400]{0:T(512)} %param.14) | copy-start | bytes 4804

commit v25 on v24

--- a/solution.py
+++ b/solution.py
@@ -299,7 +299,7 @@
     return pl.pallas_call(
         functools.partial(exchange_kernel, axis, offsets),
         out_shape=jax.ShapeDtypeStruct((slots,) + block.shape, block.dtype),
-        in_specs=[pl.BlockSpec(memory_space=pl.ANY)],
+        in_specs=[pl.BlockSpec(memory_space=pltpu.VMEM)],
         out_specs=pl.BlockSpec(memory_space=pl.ANY),
         scratch_shapes=[
             pltpu.SemaphoreType.DMA((count,)),

time: 151 us -> 152 us (level)
  no operation moved by 1% of the time
where the time goes in v25:
time: 152 us; the launch traced here: 151 us
  Pallas kernels  102 us (67%)
  matrix products  14.1 us (9%)
  starting transfers between devices  12.1 us (8%)
  waiting for transfers between devices  8.39 us (6%)
  other arithmetic  7.22 us (5%)
  local copies, waits for them, and re-layouts  6.47 us (4%)
    pallas_call x1, Pallas kernels, gather_seq(): pl.pallas_call(gather_kernel, out_shape=jax.ShapeDtypeStruct((rings, slab...  62.6 us
    pallas_call x1, Pallas kernels, scatter_chips(): pl.pallas_call(scatter_kernel, out_shape=jax.ShapeDtypeStruct(block[1:],...  24.9 us
    pallas_call x1, Pallas kernels, exchange(): pl.pallas_call(functools.partial(exchange_kernel, axis, offsets), out_sha...  14.8 us
    ppermute x4, starting transfers between devices, passed_along(): return lax.ppermute(x, axis, pairs)  12.1 us
    ppermute x4, waiting for transfers between devices, passed_along(): return lax.ppermute(x, axis, pairs)  8.39 us
    dot_general x1, matrix products, shards(): jnp.einsum('tkh,ycdkh->cydt', widened_context, by_owner, preferred_elemen...  6.03 us
    unnamed x19, local copies, waits for them, and re-layouts  6 us
    dot_general x1, matrix products, shards(): jnp.einsum('td,dch->tch', normed, gathered[:, :3], preferred_element_type...  5.33 us
  transfers between devices with their start and end apart: 4, of which 2 were waited for; matrix products, arithmetic and copies ran while one was open for 4% of the time, Pallas kernels for 0%

profile of v25, /device:TPU:15, one launch (start us, length us, event | category | flops | bytes accessed | tf_op | source)
XLA Modules:
  0.0 150.9 jit_solution(7230208812533857813)
XLA Ops:
  0.0 0.0 copy-start
  0.0 0.0 copy-start.2
  0.0 3.0 %copy.18 = bf16[256,3200]{0,1:T(8,128)(2,1)S(1)} copy(bf16[256,3200]{1,0:T(8,128)(2,1)} %param.8) | data formatting | bytes 3276800 | tf_op args[0]
  3.0 0.5 multiply_reduce_fusion
  3.5 0.0 copy-done
  3.6 0.0 copy-done.2
  3.6 0.8 pad_maximum_fusion.1.x_ref
  4.4 62.6 %shard_map.82 = bf16[8,8,50,4,256]{4,3,2,1,0:T(4,128)(2,1)} custom-call(bf16[50,4,256]{2,1,0:T(4,128)(2,1)} %pad_maximum_fusion.1.x_ref), custom_call_target="tpu_custom_call" | custom-call | tf_op jit(solution)/shard_map/pallas_call | solution.py:149
  66.9 0.0 copy-done.6
  67.0 0.0 copy-start.4
  67.0 5.3 %fusion.3 = f32[256,3,256]{0,2,1:T(8,128)S(1)} fusion(bf16[3200,3,256]{2,1,0:T(4,128)(2,1)} %bitcast.44, f32[3200]{0:T(1024)S(1)} %copy-done.6, f32[256]{0:T(256)S(1)} %add_rsqrt_fusion, bf16[256,3200]{0,1:T(8,128)(2,1)S(1)} %copy.18), kind=kOutput, calls=%fused_computation.3 | convolution fusion | flops 1261568000 | bytes 7353856 | tf_op jit(solution)/shard_map/td,dch->tch/dot_general | solution.py:335
  72.3 0.0 copy-start.1
  72.3 0.0 copy-start.5
  72.3 0.1 multiply_reduce_fusion.2
  72.4 0.6 pad_maximum_fusion.2.x_ref
  73.0 14.8 %shard_map.83 = f32[8,2,256]{2,1,0:T(2,128)} custom-call(f32[2,256]{1,0:T(2,128)} %pad_maximum_fusion.2.x_ref), custom_call_target="tpu_custom_call" | custom-call | tf_op jit(solution)/shard_map/pallas_call | solution.py:299
  87.8 0.7 reduce_sum.48
  88.6 0.0 copy-done.4
  88.6 0.1 fusion.50
  88.7 2.9 %collective-permute-start = (bf16[256,2,256]{0,2,1:T(8,128)(2,1)S(1)}, bf16[256,2,256]{0,2,1:T(8,128)(2,1)}, u32[]{:S(2)}, u32[]{:S(2)}) collective-permute-start(bf16[256,2,256]{0,2,1:T(8,128)(2,1)S(1)} %pad_maximum_fusion), channel_id=1, source_target_pairs={{0,16},{8,24},{16,32},{24,40},{32,48},{40,56},{48,64},{56,72},{64,... | collective-permute-start | bytes 786440 | tf_op jit(solution)/shard_map/ppermute | solution.py:20
  91.6 4.6 %collective-permute-start.1 = (bf16[256,2,256]{0,2,1:T(8,128)(2,1)S(1)}, bf16[256,2,256]{0,2,1:T(8,128)(2,1)}, u32[]{:S(2)}, u32[]{:S(2)}) collective-permute-start(bf16[256,2,256]{0,2,1:T(8,128)(2,1)S(1)} %pad_maximum_fusion), channel_id=1, source_target_pairs={{0,8},{8,16},{16,24},{24,32},{32,40},{40,48},{48,56},{56,64},{64,7... | collective-permute-start | bytes 786440 | tf_op jit(solution)/shard_map/ppermute | solution.py:20
  96.2 1.9 %collective-permute-start.2 = (bf16[256,2,256]{0,2,1:T(8,128)(2,1)S(1)}, bf16[256,2,256]{0,2,1:T(8,128)(2,1)}, u32[]{:S(2)}, u32[]{:S(2)}) collective-permute-start(bf16[256,2,256]{0,2,1:T(8,128)(2,1)S(1)} %pad_maximum_fusion), channel_id=1, source_target_pairs={{8,0},{16,8},{24,16},{32,24},{40,32},{48,40},{56,48},{64,56},{72,6... | collective-permute-start | bytes 786440 | tf_op jit(solution)/shard_map/ppermute | solution.py:20
  98.1 2.7 %collective-permute-start.3 = (bf16[256,2,256]{0,2,1:T(8,128)(2,1)S(1)}, bf16[256,2,256]{0,2,1:T(8,128)(2,1)S(1)}, u32[]{:S(2)}, u32[]{:S(2)}) collective-permute-start(bf16[256,2,256]{0,2,1:T(8,128)(2,1)S(1)} %pad_maximum_fusion), channel_id=1, source_target_pairs={{16,0},{24,8},{32,16},{40,24},{48,32},{56,40},{64,48},{72,56},{80,... | collective-permute-start | bytes 786440 | tf_op jit(solution)/shard_map/ppermute | solution.py:20
  100.8 0.1 copy.23
  101.0 0.0 copy-done.1
  101.0 0.1 dynamic_slice.10
  101.1 0.1 fusion.34
  101.2 0.3 broadcast_compare_fusion
  101.4 0.0 copy-done.5
  101.4 0.1 multiply_convert_fusion.1
  101.5 2.0 %convert_element_type.40 = f32[256,3200]{0,1:T(8,128)} convert(bf16[256,3200]{0,1:T(8,128)(2,1)S(1)} %copy.18) | non-fusion elementwise | flops 819200 | bytes 4915200 | tf_op jit(solution)/shard_map/convert_element_type | solution.py:325
  103.5 0.1 pad_maximum_fusion.3
  103.6 0.0 collective-permute-done
  103.6 1.0 constant_dynamic-update-slice_fusion.4
  104.6 0.0 collective-permute-done.1
  104.6 1.0 constant_dynamic-update-slice_fusion.3
  105.6 2.5 %collective-permute-done.2 = bf16[256,2,256]{0,2,1:T(8,128)(2,1)} collective-permute-done((bf16[256,2,256]{0,2,1:T(8,128)(2,1)S(1)}, bf16[256,2,256]{0,2,1:T(8,128)(2,1)}, u32[]{:S(2)}, u32[]{:S(2)}) %collective-permute-start.2) | collective-permute-done | bytes 262176 | tf_op jit(solution)/shard_map/ppermute | solution.py:20
  108.1 1.0 constant_dynamic-update-slice_fusion.1
  109.0 5.9 %collective-permute-done.3 = bf16[256,2,256]{0,2,1:T(8,128)(2,1)S(1)} collective-permute-done((bf16[256,2,256]{0,2,1:T(8,128)(2,1)S(1)}, bf16[256,2,256]{0,2,1:T(8,128)(2,1)S(1)}, u32[]{:S(2)}, u32[]{:S(2)}) %collective-permute-start.3) | collective-permute-done | bytes 262176 | tf_op jit(solution)/shard_map/ppermute | solution.py:20
  115.0 0.1 fusion.49
  115.1 1.4 fusion.51
  116.5 1.4 fusion.27
  117.9 0.1 copy.25
  118.0 0.0 copy-start.3
  118.0 6.0 %fusion.16.terms_ref = bf16[2,4,400,256]{3,2,1,0:T(8,128)(2,1)} fusion(bf16[4,2,400,4,256]{4,3,2,1,0:T(4,128)(2,1)} %bitcast.45, bf16[256,1,256]{2,0,1:T(8,128)(2,1)S(1)} %copy.25, bf16[4]{0:T(256)(128)(2,1)S(1)} %pad_maximum_fusion.3), kind=kOutput, calls=%fused_computation.17 | convolution fusion | flops 1678802944 | bytes 8323080 | tf_op jit(solution)/shard_map/tkh,ycdkh->cydt/dot_general | solution.py:384
  124.0 24.9 %shard_map.84 = f32[400,256]{1,0:T(8,128)} custom-call(bf16[2,4,400,256]{3,2,1,0:T(8,128)(2,1)} %fusion.16.terms_ref), custom_call_target="tpu_custom_call" | custom-call | tf_op jit(solution)/shard_map/pallas_call | solution.py:232
  148.9 0.0 copy-done.3
  149.0 1.9 %fusion.31 = bf16[256,400]{0,1:T(8,128)(2,1)} fusion(f32[400,256]{1,0:T(8,128)} %shard_map.84, f32[256,3200]{0,1:T(8,128)} %convert_element_type.40, s32[]{:T(128)S(6)} %select_n.16, f32[400]{0:T(512)S(1)} %copy-done.3), kind=kLoop, calls=%fused_computation.27 | loop fusion | flops 307200 | bytes 1025604 | tf_op jit(solution)/shard_map/convert_element_type | solution.py:390
  (11 shorter events, 0.2 us)
Async XLA Ops:
  0.0 3.5 %copy-start = (bf16[50,3,256]{2,0,1:T(8,128)(2,1)S(1)}, bf16[50,3,256]{2,0,1:T(8,128)(2,1)}, u32[]{:S(2)}) copy-start(bf16[50,3,256]{2,0,1:T(8,128)(2,1)} %param.10) | copy-start | bytes 230404
  0.0 3.6 %copy-start.2 = (bf16[256,50]{0,1:T(8,128)(2,1)S(1)}, bf16[256,50]{0,1:T(8,128)(2,1)}, u32[]{:S(2)}) copy-start(bf16[256,50]{0,1:T(8,128)(2,1)} %param.13) | copy-start | bytes 76804
  4.4 62.6 %copy-start.6 = (f32[3200]{0:T(1024)S(1)}, f32[3200]{0:T(1024)}, u32[]{:S(2)}) copy-start(f32[3200]{0:T(1024)} %param.9) | copy-start | bytes 38404
  67.0 21.6 %copy-start.4 = (f32[256]{0:T(256)S(1)}, f32[256]{0:T(256)}, u32[]{:S(2)}) copy-start(f32[256]{0:T(256)} %param.12) | copy-start | bytes 3076
  72.3 28.7 %copy-start.1 = (s32[16384]{0:T(1024)S(1)}, s32[16384]{0:T(1024)}, u32[]{:S(2)}) copy-start(s32[16384]{0:T(1024)} %param.15) | copy-start | bytes 196612
  72.3 29.1 %copy-start.5 = (f32[256]{0:T(256)S(1)}, f32[256]{0:T(256)}, u32[]{:S(2)}) copy-start(f32[256]{0:T(256)} %param.11) | copy-start | bytes 3076
  88.7 14.9 %collective-permute-start = (bf16[256,2,256]{0,2,1:T(8,128)(2,1)S(1)}, bf16[256,2,256]{0,2,1:T(8,128)(2,1)}, u32[]{:S(2)}, u32[]{:S(2)}) collective-permute-start(bf16[256,2,256]{0,2,1:T(8,128)(2,1)S(1)} %pad_maximum_fusion), channel_id=1, source_target_pairs={{0,16},{8,24},{16,32},{24,40},{32,48},{40,56},{48,64},{56,72},{64,... | collective-permute-start | bytes 786440 | tf_op jit(solution)/shard_map/ppermute | solution.py:20
  91.6 13.0 %collective-permute-start.1 = (bf16[256,2,256]{0,2,1:T(8,128)(2,1)S(1)}, bf16[256,2,256]{0,2,1:T(8,128)(2,1)}, u32[]{:S(2)}, u32[]{:S(2)}) collective-permute-start(bf16[256,2,256]{0,2,1:T(8,128)(2,1)S(1)} %pad_maximum_fusion), channel_id=1, source_target_pairs={{0,8},{8,16},{16,24},{24,32},{32,40},{40,48},{48,56},{56,64},{64,7... | collective-permute-start | bytes 786440 | tf_op jit(solution)/shard_map/ppermute | solution.py:20
  96.2 11.9 %collective-permute-start.2 = (bf16[256,2,256]{0,2,1:T(8,128)(2,1)S(1)}, bf16[256,2,256]{0,2,1:T(8,128)(2,1)}, u32[]{:S(2)}, u32[]{:S(2)}) collective-permute-start(bf16[256,2,256]{0,2,1:T(8,128)(2,1)S(1)} %pad_maximum_fusion), channel_id=1, source_target_pairs={{8,0},{16,8},{24,16},{32,24},{40,32},{48,40},{56,48},{64,56},{72,6... | collective-permute-start | bytes 786440 | tf_op jit(solution)/shard_map/ppermute | solution.py:20
  98.1 16.8 %collective-permute-start.3 = (bf16[256,2,256]{0,2,1:T(8,128)(2,1)S(1)}, bf16[256,2,256]{0,2,1:T(8,128)(2,1)S(1)}, u32[]{:S(2)}, u32[]{:S(2)}) collective-permute-start(bf16[256,2,256]{0,2,1:T(8,128)(2,1)S(1)} %pad_maximum_fusion), channel_id=1, source_target_pairs={{16,0},{24,8},{32,16},{40,24},{48,32},{56,40},{64,48},{72,56},{80,... | collective-permute-start | bytes 786440 | tf_op jit(solution)/shard_map/ppermute | solution.py:20
  118.0 31.0 %copy-start.3 = (f32[400]{0:T(512)S(1)}, f32[400]{0:T(512)}, u32[]{:S(2)}) copy-start(f32[400]{0:T(512)} %param.14) | copy-start | bytes 4804
